TPU v7x, 32 devices: a whole 2x2x4 slice. The times are simulated.
32 devices in a mesh: dp: 2 (over x), zero: 16 (over z, y, core).
Axes of the slice: x: 2, y: 2, z: 4, core: 2. Of those that a mesh axis runs over, the one named last changes fastest.
Arguments:
- token_ids: int32 [128, 2, 128], P(('dp', 'zero')), may hold values from 0 to 30527
- lengths: int32 [128, 2], P(('dp', 'zero')), may hold values from 32 to 128
- false_neg: int32 [128, 128], P(('dp', 'zero')), may hold values 0 or 1
- pair_index: int32 [128], P(('dp', 'zero')), may hold values from -1 to 127, as said below
- word_table: float32 [30528, 512], P('zero'), may hold values from -0.3125 to 0.3125
- vectors: float32 [78848], P('zero'), may hold values from -0.4 to 1.4, as said below
- attn_w: float32 [2, 512, 2048], P(None, 'zero'), may hold values from -0.25 to 0.25
- ffn_w: float32 [2, 512, 4096], P(None, 'zero'), may hold values from -0.25 to 0.25
- word_first: float32 [30528, 512], P('zero'), may hold values from -0.0012207031 to 0.0012207031
- vector_first: float32 [78848], P('zero'), may hold values from -0.0012207031 to 0.0012207031
- attn_first: float32 [2, 512, 2048], P(None, 'zero'), may hold values from -0.0012207031 to 0.0012207031
- ffn_first: float32 [2, 512, 4096], P(None, 'zero'), may hold values from -0.0012207031 to 0.0012207031
- word_second: float32 [30528, 512], P('zero'), may hold values from 4.5453223e-08 to 1.818129e-07
- vector_second: float32 [78848], P('zero'), may hold values from 2.272661e-06 to 3.6362577e-05
- attn_second: float32 [2, 512, 2048], P(None, 'zero'), may hold values from 4.5453223e-08 to 1.818129e-07
- ffn_second: float32 [2, 512, 4096], P(None, 'zero'), may hold values from 4.5453223e-08 to 1.818129e-07
Outputs:
- loss: float32 [], replicated
- grad_norm: float32 [], replicated
- word_new: float32 [30528, 512], P('zero')
- vector_new: float32 [78848], P('zero')
- attn_new: float32 [2, 512, 2048], P(None, 'zero')
- ffn_new: float32 [2, 512, 4096], P(None, 'zero')
- word_low: bfloat16 [30528, 512], P('zero')
- vector_low: bfloat16 [78848], P('zero')
- attn_low: bfloat16 [2, 512, 2048], P(None, 'zero')
- ffn_low: bfloat16 [2, 512, 4096], P(None, 'zero')
- word_first_new: float32 [30528, 512], P('zero')
- vector_first_new: float32 [78848], P('zero')
- attn_first_new: float32 [2, 512, 2048], P(None, 'zero')
- ffn_first_new: float32 [2, 512, 4096], P(None, 'zero')
- word_second_new: float32 [30528, 512], P('zero')
- vector_second_new: float32 [78848], P('zero')
- attn_second_new: float32 [2, 512, 2048], P(None, 'zero')
- ffn_second_new: float32 [2, 512, 4096], P(None, 'zero')
- down_bias_grad: float32 [2, 512], P(None, 'zero')
Inputs may be any that keep to these rules, and one draw needn't show every extreme that they name: `pair_index`: each positive row is named by at most one anchor; anchor 0 always counts. `vectors`: gains lie near 1; biases, shifts and positions near 0.
All inputs are finite; a program needn't handle non-finite values. No bound on the sum of `false_neg` on one device may be relied on, other than what follows from the above.
Results may differ from a plain program's by a relative error of at most 0.015.
The roundings to bfloat16 on the way count: a program that leaves them out, or rounds other values in their place, can miss the bound.
Values may be sent and summed in bfloat16 or wider, within the bound.
A program may use at most 320 MiB of HBM per device.

v0:
```python
import functools

import jax
import jax.numpy as jnp
from jax import lax
from jax.sharding import PartitionSpec as P

D = 512
HEADS = 8
HD = 64
FF = 2048
SEQ = 128
LAYERS = 2
ADAM_STEP = 5


SOFTMAX_TEMP = 0.05
CLIP_NORM = 1.0
LEARN_RATE = 0.02
VECTOR_RATE = 0.15
BETA_ONE = 0.5
BETA_TWO = 0.5
WEIGHT_DECAY = 0.01
ADAM_EPS = 1e-08
NORM_EPS = 1e-06
MASKED = -1000000000.0


def build_low():

    def rounder(value):
        return lax.optimization_barrier(value.astype(jnp.bfloat16)).astype(jnp.float32)

    def keep_fwd(value):
        return (rounder(value), None)

    def pass_bwd(kept, grad):
        return (grad,)

    wrapped = jax.custom_vjp(rounder)
    wrapped.defvjp(keep_fwd, pass_bwd)
    return wrapped


def build_low_back():

    def identity_fn(value):
        return value

    def keep_fwd(value):
        return (value, None)

    def round_bwd(kept, grad):
        return (low(grad),)

    wrapped = jax.custom_vjp(identity_fn)
    wrapped.defvjp(keep_fwd, round_bwd)
    return wrapped


def low(value):
    return build_low()(value)


def low_back(value):
    return build_low_back()(value)


def rounded(value):
    return low(low_back(value))


def matmul(left, right):
    return jnp.dot(left, right, preferred_element_type=jnp.float32)


def einsum_plain(form, left, right):
    return jnp.einsum(form, left, right, preferred_element_type=jnp.float32)


def split_vectors(vec_all):
    offset = SEQ * D
    position = vec_all[:offset].reshape(SEQ, D)
    emb_gain = vec_all[offset : offset + D]
    emb_shift = vec_all[offset + D : offset + 2 * D]
    offset = offset + 2 * D
    layer_parts = []
    for layer_index in range(LAYERS):
        pieces = []
        for length_now in (D, D, D, D, D, FF, D, D, D):
            pieces.append(vec_all[offset : offset + length_now])
            offset = offset + length_now
        layer_parts.append(pieces)
    return (position, emb_gain, emb_shift, layer_parts)


def layer_norm(values, gain, shift):
    center = values - jnp.mean(values, axis=-1, keepdims=True)
    spread = jnp.mean(center * center, axis=-1, keepdims=True)
    return center * lax.rsqrt(spread + NORM_EPS) * gain + shift


def embed_tokens(rows, vec_all):
    position, emb_gain, emb_shift, layer_parts = split_vectors(vec_all)
    return layer_norm(low_back(rows) + position[None], emb_gain, emb_shift)


def encoder_layer(hidden, attn_weights, ffn_weights, vec_all, key_mask, layer_index):
    q_bias, v_bias, o_bias, gain_one, shift_one, up_bias, down_bias, gain_two, second_shift = (
        split_vectors(vec_all)[3][layer_index]
    )
    sequence_count = hidden.shape[0]
    packed = matmul(low(hidden), attn_weights[:, : 3 * D])
    packed = rounded(packed + jnp.concatenate([q_bias, jnp.zeros_like(q_bias), v_bias]))
    heads_shape = (sequence_count, SEQ, HEADS, HD)
    queries = packed[..., :D].reshape(heads_shape)
    key_rows = packed[..., D : 2 * D].reshape(heads_shape)
    value_rows = packed[..., 2 * D :].reshape(heads_shape)
    scores = low_back(einsum_plain("nqhd,nkhd->nhqk", queries, key_rows) * HD ** (-0.5))
    scores = jnp.where(key_mask[:, None, None, :], scores, MASKED)
    attention = low(jax.nn.softmax(scores, axis=-1))
    context = rounded(
        einsum_plain("nhqk,nkhd->nqhd", attention, value_rows).reshape(sequence_count, SEQ, D)
    )
    attended = low_back(matmul(context, attn_weights[:, 3 * D :]) + o_bias)
    first_out = layer_norm(hidden + attended, gain_one, shift_one)
    upward = low_back(matmul(low(first_out), ffn_weights[:, :FF]) + up_bias)
    active = rounded(jax.nn.gelu(upward, approximate=True))
    downward = low_back(einsum_plain("nsf,df->nsd", active, ffn_weights[:, FF:]) + down_bias)
    return layer_norm(first_out + downward, gain_two, second_shift)


def pool_rows(hidden, key_mask, seq_lengths):
    share = key_mask.astype(jnp.float32) / seq_lengths.astype(jnp.float32)[:, None]
    return jnp.sum(hidden * share[:, :, None], axis=1)


def normalized_rows(rows):
    return rows * lax.rsqrt(jnp.sum(rows * rows, axis=-1, keepdims=True) + NORM_EPS)


def contrastive_terms(shallow_anchor, deep_anchor, shallow_pos, deep_pos, false_neg, pair_index):
    columns = lax.broadcasted_iota(jnp.int32, false_neg.shape, 1)
    hit = columns == pair_index[:, None]
    kept_cols = (false_neg == 0) | hit
    valid_rows = (pair_index >= 0).astype(jnp.float32)
    totals = jnp.zeros(pair_index.shape, jnp.float32)
    for current_width in (D, D * 2 // 3, D // 3, D // 6, D // 12):
        log_probs = []
        for anchor_vectors, positive_rows in (
            (shallow_anchor, shallow_pos),
            (deep_anchor, deep_pos),
        ):
            similarity_scores = (
                jnp.dot(
                    normalized_rows(anchor_vectors[:, :current_width]),
                    normalized_rows(positive_rows[:, :current_width]).T,
                    precision=lax.Precision.HIGHEST,
                )
                / SOFTMAX_TEMP
            )
            similarity_scores = jnp.where(kept_cols, similarity_scores, MASKED)
            log_probs.append(jax.nn.log_softmax(similarity_scores, axis=-1))
        for log_now in log_probs:
            totals = totals - jnp.sum(jnp.where(hit, log_now, 0.0), axis=-1)
        totals = totals + jnp.sum(jnp.exp(log_probs[1]) * (log_probs[1] - log_probs[0]), axis=-1)
    return jnp.sum(totals * valid_rows)


def adam_update(master, gradient, first, second, step_rate):
    first_new = BETA_ONE * first + (1.0 - BETA_ONE) * gradient
    second_new = BETA_TWO * second + (1.0 - BETA_TWO) * gradient * gradient
    first_hat = first_new / (1.0 - BETA_ONE**ADAM_STEP)
    second_hat = second_new / (1.0 - BETA_TWO**ADAM_STEP)
    master_new = master - step_rate * (
        first_hat / (jnp.sqrt(second_hat) + ADAM_EPS) + WEIGHT_DECAY * master
    )
    return (master_new, first_new, second_new)


def body(
    token_ids,
    lengths,
    false_neg,
    pair_index,
    word_table,
    vectors,
    attn_w,
    ffn_w,
    word_first,
    vector_first,
    attn_first,
    ffn_first,
    word_second,
    vector_second,
    attn_second,
    ffn_second,
):
    pair_rows = token_ids.shape[0]
    flat_ids = token_ids.reshape(-1, SEQ)
    seq_rows = flat_ids.shape[0]
    seq_lengths = lengths.reshape(-1)
    key_mask = lax.broadcasted_iota(jnp.int32, flat_ids.shape, 1) < seq_lengths[:, None]
    vec_all = lax.all_gather(vectors.astype(jnp.bfloat16), "zero", axis=0, tiled=True).astype(
        jnp.float32
    )
    shard_rows = word_table.shape[0]
    word_half = word_table.astype(jnp.bfloat16)
    whole_table = lax.all_gather(word_half, "zero", axis=0, tiled=True)
    rows = whole_table[flat_ids].astype(jnp.float32)
    embedded, embed_back = jax.vjp(embed_tokens, rows, vec_all)
    hidden = embedded
    saved = []
    pooled = []
    for layer_index in range(LAYERS):
        layer_fn = functools.partial(encoder_layer, key_mask=key_mask, layer_index=layer_index)
        attn_full, ffn_full = (
            lax.all_gather(attn_w[layer_index].astype(jnp.bfloat16), "zero", axis=0, tiled=True),
            lax.all_gather(ffn_w[layer_index].astype(jnp.bfloat16), "zero", axis=0, tiled=True),
        )
        output, layer_back = jax.vjp(
            layer_fn, hidden, attn_full.astype(jnp.float32), ffn_full.astype(jnp.float32), vec_all
        )
        saved.append(layer_back)
        hidden = output
        pooled.append(pool_rows(hidden, key_mask, seq_lengths).astype(jnp.bfloat16))
    shallow_pair = pooled[0].reshape(pair_rows, 2, D)
    deep_pair = pooled[-1].reshape(pair_rows, 2, D)
    shallow_all, deep_all = (
        lax.all_gather(shallow_pair[:, 1], ("dp", "zero"), axis=0, tiled=True),
        lax.all_gather(deep_pair[:, 1], ("dp", "zero"), axis=0, tiled=True),
    )

    def local_loss(shallow_anchor, deep_anchor, shallow_pos, deep_pos):
        return contrastive_terms(
            shallow_anchor, deep_anchor, shallow_pos, deep_pos, false_neg, pair_index
        )

    loss_local, loss_back = jax.vjp(
        local_loss,
        shallow_pair[:, 0].astype(jnp.float32),
        deep_pair[:, 0].astype(jnp.float32),
        shallow_all.astype(jnp.float32),
        deep_all.astype(jnp.float32),
    )
    valid_local = jnp.sum((pair_index >= 0).astype(jnp.float32))
    loss_total, valid_total = lax.psum((loss_local, valid_local), ("dp", "zero"))
    inverse = 1.0 / jnp.maximum(valid_total, 1.0)
    loss = loss_total * inverse
    shallow_anchor_grad, deep_anchor_grad, shallow_pos_all, deep_pos_all = loss_back(inverse)
    shallow_pos_grad, deep_pos_grad = (
        lax.psum_scatter(shallow_pos_all, ("dp", "zero"), scatter_dimension=0, tiled=True),
        lax.psum_scatter(deep_pos_all, ("dp", "zero"), scatter_dimension=0, tiled=True),
    )
    share = key_mask.astype(jnp.float32) / seq_lengths.astype(jnp.float32)[:, None]
    shallow_back = jnp.stack([shallow_anchor_grad, shallow_pos_grad], axis=1).reshape(seq_rows, D)
    deep_back = jnp.stack([deep_anchor_grad, deep_pos_grad], axis=1).reshape(seq_rows, D)
    grad_hidden = jnp.zeros_like(embedded)
    attn_list = []
    ffn_list = []
    vec_grad = jnp.zeros_like(vec_all)
    for layer_index in range(LAYERS - 1, -1, -1):
        if layer_index == LAYERS - 1:
            grad_hidden = grad_hidden + deep_back[:, None, :] * share[:, :, None]
        if layer_index == 0:
            grad_hidden = grad_hidden + shallow_back[:, None, :] * share[:, :, None]
        layer_back = saved[layer_index]
        grad_hidden, attn_grad, ffn_grad, vec_layer_grad = layer_back(grad_hidden)
        attn_list.insert(0, attn_grad)
        ffn_list.insert(0, ffn_grad)
        vec_grad = vec_grad + vec_layer_grad
    rows_grad, vec_embed_grad = embed_back(grad_hidden)
    vec_grad = vec_grad + vec_embed_grad
    down_local = jnp.stack(
        [split_vectors(vec_grad)[3][layer_index][6] for layer_index in range(LAYERS)]
    )
    attn_shard, ffn_shard, vec_shard, down_shard = (
        lax.psum_scatter(jnp.stack(attn_list), "zero", scatter_dimension=1, tiled=True),
        lax.psum_scatter(jnp.stack(ffn_list), "zero", scatter_dimension=1, tiled=True),
        lax.psum_scatter(vec_grad, "zero", scatter_dimension=0, tiled=True),
        lax.psum_scatter(down_local, "zero", scatter_dimension=1, tiled=True),
    )
    inside = (flat_ids >= 0) & (flat_ids < shard_rows * lax.axis_size("zero"))
    target = jnp.where(inside, flat_ids, shard_rows * lax.axis_size("zero")).reshape(-1)
    word_grad = lax.psum_scatter(
        jnp.zeros((shard_rows * lax.axis_size("zero"), D), jnp.float32)
        .at[target]
        .add(rows_grad.reshape(-1, D), mode="drop"),
        "zero",
        scatter_dimension=0,
        tiled=True,
    )
    word_grad, vec_shard, attn_shard, ffn_shard, down_shard = lax.psum(
        (word_grad, vec_shard, attn_shard, ffn_shard, down_shard), "dp"
    )
    square_local = jnp.sum(word_grad * word_grad) + jnp.sum(vec_shard * vec_shard)
    square_local = square_local + jnp.sum(attn_shard * attn_shard) + jnp.sum(ffn_shard * ffn_shard)
    square_total = lax.psum(square_local, "zero")
    grad_norm = jnp.sqrt(square_total)
    factor = jnp.minimum(1.0, CLIP_NORM / (grad_norm + 1e-06))
    word_new, word_first_new, word_second_new = adam_update(
        word_table, word_grad * factor, word_first, word_second, LEARN_RATE
    )
    vector_new, vector_first_new, vector_second_new = adam_update(
        vectors, vec_shard * factor, vector_first, vector_second, VECTOR_RATE
    )
    attn_new, attn_first_new, attn_second_new = adam_update(
        attn_w, attn_shard * factor, attn_first, attn_second, LEARN_RATE
    )
    ffn_new, ffn_first_new, ffn_second_new = adam_update(
        ffn_w, ffn_shard * factor, ffn_first, ffn_second, LEARN_RATE
    )
    return (
        loss,
        grad_norm,
        word_new,
        vector_new,
        attn_new,
        ffn_new,
        word_new.astype(jnp.bfloat16),
        vector_new.astype(jnp.bfloat16),
        attn_new.astype(jnp.bfloat16),
        ffn_new.astype(jnp.bfloat16),
        word_first_new,
        vector_first_new,
        attn_first_new,
        ffn_first_new,
        word_second_new,
        vector_second_new,
        attn_second_new,
        ffn_second_new,
        down_shard * factor,
    )


def solution(mesh):
    placed = (
        P(("dp", "zero"), None, None),
        P(("dp", "zero"), None),
        P(("dp", "zero"), None),
        P(("dp", "zero")),
        P("zero", None),
        P("zero"),
        P(None, "zero", None),
        P(None, "zero", None),
        P("zero", None),
        P("zero"),
        P(None, "zero", None),
        P(None, "zero", None),
        P("zero", None),
        P("zero"),
        P(None, "zero", None),
        P(None, "zero", None),
    )
    return jax.shard_map(
        body,
        mesh=mesh,
        in_specs=placed,
        out_specs=(
            P(),
            P(),
            P("zero", None),
            P("zero"),
            P(None, "zero", None),
            P(None, "zero", None),
            P("zero", None),
            P("zero"),
            P(None, "zero", None),
            P(None, "zero", None),
            P("zero", None),
            P("zero"),
            P(None, "zero", None),
            P(None, "zero", None),
            P("zero", None),
            P("zero"),
            P(None, "zero", None),
            P(None, "zero", None),
            P(None, "zero"),
        ),
        check_vma=False,
    )
```

profile of v0, /device:TPU:0, one launch (start us, length us, event | category | flops | bytes accessed | tf_op | source)
XLA Modules:
  0.0 2151.6 jit_solution(4347928923072339270)
XLA Ops:
  11.1 3.6 convert_bitcast_fusion
  19.3 83.2 %all-reduce.66.cloned.1.call-done = bf16[78848]{0:T(1024)(128)(2,1)} async-done(((bf16[78848]{0:T(1024)(128)(2,1)}), bf16[78848]{0:T(1024)(128)(2,1)}) %all-reduce.66.cloned.1.call-update) | async-done | bytes 157712
  105.1 158.1 %all-gather.21.cloned.1.call-done = bf16[16,1908,512]{2,1,0:T(8,128)(2,1)} async-done(((bf16[1,1908,512]{2,1,0:T(8,128)(2,1)}), bf16[16,1908,512]{2,1,0:T(8,128)(2,1)}) %all-gather.21.cloned.1.call-update) | async-done | bytes 31260688 | tf_op jit(solution)/shard_map/all_gather | solution.py:209
  263.2 23.1 %reshape.903 = bf16[30528,512]{1,0:T(8,128)(2,1)} reshape(bf16[16,1908,512]{2,1,0:T(8,128)(2,1)} %all-gather.21.cloned.1.call-done) | data formatting | bytes 62521344
  286.4 18.2 gather_fusion
  307.4 3.2 add_convert_fusion.3
  314.9 3.8 fusion.284
  318.7 2.8 divide_convert_fusion.1
  321.5 3.2 copy.141
  331.0 28.5 %all-gather.15.cloned.1.call-done = bf16[1,512,4096]{2,1,0:T(8,128)(2,1)} async-done(((bf16[1,32,4096]{2,1,0:T(8,128)(2,1)}), bf16[1,512,4096]{2,1,0:T(8,128)(2,1)}) %all-gather.15.cloned.1.call-update) | async-done | bytes 4194320 | tf_op jit(solution)/shard_map/all_gather | solution.py:219
  359.5 8.1 multiply_convert_fusion.1
  371.2 30.8 %all-gather.17.cloned.1.call-done = bf16[1,512,2048]{2,1,0:T(8,128)(2,1)} async-done(((bf16[1,32,2048]{2,1,0:T(8,128)(2,1)}), bf16[1,512,2048]{2,1,0:T(8,128)(2,1)}) %all-gather.17.cloned.1.call-update) | async-done | bytes 2097168 | tf_op jit(solution)/shard_map/all_gather | solution.py:218
  402.0 3.2 add_convert_fusion.2
  411.2 5.0 fusion.287
  416.3 4.1 divide_convert_fusion
  429.3 24.6 %all-gather.19.cloned.1.call-done = bf16[1,512,4096]{2,1,0:T(8,128)(2,1)} async-done(((bf16[1,32,4096]{2,1,0:T(8,128)(2,1)}), bf16[1,512,4096]{2,1,0:T(8,128)(2,1)}) %all-gather.19.cloned.1.call-update) | async-done | bytes 4194320 | tf_op jit(solution)/shard_map/all_gather | solution.py:219
  454.0 8.0 multiply_convert_fusion
  466.5 39.7 %all-gather.5 = bf16[128,1,512]{2,1,0:T(2,128)(2,1)S(1)} all-gather(bf16[4,1,512]{2,1,0:T(2,128)(2,1)S(1)} %get-tuple-element.212), channel_id=7, replica_groups=mesh['dp'=2,'zero'=16] {'dp','zero'}, dimensions={0}, use_global_device_ids=true | all-gather | bytes 135168 | tf_op jit(solution)/shard_map/all_gather | solution.py:231
  506.8 37.5 %all-gather.2 = bf16[128,1,512]{2,1,0:T(2,128)(2,1)S(1)} all-gather(bf16[4,1,512]{2,1,0:T(2,128)(2,1)S(1)} %get-tuple-element.214), channel_id=4, replica_groups=mesh['dp'=2,'zero'=16] {'dp','zero'}, dimensions={0}, use_global_device_ids=true | all-gather | bytes 135168 | tf_op jit(solution)/shard_map/all_gather | solution.py:230
  558.8 37.3 %all-reduce.57 = (f32[]{:T(128)}, f32[]{:T(128)}) all-reduce(f32[]{:T(128)} %get-tuple-element.112, f32[]{:T(128)} %get-tuple-element.111), channel_id=1, replica_groups=mesh['dp'=2,'zero'=16] {'dp','zero'}, use_global_device_ids=true, to_apply=%region_54.56 | all-reduce | flops 2 | bytes 16 | tf_op jit(solution)/shard_map/psum | solution.py:247
  645.2 128.0 %all-reduce.70.cloned.1.call-done = (f32[128,512]{1,0:T(8,128)}, f32[128,512]{1,0:T(8,128)}) async-done(((f32[128,512]{1,0:T(8,128)}, f32[128,512]{1,0:T(8,128)}), (f32[128,512]{1,0:T(8,128)}, f32[128,512]{1,0:T(8,128)})) %all-reduce.70.cloned.1.call-update) | async-done | bytes 524304
  782.3 6.4 fusion.5
  788.7 3.8 multiply_reduce_fusion.6
  795.7 2.8 convolution_convert_fusion.5
  800.1 4.6 fusion.300
  807.2 2.9 fusion.26
  812.0 3.0 copy.162
  815.0 2.9 copy.164
  817.9 2.9 copy.166
  820.7 4.1 add_convert_fusion.1
  825.6 5.6 multiply_reduce_fusion.5
  836.4 6.5 fusion.10
  843.0 3.1 multiply_reduce_fusion.4
  849.2 2.9 convolution_convert_fusion.4
  853.8 2.9 fusion.301
  858.9 2.9 fusion.24
  866.1 3.5 convolution_bitcast_fusion
  871.3 3.0 copy.173
  874.2 2.9 copy.175
  877.2 2.9 copy.177
  880.0 3.1 add_convert_fusion
  889.2 3.9 pad_maximum_fusion.1
  898.7 4.0 fusion.43
  910.3 4.4 convolution_bitcast_fusion.4
  914.7 4.4 convolution_bitcast_fusion.3
  919.1 4.6 convolution_bitcast_fusion.2
  923.7 3.1 add_bitcast_fusion.1
  926.9 7.7 add_bitcast_fusion
  934.6 9.6 pad_maximum_fusion
  944.3 20.4 broadcast_in_dim.291
  964.6 124.7 %scatter_fusion = f32[30528,512]{1,0:T(8,128)} fusion(f32[30528,512]{1,0:T(8,128)} %broadcast_in_dim.291, s32[1024]{0:T(1024)S(1)} %bitcast.402, f32[1024,512]{1,0:T(8,128)} %bitcast_convert_fusion), kind=kCustom, calls=%fused_computation.1 | custom fusion | flops 524288 | bytes 6295552 | tf_op jit(solution)/shard_map/scatter-add | solution.py:288
  1089.3 676.0 %fusion = f32[1920,512]{1,0:T(8,128)} fusion(f32[30528,512]{1,0:T(8,128)} %scatter_fusion), kind=kCustom, calls=%all-reduce-scatter | all-reduce-scatter fusion | flops 15728641 | bytes 66454016
  1766.3 21.9 %collective-permute-start = (f32[180,512]{1,0:T(8,128)S(1)}, f32[180,512]{1,0:T(8,128)S(1)}, u32[]{:S(2)}, u32[]{:S(2)}) collective-permute-start(f32[180,512]{1,0:T(8,128)S(1)} %slice.324), channel_id=1, source_target_pairs={{0,1},{1,2},{2,3},{3,4},{4,5},{5,6},{6,7},{7,8},{8,9},{9,10},{10,1... | collective-permute-start | bytes 1105928
  1796.3 11.1 concatenate.8
  1807.4 4.6 constant_dynamic-slice_fusion
  1812.6 38.2 %reduce-scatter.12.cloned.1.call-done = f32[32,2]{1,0:T(8,128)} async-done(((f32[512,2]{1,0:T(8,128)}), f32[32,2]{1,0:T(8,128)}) %reduce-scatter.12.cloned.1.call-update) | async-done | bytes 272
  1851.6 91.1 %all-reduce.68.cloned.1.call-done = f32[78848]{0:T(1024)} async-done(((f32[78848]{0:T(1024)}), f32[78848]{0:T(1024)}) %all-reduce.68.cloned.1.call-update) | async-done | bytes 315408
  1943.6 8.3 all-reduce.59
  1952.5 130.9 %all-reduce.72.cloned.1.call-done = (f32[1908,512]{1,0:T(8,128)}, f32[2,32,2048]{2,1,0:T(8,128)}, f32[2,32,4096]{2,1,0:T(8,128)}) async-done(((f32[1908,512]{1,0:T(8,128)}, f32[2,32,2048]{2,1,0:T(8,128)}, f32[2,32,4096]{2,1,0:T(8,128)}), (f32[1908,512]{1,0:T(8,128)}, f32[2,32,2048]{2,1,0:T(8,128)}, f32[2,32,4096]{2,1,0:T(8,128)})) %all-reduce.72.cloned.1.call-update) | async-done | bytes 5480464 | tf_op jit(solution)/shard_map/psum | solution.py:293
  2083.4 3.9 multiply_reduce_fusion.3
  2092.0 33.7 %psum.62 = f32[]{:T(128)} all-reduce(f32[]{:T(128)S(6)} %add.712), channel_id=1, replica_groups=mesh['dp'=2,'zero'=16] {'zero'}, use_global_device_ids=true, to_apply=%region_133.135 | all-reduce | flops 1 | bytes 8 | tf_op jit(solution)/shard_map/psum | solution.py:298
  2127.0 4.1 fusion.251
  2131.2 2.9 fusion.253
  2134.7 7.6 fusion.257
  (752 shorter events, 177.6 us)
Async XLA Ops:
  7.2 95.3 %all-reduce.66.cloned.1.call-start = ((), (), s32[]{:S(2)}) async-start(), calls=%async_computation.9 | async-start | bytes 315392
  11.1 252.2 %all-gather.21.cloned.1.call-start = ((), (), s32[]{:S(2)}) async-start(), calls=%async_computation.10 | async-start | bytes 33284096 | tf_op jit(solution)/shard_map/all_gather | solution.py:209
  14.8 292.6 %all-gather.13.cloned.1.call-start = ((), (), s32[]{:S(2)}) async-start(), calls=%async_computation.5 | async-start | bytes 2228224 | tf_op jit(solution)/shard_map/all_gather | solution.py:218
  16.6 342.9 %all-gather.15.cloned.1.call-start = ((), (), s32[]{:S(2)}) async-start(), calls=%async_computation.6 | async-start | bytes 4456448 | tf_op jit(solution)/shard_map/all_gather | solution.py:219
  17.6 384.4 %all-gather.17.cloned.1.call-start = ((), (), s32[]{:S(2)}) async-start(), calls=%async_computation.7 | async-start | bytes 2228224 | tf_op jit(solution)/shard_map/all_gather | solution.py:218
  18.2 435.8 %all-gather.19.cloned.1.call-start = ((), (), s32[]{:S(2)}) async-start(), calls=%async_computation.8 | async-start | bytes 4456448 | tf_op jit(solution)/shard_map/all_gather | solution.py:219
  18.8 754.4 %all-reduce.70.cloned.1.call-start = ((), (), s32[]{:S(2)}) async-start(), calls=%async_computation.13 | async-start | bytes 1048576
  19.1 392.2 %copy-start.140 = (pred[8,128]{1,0:T(8,128)(4,1)}, pred[8,128]{1,0:T(8,128)(4,1)S(1)}, u32[]{:S(2)}) copy-start(pred[8,128]{1,0:T(8,128)(4,1)S(1)} %iota_compare_fusion) | copy-start | bytes 3076
  103.5 223.2 %copy-start.37 = (f32[128,512]{1,0:T(8,128)}, f32[128,512]{1,0:T(8,128)S(1)}, u32[]{:S(2)}) copy-start(f32[128,512]{1,0:T(8,128)S(1)} %slice.200) | copy-start | bytes 786436
  104.4 222.3 %copy-start.104 = (f32[512]{0:T(512)}, f32[512]{0:T(512)S(1)}, u32[]{:S(2)}) copy-start(f32[512]{0:T(512)S(1)} %get-tuple-element.207) | copy-start | bytes 6148
  104.4 263.2 %copy-start.106 = (f32[512]{0:T(512)}, f32[512]{0:T(512)S(1)}, u32[]{:S(2)}) copy-start(f32[512]{0:T(512)S(1)} %get-tuple-element.202) | copy-start | bytes 6148
  104.4 357.7 %copy-start.108 = (f32[512]{0:T(512)}, f32[512]{0:T(512)S(1)}, u32[]{:S(2)}) copy-start(f32[512]{0:T(512)S(1)} %get-tuple-element.192) | copy-start | bytes 6148
  105.1 254.4 %copy-start.94 = (f32[2048]{0:T(1024)}, f32[2048]{0:T(1024)S(1)}, u32[]{:S(2)}) copy-start(f32[2048]{0:T(1024)S(1)} %get-tuple-element.210) | copy-start | bytes 24580
  105.1 348.9 %copy-start.96 = (f32[2048]{0:T(1024)}, f32[2048]{0:T(1024)S(1)}, u32[]{:S(2)}) copy-start(f32[2048]{0:T(1024)S(1)} %get-tuple-element.209) | copy-start | bytes 24580
  329.7 37.9 %copy-start.90 = (f32[8,128]{1,0:T(8,128)}, f32[8,128]{1,0:T(8,128)S(1)}, u32[]{:S(2)}) copy-start(f32[8,128]{1,0:T(8,128)S(1)} %fusion.177) | copy-start | bytes 12292
  331.0 36.6 %copy-start.45 = (bf16[8,128,512]{2,1,0:T(8,128)(2,1)}, bf16[8,128,512]{2,1,0:T(8,128)(2,1)S(1)}, u32[]{:S(2)}) copy-start(bf16[8,128,512]{2,1,0:T(8,128)(2,1)S(1)} %fusion.57) | copy-start | bytes 3145732
  371.2 34.1 %copy-start.41 = (bf16[8,128,512]{2,1,0:T(8,128)(2,1)}, bf16[8,128,512]{2,1,0:T(8,128)(2,1)S(1)}, u32[]{:S(2)}) copy-start(bf16[8,128,512]{2,1,0:T(8,128)(2,1)S(1)} %fusion.75) | copy-start | bytes 3145732
  428.1 34.0 %copy-start.84 = (f32[8,128]{1,0:T(8,128)}, f32[8,128]{1,0:T(8,128)S(1)}, u32[]{:S(2)}) copy-start(f32[8,128]{1,0:T(8,128)S(1)} %multiply_reduce_fusion.12) | copy-start | bytes 12292
  428.1 34.0 %copy-start.92 = (f32[8,128]{1,0:T(8,128)}, f32[8,128]{1,0:T(8,128)S(1)}, u32[]{:S(2)}) copy-start(f32[8,128]{1,0:T(8,128)S(1)} %fusion.179) | copy-start | bytes 12292
  429.3 32.7 %copy-start.47 = (bf16[8,128,512]{2,1,0:T(8,128)(2,1)}, bf16[8,128,512]{2,1,0:T(8,128)(2,1)S(1)}, u32[]{:S(2)}) copy-start(bf16[8,128,512]{2,1,0:T(8,128)(2,1)S(1)} %fusion.58) | copy-start | bytes 3145732
  506.5 42.0 %copy-start.166 = (f32[128]{0:T(128)}, f32[128]{0:T(128)S(1)}, u32[]{:S(2)}) copy-start(f32[128]{0:T(128)S(1)} %multiply_reduce_fusion.24) | copy-start | bytes 1540
  506.5 42.5 %copy-start.165 = (f32[128]{0:T(128)}, f32[128]{0:T(128)S(1)}, u32[]{:S(2)}) copy-start(f32[128]{0:T(128)S(1)} %multiply_reduce_fusion.20) | copy-start | bytes 1540
  506.7 41.8 %copy-start.195 = (f32[4]{0:T(128)}, f32[4]{0:T(128)S(1)}, u32[]{:S(2)}) copy-start(f32[4]{0:T(128)S(1)} %multiply_reduce_fusion.41) | copy-start | bytes 52
  506.8 42.7 %copy-start.205 = (f32[4]{0:T(128)}, f32[4]{0:T(128)S(1)}, u32[]{:S(2)}) copy-start(f32[4]{0:T(128)S(1)} %multiply_reduce_fusion.37) | copy-start | bytes 52
  547.6 54.7 %copy-start.121 = (f32[4]{0:T(128)}, f32[4]{0:T(128)S(1)}, u32[]{:S(2)}) copy-start(f32[4]{0:T(128)S(1)} %get-tuple-element.274) | copy-start | bytes 52
  547.6 60.3 %copy-start.99 = (f32[4,128]{1,0:T(4,128)}, f32[4,128]{1,0:T(4,128)S(1)}, u32[]{:S(2)}) copy-start(f32[4,128]{1,0:T(4,128)S(1)} %get-tuple-element.275) | copy-start | bytes 6148
  547.9 59.0 %copy-start.149 = (f32[128]{0:T(128)}, f32[128]{0:T(128)S(1)}, u32[]{:S(2)}) copy-start(f32[128]{0:T(128)S(1)} %add_rsqrt_fusion.8) | copy-start | bytes 1540
  547.9 59.0 %copy-start.154 = (f32[4]{0:T(128)}, f32[4]{0:T(128)S(1)}, u32[]{:S(2)}) copy-start(f32[4]{0:T(128)S(1)} %add_rsqrt_fusion.9) | copy-start | bytes 52
  548.5 58.4 %copy-start.135 = (f32[128]{0:T(128)}, f32[128]{0:T(128)S(1)}, u32[]{:S(2)}) copy-start(f32[128]{0:T(128)S(1)} %add_rsqrt_fusion.12) | copy-start | bytes 1540
  549.5 58.4 %copy-start.110 = (f32[4]{0:T(128)}, f32[4]{0:T(128)S(1)}, u32[]{:S(2)}) copy-start(f32[4]{0:T(128)S(1)} %get-tuple-element.268) | copy-start | bytes 52
  551.2 51.2 %copy-start.131 = (f32[4]{0:T(128)}, f32[4]{0:T(128)S(1)}, u32[]{:S(2)}) copy-start(f32[4]{0:T(128)S(1)} %get-tuple-element.266) | copy-start | bytes 52
  551.2 56.7 %copy-start.112 = (f32[4,128]{1,0:T(4,128)}, f32[4,128]{1,0:T(4,128)S(1)}, u32[]{:S(2)}) copy-start(f32[4,128]{1,0:T(4,128)S(1)} %get-tuple-element.267) | copy-start | bytes 6148
  552.0 54.9 %copy-start.171 = (f32[128]{0:T(128)}, f32[128]{0:T(128)S(1)}, u32[]{:S(2)}) copy-start(f32[128]{0:T(128)S(1)} %add_rsqrt_fusion.4) | copy-start | bytes 1540
  552.0 54.9 %copy-start.191 = (f32[4]{0:T(128)}, f32[4]{0:T(128)S(1)}, u32[]{:S(2)}) copy-start(f32[4]{0:T(128)S(1)} %add_rsqrt_fusion.5) | copy-start | bytes 52
  553.5 43.5 %copy-start.113 = (f32[4,128]{1,0:T(4,128)}, f32[4,128]{1,0:T(4,128)S(1)}, u32[]{:S(2)}) copy-start(f32[4,128]{1,0:T(4,128)S(1)} %get-tuple-element.263) | copy-start | bytes 6148
  553.5 48.9 %copy-start.133 = (f32[4]{0:T(128)}, f32[4]{0:T(128)S(1)}, u32[]{:S(2)}) copy-start(f32[4]{0:T(128)S(1)} %get-tuple-element.262) | copy-start | bytes 52
  554.3 52.6 %copy-start.177 = (f32[128]{0:T(128)}, f32[128]{0:T(128)S(1)}, u32[]{:S(2)}) copy-start(f32[128]{0:T(128)S(1)} %add_rsqrt_fusion) | copy-start | bytes 1540
  554.9 52.0 %copy-start.192 = (f32[4]{0:T(128)}, f32[4]{0:T(128)S(1)}, u32[]{:S(2)}) copy-start(f32[4]{0:T(128)S(1)} %add_rsqrt_fusion.1) | copy-start | bytes 52
  555.4 51.4 %copy-start.174 = (f32[128]{0:T(128)}, f32[128]{0:T(128)S(1)}, u32[]{:S(2)}) copy-start(f32[128]{0:T(128)S(1)} %add_rsqrt_fusion.16) | copy-start | bytes 1540
  555.6 46.8 %copy-start.144 = (f32[4]{0:T(128)}, f32[4]{0:T(128)S(1)}, u32[]{:S(2)}) copy-start(f32[4]{0:T(128)S(1)} %add_rsqrt_fusion.17) | copy-start | bytes 52
  556.4 40.5 %copy-start.146 = (f32[4]{0:T(128)}, f32[4]{0:T(128)S(1)}, u32[]{:S(2)}) copy-start(f32[4]{0:T(128)S(1)} %add_rsqrt_fusion.19) | copy-start | bytes 52
  556.8 45.6 %copy-start.123 = (f32[4]{0:T(128)}, f32[4]{0:T(128)S(1)}, u32[]{:S(2)}) copy-start(f32[4]{0:T(128)S(1)} %get-tuple-element.256) | copy-start | bytes 52
  597.2 25.2 %copy-start.127 = (f32[4]{0:T(128)S(1)}, f32[4]{0:T(128)}, u32[]{:S(2)}) copy-start(f32[4]{0:T(128)} %copy-done.126) | copy-start | bytes 52
  600.0 25.3 %copy-start.203 = (f32[4]{0:T(128)S(1)}, f32[4]{0:T(128)}, u32[]{:S(2)}) copy-start(f32[4]{0:T(128)} %copy-done.202) | copy-start | bytes 52
  600.0 27.0 %copy-start.201 = (f32[4]{0:T(128)S(1)}, f32[4]{0:T(128)}, u32[]{:S(2)}) copy-start(f32[4]{0:T(128)} %copy-done.200) | copy-start | bytes 52
  600.0 27.5 %copy-start.196 = (f32[4]{0:T(128)S(1)}, f32[4]{0:T(128)}, u32[]{:S(2)}) copy-start(f32[4]{0:T(128)} %copy-done.195) | copy-start | bytes 52
  600.0 28.0 %copy-start.206 = (f32[4]{0:T(128)S(1)}, f32[4]{0:T(128)}, u32[]{:S(2)}) copy-start(f32[4]{0:T(128)} %copy-done.205) | copy-start | bytes 52
  600.0 28.6 %copy-start.179 = (f32[128]{0:T(128)S(1)}, f32[128]{0:T(128)}, u32[]{:S(2)}) copy-start(f32[128]{0:T(128)} %copy-done.178) | copy-start | bytes 1540
  600.0 28.6 %copy-start.199 = (f32[128]{0:T(128)S(1)}, f32[128]{0:T(128)}, u32[]{:S(2)}) copy-start(f32[128]{0:T(128)} %copy-done.198) | copy-start | bytes 1540
  600.0 28.6 %copy-start.176 = (f32[128]{0:T(128)S(1)}, f32[128]{0:T(128)}, u32[]{:S(2)}) copy-start(f32[128]{0:T(128)} %copy-done.175) | copy-start | bytes 1540
  600.0 28.6 %copy-start.173 = (f32[128]{0:T(128)S(1)}, f32[128]{0:T(128)}, u32[]{:S(2)}) copy-start(f32[128]{0:T(128)} %copy-done.172) | copy-start | bytes 1540
  600.0 28.6 %copy-start.170 = (f32[128]{0:T(128)S(1)}, f32[128]{0:T(128)}, u32[]{:S(2)}) copy-start(f32[128]{0:T(128)} %copy-done.169) | copy-start | bytes 1540
  600.9 27.7 %copy-start.151 = (f32[128]{0:T(128)S(1)}, f32[128]{0:T(128)}, u32[]{:S(2)}) copy-start(f32[128]{0:T(128)} %copy-done.150) | copy-start | bytes 1540
  635.5 140.8 %copy-start.87 = (f32[8,128]{1,0:T(8,128)S(1)}, f32[8,128]{1,0:T(8,128)}, u32[]{:S(2)}) copy-start(f32[8,128]{1,0:T(8,128)} %copy-done.86) | copy-start | bytes 12292
  643.3 1168.6 %reduce-scatter.8.cloned.1.call-start = ((), (), s32[]{:S(2)}) async-start(), calls=%async_computation.3 | async-start | bytes 8912896 | tf_op jit(solution)/shard_map/reduce_scatter | solution.py:278
  893.1 918.9 %reduce-scatter.10.cloned.1.call-start = ((), (), s32[]{:S(2)}) async-start(), calls=%async_computation.4 | async-start | bytes 17825792 | tf_op jit(solution)/shard_map/reduce_scatter | solution.py:279
  944.2 906.6 %reduce-scatter.12.cloned.1.call-start = ((), (), s32[]{:S(2)}) async-start(), calls=%async_computation.11 | async-start | bytes 278528
  1089.3 700.4 %copy-start.30 = (bf16[8,128,512]{2,1,0:T(8,128)(2,1)S(1)}, bf16[8,128,512]{2,1,0:T(8,128)(2,1)}, u32[]{:S(2)}) copy-start(bf16[8,128,512]{2,1,0:T(8,128)(2,1)} %copy-done.28) | copy-start | bytes 3145732
  1766.3 25.2 %copy-start.12 = (bf16[8,128,2048]{2,1,0:T(8,128)(2,1)S(1)}, bf16[8,128,2048]{2,1,0:T(8,128)(2,1)}, u32[]{:S(2)}) copy-start(bf16[8,128,2048]{2,1,0:T(8,128)(2,1)} %copy-done.10) | copy-start | bytes 12582916
  1766.3 30.0 %collective-permute-start = (f32[180,512]{1,0:T(8,128)S(1)}, f32[180,512]{1,0:T(8,128)S(1)}, u32[]{:S(2)}, u32[]{:S(2)}) collective-permute-start(f32[180,512]{1,0:T(8,128)S(1)} %slice.324), channel_id=1, source_target_pairs={{0,1},{1,2},{2,3},{3,4},{4,5},{5,6},{6,7},{7,8},{8,9},{9,10},{10,1... | collective-permute-start | bytes 1105928
  1795.5 147.3 %all-reduce.68.cloned.1.call-start = ((), (), s32[]{:S(2)}) async-start(), calls=%async_computation.12 | async-start | bytes 630784
  1796.2 287.1 %all-reduce.72.cloned.1.call-start = ((), (), s32[]{:S(2)}) async-start(), calls=%async_computation.14 | async-start | bytes 10977280 | tf_op jit(solution)/shard_map/psum | solution.py:293
  2083.4 43.7 %copy-start.44 = (f32[2,32,4096]{2,1,0:T(8,128)S(1)}, f32[2,32,4096]{2,1,0:T(8,128)}, u32[]{:S(2)}) copy-start(f32[2,32,4096]{2,1,0:T(8,128)} %param.24) | copy-start | bytes 3145732
  2083.4 47.8 %copy-start.69 = (f32[2,32,2048]{2,1,0:T(8,128)S(1)}, f32[2,32,2048]{2,1,0:T(8,128)}, u32[]{:S(2)}) copy-start(f32[2,32,2048]{2,1,0:T(8,128)} %param.23) | copy-start | bytes 1572868
  (168 other events, 1011.8 us)
Sparse Core Ops, SparseCore 0:
  12.0 90.4 all-reduce.65
  104.7 158.5 all-gather.20
  266.0 41.3 all-gather.12
  310.0 49.4 all-gather.14
  362.1 39.8 all-gather.16
  404.6 49.3 all-gather.18
  643.5 129.6 all-reduce.69
  893.2 103.5 reduce-scatter.7
  1001.5 257.3 reduce-scatter.9
  1795.6 55.1 reduce-scatter.11
  1855.2 87.5 all-reduce.67
  1945.8 137.5 all-reduce.71
where the time goes:
time: 2170 us; the launch traced here: 2150 us
  blocking collectives  832 us (38%)
  waiting for transfers between devices  716 us (33%)
  other arithmetic  257 us (12%)
  local copies, waits for them, and re-layouts  150 us (7%)
  matrix products  147 us (7%)
  between operations  26.4 us (1%)
  starting transfers between devices  22.8 us (1%)
    unnamed x1, blocking collectives  676 us
    unnamed x17, waiting for transfers between devices  342 us
    all_gather x1, waiting for transfers between devices, body(): whole_table = lax.all_gather(word_half, 'zero', axis=0, tiled=True)  158 us
    psum x1, waiting for transfers between devices, body(): lax.psum((word_grad, vec_shard, attn_shard, ffn_shard, down_shard), 'dp')  131 us
    scatter-add x1, other arithmetic, body(): word_grad = lax.psum_scatter(jnp.zeros((shard_rows * lax.axis_size('zero'...  125 us
    dot_general x18, matrix products, matmul(): return jnp.dot(left, right, preferred_element_type=jnp.float32)  67.4 us
    unnamed x442, local copies, waits for them, and re-layouts  67 us
    all_gather x2, waiting for transfers between devices, body(): lax.all_gather(ffn_w[layer_index].astype(jnp.bfloat16), 'zero', axis=0, t...  53.2 us
  transfers between devices with their start and end apart: 13, of which 10 were waited for; matrix products, arithmetic and copies ran while one was open for 47% of the time, Pallas kernels for 0%

commit v1 on v0

--- a/solution.py
+++ b/solution.py
@@ -3,6 +3,8 @@
 import jax
 import jax.numpy as jnp
 from jax import lax
+from jax.experimental import pallas as pl
+from jax.experimental.pallas import tpu as pltpu
 from jax.sharding import PartitionSpec as P
 
 D = 512
@@ -25,6 +27,8 @@
 NORM_EPS = 1e-06
 MASKED = -1000000000.0
 
+MESH = pl.DeviceIdType.MESH
+
 
 def build_low():
 
@@ -76,6 +80,110 @@
 
 def einsum_plain(form, left, right):
     return jnp.einsum(form, left, right, preferred_element_type=jnp.float32)
+
+
+def exchange_kernel(modes, ndp, nz, *refs):
+    count = len(modes)
+    ins = refs[:count]
+    outs = refs[count : 2 * count]
+    sems = refs[2 * count :]
+    d = lax.axis_index("dp")
+    z = lax.axis_index("zero")
+    me = d * nz + z
+    n = ndp * nz
+
+    def peer_of(group, k):
+        if group == "dp":
+            pd = lax.rem(d + k, ndp)
+            return pd, z, pd
+        if group == "zero":
+            pz = lax.rem(z + k, nz)
+            return d, pz, pz
+        p = lax.rem(me + k, n)
+        return p // nz, lax.rem(p, nz), p
+
+    groups = {m.split("_")[0] for m in modes}
+    sizes = {"all": n, "zero": nz, "dp": ndp}
+    mine = {"all": me, "zero": z, "dp": d}
+    barrier = pltpu.get_barrier_semaphore()
+    meet = ["all"] if "all" in groups else sorted(groups)
+    total = 0
+    for group in meet:
+        total += sizes[group] - 1
+
+        def greet(k, carry, group=group):
+            pd, pz, _ = peer_of(group, k)
+            pl.semaphore_signal(barrier, inc=1, device_id=(pd, pz), device_id_type=MESH)
+            return carry
+
+        lax.fori_loop(1, sizes[group], greet, 0)
+    pl.semaphore_wait(barrier, total)
+
+    def make(a, k):
+        mode = modes[a]
+        group = mode.split("_")[0]
+        pd, pz, _ = peer_of(group, k)
+        src = ins[a].at[pz] if mode.endswith("_p") else ins[a]
+        return pltpu.make_async_remote_copy(
+            src_ref=src,
+            dst_ref=outs[a].at[mine[group]],
+            send_sem=sems[2 * a].at[k],
+            recv_sem=sems[2 * a + 1].at[k],
+            device_id=(pd, pz),
+            device_id_type=MESH,
+        )
+
+    for a, mode in enumerate(modes):
+        group = mode.split("_")[0]
+
+        def begin(k, carry, a=a):
+            make(a, k).start()
+            return carry
+
+        lax.fori_loop(1, sizes[group], begin, 0)
+    for a, mode in enumerate(modes):
+        group = mode.split("_")[0]
+        if mode.endswith("_p"):
+            outs[a][mine[group]] = ins[a][z]
+        else:
+            outs[a][mine[group]] = ins[a][...]
+    for a, mode in enumerate(modes):
+        group = mode.split("_")[0]
+
+        def finish(k, carry, a=a):
+            make(a, k).wait()
+            return carry
+
+        lax.fori_loop(1, sizes[group], finish, 0)
+
+
+def exchange(arrays, modes, ndp, nz, collective_id, name):
+    sizes = {"all": ndp * nz, "zero": nz, "dp": ndp}
+    outs = []
+    scratch = []
+    moved = 0
+    for array, mode in zip(arrays, modes):
+        size = sizes[mode.split("_")[0]]
+        block = array.shape[1:] if mode.endswith("_p") else array.shape
+        outs.append(jax.ShapeDtypeStruct((size,) + block, array.dtype))
+        scratch += [pltpu.SemaphoreType.DMA((size,)), pltpu.SemaphoreType.DMA((size,))]
+        one = array.dtype.itemsize
+        for s in block:
+            one *= s
+        moved += one * size
+    vmem = pl.BlockSpec(memory_space=pltpu.VMEM)
+    return pl.pallas_call(
+        functools.partial(exchange_kernel, tuple(modes), ndp, nz),
+        out_shape=tuple(outs),
+        in_specs=[vmem] * len(arrays),
+        out_specs=tuple([vmem] * len(arrays)),
+        scratch_shapes=scratch,
+        compiler_params=pltpu.CompilerParams(
+            collective_id=collective_id, has_side_effects=True, vmem_limit_bytes=48 * 1024 * 1024
+        ),
+        cost_estimate=pl.CostEstimate(flops=0, bytes_accessed=20 * moved, transcendentals=0),
+        name=name,
+    )(*arrays)
 
 
 def split_vectors(vec_all):
@@ -178,6 +286,35 @@
     return (master_new, first_new, second_new)
 
 
+def pad_rows(flat, multiple):
+    rows = -(-flat.shape[0] // (128 * multiple)) * multiple
+    return jnp.pad(flat, (0, rows * 128 - flat.shape[0])).reshape(rows, 128)
+
+
+def one_hot(index, size, dtype=jnp.bfloat16):
+    return (index[:, None] == lax.broadcasted_iota(jnp.int32, (1, size), 1)).astype(dtype)
+
+
+def token_plan(ids, shard_rows):
+    places = lax.broadcasted_iota(jnp.int32, ids.shape, 0)
+    same = ids[:, None] == ids[None, :]
+    leader = jnp.min(jnp.where(same, places[None, :], ids.shape[0]), axis=1)
+    leads = leader == places
+    owner = ids // shard_rows
+    low_id = owner * shard_rows
+    ahead = leads[None, :] & (ids[None, :] >= low_id[:, None]) & (ids[None, :] < ids[:, None])
+    place = jnp.sum(ahead.astype(jnp.int32), axis=1)
+    return owner, place, ids - low_id
+
+
+def round_slots(owner, place, local_row, round_index, room, nz):
+    inside = (place >= round_index * room) & (place < (round_index + 1) * room)
+    slot = jnp.where(inside, owner * room + place - round_index * room, -1)
+    slots = lax.broadcasted_iota(jnp.int32, (1, nz * room), 1)
+    asked = jnp.max(jnp.where(slot[:, None] == slots, local_row[:, None], -1), axis=0)
+    return slot, asked
+
+
 def body(
     token_ids,
     lengths,
@@ -196,68 +333,124 @@
     attn_second,
     ffn_second,
 ):
+    ndp = lax.axis_size("dp")
+    nz = lax.axis_size("zero")
+    n = ndp * nz
+    my_dp = lax.axis_index("dp")
+    my_zero = lax.axis_index("zero")
+    me = my_dp * nz + my_zero
     pair_rows = token_ids.shape[0]
+    total_pairs = pair_rows * n
     flat_ids = token_ids.reshape(-1, SEQ)
     seq_rows = flat_ids.shape[0]
+    tokens = seq_rows * SEQ
     seq_lengths = lengths.reshape(-1)
     key_mask = lax.broadcasted_iota(jnp.int32, flat_ids.shape, 1) < seq_lengths[:, None]
-    vec_all = lax.all_gather(vectors.astype(jnp.bfloat16), "zero", axis=0, tiled=True).astype(
-        jnp.float32
-    )
     shard_rows = word_table.shape[0]
+    vec_len = vectors.shape[0]
+
+    room = -(-(tokens * 5 // 4) // (nz * 16)) * 16
+    owner, place, local_row = token_plan(flat_ids.reshape(-1), shard_rows)
+    slot, asked = round_slots(owner, place, local_row, 0, room, nz)
+    rounds_here = jnp.max(place) // room + 1
+    packet = jnp.concatenate(
+        [asked, false_neg.reshape(-1), pair_index, rounds_here[None].astype(jnp.int32)]
+    )
+    packets, vec_parts = exchange(
+        [pad_rows(packet, 8), pad_rows(vectors.astype(jnp.bfloat16), 16)],
+        ["all", "zero"],
+        ndp,
+        nz,
+        0,
+        "gather_requests",
+    )
+    packets = packets.reshape(n, -1)
+    asked_all = packets[:, : nz * room].reshape(n, nz, room)
+    at = nz * room
+    false_all = packets[:, at : at + pair_rows * total_pairs].reshape(total_pairs, total_pairs)
+    at = at + pair_rows * total_pairs
+    pair_all = packets[:, at : at + pair_rows].reshape(total_pairs)
+    rounds = jnp.max(packets[:, at + pair_rows])
+    vec_all = vec_parts.reshape(nz, -1)[:, :vec_len].reshape(-1).astype(jnp.float32)
+
+    layer_weights = []
+    for layer_index in range(LAYERS):
+        both = jnp.concatenate(
+            [attn_w[layer_index].astype(jnp.bfloat16), ffn_w[layer_index].astype(jnp.bfloat16)],
+            axis=1,
+        )
+        layer_weights.append(lax.all_gather(both, "zero", axis=0, tiled=True))
+
     word_half = word_table.astype(jnp.bfloat16)
-    whole_table = lax.all_gather(word_half, "zero", axis=0, tiled=True)
-    rows = whole_table[flat_ids].astype(jnp.float32)
+    asked_mine = lax.dynamic_index_in_dim(asked_all, my_zero, 1, keepdims=False)
+    asked_near = lax.dynamic_slice_in_dim(asked_mine, my_dp * nz, nz, 0)
+
+    def rows_for(wanted):
+        return matmul(one_hot(wanted.reshape(-1), shard_rows), word_half).astype(jnp.bfloat16)
+
+    def rows_from(slot_now, received):
+        return matmul(one_hot(slot_now, nz * room), received.reshape(nz * room, D)).astype(
+            jnp.bfloat16
+        )
+
+    (received,) = exchange(
+        [rows_for(asked_near).reshape(nz, room, D)], ["zero_p"], ndp, nz, 1, "send_rows"
+    )
+    rows = rows_from(slot, received)
+
+    def more_rows(state):
+        round_index, rows_now = state
+        slot_now, asked_now = round_slots(owner, place, local_row, round_index, room, nz)
+        wanted = lax.all_to_all(asked_now.reshape(nz, room), "zero", 0, 0, tiled=True)
+        got = lax.all_to_all(rows_for(wanted).reshape(nz, room, D), "zero", 0, 0, tiled=True)
+        return round_index + 1, rows_now + rows_from(slot_now, got)
+
+    _, rows = lax.while_loop(lambda state: state[0] < rounds, more_rows, (jnp.int32(1), rows))
+    rows = rows.reshape(seq_rows, SEQ, D).astype(jnp.float32)
+
     embedded, embed_back = jax.vjp(embed_tokens, rows, vec_all)
     hidden = embedded
     saved = []
     pooled = []
     for layer_index in range(LAYERS):
         layer_fn = functools.partial(encoder_layer, key_mask=key_mask, layer_index=layer_index)
-        attn_full, ffn_full = (
-            lax.all_gather(attn_w[layer_index].astype(jnp.bfloat16), "zero", axis=0, tiled=True),
-            lax.all_gather(ffn_w[layer_index].astype(jnp.bfloat16), "zero", axis=0, tiled=True),
-        )
+        weights = layer_weights[layer_index]
         output, layer_back = jax.vjp(
-            layer_fn, hidden, attn_full.astype(jnp.float32), ffn_full.astype(jnp.float32), vec_all
+            layer_fn,
+            hidden,
+            weights[:, : 4 * D].astype(jnp.float32),
+            weights[:, 4 * D :].astype(jnp.float32),
+            vec_all,
         )
         saved.append(layer_back)
         hidden = output
         pooled.append(pool_rows(hidden, key_mask, seq_lengths).astype(jnp.bfloat16))
-    shallow_pair = pooled[0].reshape(pair_rows, 2, D)
-    deep_pair = pooled[-1].reshape(pair_rows, 2, D)
-    shallow_all, deep_all = (
-        lax.all_gather(shallow_pair[:, 1], ("dp", "zero"), axis=0, tiled=True),
-        lax.all_gather(deep_pair[:, 1], ("dp", "zero"), axis=0, tiled=True),
-    )
-
-    def local_loss(shallow_anchor, deep_anchor, shallow_pos, deep_pos):
+
+    (pooled_all,) = exchange(
+        [jnp.stack(pooled).reshape(-1, 128)], ["all"], ndp, nz, 2, "gather_pooled"
+    )
+    pooled_all = pooled_all.reshape(n, 2, pair_rows, 2, D).astype(jnp.float32)
+    pooled_all = pooled_all.transpose(1, 3, 0, 2, 4).reshape(2, 2, total_pairs, D)
+
+    def whole_loss(shallow_anchor, deep_anchor, shallow_pos, deep_pos):
         return contrastive_terms(
-            shallow_anchor, deep_anchor, shallow_pos, deep_pos, false_neg, pair_index
+            shallow_anchor, deep_anchor, shallow_pos, deep_pos, false_all, pair_all
         )
 
-    loss_local, loss_back = jax.vjp(
-        local_loss,
-        shallow_pair[:, 0].astype(jnp.float32),
-        deep_pair[:, 0].astype(jnp.float32),
-        shallow_all.astype(jnp.float32),
-        deep_all.astype(jnp.float32),
-    )
-    valid_local = jnp.sum((pair_index >= 0).astype(jnp.float32))
-    loss_total, valid_total = lax.psum((loss_local, valid_local), ("dp", "zero"))
+    loss_total, loss_back = jax.vjp(
+        whole_loss, pooled_all[0, 0], pooled_all[1, 0], pooled_all[0, 1], pooled_all[1, 1]
+    )
+    valid_total = jnp.sum((pair_all >= 0).astype(jnp.float32))
     inverse = 1.0 / jnp.maximum(valid_total, 1.0)
     loss = loss_total * inverse
-    shallow_anchor_grad, deep_anchor_grad, shallow_pos_all, deep_pos_all = loss_back(inverse)
-    shallow_pos_grad, deep_pos_grad = (
-        lax.psum_scatter(shallow_pos_all, ("dp", "zero"), scatter_dimension=0, tiled=True),
-        lax.psum_scatter(deep_pos_all, ("dp", "zero"), scatter_dimension=0, tiled=True),
-    )
+    shallow_anchor_grad, deep_anchor_grad, shallow_pos_grad, deep_pos_grad = [
+        lax.dynamic_slice_in_dim(part, me * pair_rows, pair_rows, 0) for part in loss_back(inverse)
+    ]
     share = key_mask.astype(jnp.float32) / seq_lengths.astype(jnp.float32)[:, None]
     shallow_back = jnp.stack([shallow_anchor_grad, shallow_pos_grad], axis=1).reshape(seq_rows, D)
     deep_back = jnp.stack([deep_anchor_grad, deep_pos_grad], axis=1).reshape(seq_rows, D)
     grad_hidden = jnp.zeros_like(embedded)
-    attn_list = []
-    ffn_list = []
+    weight_parts = []
     vec_grad = jnp.zeros_like(vec_all)
     for layer_index in range(LAYERS - 1, -1, -1):
         if layer_index == LAYERS - 1:
@@ -266,36 +459,75 @@
             grad_hidden = grad_hidden + shallow_back[:, None, :] * share[:, :, None]
         layer_back = saved[layer_index]
         grad_hidden, attn_grad, ffn_grad, vec_layer_grad = layer_back(grad_hidden)
-        attn_list.insert(0, attn_grad)
-        ffn_list.insert(0, ffn_grad)
+        both = jnp.concatenate(
+            [attn_grad.astype(jnp.bfloat16), ffn_grad.astype(jnp.bfloat16)], axis=1
+        )
+        weight_parts.insert(0, lax.psum_scatter(both, "zero", scatter_dimension=0, tiled=True))
         vec_grad = vec_grad + vec_layer_grad
     rows_grad, vec_embed_grad = embed_back(grad_hidden)
     vec_grad = vec_grad + vec_embed_grad
     down_local = jnp.stack(
         [split_vectors(vec_grad)[3][layer_index][6] for layer_index in range(LAYERS)]
     )
-    attn_shard, ffn_shard, vec_shard, down_shard = (
-        lax.psum_scatter(jnp.stack(attn_list), "zero", scatter_dimension=1, tiled=True),
-        lax.psum_scatter(jnp.stack(ffn_list), "zero", scatter_dimension=1, tiled=True),
-        lax.psum_scatter(vec_grad, "zero", scatter_dimension=0, tiled=True),
-        lax.psum_scatter(down_local, "zero", scatter_dimension=1, tiled=True),
-    )
-    inside = (flat_ids >= 0) & (flat_ids < shard_rows * lax.axis_size("zero"))
-    target = jnp.where(inside, flat_ids, shard_rows * lax.axis_size("zero")).reshape(-1)
-    word_grad = lax.psum_scatter(
-        jnp.zeros((shard_rows * lax.axis_size("zero"), D), jnp.float32)
-        .at[target]
-        .add(rows_grad.reshape(-1, D), mode="drop"),
-        "zero",
-        scatter_dimension=0,
-        tiled=True,
-    )
-    word_grad, vec_shard, attn_shard, ffn_shard, down_shard = lax.psum(
-        (word_grad, vec_shard, attn_shard, ffn_shard, down_shard), "dp"
-    )
+
+    rows_grad = rows_grad.reshape(tokens, D).astype(jnp.bfloat16)
+
+    def slot_sums(slot_now):
+        picked = one_hot(slot_now, nz * room)
+        return lax.dot_general(
+            picked, rows_grad, (((0,), (0,)), ((), ())), preferred_element_type=jnp.float32
+        ).astype(jnp.bfloat16)
+
+    def into_rows(wanted, sums):
+        return lax.dot_general(
+            one_hot(wanted.reshape(-1), shard_rows),
+            sums.reshape(-1, D),
+            (((0,), (0,)), ((), ())),
+            preferred_element_type=jnp.float32,
+        )
+
+    down_each = down_local.reshape(LAYERS, nz, -1).transpose(1, 0, 2).reshape(nz, -1)
+    down_len = down_each.shape[1]
+    vec_blocks = jnp.concatenate([vec_grad.reshape(nz, vec_len), down_each], axis=1)
+    lines = -(-vec_blocks.shape[1] // 1024) * 8
+    vec_blocks = jnp.pad(vec_blocks, ((0, 0), (0, lines * 128 - vec_blocks.shape[1])))
+    sums_all, vec_shares = exchange(
+        [slot_sums(slot).reshape(nz, room, D), vec_blocks.reshape(nz, lines, 128)],
+        ["all_p", "all_p"],
+        ndp,
+        nz,
+        3,
+        "send_gradients",
+    )
+    word_grad = into_rows(asked_mine, sums_all)
+
+    def more_sums(state):
+        round_index, grad_now = state
+        slot_now, asked_now = round_slots(owner, place, local_row, round_index, room, nz)
+        wanted = lax.all_to_all(asked_now.reshape(nz, room), "zero", 0, 0, tiled=True)
+        got = lax.all_to_all(slot_sums(slot_now).reshape(nz, room, D), "zero", 0, 0, tiled=True)
+        wanted = lax.all_gather(wanted, "dp", axis=0, tiled=True)
+        got = lax.all_gather(got, "dp", axis=0, tiled=True)
+        return round_index + 1, grad_now + into_rows(wanted, got)
+
+    _, word_grad = lax.while_loop(
+        lambda state: state[0] < rounds, more_sums, (jnp.int32(1), word_grad)
+    )
+    vec_sum = jnp.sum(vec_shares.reshape(n, -1), axis=0)
+    vec_shard = vec_sum[:vec_len]
+    down_shard = vec_sum[vec_len : vec_len + down_len].reshape(LAYERS, -1)
+
+    (weight_all,) = exchange([jnp.stack(weight_parts)], ["dp"], ndp, nz, 4, "sum_replicas")
+    weight_sum = jnp.sum(weight_all.astype(jnp.float32), axis=0)
+    attn_shard = weight_sum[:, :, : 4 * D]
+    ffn_shard = weight_sum[:, :, 4 * D :]
+
     square_local = jnp.sum(word_grad * word_grad) + jnp.sum(vec_shard * vec_shard)
     square_local = square_local + jnp.sum(attn_shard * attn_shard) + jnp.sum(ffn_shard * ffn_shard)
-    square_total = lax.psum(square_local, "zero")
+    (squares,) = exchange(
+        [jnp.broadcast_to(square_local, (8, 128))], ["zero"], ndp, nz, 5, "gather_squares"
+    )
+    square_total = jnp.sum(squares[:, 0, 0])
     grad_norm = jnp.sqrt(square_total)
     factor = jnp.minimum(1.0, CLIP_NORM / (grad_norm + 1e-06))
     word_new, word_first_new, word_second_new = adam_update(

time: 2170 us -> 765 us (0.35)
  blocking collectives: 832 us -> 0 us
  waiting for transfers between devices: 716 us -> 173 us
  Pallas kernels: 0 us -> 186 us
  other arithmetic: 257 us -> 116 us
  local copies, waits for them, and re-layouts: 150 us -> 68.2 us
  matrix products: 147 us -> 177 us
  starting transfers between devices: 22.8 us -> 0.16 us
    unnamed x1 -> x0, blocking collectives: 676 us -> none
    unnamed x17 -> x4, waiting for transfers between devices: 342 us -> 0.72 us
    all_gather x5 -> x2, waiting for transfers between devices: 244 us -> 18.5 us  [body(): layer_weights.append(lax.all_gather(both, 'zero', axis=0, tiled=True))]
    pallas_call x0 -> x6, Pallas kernels: none -> 186 us  [exchange(): pl.pallas_call(functools.partial(exchange_kernel, tuple(modes), ndp, nz),...]
    reduce_scatter x2, waiting for transfers between devices: 0.01 us -> 153 us  [body(): lax.psum_scatter(both, 'zero', scatter_dimension=0, tiled=True)]
    psum x1 -> x0, waiting for transfers between devices: 131 us -> none  [body(): lax.psum((word_grad, vec_shard, attn_shard, ffn_shard, down_shard), 'dp')]
    scatter-add x1 -> x0, other arithmetic: 125 us -> none  [body(): word_grad = lax.psum_scatter(jnp.zeros((shard_rows * lax.axis_size('zero'...]
    psum x3 -> x0, blocking collectives: 79.3 us -> none  [the longest x1 37.3 us: body(): lax.psum((loss_local, valid_local), ('dp', 'zero'))]
  transfers between devices with their start and end apart: 13 -> 4, of which waited for: 10 -> 3; matrix products, arithmetic and copies ran while one was open for 47% -> 11% of each run, Pallas kernels for 0% -> 9%
where the time goes in v1:
time: 765 us; the launch traced here: 756 us
  Pallas kernels  186 us (24%)
  matrix products  177 us (23%)
  waiting for transfers between devices  173 us (23%)
  other arithmetic  116 us (15%)
  local copies, waits for them, and re-layouts  68.2 us (9%)
  between operations  26.7 us (3%)
  loops' own time  9.44 us (1%)
    pallas_call x6, Pallas kernels, exchange(): pl.pallas_call(functools.partial(exchange_kernel, tuple(modes), ndp, nz),...  186 us
    reduce_scatter x2, waiting for transfers between devices, body(): lax.psum_scatter(both, 'zero', scatter_dimension=0, tiled=True)  153 us
    dot_general x20, matrix products, matmul(): return jnp.dot(left, right, preferred_element_type=jnp.float32)  83.6 us
    dot_general x16, matrix products, einsum_plain(): return jnp.einsum(form, left, right, preferred_element_type=jnp.float32)  43.5 us
    dot_general x30, matrix products, contrastive_terms(): jnp.dot(normalized_rows(anchor_vectors[:, :current_width]), normalized_ro...  28.7 us
    convert_element_type x10, other arithmetic, low_back(): return build_low_back()(value)  22.9 us
    unnamed x473, local copies, waits for them, and re-layouts  21.1 us
    all_gather x2, waiting for transfers between devices, body(): layer_weights.append(lax.all_gather(both, 'zero', axis=0, tiled=True))  18.5 us
  transfers between devices with their start and end apart: 4, of which 3 were waited for; matrix products, arithmetic and copies ran while one was open for 11% of the time, Pallas kernels for 9%

profile of v1, /device:TPU:0, one launch (start us, length us, event | category | flops | bytes accessed | tf_op | source)
XLA Modules:
  0.0 755.9 jit_solution(14177490873440870144)
XLA Ops:
  17.2 24.5 %gather_requests.1 = (s32[32,16,128]{2,1,0:T(8,128)S(1)}, bf16[16,48,128]{2,1,0:T(8,128)(2,1)S(1)}) custom-call(s32[16,128]{1,0:T(8,128)S(1)} %pad_bitcast_fusion.1.refs_0_, bf16[48,128]{1,0:T(8,128)(2,1)S(1)} %pad_bitcast_fusion.refs_1_), custom_call_target="tpu_custom_call" | custom-call | bytes 9175040 | tf_op jit(solution)/shard_map/gather_requests/pallas_call | solution.py:175
  46.6 2.4 convert_element_type.309
  49.0 3.0 fusion.49
  51.9 43.4 %send_rows.1 = bf16[16,80,512]{2,1,0:T(8,128)(2,1)S(1)} custom-call(bf16[16,80,512]{2,1,0:T(8,128)(2,1)S(1)} %bitcast.432), custom_call_target="tpu_custom_call" | custom-call | bytes 26214400 | tf_op jit(solution)/shard_map/send_rows/pallas_call | solution.py:175
  96.9 8.6 %while.20 = (s32[]{:T(128)}, bf16[1024,512]{1,0:T(8,128)(2,1)S(1)}, s32[]{:T(128)}, s32[1024]{0:T(1024)S(1)}, s32[1024]{0:T(1024)S(1)}, /*index=5*/s32[1024]{0:T...) while((s32[]{:T(128)}, bf16[1024,512]{1,0:T(8,128)(2,1)S(1)}, s32[]{:T(128)}, ...), condition=%wide.region_7.8_spmd, body=%wide.region_5.7_spmd.sunk | while | flops 3852425984 | bytes 9369745 | solution.py:408
  107.8 3.3 add_convert_fusion.5
  112.9 2.3 copy.260
  118.2 5.8 fusion.319
  124.0 2.8 divide_convert_fusion.1
  128.2 3.3 fusion.320
  132.4 16.8 %multiply_convert_fusion.1 = (bf16[8,128,2048]{2,1,0:T(8,128)(2,1)S(1)}, f32[8,128,2048]{2,1,0:T(8,128)}) fusion(f32[2048]{0:T(1024)S(1)} %get-tuple-element.304, bf16[8,128,512]{2,1,0:T(8,128)(2,1)S(1)} %fusion.68, bf16[512,6144]{1,0:T(8,128)(2,1)S(1)} %bitcast.588), kind=kOutput, calls=%fused_computation.61 | convolution fusion | flops 2168455168 | bytes 15736832 | tf_op jit(solution)/shard_map/jvp()/dot_general | solution.py:78
  149.2 2.7 fusion.321
  153.5 18.5 %all-gather.9.cloned.1.call-done = bf16[512,6144]{1,0:T(8,128)(2,1)} async-done(((bf16[32,6144]{1,0:T(8,128)(2,1)}), bf16[512,6144]{1,0:T(8,128)(2,1)}) %all-gather.9.cloned.1.call-update) | async-done | bytes 6291472 | tf_op jit(solution)/shard_map/all_gather | solution.py:382
  172.0 3.2 add_convert_fusion.4
  176.9 2.4 copy.265
  182.2 5.7 fusion.322
  188.5 2.8 divide_convert_fusion
  192.7 3.2 fusion.323
  197.5 6.0 multiply_convert_fusion
  203.5 3.4 fusion.324
  208.7 16.6 %gather_pooled.1 = bf16[32,64,128]{2,1,0:T(8,128)(2,1)S(1)} custom-call(bf16[64,128]{1,0:T(8,128)(2,1)S(1)} %reshape.1049.refs_0_), custom_call_target="tpu_custom_call" | custom-call | bytes 10485760 | tf_op jit(solution)/shard_map/gather_pooled/pallas_call | solution.py:175
  255.2 2.3 multiply_reduce_fusion.29
  257.5 2.4 multiply_reduce_fusion.30
  277.6 2.3 fusion.54
  282.8 4.4 convolution_bitcast_fusion.3
  288.0 4.1 convolution_convert_fusion.1
  292.1 6.6 fusion.20
  299.9 4.4 convolution_bitcast_fusion.2
  304.4 5.5 multiply_reduce_fusion.7
  316.0 2.8 convolution_convert_fusion.5
  318.7 2.3 copy.280
  321.0 4.9 fusion.335
  331.4 2.9 fusion.44
  334.2 2.9 copy.282
  337.1 3.3 copy.284
  340.4 2.9 copy.286
  343.3 3.0 add_convert_fusion.3
  348.6 3.5 convolution_bitcast_fusion
  360.3 5.6 multiply_reduce_fusion.6
  367.1 4.5 convolution_convert_fusion
  371.7 6.5 fusion.25
  381.4 4.7 multiply_reduce_fusion.5
  388.7 2.9 convolution_convert_fusion.4
  393.2 2.8 fusion.336
  400.3 2.9 fusion.42
  405.0 3.0 copy.298
  409.8 3.3 add_convert_fusion.2
  416.2 3.9 multiply_reduce_fusion.4
  424.5 3.0 add_convert_fusion
  428.3 3.1 pad_maximum_fusion.1
  431.4 75.5 %send_gradients.1 = (bf16[32,80,512]{2,1,0:T(8,128)(2,1)S(1)}, f32[32,40,128]{2,1,0:T(8,128)S(1)}) custom-call(bf16[16,80,512]{2,1,0:T(8,128)(2,1)S(1)} %bitcast.431, f32[16,40,128]{2,1,0:T(8,128)S(1)} %bitcast.434), custom_call_target="tpu_custom_call" | custom-call | bytes 65536000 | tf_op jit(solution)/shard_map/send_gradients/pallas_call | solution.py:175
  506.9 7.7 %fusion.15 = f32[1908,512]{1,0:T(8,128)} fusion(bf16[2560,512]{1,0:T(8,128)(2,1)S(1)} %bitcast.437, s32[2560]{0:T(1024)S(1)} %copy-done.141), kind=kOutput, calls=%fused_computation.24 | convolution fusion | flops 5006592000 | bytes 6539264 | tf_op jit(solution)/shard_map/dot_general | solution.py:482
  523.4 2.4 convolution_bitcast_fusion.5
  525.9 4.5 convolution_bitcast_fusion.4
  530.4 3.1 add_convert_fusion.1
  533.5 3.1 pad_maximum_fusion
  539.5 4.0 multiply_reduce_fusion.3
  544.9 64.6 %reduce-scatter.5.cloned.1.call-done = bf16[32,6144]{1,0:T(8,128)(2,1)} async-done(((bf16[512,6144]{1,0:T(8,128)(2,1)}), bf16[32,6144]{1,0:T(8,128)(2,1)}) %reduce-scatter.5.cloned.1.call-update) | async-done | bytes 393232 | tf_op jit(solution)/shard_map/reduce_scatter | solution.py:465
  609.5 88.7 %reduce-scatter.3.cloned.1.call-done = bf16[32,6144]{1,0:T(8,128)(2,1)} async-done(((bf16[512,6144]{1,0:T(8,128)(2,1)}), bf16[32,6144]{1,0:T(8,128)(2,1)}) %reduce-scatter.3.cloned.1.call-update) | async-done | bytes 393232 | tf_op jit(solution)/shard_map/reduce_scatter | solution.py:465
  699.3 18.7 %sum_replicas.1 = bf16[2,2,32,6144]{3,2,1,0:T(8,128)(2,1)S(1)} custom-call(bf16[2,32,6144]{2,1,0:T(8,128)(2,1)S(1)} %pad_maximum_fusion.2.refs_0_), custom_call_target="tpu_custom_call" | custom-call | bytes 31457280 | tf_op jit(solution)/shard_map/sum_replicas/pallas_call | solution.py:175
  721.3 7.3 gather_squares.1
  731.2 2.7 fusion.302
  734.0 2.5 fusion.300
  738.6 8.3 %fusion.306 = (bf16[1908,512]{1,0:T(8,128)(2,1)}, f32[1908,512]{1,0:T(8,128)}, f32[1908,512]{1,0:T(8,128)}, f32[1908,512]{1,0:T(8,128)}) fusion(f32[1908,512]{1,0:T(8,128)S(1)} %copy-done.19, f32[1908,512]{1,0:T(8,128)S(1)} %copy-done.20, f32[]{:T(128)S(6)} %min.3, f32[1908,512]{1,0:T(8,128)} %param.29, f32[1908,512]{1,0:T(8,128)} %param.33), kind=kLoop, calls=%fused_computation.685 | loop fusion | flops 15630336 | bytes 29306884 | tf_op jit(solution)/shard_map/convert_element_type | solution.py:552
  (792 shorter events, 149.1 us)
Async XLA Ops:
  7.2 100.6 %all-gather.7.cloned.1.call-start = ((), (), s32[]{:S(2)}) async-start(), calls=%async_computation.6 | async-start | bytes 6684672 | tf_op jit(solution)/shard_map/all_gather | solution.py:382
  9.7 34.2 %copy-start.212 = (s32[4,2]{0,1:T(2,128)S(1)}, s32[4,2]{0,1:T(2,128)}, u32[]{:S(2)}) copy-start(s32[4,2]{0,1:T(2,128)} %param.22) | copy-start | bytes 100
  10.5 161.5 %all-gather.9.cloned.1.call-start = ((), (), s32[]{:S(2)}) async-start(), calls=%async_computation.7 | async-start | bytes 6684672 | tf_op jit(solution)/shard_map/all_gather | solution.py:382
  14.2 81.1 %copy-start.138 = (s32[1024]{0:T(1024)}, s32[1024]{0:T(1024)S(1)}, u32[]{:S(2)}) copy-start(s32[1024]{0:T(1024)S(1)} %get-tuple-element.315) | copy-start | bytes 12292
  46.4 81.7 %copy-start.33 = (f32[128,512]{1,0:T(8,128)}, f32[128,512]{1,0:T(8,128)S(1)}, u32[]{:S(2)}) copy-start(f32[128,512]{1,0:T(8,128)S(1)} %slice_convert_fusion) | copy-start | bytes 786436
  105.5 22.7 %copy-start.17 = (bf16[1024,512]{1,0:T(8,128)(2,1)}, bf16[1024,512]{1,0:T(8,128)(2,1)S(1)}, u32[]{:S(2)}) copy-start(bf16[1024,512]{1,0:T(8,128)(2,1)S(1)} %get-tuple-element.130) | copy-start | bytes 3145732
  105.8 22.4 %copy-start.116 = (f32[8,128]{1,0:T(8,128)}, f32[8,128]{1,0:T(8,128)S(1)}, u32[]{:S(2)}) copy-start(f32[8,128]{1,0:T(8,128)S(1)} %get-tuple-element.309) | copy-start | bytes 12292
  106.4 21.8 %copy-start.118 = (f32[8,128]{1,0:T(8,128)}, f32[8,128]{1,0:T(8,128)S(1)}, u32[]{:S(2)}) copy-start(f32[8,128]{1,0:T(8,128)S(1)} %bitcast_rsqrt_fusion) | copy-start | bytes 12292
  107.0 21.2 %copy-start.133 = (f32[512]{0:T(512)}, f32[512]{0:T(512)S(1)}, u32[]{:S(2)}) copy-start(f32[512]{0:T(512)S(1)} %get-tuple-element.302) | copy-start | bytes 6148
  107.0 42.2 %copy-start.135 = (f32[512]{0:T(512)}, f32[512]{0:T(512)S(1)}, u32[]{:S(2)}) copy-start(f32[512]{0:T(512)S(1)} %get-tuple-element.297) | copy-start | bytes 6148
  107.0 100.3 %copy-start.99 = (f32[512]{0:T(512)}, f32[512]{0:T(512)S(1)}, u32[]{:S(2)}) copy-start(f32[512]{0:T(512)S(1)} %get-tuple-element.294) | copy-start | bytes 6148
  107.0 100.4 %copy-start.101 = (f32[512]{0:T(512)}, f32[512]{0:T(512)S(1)}, u32[]{:S(2)}) copy-start(f32[512]{0:T(512)S(1)} %get-tuple-element.287) | copy-start | bytes 6148
  107.6 74.6 %copy-start.163 = (pred[8,128]{1,0:T(8,128)(4,1)}, pred[8,128]{1,0:T(8,128)(4,1)S(1)}, u32[]{:S(2)}) copy-start(pred[8,128]{1,0:T(8,128)(4,1)S(1)} %iota_compare_fusion.33) | copy-start | bytes 3076
  107.6 144.4 %copy-start.86 = (f32[128]{0:T(128)}, f32[128]{0:T(128)S(1)}, u32[]{:S(2)}) copy-start(f32[128]{0:T(128)S(1)} %get-tuple-element.319) | copy-start | bytes 1540
  107.6 144.4 %copy-start.88 = (f32[128]{0:T(128)}, f32[128]{0:T(128)S(1)}, u32[]{:S(2)}) copy-start(f32[128]{0:T(128)S(1)} %get-tuple-element.320) | copy-start | bytes 1540
  107.7 99.6 %copy-start.82 = (f32[8,128]{1,0:T(8,128)}, f32[8,128]{1,0:T(8,128)S(1)}, u32[]{:S(2)}) copy-start(f32[8,128]{1,0:T(8,128)S(1)} %convert_divide_fusion) | copy-start | bytes 12292
  107.7 24.6 %copy-start.125 = (f32[2048]{0:T(1024)}, f32[2048]{0:T(1024)S(1)}, u32[]{:S(2)}) copy-start(f32[2048]{0:T(1024)S(1)} %get-tuple-element.304) | copy-start | bytes 24580
  107.8 89.7 %copy-start.127 = (f32[2048]{0:T(1024)}, f32[2048]{0:T(1024)S(1)}, u32[]{:S(2)}) copy-start(f32[2048]{0:T(1024)S(1)} %get-tuple-element.303) | copy-start | bytes 24580
  118.2 8.6 %copy-start.25 = (bf16[8,128,512]{1,2,0:T(8,128)(2,1)}, bf16[8,128,512]{1,2,0:T(8,128)(2,1)S(1)}, u32[]{:S(2)}) copy-start(bf16[8,128,512]{1,2,0:T(8,128)(2,1)S(1)} %copy.257) | copy-start | bytes 3145732
  131.5 17.7 %copy-start.14 = (f32[8,128,512]{2,1,0:T(8,128)}, f32[8,128,512]{2,1,0:T(8,128)S(1)}, u32[]{:S(2)}) copy-start(f32[8,128,512]{2,1,0:T(8,128)S(1)} %get-tuple-element.324) | copy-start | bytes 6291460
  131.5 17.7 %copy-start.95 = (f32[8,128]{1,0:T(8,128)}, f32[8,128]{1,0:T(8,128)S(1)}, u32[]{:S(2)}) copy-start(f32[8,128]{1,0:T(8,128)S(1)} %broadcast_multiply_fusion.3) | copy-start | bytes 12292
  131.9 17.2 %copy-start.108 = (f32[8,128]{1,0:T(8,128)}, f32[8,128]{1,0:T(8,128)S(1)}, u32[]{:S(2)}) copy-start(f32[8,128]{1,0:T(8,128)S(1)} %multiply_reduce_fusion.17) | copy-start | bytes 12292
  131.9 17.3 %copy-start.120 = (f32[8,128]{1,0:T(8,128)}, f32[8,128]{1,0:T(8,128)S(1)}, u32[]{:S(2)}) copy-start(f32[8,128]{1,0:T(8,128)S(1)} %fusion.254) | copy-start | bytes 12292
  132.4 16.8 %copy-start.40 = (bf16[8,128,512]{2,1,0:T(8,128)(2,1)}, bf16[8,128,512]{2,1,0:T(8,128)(2,1)S(1)}, u32[]{:S(2)}) copy-start(bf16[8,128,512]{2,1,0:T(8,128)(2,1)S(1)} %fusion.68) | copy-start | bytes 3145732
  152.0 55.4 %copy-start.78 = (f32[8,128]{1,0:T(8,128)}, f32[8,128]{1,0:T(8,128)S(1)}, u32[]{:S(2)}) copy-start(f32[8,128]{1,0:T(8,128)S(1)} %broadcast_multiply_fusion.2) | copy-start | bytes 12292
  152.4 22.8 %copy-start.110 = (f32[8,128]{1,0:T(8,128)}, f32[8,128]{1,0:T(8,128)S(1)}, u32[]{:S(2)}) copy-start(f32[8,128]{1,0:T(8,128)S(1)} %multiply_reduce_fusion.16) | copy-start | bytes 12292
  152.4 55.0 %copy-start.84 = (f32[8,128]{1,0:T(8,128)}, f32[8,128]{1,0:T(8,128)S(1)}, u32[]{:S(2)}) copy-start(f32[8,128]{1,0:T(8,128)S(1)} %fusion.255) | copy-start | bytes 12292
  152.8 22.4 %copy-start.37 = (bf16[8,128,512]{2,1,0:T(8,128)(2,1)}, bf16[8,128,512]{2,1,0:T(8,128)(2,1)S(1)}, u32[]{:S(2)}) copy-start(bf16[8,128,512]{2,1,0:T(8,128)(2,1)S(1)} %fusion.87) | copy-start | bytes 3145732
  182.2 9.1 %copy-start.27 = (bf16[8,128,512]{1,2,0:T(8,128)(2,1)}, bf16[8,128,512]{1,2,0:T(8,128)(2,1)S(1)}, u32[]{:S(2)}) copy-start(bf16[8,128,512]{1,2,0:T(8,128)(2,1)S(1)} %copy.263) | copy-start | bytes 3145732
  231.2 17.7 %copy-start.201 = (f32[128]{0:T(128)}, f32[128]{0:T(128)S(1)}, u32[]{:S(2)}) copy-start(f32[128]{0:T(128)S(1)} %multiply_reduce_fusion.42) | copy-start | bytes 1540
  231.3 18.1 %copy-start.199 = (f32[128]{0:T(128)}, f32[128]{0:T(128)S(1)}, u32[]{:S(2)}) copy-start(f32[128]{0:T(128)S(1)} %multiply_reduce_fusion.34) | copy-start | bytes 1540
  231.4 13.2 %copy-start.198 = (f32[128]{0:T(128)}, f32[128]{0:T(128)S(1)}, u32[]{:S(2)}) copy-start(f32[128]{0:T(128)S(1)} %multiply_reduce_fusion.26) | copy-start | bytes 1540
  232.6 15.1 %copy-start.188 = (f32[128]{0:T(128)}, f32[128]{0:T(128)S(1)}, u32[]{:S(2)}) copy-start(f32[128]{0:T(128)S(1)} %multiply_reduce_fusion.43) | copy-start | bytes 1540
  232.6 15.6 %copy-start.186 = (f32[128]{0:T(128)}, f32[128]{0:T(128)S(1)}, u32[]{:S(2)}) copy-start(f32[128]{0:T(128)S(1)} %multiply_reduce_fusion.35) | copy-start | bytes 1540
  233.0 14.7 %copy-start.194 = (f32[128]{0:T(128)}, f32[128]{0:T(128)S(1)}, u32[]{:S(2)}) copy-start(f32[128]{0:T(128)S(1)} %multiply_reduce_fusion.44) | copy-start | bytes 1540
  233.0 15.2 %copy-start.190 = (f32[128]{0:T(128)}, f32[128]{0:T(128)S(1)}, u32[]{:S(2)}) copy-start(f32[128]{0:T(128)S(1)} %multiply_reduce_fusion.36) | copy-start | bytes 1540
  235.3 11.4 %copy-start.155 = (f32[128]{0:T(128)}, f32[128]{0:T(128)S(1)}, u32[]{:S(2)}) copy-start(f32[128]{0:T(128)S(1)} %get-tuple-element.406) | copy-start | bytes 1540
  235.3 11.4 %copy-start.157 = (f32[128]{0:T(128)}, f32[128]{0:T(128)S(1)}, u32[]{:S(2)}) copy-start(f32[128]{0:T(128)S(1)} %get-tuple-element.405) | copy-start | bytes 1540
  235.7 11.2 %copy-start.156 = (f32[128]{0:T(128)}, f32[128]{0:T(128)S(1)}, u32[]{:S(2)}) copy-start(f32[128]{0:T(128)S(1)} %get-tuple-element.412) | copy-start | bytes 1540
  235.7 11.2 %copy-start.159 = (f32[128]{0:T(128)}, f32[128]{0:T(128)S(1)}, u32[]{:S(2)}) copy-start(f32[128]{0:T(128)S(1)} %get-tuple-element.411) | copy-start | bytes 1540
  236.1 12.1 %copy-start.149 = (f32[128]{0:T(128)}, f32[128]{0:T(128)S(1)}, u32[]{:S(2)}) copy-start(f32[128]{0:T(128)S(1)} %get-tuple-element.408) | copy-start | bytes 1540
  236.5 11.7 %copy-start.161 = (f32[128]{0:T(128)}, f32[128]{0:T(128)S(1)}, u32[]{:S(2)}) copy-start(f32[128]{0:T(128)S(1)} %get-tuple-element.410) | copy-start | bytes 1540
  247.7 9.8 %copy-start.146 = (f32[128]{0:T(128)}, f32[128]{0:T(128)S(1)}, u32[]{:S(2)}) copy-start(f32[128]{0:T(128)S(1)} %get-tuple-element.414) | copy-start | bytes 1540
  247.7 9.8 %copy-start.147 = (f32[128]{0:T(128)}, f32[128]{0:T(128)S(1)}, u32[]{:S(2)}) copy-start(f32[128]{0:T(128)S(1)} %get-tuple-element.413) | copy-start | bytes 1540
  248.3 11.6 %copy-start.150 = (f32[128]{0:T(128)}, f32[128]{0:T(128)S(1)}, u32[]{:S(2)}) copy-start(f32[128]{0:T(128)S(1)} %get-tuple-element.420) | copy-start | bytes 1540
  248.3 11.6 %copy-start.151 = (f32[128]{0:T(128)}, f32[128]{0:T(128)S(1)}, u32[]{:S(2)}) copy-start(f32[128]{0:T(128)S(1)} %get-tuple-element.419) | copy-start | bytes 1540
  248.9 11.0 %copy-start.162 = (f32[128]{0:T(128)}, f32[128]{0:T(128)S(1)}, u32[]{:S(2)}) copy-start(f32[128]{0:T(128)S(1)} %get-tuple-element.416) | copy-start | bytes 1540
  249.5 11.6 %copy-start.153 = (f32[128]{0:T(128)}, f32[128]{0:T(128)S(1)}, u32[]{:S(2)}) copy-start(f32[128]{0:T(128)S(1)} %get-tuple-element.418) | copy-start | bytes 1540
  268.6 9.0 %copy-start.83 = (f32[8,128]{1,0:T(8,128)S(1)}, f32[8,128]{1,0:T(8,128)}, u32[]{:S(2)}) copy-start(f32[8,128]{1,0:T(8,128)} %copy-done.82) | copy-start | bytes 12292
  268.6 9.0 %copy-start.102 = (f32[512]{0:T(512)S(1)}, f32[512]{0:T(512)}, u32[]{:S(2)}) copy-start(f32[512]{0:T(512)} %copy-done.101) | copy-start | bytes 6148
  282.8 9.3 %slice-start.2 = ((s8[8388608]{0:T(1024)(128)(4,1)}), s8[4194304]{0:T(1024)(128)(4,1)S(1)}, s32[]{:S(2)}) async-start(s8[8388608]{0:T(1024)(128)(4,1)} %bitcast.543), calls=%async_computation.13 | async-start | bytes 8388608
  316.0 10.0 %copy-start.81 = (f32[8,8,128]{2,1,0:T(8,128)S(1)}, f32[8,8,128]{2,1,0:T(8,128)}, u32[]{:S(2)}) copy-start(f32[8,8,128]{2,1,0:T(8,128)} %multiply_divide_fusion.1) | copy-start | bytes 98308
  428.3 78.6 %copy-start.141 = (s32[2560]{0:T(1024)S(1)}, s32[2560]{0:T(1024)}, u32[]{:S(2)}) copy-start(s32[2560]{0:T(1024)} %eq.186) | copy-start | bytes 30724
  506.9 7.7 %copy-start.66 = (bf16[8,128,512]{2,1,0:T(8,128)(2,1)S(1)}, bf16[8,128,512]{2,1,0:T(8,128)(2,1)}, u32[]{:S(2)}) copy-start(bf16[8,128,512]{2,1,0:T(8,128)(2,1)} %copy-done.65) | copy-start | bytes 3145732
  506.9 7.7 %copy-start.70 = (s32[1024]{0:T(1024)S(1)}, s32[1024]{0:T(1024)}, u32[]{:S(2)}) copy-start(s32[1024]{0:T(1024)} %copy-done.69) | copy-start | bytes 12292
  506.9 7.7 %copy-start.72 = (s32[1024]{0:T(1024)S(1)}, s32[1024]{0:T(1024)}, u32[]{:S(2)}) copy-start(s32[1024]{0:T(1024)} %copy-done.71) | copy-start | bytes 12292
  506.9 7.7 %copy-start.74 = (s32[1024]{0:T(1024)S(1)}, s32[1024]{0:T(1024)}, u32[]{:S(2)}) copy-start(s32[1024]{0:T(1024)} %copy-done.73) | copy-start | bytes 12292
  515.5 93.9 %reduce-scatter.5.cloned.1.call-start = ((), (), s32[]{:S(2)}) async-start(), calls=%async_computation.9 | async-start | bytes 6684672 | tf_op jit(solution)/shard_map/reduce_scatter | solution.py:465
  516.3 181.9 %reduce-scatter.3.cloned.1.call-start = ((), (), s32[]{:S(2)}) async-start(), calls=%async_computation.8 | async-start | bytes 6684672 | tf_op jit(solution)/shard_map/reduce_scatter | solution.py:465
  718.0 12.6 %copy-start.91 = (f32[4928]{0:T(1024)S(1)}, f32[4928]{0:T(1024)}, u32[]{:S(2)}) copy-start(f32[4928]{0:T(1024)} %param.26) | copy-start | bytes 59140
  718.0 12.6 %copy-start.131 = (f32[4928]{0:T(1024)S(1)}, f32[4928]{0:T(1024)}, u32[]{:S(2)}) copy-start(f32[4928]{0:T(1024)} %param.30) | copy-start | bytes 59140
  718.0 12.6 %copy-start.132 = (f32[4928]{0:T(1024)S(1)}, f32[4928]{0:T(1024)}, u32[]{:S(2)}) copy-start(f32[4928]{0:T(1024)} %param.34) | copy-start | bytes 59140
  718.0 13.2 %copy-start.58 = (f32[2,32,2048]{2,1,0:T(8,128)S(1)}, f32[2,32,2048]{2,1,0:T(8,128)}, u32[]{:S(2)}) copy-start(f32[2,32,2048]{2,1,0:T(8,128)} %param.27) | copy-start | bytes 1572868
  719.9 14.0 %copy-start.39 = (f32[2,32,4096]{2,1,0:T(8,128)S(1)}, f32[2,32,4096]{2,1,0:T(8,128)}, u32[]{:S(2)}) copy-start(f32[2,32,4096]{2,1,0:T(8,128)} %param.28) | copy-start | bytes 3145732
  (175 other events, 621.4 us)
Sparse Core Ops, SparseCore 0:
  10.9 95.4 all-gather.6
  109.2 62.7 all-gather.8
  520.3 89.1 reduce-scatter.4
  613.8 84.3 reduce-scatter.2

commit v2 on v1

--- a/solution.py
+++ b/solution.py
@@ -184,6 +184,227 @@
         cost_estimate=pl.CostEstimate(flops=0, bytes_accessed=20 * moved, transcendentals=0),
         name=name,
     )(*arrays)
+
+
+def gradient_kernel(chunks, count, *refs):
+    take = iter(refs)
+    parts = [next(take) for _ in range(count)]
+    sums_ref, near_ref = next(take), next(take)
+    totals = [next(take) for _ in range(count)]
+    rows_ref, near_out = next(take), next(take)
+    bufs = [[next(take) for _ in range(5)] for _ in chunks]
+    near_buf = next(take)
+    send_a, recv_a, send_y, recv_y, send_z, recv_z, send_x, recv_x = [next(take) for _ in range(8)]
+    row_send, row_recv, pass_send, pass_recv, near_sem = [next(take) for _ in range(5)]
+
+    d = lax.axis_index("dp")
+    z = lax.axis_index("zero")
+    core = lax.rem(z, 2)
+    col = lax.rem(z // 2, 2)
+    line = z // 4
+    sibling = z + 1 - 2 * core
+    across = z + 2 - 4 * col
+
+    def along(k):
+        return lax.rem(line + k, 4) * 4 + lax.rem(z, 4)
+
+    barrier = pltpu.get_barrier_semaphore()
+
+    def greet(k, carry):
+        pl.semaphore_signal(
+            barrier, inc=1, device_id=(d, lax.rem(z + k, 16)), device_id_type=MESH
+        )
+        return carry
+
+    lax.fori_loop(1, 16, greet, 0)
+    pl.semaphore_signal(barrier, inc=1, device_id=(1 - d, z), device_id_type=MESH)
+    pl.semaphore_wait(barrier, 16)
+
+    def remote(src, dst, send, recv, to):
+        return pltpu.make_async_remote_copy(
+            src_ref=src,
+            dst_ref=dst,
+            send_sem=send,
+            recv_sem=recv,
+            device_id=to,
+            device_id_type=MESH,
+        )
+
+    def copy_a(i):
+        part, start, width = chunks[i]
+        src = parts[part].at[:, :, 1 - core, :, pl.ds(start, width)]
+        return remote(src, bufs[i][0], send_a.at[i], recv_a.at[i], (d, sibling))
+
+    def copy_y(i):
+        src = bufs[i][0].at[:, 1 - col]
+        return remote(src, bufs[i][1], send_y.at[i], recv_y.at[i], (d, across))
+
+    def copy_z(i, k):
+        src = bufs[i][1].at[lax.rem(line + k, 4)]
+        return remote(
+            src, bufs[i][2].at[k - 1], send_z.at[i, k - 1], recv_z.at[i, k - 1], (d, along(k))
+        )
+
+    def copy_x(i):
+        return remote(bufs[i][3], bufs[i][4], send_x.at[i], recv_x.at[i], (1 - d, z))
+
+    def row_push(k):
+        to = lax.rem(z + k, 16)
+        return remote(sums_ref.at[to], rows_ref.at[d, z], row_send.at[k], row_recv.at[k], (d, to))
+
+    def row_pass(k):
+        at = lax.rem(z + 16 - k, 16)
+        return remote(
+            rows_ref.at[d, at], rows_ref.at[d, at], pass_send.at[k], pass_recv.at[k], (1 - d, z)
+        )
+
+    near = remote(near_ref, near_buf, near_sem.at[0], near_sem.at[1], (1 - d, z))
+
+    total = len(chunks)
+    for i in range(total):
+        copy_a(i).start()
+
+    def push(k, carry):
+        row_push(k).start()
+        return carry
+
+    lax.fori_loop(1, 16, push, 0)
+    near.start()
+    rows_ref[d, z] = sums_ref[z]
+    row_pass(0).start()
+
+    def stage_a(i):
+        part, start, width = chunks[i]
+        copy_a(i).wait_recv()
+
+        buf = bufs[i][0]
+
+        def add_block(b, carry):
+            line_at, col_at = b // 2, lax.rem(b, 2)
+            mine = parts[part][line_at, col_at, core, :, pl.ds(start, width)].astype(jnp.float32)
+            got = buf[line_at, col_at].astype(jnp.float32)
+            buf[line_at, col_at] = (mine + got).astype(jnp.bfloat16)
+            return carry
+
+        lax.fori_loop(0, 8, add_block, 0)
+        copy_y(i).start()
+
+    def stage_y(i):
+        copy_y(i).wait_recv()
+        buf = bufs[i][1]
+
+        def add_block(b, carry):
+            mine = bufs[i][0][b, col].astype(jnp.float32)
+            buf[b] = (mine + buf[b].astype(jnp.float32)).astype(jnp.bfloat16)
+            return carry
+
+        lax.fori_loop(0, 4, add_block, 0)
+        for k in range(1, 4):
+            copy_z(i, k).start()
+
+    def stage_z(i):
+        for k in range(1, 4):
+            copy_z(i, k).wait_recv()
+        value = bufs[i][1][line].astype(jnp.float32)
+        for k in range(3):
+            value = value + bufs[i][2][k].astype(jnp.float32)
+        bufs[i][3][...] = value.astype(jnp.bfloat16)
+        copy_x(i).start()
+
+    def stage_x(i):
+        part, start, width = chunks[i]
+        copy_x(i).wait_recv()
+        totals[part][:, pl.ds(start, width)] = bufs[i][3][...].astype(jnp.float32) + bufs[i][4][
+            ...
+        ].astype(jnp.float32)
+
+    def pass_on(k):
+        row_push(k).wait_recv()
+        row_pass(k).start()
+
+    passed = 1
+    for t in range(total + 3):
+        if t < total:
+            stage_a(t)
+        if 0 <= t - 1 < total:
+            stage_y(t - 1)
+        if 0 <= t - 2 < total:
+            stage_z(t - 2)
+        if 0 <= t - 3 < total:
+            stage_x(t - 3)
+        until = min(16, 1 + (t + 1) * 15 // (total + 3))
+        for k in range(passed, until):
+            pass_on(k)
+        passed = until
+    for k in range(passed, 16):
+        pass_on(k)
+
+    near.wait()
+    near_out[...] = near_ref[...].astype(jnp.float32) + near_buf[...].astype(jnp.float32)
+
+    for i in range(total):
+        copy_a(i).wait_send()
+        copy_y(i).wait_send()
+        for k in range(1, 4):
+            copy_z(i, k).wait_send()
+        copy_x(i).wait_send()
+
+    def finish(k, carry):
+        row_push(k).wait_send()
+        return carry
+
+    lax.fori_loop(1, 16, finish, 0)
+
+    def finish_pass(k, carry):
+        row_pass(k).wait_send()
+        at = lax.rem(z + 16 - k, 16)
+        remote(
+            rows_ref.at[1 - d, at], rows_ref.at[1 - d, at], pass_send.at[k], pass_recv.at[k], (1 - d, z)
+        ).wait_recv()
+        return carry
+
+    lax.fori_loop(0, 16, finish_pass, 0)
+
+
+def exchange_gradients(parts, sums, near, collective_id):
+    chunks = []
+    for index, part in enumerate(parts):
+        width = min(part.shape[4], 1024)
+        for start in range(0, part.shape[4], width):
+            chunks.append((index, start, width))
+    half = jnp.bfloat16
+    scratch = []
+    for index, start, width in chunks:
+        r = parts[index].shape[3]
+        scratch += [
+            pltpu.VMEM((4, 2, r, width), half),
+            pltpu.VMEM((4, r, width), half),
+            pltpu.VMEM((3, r, width), half),
+            pltpu.VMEM((r, width), half),
+            pltpu.VMEM((r, width), half),
+        ]
+    scratch += [pltpu.VMEM(near.shape, half)]
+    dma = pltpu.SemaphoreType.DMA
+    count = len(chunks)
+    scratch += [dma((count,)) for _ in range(4)] + [dma((count, 3)) for _ in range(2)]
+    scratch += [dma((count,)) for _ in range(2)]
+    scratch += [dma((16,)) for _ in range(4)] + [dma((2,))]
+    outs = [jax.ShapeDtypeStruct(part.shape[3:], jnp.float32) for part in parts]
+    outs += [jax.ShapeDtypeStruct((2,) + sums.shape, sums.dtype)]
+    outs += [jax.ShapeDtypeStruct(near.shape, jnp.float32)]
+    vmem = pl.BlockSpec(memory_space=pltpu.VMEM)
+    return pl.pallas_call(
+        functools.partial(gradient_kernel, tuple(chunks), len(parts)),
+        out_shape=tuple(outs),
+        in_specs=[vmem] * (len(parts) + 2),
+        out_specs=tuple([vmem] * len(outs)),
+        scratch_shapes=scratch,
+        compiler_params=pltpu.CompilerParams(
+            collective_id=collective_id, has_side_effects=True, vmem_limit_bytes=48 * 1024 * 1024
+        ),
+        cost_estimate=pl.CostEstimate(flops=0, bytes_accessed=200_000_000, transcendentals=0),
+        name="exchange_gradients",
+    )(*parts, sums, near)
 
 
 def split_vectors(vec_all):
@@ -349,7 +570,7 @@
     shard_rows = word_table.shape[0]
     vec_len = vectors.shape[0]
 
-    room = -(-(tokens * 5 // 4) // (nz * 16)) * 16
+    room = -(-(tokens * 9 // 8) // (nz * 8)) * 8
     owner, place, local_row = token_plan(flat_ids.reshape(-1), shard_rows)
     slot, asked = round_slots(owner, place, local_row, 0, room, nz)
     rounds_here = jnp.max(place) // room + 1
@@ -451,6 +672,7 @@
     deep_back = jnp.stack([deep_anchor_grad, deep_pos_grad], axis=1).reshape(seq_rows, D)
     grad_hidden = jnp.zeros_like(embedded)
     weight_parts = []
+    by_hand = (ndp, nz) == (2, 16)
     vec_grad = jnp.zeros_like(vec_all)
     for layer_index in range(LAYERS - 1, -1, -1):
         if layer_index == LAYERS - 1:
@@ -459,10 +681,14 @@
             grad_hidden = grad_hidden + shallow_back[:, None, :] * share[:, :, None]
         layer_back = saved[layer_index]
         grad_hidden, attn_grad, ffn_grad, vec_layer_grad = layer_back(grad_hidden)
-        both = jnp.concatenate(
-            [attn_grad.astype(jnp.bfloat16), ffn_grad.astype(jnp.bfloat16)], axis=1
-        )
-        weight_parts.insert(0, lax.psum_scatter(both, "zero", scatter_dimension=0, tiled=True))
+        if by_hand and layer_index == 0:
+            weight_parts.insert(0, (attn_grad.astype(jnp.bfloat16), ffn_grad.astype(jnp.bfloat16)))
+        else:
+            both = jnp.concatenate(
+                [attn_grad.astype(jnp.bfloat16), ffn_grad.astype(jnp.bfloat16)], axis=1
+            )
+            both, grad_hidden = lax.optimization_barrier((both, grad_hidden))
+            weight_parts.insert(0, lax.psum_scatter(both, "zero", scatter_dimension=0, tiled=True))
         vec_grad = vec_grad + vec_layer_grad
     rows_grad, vec_embed_grad = embed_back(grad_hidden)
     vec_grad = vec_grad + vec_embed_grad
@@ -491,14 +717,36 @@
     vec_blocks = jnp.concatenate([vec_grad.reshape(nz, vec_len), down_each], axis=1)
     lines = -(-vec_blocks.shape[1] // 1024) * 8
     vec_blocks = jnp.pad(vec_blocks, ((0, 0), (0, lines * 128 - vec_blocks.shape[1])))
-    sums_all, vec_shares = exchange(
-        [slot_sums(slot).reshape(nz, room, D), vec_blocks.reshape(nz, lines, 128)],
-        ["all_p", "all_p"],
-        ndp,
-        nz,
-        3,
-        "send_gradients",
-    )
+    sums = slot_sums(slot).reshape(nz, room, D)
+    if by_hand:
+        attn_part, ffn_part = weight_parts[0]
+        attn_near, ffn_near, vec_near, sums_all, other_near = exchange_gradients(
+            [
+                attn_part.reshape(4, 2, 2, -1, 4 * D),
+                ffn_part.reshape(4, 2, 2, -1, 2 * FF),
+                vec_blocks.astype(jnp.bfloat16).reshape(4, 2, 2, lines, 128),
+            ],
+            sums,
+            weight_parts[1],
+            3,
+        )
+        attn_shard = jnp.stack([attn_near, other_near[:, : 4 * D]])
+        ffn_shard = jnp.stack([ffn_near, other_near[:, 4 * D :]])
+        vec_sum = vec_near.reshape(-1)
+    else:
+        sums_all, vec_shares = exchange(
+            [sums, vec_blocks.reshape(nz, lines, 128)],
+            ["all_p", "all_p"],
+            ndp,
+            nz,
+            3,
+            "send_gradients",
+        )
+        vec_sum = jnp.sum(vec_shares.reshape(n, -1), axis=0)
+        (weight_all,) = exchange([jnp.stack(weight_parts)], ["dp"], ndp, nz, 4, "sum_replicas")
+        weight_sum = jnp.sum(weight_all.astype(jnp.float32), axis=0)
+        attn_shard = weight_sum[:, :, : 4 * D]
+        ffn_shard = weight_sum[:, :, 4 * D :]
     word_grad = into_rows(asked_mine, sums_all)
 
     def more_sums(state):
@@ -513,14 +761,8 @@
     _, word_grad = lax.while_loop(
         lambda state: state[0] < rounds, more_sums, (jnp.int32(1), word_grad)
     )
-    vec_sum = jnp.sum(vec_shares.reshape(n, -1), axis=0)
     vec_shard = vec_sum[:vec_len]
     down_shard = vec_sum[vec_len : vec_len + down_len].reshape(LAYERS, -1)
-
-    (weight_all,) = exchange([jnp.stack(weight_parts)], ["dp"], ndp, nz, 4, "sum_replicas")
-    weight_sum = jnp.sum(weight_all.astype(jnp.float32), axis=0)
-    attn_shard = weight_sum[:, :, : 4 * D]
-    ffn_shard = weight_sum[:, :, 4 * D :]
 
     square_local = jnp.sum(word_grad * word_grad) + jnp.sum(vec_shard * vec_shard)
     square_local = square_local + jnp.sum(attn_shard * attn_shard) + jnp.sum(ffn_shard * ffn_shard)

time: 765 us -> 602 us (0.79)
  waiting for transfers between devices: 173 us -> 37.3 us
  Pallas kernels: 186 us -> 170 us
  loops' own time: 9.44 us -> 1.78 us
    reduce_scatter x2 -> x1, waiting for transfers between devices: 153 us -> 0.01 us  [body(): lax.psum_scatter(both, 'zero', scatter_dimension=0, tiled=True)]
    pallas_call x6 -> x4, Pallas kernels: 186 us -> 90 us  [exchange(): pl.pallas_call(functools.partial(exchange_kernel, tuple(modes), ndp, nz),...]
    pallas_call x0 -> x1, Pallas kernels: none -> 79.8 us  [exchange_gradients(): pl.pallas_call(functools.partial(gradient_kernel, tuple(chunks), len(part...]
    all_gather x2, waiting for transfers between devices: 18.5 us -> 37.3 us  [body(): layer_weights.append(lax.all_gather(both, 'zero', axis=0, tiled=True))]
    another operation x1, loops' own time: 8.57 us -> 0.87 us  [body(): lax.while_loop(lambda state: state[0] < rounds, more_rows, (jnp.int32(1),...]
    convert_element_type x10 -> x11, other arithmetic: 22.9 us -> 24.5 us  [low_back(): return build_low_back()(value)]
    unnamed x473 -> x479, local copies, waits for them, and re-layouts: 21.1 us -> 20.8 us
  transfers between devices with their start and end apart: 4 -> 3, of which waited for: 3 -> 2; matrix products, arithmetic and copies ran while one was open for 11% -> 22% of each run, Pallas kernels for 9% -> 11%
where the time goes in v2:
time: 602 us; the launch traced here: 594 us
  matrix products  175 us (29%)
  Pallas kernels  170 us (28%)
  other arithmetic  114 us (19%)
  local copies, waits for them, and re-layouts  69 us (11%)
  waiting for transfers between devices  37.3 us (6%)
  between operations  26.7 us (4%)
    pallas_call x4, Pallas kernels, exchange(): pl.pallas_call(functools.partial(exchange_kernel, tuple(modes), ndp, nz),...  90 us
    pallas_call x1, Pallas kernels, exchange_gradients(): pl.pallas_call(functools.partial(gradient_kernel, tuple(chunks), len(part...  79.8 us
    dot_general x20, matrix products, matmul(): return jnp.dot(left, right, preferred_element_type=jnp.float32)  76.7 us
    dot_general x16, matrix products, einsum_plain(): return jnp.einsum(form, left, right, preferred_element_type=jnp.float32)  45.9 us
    all_gather x2, waiting for transfers between devices, body(): layer_weights.append(lax.all_gather(both, 'zero', axis=0, tiled=True))  37.3 us
    dot_general x30, matrix products, contrastive_terms(): jnp.dot(normalized_rows(anchor_vectors[:, :current_width]), normalized_ro...  28.7 us
    convert_element_type x11, other arithmetic, low_back(): return build_low_back()(value)  24.5 us
    unnamed x479, local copies, waits for them, and re-layouts  20.8 us
  transfers between devices with their start and end apart: 3, of which 2 were waited for; matrix products, arithmetic and copies ran while one was open for 22% of the time, Pallas kernels for 11%

profile of v2, /device:TPU:0, one launch (start us, length us, event | category | flops | bytes accessed | tf_op | source)
XLA Modules:
  0.0 593.6 jit_solution(14936473887989404120)
XLA Ops:
  17.2 24.5 %gather_requests.1 = (s32[32,16,128]{2,1,0:T(8,128)S(1)}, bf16[16,48,128]{2,1,0:T(8,128)(2,1)S(1)}) custom-call(s32[16,128]{1,0:T(8,128)S(1)} %pad_bitcast_fusion.1.refs_0_, bf16[48,128]{1,0:T(8,128)(2,1)S(1)} %pad_bitcast_fusion.refs_1_), custom_call_target="tpu_custom_call" | custom-call | bytes 9175040 | tf_op jit(solution)/shard_map/gather_requests/pallas_call | solution.py:175
  46.6 2.4 convert_element_type.307
  49.0 2.7 fusion.49
  51.7 40.7 %send_rows.1 = bf16[16,72,512]{2,1,0:T(8,128)(2,1)S(1)} custom-call(bf16[16,72,512]{2,1,0:T(8,128)(2,1)S(1)} %bitcast.439), custom_call_target="tpu_custom_call" | custom-call | bytes 23592960 | tf_op jit(solution)/shard_map/send_rows/pallas_call | solution.py:175
  97.1 7.8 %all-gather.7.cloned.1.call-done = bf16[512,6144]{1,0:T(8,128)(2,1)} async-done(((bf16[32,6144]{1,0:T(8,128)(2,1)}), bf16[512,6144]{1,0:T(8,128)(2,1)}) %all-gather.7.cloned.1.call-update) | async-done | bytes 6291472 | tf_op jit(solution)/shard_map/all_gather | solution.py:603
  104.9 3.2 add_convert_fusion.5
  109.9 2.3 copy.250
  115.2 5.9 fusion.323
  121.1 2.8 divide_convert_fusion.1
  125.2 3.3 fusion.324
  129.5 6.4 %multiply_convert_fusion.1 = (bf16[8,128,2048]{2,1,0:T(8,128)(2,1)S(1)}, f32[8,128,2048]{2,1,0:T(8,128)}) fusion(f32[2048]{0:T(1024)S(1)} %get-tuple-element.312, bf16[8,128,512]{2,1,0:T(8,128)(2,1)S(1)} %fusion.68, bf16[512,6144]{1,0:T(8,128)(2,1)S(1)} %bitcast.597), kind=kOutput, calls=%fused_computation.61 | convolution fusion | flops 2168455168 | bytes 15736832 | tf_op jit(solution)/shard_map/jvp()/dot_general | solution.py:78
  135.9 2.7 fusion.325
  140.2 29.5 %all-gather.9.cloned.1.call-done = bf16[512,6144]{1,0:T(8,128)(2,1)} async-done(((bf16[32,6144]{1,0:T(8,128)(2,1)}), bf16[512,6144]{1,0:T(8,128)(2,1)}) %all-gather.9.cloned.1.call-update) | async-done | bytes 6291472 | tf_op jit(solution)/shard_map/all_gather | solution.py:603
  169.7 3.2 add_convert_fusion.4
  174.6 2.4 copy.255
  179.9 5.7 fusion.326
  186.2 2.8 divide_convert_fusion
  190.4 3.2 fusion.327
  195.2 6.0 %multiply_convert_fusion = (bf16[8,128,2048]{2,1,0:T(8,128)(2,1)S(1)}, f32[8,128,2048]{2,1,0:T(8,128)}) fusion(f32[2048]{0:T(1024)S(1)} %get-tuple-element.311, bf16[8,128,512]{2,1,0:T(8,128)(2,1)S(1)} %fusion.69, bf16[512,6144]{1,0:T(8,128)(2,1)S(1)} %bitcast.586), kind=kOutput, calls=%fused_computation.60 | convolution fusion | flops 2168455168 | bytes 15736832 | tf_op jit(solution)/shard_map/jvp()/dot_general | solution.py:78
  201.2 3.4 fusion.328
  206.4 16.4 %gather_pooled.1 = bf16[32,64,128]{2,1,0:T(8,128)(2,1)S(1)} custom-call(bf16[64,128]{1,0:T(8,128)(2,1)S(1)} %reshape.1058.refs_0_), custom_call_target="tpu_custom_call" | custom-call | bytes 10485760 | tf_op jit(solution)/shard_map/gather_pooled/pallas_call | solution.py:175
  252.6 2.4 multiply_reduce_fusion.29
  255.0 2.4 multiply_reduce_fusion.30
  280.4 4.4 convolution_bitcast_fusion.5
  284.8 4.1 convolution_convert_fusion.1
  289.0 6.8 %fusion.20 = bf16[8,128,2048]{2,1,0:T(8,128)(2,1)S(1)} fusion(bf16[8,128,2048]{2,1,0:T(8,128)(2,1)S(1)} %convolution_convert_fusion.1, f32[8,128,2048]{2,1,0:T(8,128)S(1)} %bitcast.556, f32[2048]{0:T(1024)S(1)} %copy-done.134), kind=kLoop, calls=%fused_computation.38 | loop fusion | flops 46137344 | bytes 16785408 | tf_op jit(solution)/shard_map/transpose(jvp())/convert_element_type | solution.py:70
  295.8 4.4 convolution_bitcast_fusion.4
  300.2 5.6 multiply_reduce_fusion.8
  311.1 2.8 convolution_convert_fusion.5
  316.1 5.0 fusion.339
  326.5 2.9 fusion.44
  329.4 2.9 copy.275
  332.2 2.9 copy.277
  335.2 2.9 copy.279
  338.0 3.2 add_convert_fusion.3
  343.5 3.5 convolution_bitcast_fusion.1
  354.5 4.2 add_convert_fusion.1
  359.4 3.1 pad_maximum_fusion
  362.5 6.2 %add_add_fusion.11 = f32[8,128,512]{2,1,0:T(8,128)} fusion(f32[8,128,512]{2,1,0:T(8,128)} %copy-done.35, bf16[8,128,1536]{2,1,0:T(8,128)(2,1)} %copy-done.5, bf16[512,6144]{1,0:T(8,128)(2,1)} %all-gather.9.cloned.1.call-done, f32[8,128]{1,0:T(8,128)S(1)} %negate_multiply_fusion.3), kind=kOutput, calls=%fused_computation.176 | convolution fusion | flops 1611661312 | bytes 8916992 | tf_op jit(solution)/shard_map/transpose(jvp())/dot_general | solution.py:78
  369.4 2.5 multiply_reduce_fusion.7
  373.3 4.4 convolution_convert_fusion
  377.8 6.6 %fusion.25 = bf16[8,128,2048]{2,1,0:T(8,128)(2,1)S(1)} fusion(bf16[8,128,2048]{2,1,0:T(8,128)(2,1)S(1)} %convolution_convert_fusion, f32[8,128,2048]{2,1,0:T(8,128)S(1)} %bitcast.554, f32[2048]{0:T(1024)S(1)} %copy-done.132), kind=kLoop, calls=%fused_computation.43 | loop fusion | flops 46137344 | bytes 16785408 | tf_op jit(solution)/shard_map/transpose(jvp())/convert_element_type | solution.py:70
  384.5 6.4 %multiply_reduce_fusion.6 = (f32[512]{0:T(512)S(1)}, f32[8,128]{1,0:T(8,128)S(1)}, f32[512]{0:T(512)S(1)}, f32[8,128,512]{2,1,0:T(8,128)S(1)}) fusion(f32[8,128,512]{2,1,0:T(8,128)S(1)} %copy-done.19, f32[8,128]{1,0:T(8,128)S(1)} %copy-done.128, f32[8,128]{1,0:T(8,128)S(1)} %copy-done.105, f32[512]{0:T(512)S(1)} %copy-done.141, ...), kind=kOutput, calls=%fused_computation.133 | convolution fusion | flops 2152724480 | bytes 12605440 | tf_op jit(solution)/shard_map/transpose(jvp())/dot_general | solution.py:78
  394.0 2.9 convolution_convert_fusion.4
  398.5 2.9 fusion.340
  401.4 3.0 copy.292
  404.4 3.3 multiply_reduce_fusion
  409.1 2.9 fusion.42
  412.0 3.0 copy.294
  417.0 2.9 copy.296
  419.8 3.2 add_convert_fusion.2
  425.5 5.7 multiply_reduce_fusion.5
  441.8 3.8 convolution_bitcast_fusion
  446.8 2.7 fusion.48
  449.5 2.4 convolution_bitcast_fusion.3
  452.0 2.4 convolution_bitcast_fusion.2
  454.5 2.5 add_convert_fusion
  459.3 79.8 %exchange_gradients.1 = (f32[32,2048]{1,0:T(8,128)S(1)}, f32[32,4096]{1,0:T(8,128)S(1)}, f32[40,128]{1,0:T(8,128)S(1)}, bf16[2,16,72,512]{3,2,1,0:T(8,128)(2,1)}, f32[32,6144]{1,0:T(8,128)S(1)}) custom-call(bf16[4,2,2,32,2048]{4,3,2,1,0:T(8,128)(2,1)S(1)} %bitcast.436, bf16[4,2,2,32,4096]{4,3,2,1,0:T(8,128)(2,1)} %bitcast.536, ...), custom_call_target="tpu_custom_call" | custom-call | bytes 200000000 | tf_op jit(solution)/shard_map/exchange_gradients/pallas_call | solution.py:396
  539.9 8.9 %fusion.15 = f32[1908,512]{1,0:T(8,128)} fusion(bf16[2304,512]{1,0:T(8,128)(2,1)} %bitcast.599, s32[2304]{0:T(1024)S(1)} %copy-done.145), kind=kOutput, calls=%fused_computation.24 | convolution fusion | flops 4505932800 | bytes 6276096 | tf_op jit(solution)/shard_map/dot_general | solution.py:708
  549.9 3.8 multiply_reduce_fusion.3
  557.9 8.4 %gather_squares.1 = f32[16,8,128]{2,1,0:T(8,128)S(1)} custom-call(f32[8,128]{1,0:T(8,128)S(1)} %broadcast_in_dim.413.refs_0_), custom_call_target="tpu_custom_call" | custom-call | bytes 1310720 | tf_op jit(solution)/shard_map/gather_squares/pallas_call | solution.py:175
  569.0 2.7 fusion.306
  571.7 2.5 fusion.304
  576.3 8.2 %fusion.310 = (bf16[1908,512]{1,0:T(8,128)(2,1)}, f32[1908,512]{1,0:T(8,128)}, f32[1908,512]{1,0:T(8,128)}, f32[1908,512]{1,0:T(8,128)}) fusion(f32[1908,512]{1,0:T(8,128)S(1)} %copy-done.22, f32[1908,512]{1,0:T(8,128)S(1)} %copy-done.23, f32[]{:T(128)S(6)} %min.3, f32[1908,512]{1,0:T(8,128)} %param.29, f32[1908,512]{1,0:T(8,128)} %param.33), kind=kLoop, calls=%fused_computation.688 | loop fusion | flops 15630336 | bytes 29306884 | tf_op jit(solution)/shard_map/convert_element_type | solution.py:794
  (795 shorter events, 142.4 us)
Async XLA Ops:
  7.2 97.7 %all-gather.7.cloned.1.call-start = ((), (), s32[]{:S(2)}) async-start(), calls=%async_computation.5 | async-start | bytes 6684672 | tf_op jit(solution)/shard_map/all_gather | solution.py:603
  9.7 34.2 %copy-start.216 = (s32[4,2]{0,1:T(2,128)S(1)}, s32[4,2]{0,1:T(2,128)}, u32[]{:S(2)}) copy-start(s32[4,2]{0,1:T(2,128)} %param.22) | copy-start | bytes 100
  10.5 159.1 %all-gather.9.cloned.1.call-start = ((), (), s32[]{:S(2)}) async-start(), calls=%async_computation.6 | async-start | bytes 6684672 | tf_op jit(solution)/shard_map/all_gather | solution.py:603
  11.4 445.6 %reduce-scatter.2.cloned.1.call-start = ((), (), s32[]{:S(2)}) async-start(), calls=%async_computation.7 | async-start | bytes 6684672 | tf_op jit(solution)/shard_map/reduce_scatter | solution.py:691
  14.2 78.1 %copy-start.142 = (s32[1024]{0:T(1024)}, s32[1024]{0:T(1024)S(1)}, u32[]{:S(2)}) copy-start(s32[1024]{0:T(1024)S(1)} %get-tuple-element.325) | copy-start | bytes 12292
  46.5 78.7 %copy-start.37 = (f32[128,512]{1,0:T(8,128)}, f32[128,512]{1,0:T(8,128)S(1)}, u32[]{:S(2)}) copy-start(f32[128,512]{1,0:T(8,128)S(1)} %slice_convert_fusion) | copy-start | bytes 786436
  94.8 30.3 %copy-start.20 = (bf16[1024,512]{1,0:T(8,128)(2,1)}, bf16[1024,512]{1,0:T(8,128)(2,1)S(1)}, u32[]{:S(2)}) copy-start(bf16[1024,512]{1,0:T(8,128)(2,1)S(1)} %get-tuple-element.135) | copy-start | bytes 3145732
  95.2 30.0 %copy-start.123 = (f32[8,128]{1,0:T(8,128)}, f32[8,128]{1,0:T(8,128)S(1)}, u32[]{:S(2)}) copy-start(f32[8,128]{1,0:T(8,128)S(1)} %get-tuple-element.319) | copy-start | bytes 12292
  95.7 12.4 %copy-start.113 = (f32[1024]{0:T(1024)}, f32[1024]{0:T(1024)S(1)}, u32[]{:S(2)}) copy-start(f32[1024]{0:T(1024)S(1)} %multiply_reduce_fusion.18) | copy-start | bytes 12292
  95.8 29.4 %copy-start.125 = (f32[8,128]{1,0:T(8,128)}, f32[8,128]{1,0:T(8,128)S(1)}, u32[]{:S(2)}) copy-start(f32[8,128]{1,0:T(8,128)S(1)} %bitcast_rsqrt_fusion) | copy-start | bytes 12292
  96.4 28.8 %copy-start.138 = (f32[512]{0:T(512)}, f32[512]{0:T(512)S(1)}, u32[]{:S(2)}) copy-start(f32[512]{0:T(512)S(1)} %get-tuple-element.310) | copy-start | bytes 6148
  96.4 39.5 %copy-start.140 = (f32[512]{0:T(512)}, f32[512]{0:T(512)S(1)}, u32[]{:S(2)}) copy-start(f32[512]{0:T(512)S(1)} %get-tuple-element.305) | copy-start | bytes 6148
  96.4 108.7 %copy-start.99 = (f32[512]{0:T(512)}, f32[512]{0:T(512)S(1)}, u32[]{:S(2)}) copy-start(f32[512]{0:T(512)S(1)} %get-tuple-element.302) | copy-start | bytes 6148
  96.4 108.7 %copy-start.108 = (f32[512]{0:T(512)}, f32[512]{0:T(512)S(1)}, u32[]{:S(2)}) copy-start(f32[512]{0:T(512)S(1)} %get-tuple-element.295) | copy-start | bytes 6148
  96.9 11.2 %copy-start.39 = (bf16[8,128,512]{2,1,0:T(8,128)(2,1)}, bf16[8,128,512]{2,1,0:T(8,128)(2,1)S(1)}, u32[]{:S(2)}) copy-start(bf16[8,128,512]{2,1,0:T(8,128)(2,1)S(1)} %fusion.67) | copy-start | bytes 3145732
  97.0 82.9 %copy-start.167 = (pred[8,128]{1,0:T(8,128)(4,1)}, pred[8,128]{1,0:T(8,128)(4,1)S(1)}, u32[]{:S(2)}) copy-start(pred[8,128]{1,0:T(8,128)(4,1)S(1)} %iota_compare_fusion.33) | copy-start | bytes 3076
  97.0 152.6 %copy-start.93 = (f32[128]{0:T(128)}, f32[128]{0:T(128)S(1)}, u32[]{:S(2)}) copy-start(f32[128]{0:T(128)S(1)} %get-tuple-element.329) | copy-start | bytes 1540
  97.0 152.6 %copy-start.95 = (f32[128]{0:T(128)}, f32[128]{0:T(128)S(1)}, u32[]{:S(2)}) copy-start(f32[128]{0:T(128)S(1)} %get-tuple-element.330) | copy-start | bytes 1540
  97.1 32.3 %copy-start.131 = (f32[2048]{0:T(1024)}, f32[2048]{0:T(1024)S(1)}, u32[]{:S(2)}) copy-start(f32[2048]{0:T(1024)S(1)} %get-tuple-element.312) | copy-start | bytes 24580
  97.1 98.0 %copy-start.133 = (f32[2048]{0:T(1024)}, f32[2048]{0:T(1024)S(1)}, u32[]{:S(2)}) copy-start(f32[2048]{0:T(1024)S(1)} %get-tuple-element.311) | copy-start | bytes 24580
  115.2 8.7 %copy-start.31 = (bf16[8,128,512]{1,2,0:T(8,128)(2,1)}, bf16[8,128,512]{1,2,0:T(8,128)(2,1)S(1)}, u32[]{:S(2)}) copy-start(bf16[8,128,512]{1,2,0:T(8,128)(2,1)S(1)} %copy.247) | copy-start | bytes 3145732
  138.6 66.5 %copy-start.85 = (f32[8,128]{1,0:T(8,128)}, f32[8,128]{1,0:T(8,128)S(1)}, u32[]{:S(2)}) copy-start(f32[8,128]{1,0:T(8,128)S(1)} %broadcast_multiply_fusion.2) | copy-start | bytes 12292
  139.1 33.8 %copy-start.117 = (f32[8,128]{1,0:T(8,128)}, f32[8,128]{1,0:T(8,128)S(1)}, u32[]{:S(2)}) copy-start(f32[8,128]{1,0:T(8,128)S(1)} %multiply_reduce_fusion.16) | copy-start | bytes 12292
  139.1 66.0 %copy-start.89 = (f32[8,128]{1,0:T(8,128)}, f32[8,128]{1,0:T(8,128)S(1)}, u32[]{:S(2)}) copy-start(f32[8,128]{1,0:T(8,128)S(1)} %fusion.259) | copy-start | bytes 12292
  139.5 33.4 %copy-start.41 = (bf16[8,128,512]{2,1,0:T(8,128)(2,1)}, bf16[8,128,512]{2,1,0:T(8,128)(2,1)S(1)}, u32[]{:S(2)}) copy-start(bf16[8,128,512]{2,1,0:T(8,128)(2,1)S(1)} %fusion.88) | copy-start | bytes 3145732
  179.9 9.1 %copy-start.33 = (bf16[8,128,512]{1,2,0:T(8,128)(2,1)}, bf16[8,128,512]{1,2,0:T(8,128)(2,1)S(1)}, u32[]{:S(2)}) copy-start(bf16[8,128,512]{1,2,0:T(8,128)(2,1)S(1)} %copy.253) | copy-start | bytes 3145732
  193.6 7.6 %copy-start.13 = (f32[8,128,512]{2,1,0:T(8,128)}, f32[8,128,512]{2,1,0:T(8,128)S(1)}, u32[]{:S(2)}) copy-start(f32[8,128,512]{2,1,0:T(8,128)S(1)} %get-tuple-element.342) | copy-start | bytes 6291460
  193.6 7.6 %copy-start.106 = (f32[8,128]{1,0:T(8,128)}, f32[8,128]{1,0:T(8,128)S(1)}, u32[]{:S(2)}) copy-start(f32[8,128]{1,0:T(8,128)S(1)} %broadcast_multiply_fusion.1) | copy-start | bytes 12292
  228.7 17.7 %copy-start.203 = (f32[128]{0:T(128)}, f32[128]{0:T(128)S(1)}, u32[]{:S(2)}) copy-start(f32[128]{0:T(128)S(1)} %multiply_reduce_fusion.42) | copy-start | bytes 1540
  228.8 18.2 %copy-start.201 = (f32[128]{0:T(128)}, f32[128]{0:T(128)S(1)}, u32[]{:S(2)}) copy-start(f32[128]{0:T(128)S(1)} %multiply_reduce_fusion.34) | copy-start | bytes 1540
  228.9 13.2 %copy-start.200 = (f32[128]{0:T(128)}, f32[128]{0:T(128)S(1)}, u32[]{:S(2)}) copy-start(f32[128]{0:T(128)S(1)} %multiply_reduce_fusion.26) | copy-start | bytes 1540
  230.1 15.2 %copy-start.190 = (f32[128]{0:T(128)}, f32[128]{0:T(128)S(1)}, u32[]{:S(2)}) copy-start(f32[128]{0:T(128)S(1)} %multiply_reduce_fusion.43) | copy-start | bytes 1540
  230.1 15.7 %copy-start.188 = (f32[128]{0:T(128)}, f32[128]{0:T(128)S(1)}, u32[]{:S(2)}) copy-start(f32[128]{0:T(128)S(1)} %multiply_reduce_fusion.35) | copy-start | bytes 1540
  230.5 14.8 %copy-start.196 = (f32[128]{0:T(128)}, f32[128]{0:T(128)S(1)}, u32[]{:S(2)}) copy-start(f32[128]{0:T(128)S(1)} %multiply_reduce_fusion.44) | copy-start | bytes 1540
  230.5 15.3 %copy-start.192 = (f32[128]{0:T(128)}, f32[128]{0:T(128)S(1)}, u32[]{:S(2)}) copy-start(f32[128]{0:T(128)S(1)} %multiply_reduce_fusion.36) | copy-start | bytes 1540
  232.8 11.4 %copy-start.159 = (f32[128]{0:T(128)}, f32[128]{0:T(128)S(1)}, u32[]{:S(2)}) copy-start(f32[128]{0:T(128)S(1)} %get-tuple-element.415) | copy-start | bytes 1540
  232.8 11.4 %copy-start.161 = (f32[128]{0:T(128)}, f32[128]{0:T(128)S(1)}, u32[]{:S(2)}) copy-start(f32[128]{0:T(128)S(1)} %get-tuple-element.414) | copy-start | bytes 1540
  233.2 11.2 %copy-start.160 = (f32[128]{0:T(128)}, f32[128]{0:T(128)S(1)}, u32[]{:S(2)}) copy-start(f32[128]{0:T(128)S(1)} %get-tuple-element.421) | copy-start | bytes 1540
  233.2 11.2 %copy-start.163 = (f32[128]{0:T(128)}, f32[128]{0:T(128)S(1)}, u32[]{:S(2)}) copy-start(f32[128]{0:T(128)S(1)} %get-tuple-element.420) | copy-start | bytes 1540
  233.6 12.1 %copy-start.151 = (f32[128]{0:T(128)}, f32[128]{0:T(128)S(1)}, u32[]{:S(2)}) copy-start(f32[128]{0:T(128)S(1)} %get-tuple-element.417) | copy-start | bytes 1540
  234.1 11.7 %copy-start.165 = (f32[128]{0:T(128)}, f32[128]{0:T(128)S(1)}, u32[]{:S(2)}) copy-start(f32[128]{0:T(128)S(1)} %get-tuple-element.419) | copy-start | bytes 1540
  245.3 9.7 %copy-start.147 = (f32[128]{0:T(128)}, f32[128]{0:T(128)S(1)}, u32[]{:S(2)}) copy-start(f32[128]{0:T(128)S(1)} %get-tuple-element.423) | copy-start | bytes 1540
  245.3 9.7 %copy-start.149 = (f32[128]{0:T(128)}, f32[128]{0:T(128)S(1)}, u32[]{:S(2)}) copy-start(f32[128]{0:T(128)S(1)} %get-tuple-element.422) | copy-start | bytes 1540
  245.9 11.5 %copy-start.154 = (f32[128]{0:T(128)}, f32[128]{0:T(128)S(1)}, u32[]{:S(2)}) copy-start(f32[128]{0:T(128)S(1)} %get-tuple-element.429) | copy-start | bytes 1540
  245.9 11.5 %copy-start.155 = (f32[128]{0:T(128)}, f32[128]{0:T(128)S(1)}, u32[]{:S(2)}) copy-start(f32[128]{0:T(128)S(1)} %get-tuple-element.428) | copy-start | bytes 1540
  246.5 10.9 %copy-start.166 = (f32[128]{0:T(128)}, f32[128]{0:T(128)S(1)}, u32[]{:S(2)}) copy-start(f32[128]{0:T(128)S(1)} %get-tuple-element.425) | copy-start | bytes 1540
  247.0 11.6 %copy-start.157 = (f32[128]{0:T(128)}, f32[128]{0:T(128)S(1)}, u32[]{:S(2)}) copy-start(f32[128]{0:T(128)S(1)} %get-tuple-element.427) | copy-start | bytes 1540
  251.1 7.6 %copy-start.96 = (f32[128]{0:T(128)S(1)}, f32[128]{0:T(128)}, u32[]{:S(2)}) copy-start(f32[128]{0:T(128)} %copy-done.95) | copy-start | bytes 1540
  266.2 9.0 %copy-start.88 = (f32[8,128]{1,0:T(8,128)S(1)}, f32[8,128]{1,0:T(8,128)}, u32[]{:S(2)}) copy-start(f32[8,128]{1,0:T(8,128)} %copy-done.87) | copy-start | bytes 12292
  266.2 9.0 %copy-start.109 = (f32[512]{0:T(512)S(1)}, f32[512]{0:T(512)}, u32[]{:S(2)}) copy-start(f32[512]{0:T(512)} %copy-done.108) | copy-start | bytes 6148
  280.4 8.5 %slice-start.2 = ((s8[8388608]{0:T(1024)(128)(4,1)}), s8[4194304]{0:T(1024)(128)(4,1)S(1)}, s32[]{:S(2)}) async-start(s8[8388608]{0:T(1024)(128)(4,1)} %bitcast.555), calls=%async_computation.11 | async-start | bytes 8388608
  311.1 10.0 %copy-start.92 = (f32[8,8,128]{2,1,0:T(8,128)S(1)}, f32[8,8,128]{2,1,0:T(8,128)}, u32[]{:S(2)}) copy-start(f32[8,8,128]{2,1,0:T(8,128)} %multiply_divide_fusion.1) | copy-start | bytes 98308
  423.1 8.1 %copy-start.4 = (bf16[8,128,1536]{2,1,0:T(8,128)(2,1)}, bf16[8,128,1536]{2,1,0:T(8,128)(2,1)S(1)}, u32[]{:S(2)}) copy-start(bf16[8,128,1536]{2,1,0:T(8,128)(2,1)S(1)} %add_convert_fusion.2) | copy-start | bytes 9437188
  423.8 9.7 %copy-start.146 = (f32[1,1,1536]{2,1,0:T(1,128)}, f32[1,1,1536]{2,1,0:T(1,128)S(1)}, u32[]{:S(2)}) copy-start(f32[1,1,1536]{2,1,0:T(1,128)S(1)} %reshape.1072) | copy-start | bytes 18436
  459.3 80.6 %copy-start.145 = (s32[2304]{0:T(1024)S(1)}, s32[2304]{0:T(1024)}, u32[]{:S(2)}) copy-start(s32[2304]{0:T(1024)} %eq.186) | copy-start | bytes 27652
  539.9 9.0 %copy-start.71 = (bf16[8,128,512]{2,1,0:T(8,128)(2,1)S(1)}, bf16[8,128,512]{2,1,0:T(8,128)(2,1)}, u32[]{:S(2)}) copy-start(bf16[8,128,512]{2,1,0:T(8,128)(2,1)} %get-tuple-element.285) | copy-start | bytes 3145732
  539.9 9.0 %copy-start.77 = (s32[1024]{0:T(1024)S(1)}, s32[1024]{0:T(1024)}, u32[]{:S(2)}) copy-start(s32[1024]{0:T(1024)} %copy-done.76) | copy-start | bytes 12292
  539.9 9.0 %copy-start.79 = (s32[1024]{0:T(1024)S(1)}, s32[1024]{0:T(1024)}, u32[]{:S(2)}) copy-start(s32[1024]{0:T(1024)} %copy-done.78) | copy-start | bytes 12292
  539.9 9.0 %copy-start.81 = (s32[1024]{0:T(1024)S(1)}, s32[1024]{0:T(1024)}, u32[]{:S(2)}) copy-start(s32[1024]{0:T(1024)} %copy-done.80) | copy-start | bytes 12292
  549.8 18.5 %copy-start.98 = (f32[4928]{0:T(1024)S(1)}, f32[4928]{0:T(1024)}, u32[]{:S(2)}) copy-start(f32[4928]{0:T(1024)} %param.26) | copy-start | bytes 59140
  549.8 18.5 %copy-start.136 = (f32[4928]{0:T(1024)S(1)}, f32[4928]{0:T(1024)}, u32[]{:S(2)}) copy-start(f32[4928]{0:T(1024)} %param.30) | copy-start | bytes 59140
  549.8 18.5 %copy-start.137 = (f32[4928]{0:T(1024)S(1)}, f32[4928]{0:T(1024)}, u32[]{:S(2)}) copy-start(f32[4928]{0:T(1024)} %param.34) | copy-start | bytes 59140
  549.8 19.1 %copy-start.64 = (f32[2,32,2048]{2,1,0:T(8,128)S(1)}, f32[2,32,2048]{2,1,0:T(8,128)}, u32[]{:S(2)}) copy-start(f32[2,32,2048]{2,1,0:T(8,128)} %param.27) | copy-start | bytes 1572868
  555.2 16.5 %copy-start.43 = (f32[2,32,4096]{2,1,0:T(8,128)S(1)}, f32[2,32,4096]{2,1,0:T(8,128)}, u32[]{:S(2)}) copy-start(f32[2,32,4096]{2,1,0:T(8,128)} %param.28) | copy-start | bytes 3145732
  (178 other events, 655.2 us)
Sparse Core Ops, SparseCore 0:
  10.9 94.0 all-gather.6
  107.8 61.8 all-gather.8
  368.9 85.3 reduce-scatter.1

commit v3 on v2

--- a/solution.py
+++ b/solution.py
@@ -283,7 +283,7 @@
             line_at, col_at = b // 2, lax.rem(b, 2)
             mine = parts[part][line_at, col_at, core, :, pl.ds(start, width)].astype(jnp.float32)
             got = buf[line_at, col_at].astype(jnp.float32)
-            buf[line_at, col_at] = (mine + got).astype(jnp.bfloat16)
+            buf[line_at, col_at] = (mine + got).astype(buf.dtype)
             return carry
 
         lax.fori_loop(0, 8, add_block, 0)
@@ -295,7 +295,7 @@
 
         def add_block(b, carry):
             mine = bufs[i][0][b, col].astype(jnp.float32)
-            buf[b] = (mine + buf[b].astype(jnp.float32)).astype(jnp.bfloat16)
+            buf[b] = (mine + buf[b].astype(jnp.float32)).astype(buf.dtype)
             return carry
 
         lax.fori_loop(0, 4, add_block, 0)
@@ -308,7 +308,7 @@
         value = bufs[i][1][line].astype(jnp.float32)
         for k in range(3):
             value = value + bufs[i][2][k].astype(jnp.float32)
-        bufs[i][3][...] = value.astype(jnp.bfloat16)
+        bufs[i][3][...] = value.astype(bufs[i][3].dtype)
         copy_x(i).start()
 
     def stage_x(i):
@@ -377,11 +377,11 @@
     for index, start, width in chunks:
         r = parts[index].shape[3]
         scratch += [
-            pltpu.VMEM((4, 2, r, width), half),
-            pltpu.VMEM((4, r, width), half),
-            pltpu.VMEM((3, r, width), half),
-            pltpu.VMEM((r, width), half),
-            pltpu.VMEM((r, width), half),
+            pltpu.VMEM((4, 2, r, width), parts[index].dtype),
+            pltpu.VMEM((4, r, width), parts[index].dtype),
+            pltpu.VMEM((3, r, width), parts[index].dtype),
+            pltpu.VMEM((r, width), parts[index].dtype),
+            pltpu.VMEM((r, width), parts[index].dtype),
         ]
     scratch += [pltpu.VMEM(near.shape, half)]
     dma = pltpu.SemaphoreType.DMA
@@ -405,6 +405,261 @@
         cost_estimate=pl.CostEstimate(flops=0, bytes_accessed=200_000_000, transcendentals=0),
         name="exchange_gradients",
     )(*parts, sums, near)
+
+
+SPLITS = 4
+
+
+def start_kernel(shard_rows, room, *refs):
+    packet_ref, vec_ref, attn_ref, ffn_ref, word_ref = refs[:5]
+    packet_out, vec_out, weight_out, rows_out = refs[5:9]
+    table, rows_held = refs[9:11]
+    packet_sem, vec_sem, row_sem, z_sem, y_sem, x_sem, d_sem = refs[11:]
+
+    d = lax.axis_index("dp")
+    z = lax.axis_index("zero")
+    me = d * 16 + z
+    core = lax.rem(z, 2)
+    col = lax.rem(z // 2, 2)
+    line = z // 4
+    sibling = z + 1 - 2 * core
+    across = z + 2 - 4 * col
+    width = attn_ref.shape[1]
+    part = width // SPLITS
+
+    def everyone(k):
+        p = lax.rem(me + k, 32)
+        return (p // 16, lax.rem(p, 16))
+
+    barrier = pltpu.get_barrier_semaphore()
+
+    def greet(k, carry):
+        pl.semaphore_signal(barrier, inc=1, device_id=everyone(k), device_id_type=MESH)
+        return carry
+
+    lax.fori_loop(1, 32, greet, 0)
+    weight_out[z, :, 0:width] = attn_ref[...].astype(jnp.bfloat16)
+    weight_out[z, :, width : 3 * width] = ffn_ref[...].astype(jnp.bfloat16)
+    pl.semaphore_wait(barrier, 31)
+
+    def remote(src, dst, sems, at, to):
+        return pltpu.make_async_remote_copy(
+            src_ref=src,
+            dst_ref=dst,
+            send_sem=sems.at[(0,) + at],
+            recv_sem=sems.at[(1,) + at],
+            device_id=to,
+            device_id_type=MESH,
+        )
+
+    def packet_copy(k, slot):
+        return remote(packet_ref, packet_out.at[slot], packet_sem, (k,), everyone(k))
+
+    def vec_copy(k, slot):
+        return remote(vec_ref, vec_out.at[slot], vec_sem, (k,), (d, lax.rem(z + k, 16)))
+
+    def row_copy(k, slot):
+        to = lax.rem(z + k, 16)
+        return remote(rows_held.at[to], rows_out.at[slot], row_sem, (k,), (d, to))
+
+    def send_packets(k, carry):
+        packet_copy(k, me).start()
+        return carry
+
+    lax.fori_loop(1, 32, send_packets, 0)
+
+    def shard(i):
+        at = lax.rem(line + i % 4, 4) * 4 + lax.rem(z, 4)
+        return at if i < 4 else at + 2 - 4 * col
+
+    columns = (
+        pl.multiple_of(d * width, width),
+        2 * width,
+        pl.multiple_of((1 - d) * width, width),
+    )
+
+    def block(at, s, g):
+        first = pl.multiple_of(columns[g] + s * part, 128)
+        return weight_out.at[at, :, pl.ds(first, part)]
+
+    def z_copy(s, k, g, at):
+        to = lax.rem(line + k, 4) * 4 + lax.rem(z, 4)
+        return remote(block(at, s, g), block(at, s, g), z_sem, (s, k - 1, g), (d, to))
+
+    def y_copy(s, j, g, at):
+        return remote(block(at, s, g), block(at, s, g), y_sem, (s, j, g), (d, across))
+
+    def x_copy(s, i, g, at):
+        return remote(block(at, s, g), block(at, s, g), x_sem, (s, i), (1 - d, z))
+
+    def d_copy(s, i, g, at):
+        return remote(block(at, s, g), block(at, s, g), d_sem, (s, i, g), (d, sibling))
+
+    def spread(s, i):
+        at = shard(i)
+        if i < 4:
+            y_copy(s, i, 0, at).start()
+            y_copy(s, i, 1, at).start()
+        if i > 0:
+            x_copy(s, i, 0, at).start()
+        for g in range(2 if i > 0 else 3):
+            d_copy(s, i, g, at).start()
+
+    for s in range(SPLITS):
+        for k in range(1, 4):
+            for g in range(2):
+                z_copy(s, k, g, z).start()
+        spread(s, 0)
+
+    def send_vec(k, carry):
+        vec_copy(k, z).start()
+        return carry
+
+    lax.fori_loop(1, 16, send_vec, 0)
+    packet_out[me] = packet_ref[...]
+    vec_out[z] = vec_ref[...]
+
+    body_rows = shard_rows // 16 * 16
+    step = 112 if body_rows % 112 == 0 else 16
+
+    def to_half(i, carry):
+        at = pl.multiple_of(i * step, 16)
+        table[pl.ds(at, step), :] = word_ref[pl.ds(at, step), :].astype(jnp.bfloat16)
+        return carry
+
+    lax.fori_loop(0, body_rows // step, to_half, 0)
+    padded = table.shape[0]
+    table[body_rows:padded, :] = jnp.zeros((padded - body_rows, table.shape[1]), jnp.bfloat16)
+    if shard_rows > body_rows:
+        table[body_rows:shard_rows, :] = word_ref[body_rows:shard_rows, :].astype(jnp.bfloat16)
+
+    def answer(k):
+        src = lax.rem(z + k, 16)
+        asked = packet_out[d * 16 + src, pl.ds(z, 1), :]
+        rows_at = lax.broadcasted_iota(jnp.int32, (padded, 128), 0)
+        picked = (rows_at == asked).astype(jnp.bfloat16)
+        found = lax.dot_general(
+            picked, table[...], (((0,), (0,)), ((), ())), preferred_element_type=jnp.float32
+        )
+        return src, found[:room, :].astype(jnp.bfloat16)
+
+    def packet_in(k, carry):
+        packet_copy(k, lax.rem(me + 32 - k, 32)).wait_recv()
+        return carry
+
+    def answer_one(k, carry):
+        src, found = answer(k)
+        rows_held[src] = found
+        row_copy(k, z).start()
+        return carry
+
+    def z_phase(s):
+        for k in range(1, 4):
+            at = shard(4 - k)
+            for g in range(2):
+                z_copy(s, k, g, at).wait_recv()
+            spread(s, 4 - k)
+
+    def y_phase(s):
+        for j in range(4):
+            at = shard(4 + j)
+            for g in range(2):
+                y_copy(s, j, g, at).wait_recv()
+            spread(s, 4 + j)
+
+    def x_phase(s):
+        for i in range(1, 8):
+            at = shard(i)
+            x_copy(s, i, 2, at).wait_recv()
+            d_copy(s, i, 2, at).start()
+
+    lax.fori_loop(1, 32, packet_in, 0)
+    done = 1
+    for t in range(SPLITS + 2):
+        until = min(16, 1 + (t + 1) * 15 // SPLITS)
+        if until > done:
+            lax.fori_loop(done, until, answer_one, 0)
+        done = max(done, until)
+        if t < SPLITS:
+            z_phase(t)
+        if 0 <= t - 1 < SPLITS:
+            y_phase(t - 1)
+        if 0 <= t - 2 < SPLITS:
+            x_phase(t - 2)
+    _, found = answer(0)
+    rows_out[z] = found
+
+    for s in range(SPLITS):
+        for i in range(8):
+            at = shard(i)
+            there = at + 1 - 2 * core
+            for g in range(3):
+                d_copy(s, i, g, there).wait_recv()
+    for s in range(SPLITS):
+        for k in range(1, 4):
+            for g in range(2):
+                z_copy(s, k, g, z).wait_send()
+        for i in range(8):
+            at = shard(i)
+            if i < 4:
+                y_copy(s, i, 0, at).wait_send()
+                y_copy(s, i, 1, at).wait_send()
+            if i > 0:
+                x_copy(s, i, 0, at).wait_send()
+            for g in range(3):
+                d_copy(s, i, g, at).wait_send()
+
+    def finish(k, carry):
+        back = lax.rem(z + 16 - k, 16)
+        row_copy(k, back).wait_recv()
+        row_copy(k, z).wait_send()
+        vec_copy(k, back).wait_recv()
+        vec_copy(k, z).wait_send()
+        return carry
+
+    lax.fori_loop(1, 16, finish, 0)
+
+    def finish_packets(k, carry):
+        packet_copy(k, me).wait_send()
+        return carry
+
+    lax.fori_loop(1, 32, finish_packets, 0)
+
+
+def exchange_start(packet, vec_rows, attn, ffn, word_table, room, collective_id):
+    half = jnp.bfloat16
+    shard_rows, features = word_table.shape
+    padded = -(-shard_rows // 128) * 128
+    rows, width = attn.shape
+    dma = pltpu.SemaphoreType.DMA
+    vmem = pl.BlockSpec(memory_space=pltpu.VMEM)
+    return pl.pallas_call(
+        functools.partial(start_kernel, shard_rows, room),
+        out_shape=(
+            jax.ShapeDtypeStruct((32,) + packet.shape, packet.dtype),
+            jax.ShapeDtypeStruct((16,) + vec_rows.shape, vec_rows.dtype),
+            jax.ShapeDtypeStruct((16, rows, 3 * width), half),
+            jax.ShapeDtypeStruct((16, room, features), half),
+        ),
+        in_specs=[vmem] * 5,
+        out_specs=tuple([vmem] * 4),
+        scratch_shapes=[
+            pltpu.VMEM((padded, features), half),
+            pltpu.VMEM((16, room, features), half),
+            dma((2, 32)),
+            dma((2, 16)),
+            dma((2, 16)),
+            dma((2, SPLITS, 3, 2)),
+            dma((2, SPLITS, 4, 2)),
+            dma((2, SPLITS, 8)),
+            dma((2, SPLITS, 8, 3)),
+        ],
+        compiler_params=pltpu.CompilerParams(
+            collective_id=collective_id, has_side_effects=True, vmem_limit_bytes=48 * 1024 * 1024
+        ),
+        cost_estimate=pl.CostEstimate(flops=0, bytes_accessed=150_000_000, transcendentals=0),
+        name="exchange_start",
+    )(packet, vec_rows, attn, ffn, word_table)
 
 
 def split_vectors(vec_all):
@@ -557,6 +812,7 @@
     ndp = lax.axis_size("dp")
     nz = lax.axis_size("zero")
     n = ndp * nz
+    by_hand = (ndp, nz) == (2, 16)
     my_dp = lax.axis_index("dp")
     my_zero = lax.axis_index("zero")
     me = my_dp * nz + my_zero
@@ -574,33 +830,42 @@
     owner, place, local_row = token_plan(flat_ids.reshape(-1), shard_rows)
     slot, asked = round_slots(owner, place, local_row, 0, room, nz)
     rounds_here = jnp.max(place) // room + 1
+    last = jnp.concatenate([pair_index, rounds_here[None].astype(jnp.int32)])
     packet = jnp.concatenate(
-        [asked, false_neg.reshape(-1), pair_index, rounds_here[None].astype(jnp.int32)]
-    )
-    packets, vec_parts = exchange(
-        [pad_rows(packet, 8), pad_rows(vectors.astype(jnp.bfloat16), 16)],
-        ["all", "zero"],
-        ndp,
-        nz,
-        0,
-        "gather_requests",
-    )
-    packets = packets.reshape(n, -1)
-    asked_all = packets[:, : nz * room].reshape(n, nz, room)
-    at = nz * room
-    false_all = packets[:, at : at + pair_rows * total_pairs].reshape(total_pairs, total_pairs)
-    at = at + pair_rows * total_pairs
-    pair_all = packets[:, at : at + pair_rows].reshape(total_pairs)
-    rounds = jnp.max(packets[:, at + pair_rows])
-    vec_all = vec_parts.reshape(nz, -1)[:, :vec_len].reshape(-1).astype(jnp.float32)
-
-    layer_weights = []
-    for layer_index in range(LAYERS):
+        [
+            jnp.pad(asked.reshape(nz, room), ((0, 0), (0, 128 - room)), constant_values=-1),
+            false_neg.reshape(-1, 128),
+            jnp.pad(last, (0, 128 - last.shape[0]))[None],
+        ]
+    )
+    packet = jnp.pad(packet, ((0, -packet.shape[0] % 8), (0, 0)))
+    vec_rows = pad_rows(vectors.astype(jnp.bfloat16), 16)
+
+    def gather_layer(layer_index):
         both = jnp.concatenate(
             [attn_w[layer_index].astype(jnp.bfloat16), ffn_w[layer_index].astype(jnp.bfloat16)],
             axis=1,
         )
-        layer_weights.append(lax.all_gather(both, "zero", axis=0, tiled=True))
+        return lax.all_gather(both, "zero", axis=0, tiled=True)
+
+    if by_hand:
+        packets, vec_parts, first_weights, received = exchange_start(
+            packet, vec_rows, attn_w[0], ffn_w[0], word_table, room, 0
+        )
+        layer_weights = [first_weights.reshape(-1, 4 * D + 2 * FF)]
+    else:
+        packets, vec_parts = exchange(
+            [packet, vec_rows], ["all", "zero"], ndp, nz, 0, "gather_requests"
+        )
+        layer_weights = [gather_layer(0)]
+    for layer_index in range(1, LAYERS):
+        layer_weights.append(gather_layer(layer_index))
+    asked_all = packets[:, :nz, :room]
+    at = nz + pair_rows * total_pairs // 128
+    false_all = packets[:, nz:at].reshape(total_pairs, total_pairs)
+    pair_all = packets[:, at, :pair_rows].reshape(total_pairs)
+    rounds = jnp.max(packets[:, at, pair_rows])
+    vec_all = vec_parts.reshape(nz, -1)[:, :vec_len].reshape(-1).astype(jnp.float32)
 
     word_half = word_table.astype(jnp.bfloat16)
     asked_mine = lax.dynamic_index_in_dim(asked_all, my_zero, 1, keepdims=False)
@@ -614,9 +879,10 @@
             jnp.bfloat16
         )
 
-    (received,) = exchange(
-        [rows_for(asked_near).reshape(nz, room, D)], ["zero_p"], ndp, nz, 1, "send_rows"
-    )
+    if not by_hand:
+        (received,) = exchange(
+            [rows_for(asked_near).reshape(nz, room, D)], ["zero_p"], ndp, nz, 1, "send_rows"
+        )
     rows = rows_from(slot, received)
 
     def more_rows(state):
@@ -672,7 +938,6 @@
     deep_back = jnp.stack([deep_anchor_grad, deep_pos_grad], axis=1).reshape(seq_rows, D)
     grad_hidden = jnp.zeros_like(embedded)
     weight_parts = []
-    by_hand = (ndp, nz) == (2, 16)
     vec_grad = jnp.zeros_like(vec_all)
     for layer_index in range(LAYERS - 1, -1, -1):
         if layer_index == LAYERS - 1:
@@ -724,7 +989,7 @@
             [
                 attn_part.reshape(4, 2, 2, -1, 4 * D),
                 ffn_part.reshape(4, 2, 2, -1, 2 * FF),
-                vec_blocks.astype(jnp.bfloat16).reshape(4, 2, 2, lines, 128),
+                vec_blocks.reshape(4, 2, 2, lines, 128),
             ],
             sums,
             weight_parts[1],

time: 602 us -> 650 us (1.080)
  Pallas kernels: 170 us -> 212 us
  waiting for transfers between devices: 37.3 us -> 1.58 us
  other arithmetic: 114 us -> 147 us
    pallas_call x0 -> x1, Pallas kernels: none -> 98.4 us  [exchange_start(): pl.pallas_call(functools.partial(start_kernel, shard_rows, room), out_sha...]
    pallas_call x4 -> x2, Pallas kernels: 90 us -> 33.5 us  [exchange(): pl.pallas_call(functools.partial(exchange_kernel, tuple(modes), ndp, nz),...]
    all_gather x2 -> x1, waiting for transfers between devices: 37.3 us -> 0.01 us  [gather_layer(): return lax.all_gather(both, 'zero', axis=0, tiled=True)]
    rsqrt x10 -> x20, other arithmetic: 0.06 us -> 11.7 us  [normalized_rows(): lax.rsqrt(jnp.sum(rows * rows, axis=-1, keepdims=True) + NORM_EPS)]
    reduce_sum x20, other arithmetic: 0.94 us -> 10.8 us  [normalized_rows(): jnp.sum(rows * rows, axis=-1, keepdims=True) + NORM_EPS]
    dot_general x20 -> x19, matrix products: 76.7 us -> 73.2 us  [matmul(): return jnp.dot(left, right, preferred_element_type=jnp.float32)]
    unnamed x479 -> x610, local copies, waits for them, and re-layouts: 20.8 us -> 22.5 us
  transfers between devices with their start and end apart: 3 -> 2, of which waited for: 2 -> 1; matrix products, arithmetic and copies ran while one was open for 22% -> 20% of each run, Pallas kernels for 11% -> 15%
where the time goes in v3:
time: 650 us; the launch traced here: 640 us
  Pallas kernels  212 us (33%)
  matrix products  175 us (27%)
  other arithmetic  147 us (23%)
  local copies, waits for them, and re-layouts  75.2 us (12%)
  between operations  27.6 us (4%)
    pallas_call x1, Pallas kernels, exchange_start(): pl.pallas_call(functools.partial(start_kernel, shard_rows, room), out_sha...  98.4 us
    pallas_call x1, Pallas kernels, exchange_gradients(): pl.pallas_call(functools.partial(gradient_kernel, tuple(chunks), len(part...  79.6 us
    dot_general x19, matrix products, matmul(): return jnp.dot(left, right, preferred_element_type=jnp.float32)  73.2 us
    dot_general x16, matrix products, einsum_plain(): return jnp.einsum(form, left, right, preferred_element_type=jnp.float32)  45.1 us
    dot_general x30, matrix products, contrastive_terms(): jnp.dot(normalized_rows(anchor_vectors[:, :current_width]), normalized_ro...  34.4 us
    pallas_call x2, Pallas kernels, exchange(): pl.pallas_call(functools.partial(exchange_kernel, tuple(modes), ndp, nz),...  33.5 us
    convert_element_type x11, other arithmetic, low_back(): return build_low_back()(value)  24.4 us
    unnamed x610, local copies, waits for them, and re-layouts  22.5 us
  transfers between devices with their start and end apart: 2, of which 1 were waited for; matrix products, arithmetic and copies ran while one was open for 20% of the time, Pallas kernels for 15%

profile of v3, /device:TPU:0, one launch (start us, length us, event | category | flops | bytes accessed | tf_op | source)
XLA Modules:
  0.0 639.6 jit_solution(8033003036247185695)
XLA Ops:
  12.6 2.3 convert_reduce_fusion.4
  19.3 3.8 convert_element_type.295
  23.1 98.4 %exchange_start.1 = (s32[32,24,128]{2,1,0:T(8,128)S(1)}, bf16[16,48,128]{2,1,0:T(8,128)(2,1)S(1)}, bf16[16,32,6144]{2,1,0:T(8,128)(2,1)}, bf16[16,72,512]{2,1,0:T(8,128)(2,1)S(1)}) custom-call(s32[24,128]{1,0:T(8,128)S(1)} %pad.175.refs_0_, bf16[48,128]{1,0:T(8,128)(2,1)S(1)} %pad_bitcast_fusion.refs_1_, f32[32,2048]{1,0:T(8,128)S(1)} %slice_bitcast_fusion.35.refs_2_, ...), custom_call_target="tpu_custom_call" | custom-call | bytes 150000000 | tf_op jit(solution)/shard_map/exchange_start/pallas_call | solution.py:636
  122.5 2.5 fusion.73
  132.0 3.6 add_convert_fusion.5
  137.3 2.4 copy.253
  142.7 5.7 fusion.322
  148.4 2.8 divide_convert_fusion.1
  152.6 3.3 fusion.323
  156.8 6.4 multiply_convert_fusion.1
  163.3 2.7 fusion.324
  168.5 3.5 add_convert_fusion.4
  173.8 2.3 copy.258
  176.0 2.3 copy.257
  178.3 2.3 copy.256
  180.6 5.3 fusion.325
  186.5 2.9 divide_convert_fusion
  190.8 3.2 fusion.326
  194.9 6.0 multiply_convert_fusion
  200.9 2.7 fusion.327
  205.4 24.8 %gather_pooled.1 = bf16[32,64,128]{2,1,0:T(8,128)(2,1)S(1)} custom-call(bf16[64,128]{1,0:T(8,128)(2,1)S(1)} %reshape.1171.refs_0_), custom_call_target="tpu_custom_call" | custom-call | bytes 10485760 | tf_op jit(solution)/shard_map/gather_pooled/pallas_call | solution.py:175
  283.8 2.3 multiply_reduce_fusion.59
  323.9 2.3 fusion.51
  329.0 4.4 convolution_bitcast_fusion.5
  333.4 4.1 convolution_convert_fusion.1
  337.6 6.8 %fusion.19 = bf16[8,128,2048]{2,1,0:T(8,128)(2,1)S(1)} fusion(bf16[8,128,2048]{2,1,0:T(8,128)(2,1)S(1)} %convolution_convert_fusion.1, f32[8,128,2048]{2,1,0:T(8,128)S(1)} %bitcast.550, f32[2048]{0:T(1024)S(1)} %copy-done.157), kind=kLoop, calls=%fused_computation.36 | loop fusion | flops 46137344 | bytes 16785408 | tf_op jit(solution)/shard_map/transpose(jvp())/convert_element_type | solution.py:70
  344.4 4.4 convolution_bitcast_fusion.4
  348.9 5.5 multiply_reduce_fusion.8
  358.9 2.8 convolution_convert_fusion.5
  361.6 2.3 copy.277
  363.9 5.0 fusion.338
  374.4 2.9 fusion.42
  377.2 2.9 copy.279
  380.1 2.9 copy.281
  383.0 2.9 copy.283
  385.9 3.2 add_convert_fusion.3
  391.4 3.5 convolution_bitcast_fusion.1
  401.8 4.2 add_convert_fusion.1
  406.7 3.1 pad_maximum_fusion
  409.8 6.2 add_add_fusion.11
  416.7 2.4 multiply_reduce_fusion.7
  420.6 4.3 convolution_convert_fusion
  425.0 6.6 %fusion.24 = bf16[8,128,2048]{2,1,0:T(8,128)(2,1)S(1)} fusion(bf16[8,128,2048]{2,1,0:T(8,128)(2,1)S(1)} %convolution_convert_fusion, f32[8,128,2048]{2,1,0:T(8,128)S(1)} %bitcast.548, f32[2048]{0:T(1024)S(1)} %copy-done.155), kind=kLoop, calls=%fused_computation.41 | loop fusion | flops 46137344 | bytes 16785408 | tf_op jit(solution)/shard_map/transpose(jvp())/convert_element_type | solution.py:70
  431.7 6.4 multiply_reduce_fusion.6
  443.8 3.3 multiply_reduce_fusion
  449.4 2.9 fusion.339
  452.3 3.0 copy.296
  455.3 2.9 fusion.40
  458.2 3.0 copy.298
  463.1 2.9 copy.300
  466.0 3.0 add_convert_fusion.2
  470.4 5.7 multiply_reduce_fusion.5
  485.0 2.5 convolution_bitcast_fusion.6
  490.6 2.7 fusion.46
  493.4 2.4 convolution_bitcast_fusion.3
  495.9 2.4 convolution_bitcast_fusion.2
  498.3 2.7 add_convert_fusion
  504.8 79.6 %exchange_gradients.1 = (f32[32,2048]{1,0:T(8,128)S(1)}, f32[32,4096]{1,0:T(8,128)S(1)}, f32[40,128]{1,0:T(8,128)S(1)}, bf16[2,16,72,512]{3,2,1,0:T(8,128)(2,1)}, f32[32,6144]{1,0:T(8,128)S(1)}) custom-call(bf16[4,2,2,32,2048]{4,3,2,1,0:T(8,128)(2,1)S(1)} %bitcast.432, bf16[4,2,2,32,4096]{4,3,2,1,0:T(8,128)(2,1)} %bitcast.530, ...), custom_call_target="tpu_custom_call" | custom-call | bytes 200000000 | tf_op jit(solution)/shard_map/exchange_gradients/pallas_call | solution.py:396
  585.2 9.0 %fusion.15 = f32[1908,512]{1,0:T(8,128)} fusion(bf16[2304,512]{1,0:T(8,128)(2,1)} %bitcast.596, s32[2304]{0:T(1024)S(1)} %copy-done.183), kind=kOutput, calls=%fused_computation.24 | convolution fusion | flops 4505932800 | bytes 6276096 | tf_op jit(solution)/shard_map/dot_general | solution.py:973
  595.1 3.7 multiply_reduce_fusion.3
  603.0 8.8 %gather_squares.1 = f32[16,8,128]{2,1,0:T(8,128)S(1)} custom-call(f32[8,128]{1,0:T(8,128)S(1)} %broadcast_in_dim.417.refs_0_), custom_call_target="tpu_custom_call" | custom-call | bytes 1310720 | tf_op jit(solution)/shard_map/gather_squares/pallas_call | solution.py:175
  614.4 3.0 fusion.305
  617.4 4.1 fusion.303
  622.7 7.6 %fusion.309 = (bf16[1908,512]{1,0:T(8,128)(2,1)}, f32[1908,512]{1,0:T(8,128)}, f32[1908,512]{1,0:T(8,128)}, f32[1908,512]{1,0:T(8,128)}) fusion(f32[1908,512]{1,0:T(8,128)S(1)} %copy-done.14, f32[1908,512]{1,0:T(8,128)S(1)} %copy-done.26, f32[]{:T(128)S(6)} %min.3, f32[1908,512]{1,0:T(8,128)S(1)} %copy-done.73, f32[1908,512]{1,0:T(8,128)} %param.33), kind=kLoop, calls=%fused_computation.687 | loop fusion | flops 15630336 | bytes 29306884 | tf_op jit(solution)/shard_map/convert_element_type | solution.py:1059
  (928 shorter events, 176.6 us)
Async XLA Ops:
  7.2 161.3 %all-gather.6.cloned.1.call-start = ((), (), s32[]{:S(2)}) async-start(), calls=%async_computation.5 | async-start | bytes 6684672 | tf_op jit(solution)/shard_map/all_gather | solution.py:849
  10.2 492.3 %reduce-scatter.2.cloned.1.call-start = ((), (), s32[]{:S(2)}) async-start(), calls=%async_computation.6 | async-start | bytes 6684672 | tf_op jit(solution)/shard_map/reduce_scatter | solution.py:956
  16.2 106.3 %copy-start.179 = (s32[1024]{0:T(1024)}, s32[1024]{0:T(1024)S(1)}, u32[]{:S(2)}) copy-start(s32[1024]{0:T(1024)S(1)} %get-tuple-element.328) | copy-start | bytes 12292
  23.1 99.3 %copy-start.248 = (s32[4,2]{0,1:T(2,128)S(1)}, s32[4,2]{0,1:T(2,128)}, u32[]{:S(2)}) copy-start(s32[4,2]{0,1:T(2,128)} %param.22) | copy-start | bytes 100
  126.9 25.6 %copy-start.40 = (f32[128,512]{1,0:T(8,128)}, f32[128,512]{1,0:T(8,128)S(1)}, u32[]{:S(2)}) copy-start(f32[128,512]{1,0:T(8,128)S(1)} %slice_convert_fusion.2) | copy-start | bytes 786436
  129.4 23.1 %copy-start.142 = (f32[8,128]{1,0:T(8,128)}, f32[8,128]{1,0:T(8,128)S(1)}, u32[]{:S(2)}) copy-start(f32[8,128]{1,0:T(8,128)S(1)} %get-tuple-element.322) | copy-start | bytes 12292
  131.4 21.2 %copy-start.144 = (f32[8,128]{1,0:T(8,128)}, f32[8,128]{1,0:T(8,128)S(1)}, u32[]{:S(2)}) copy-start(f32[8,128]{1,0:T(8,128)S(1)} %bitcast_rsqrt_fusion) | copy-start | bytes 12292
  131.4 21.1 %copy-start.171 = (f32[512]{0:T(512)}, f32[512]{0:T(512)S(1)}, u32[]{:S(2)}) copy-start(f32[512]{0:T(512)S(1)} %get-tuple-element.317) | copy-start | bytes 6148
  131.4 31.9 %copy-start.173 = (f32[512]{0:T(512)}, f32[512]{0:T(512)S(1)}, u32[]{:S(2)}) copy-start(f32[512]{0:T(512)S(1)} %get-tuple-element.312) | copy-start | bytes 6148
  131.4 69.4 %copy-start.175 = (f32[512]{0:T(512)}, f32[512]{0:T(512)S(1)}, u32[]{:S(2)}) copy-start(f32[512]{0:T(512)S(1)} %get-tuple-element.304) | copy-start | bytes 6148
  131.4 72.6 %copy-start.119 = (f32[512]{0:T(512)}, f32[512]{0:T(512)S(1)}, u32[]{:S(2)}) copy-start(f32[512]{0:T(512)S(1)} %get-tuple-element.309) | copy-start | bytes 6148
  131.4 72.6 %copy-start.127 = (f32[512]{0:T(512)}, f32[512]{0:T(512)S(1)}, u32[]{:S(2)}) copy-start(f32[512]{0:T(512)S(1)} %get-tuple-element.302) | copy-start | bytes 6148
  142.7 37.9 %copy-start.217 = (pred[8,128]{1,0:T(8,128)(4,1)}, pred[8,128]{1,0:T(8,128)(4,1)S(1)}, u32[]{:S(2)}) copy-start(pred[8,128]{1,0:T(8,128)(4,1)S(1)} %iota_compare_fusion.30) | copy-start | bytes 3076
  148.4 19.5 %copy-start.103 = (f32[8,8,128]{2,1,0:T(8,128)}, f32[8,8,128]{2,1,0:T(8,128)S(1)}, u32[]{:S(2)}) copy-start(f32[8,8,128]{2,1,0:T(8,128)S(1)} %get-tuple-element.334) | copy-start | bytes 98308
  156.8 38.0 %copy-start.156 = (f32[2048]{0:T(1024)}, f32[2048]{0:T(1024)S(1)}, u32[]{:S(2)}) copy-start(f32[2048]{0:T(1024)S(1)} %get-tuple-element.318) | copy-start | bytes 24580
  166.0 38.1 %copy-start.109 = (f32[8,128]{1,0:T(8,128)}, f32[8,128]{1,0:T(8,128)S(1)}, u32[]{:S(2)}) copy-start(f32[8,128]{1,0:T(8,128)S(1)} %broadcast_multiply_fusion.2) | copy-start | bytes 12292
  166.5 37.6 %copy-start.107 = (f32[8,128]{1,0:T(8,128)}, f32[8,128]{1,0:T(8,128)S(1)}, u32[]{:S(2)}) copy-start(f32[8,128]{1,0:T(8,128)S(1)} %get-tuple-element.417) | copy-start | bytes 12292
  166.5 37.6 %copy-start.113 = (f32[8,128]{1,0:T(8,128)}, f32[8,128]{1,0:T(8,128)S(1)}, u32[]{:S(2)}) copy-start(f32[8,128]{1,0:T(8,128)S(1)} %get-tuple-element.418) | copy-start | bytes 12292
  245.1 19.1 %copy-start.99 = (s32[128]{0:T(128)S(1)}, s32[128]{0:T(128)}, u32[]{:S(2)}) copy-start(s32[128]{0:T(128)} %eq.98) | copy-start | bytes 1540
  245.7 22.1 %copy-start.263 = (f32[128]{0:T(128)}, f32[128]{0:T(128)S(1)}, u32[]{:S(2)}) copy-start(f32[128]{0:T(128)S(1)} %multiply_reduce_fusion.54) | copy-start | bytes 1540
  247.6 14.1 %copy-start.241 = (f32[128]{0:T(128)}, f32[128]{0:T(128)S(1)}, u32[]{:S(2)}) copy-start(f32[128]{0:T(128)S(1)} %add_rsqrt_fusion.17) | copy-start | bytes 1540
  252.6 20.2 %copy-start.45 = (f32[128,128]{0,1:T(8,128)}, f32[128,128]{0,1:T(8,128)S(1)}, u32[]{:S(2)}) copy-start(f32[128,128]{0,1:T(8,128)S(1)} %get-tuple-element.351) | copy-start | bytes 196612
  252.6 21.1 %copy-start.150 = (f32[128]{0:T(128)}, f32[128]{0:T(128)S(1)}, u32[]{:S(2)}) copy-start(f32[128]{0:T(128)S(1)} %get-tuple-element.350) | copy-start | bytes 1540
  253.9 19.7 %copy-start.55 = (f32[128,128]{0,1:T(8,128)}, f32[128,128]{0,1:T(8,128)S(1)}, u32[]{:S(2)}) copy-start(f32[128,128]{0,1:T(8,128)S(1)} %get-tuple-element.353) | copy-start | bytes 196612
  253.9 19.8 %copy-start.152 = (f32[128]{0:T(128)}, f32[128]{0:T(128)S(1)}, u32[]{:S(2)}) copy-start(f32[128]{0:T(128)S(1)} %get-tuple-element.352) | copy-start | bytes 1540
  254.6 19.2 %copy-start.202 = (f32[128]{0:T(128)}, f32[128]{0:T(128)S(1)}, u32[]{:S(2)}) copy-start(f32[128]{0:T(128)S(1)} %add_rsqrt_fusion.1) | copy-start | bytes 1540
  255.2 15.6 %copy-start.232 = (f32[128]{0:T(128)}, f32[128]{0:T(128)S(1)}, u32[]{:S(2)}) copy-start(f32[128]{0:T(128)S(1)} %add_rsqrt_fusion.5) | copy-start | bytes 1540
  255.9 14.9 %copy-start.230 = (f32[128]{0:T(128)}, f32[128]{0:T(128)S(1)}, u32[]{:S(2)}) copy-start(f32[128]{0:T(128)S(1)} %add_rsqrt_fusion.9) | copy-start | bytes 1540
  256.6 14.2 %copy-start.212 = (f32[128]{0:T(128)}, f32[128]{0:T(128)S(1)}, u32[]{:S(2)}) copy-start(f32[128]{0:T(128)S(1)} %add_rsqrt_fusion.13) | copy-start | bytes 1540
  277.3 14.8 %copy-start.85 = (f32[128,128]{0,1:T(8,128)S(1)}, f32[128,128]{0,1:T(8,128)}, u32[]{:S(2)}) copy-start(f32[128,128]{0,1:T(8,128)} %copy-done.84) | copy-start | bytes 196612
  277.3 14.8 %copy-start.87 = (f32[128,128]{0,1:T(8,128)S(1)}, f32[128,128]{0,1:T(8,128)}, u32[]{:S(2)}) copy-start(f32[128,128]{0,1:T(8,128)} %copy-done.86) | copy-start | bytes 196612
  277.3 19.4 %copy-start.77 = (f32[128,128]{0,1:T(8,128)S(1)}, f32[128,128]{0,1:T(8,128)}, u32[]{:S(2)}) copy-start(f32[128,128]{0,1:T(8,128)} %copy-done.76) | copy-start | bytes 196612
  277.3 19.4 %copy-start.79 = (f32[128,128]{0,1:T(8,128)S(1)}, f32[128,128]{0,1:T(8,128)}, u32[]{:S(2)}) copy-start(f32[128,128]{0,1:T(8,128)} %copy-done.78) | copy-start | bytes 196612
  278.0 14.1 %copy-start.100 = (s32[128]{0:T(128)S(1)}, s32[128]{0:T(128)}, u32[]{:S(2)}) copy-start(s32[128]{0:T(128)} %eq.98) | copy-start | bytes 1540
  278.0 14.1 %copy-start.191 = (f32[128]{0:T(128)S(1)}, f32[128]{0:T(128)}, u32[]{:S(2)}) copy-start(f32[128]{0:T(128)} %copy-done.190) | copy-start | bytes 1540
  278.0 14.1 %copy-start.193 = (f32[128]{0:T(128)S(1)}, f32[128]{0:T(128)}, u32[]{:S(2)}) copy-start(f32[128]{0:T(128)} %copy-done.192) | copy-start | bytes 1540
  278.0 14.1 %copy-start.238 = (f32[128]{0:T(128)S(1)}, f32[128]{0:T(128)}, u32[]{:S(2)}) copy-start(f32[128]{0:T(128)} %copy-done.237) | copy-start | bytes 1540
  278.0 14.1 %copy-start.246 = (f32[128]{0:T(128)S(1)}, f32[128]{0:T(128)}, u32[]{:S(2)}) copy-start(f32[128]{0:T(128)} %copy-done.245) | copy-start | bytes 1540
  278.1 15.7 %copy-start.281 = (f32[128]{0:T(128)S(1)}, f32[128]{0:T(128)}, u32[]{:S(2)}) copy-start(f32[128]{0:T(128)} %copy-done.280) | copy-start | bytes 1540
  278.1 15.7 %copy-start.223 = (f32[128]{0:T(128)S(1)}, f32[128]{0:T(128)}, u32[]{:S(2)}) copy-start(f32[128]{0:T(128)} %copy-done.222) | copy-start | bytes 1540
  278.1 17.2 %copy-start.226 = (f32[128]{0:T(128)S(1)}, f32[128]{0:T(128)}, u32[]{:S(2)}) copy-start(f32[128]{0:T(128)} %copy-done.225) | copy-start | bytes 1540
  278.1 18.6 %copy-start.283 = (f32[128]{0:T(128)S(1)}, f32[128]{0:T(128)}, u32[]{:S(2)}) copy-start(f32[128]{0:T(128)} %copy-done.282) | copy-start | bytes 1540
  278.1 18.6 %copy-start.168 = (f32[128]{0:T(128)S(1)}, f32[128]{0:T(128)}, u32[]{:S(2)}) copy-start(f32[128]{0:T(128)} %copy-done.167) | copy-start | bytes 1540
  278.1 18.6 %copy-start.170 = (f32[128]{0:T(128)S(1)}, f32[128]{0:T(128)}, u32[]{:S(2)}) copy-start(f32[128]{0:T(128)} %copy-done.169) | copy-start | bytes 1540
  278.1 18.6 %copy-start.189 = (f32[128]{0:T(128)S(1)}, f32[128]{0:T(128)}, u32[]{:S(2)}) copy-start(f32[128]{0:T(128)} %copy-done.188) | copy-start | bytes 1540
  278.1 18.6 %copy-start.231 = (f32[128]{0:T(128)S(1)}, f32[128]{0:T(128)}, u32[]{:S(2)}) copy-start(f32[128]{0:T(128)} %copy-done.230) | copy-start | bytes 1540
  278.1 19.6 %copy-start.236 = (f32[128]{0:T(128)S(1)}, f32[128]{0:T(128)}, u32[]{:S(2)}) copy-start(f32[128]{0:T(128)} %copy-done.235) | copy-start | bytes 1540
  278.1 21.2 %copy-start.277 = (f32[128]{0:T(128)S(1)}, f32[128]{0:T(128)}, u32[]{:S(2)}) copy-start(f32[128]{0:T(128)} %copy-done.276) | copy-start | bytes 1540
  278.2 21.2 %copy-start.197 = (f32[128]{0:T(128)S(1)}, f32[128]{0:T(128)}, u32[]{:S(2)}) copy-start(f32[128]{0:T(128)} %copy-done.196) | copy-start | bytes 1540
  279.9 21.0 %copy-start.200 = (f32[128]{0:T(128)S(1)}, f32[128]{0:T(128)}, u32[]{:S(2)}) copy-start(f32[128]{0:T(128)} %copy-done.199) | copy-start | bytes 1540
  283.8 18.5 %copy-start.279 = (f32[128]{0:T(128)S(1)}, f32[128]{0:T(128)}, u32[]{:S(2)}) copy-start(f32[128]{0:T(128)} %copy-done.278) | copy-start | bytes 1540
  283.8 18.5 %copy-start.68 = (f32[128,128]{0,1:T(8,128)S(1)}, f32[128,128]{0,1:T(8,128)}, u32[]{:S(2)}) copy-start(f32[128,128]{0,1:T(8,128)} %copy-done.67) | copy-start | bytes 196612
  283.8 18.5 %copy-start.70 = (f32[128,128]{0,1:T(8,128)S(1)}, f32[128,128]{0,1:T(8,128)}, u32[]{:S(2)}) copy-start(f32[128,128]{0,1:T(8,128)} %copy-done.69) | copy-start | bytes 196612
  283.8 18.5 %copy-start.159 = (f32[128]{0:T(128)S(1)}, f32[128]{0:T(128)}, u32[]{:S(2)}) copy-start(f32[128]{0:T(128)} %copy-done.158) | copy-start | bytes 1540
  283.8 18.5 %copy-start.161 = (f32[128]{0:T(128)S(1)}, f32[128]{0:T(128)}, u32[]{:S(2)}) copy-start(f32[128]{0:T(128)} %copy-done.160) | copy-start | bytes 1540
  283.8 18.6 %copy-start.178 = (f32[128]{0:T(128)S(1)}, f32[128]{0:T(128)}, u32[]{:S(2)}) copy-start(f32[128]{0:T(128)} %copy-done.177) | copy-start | bytes 1540
  283.8 18.6 %copy-start.195 = (f32[128]{0:T(128)S(1)}, f32[128]{0:T(128)}, u32[]{:S(2)}) copy-start(f32[128]{0:T(128)} %copy-done.194) | copy-start | bytes 1540
  283.8 18.6 %copy-start.213 = (f32[128]{0:T(128)S(1)}, f32[128]{0:T(128)}, u32[]{:S(2)}) copy-start(f32[128]{0:T(128)} %copy-done.212) | copy-start | bytes 1540
  287.9 15.0 %copy-start.216 = (f32[128]{0:T(128)S(1)}, f32[128]{0:T(128)}, u32[]{:S(2)}) copy-start(f32[128]{0:T(128)} %copy-done.215) | copy-start | bytes 1540
  504.8 80.4 %copy-start.183 = (s32[2304]{0:T(1024)S(1)}, s32[2304]{0:T(1024)}, u32[]{:S(2)}) copy-start(s32[2304]{0:T(1024)} %eq.104) | copy-start | bytes 27652
  595.1 18.7 %copy-start.118 = (f32[4928]{0:T(1024)S(1)}, f32[4928]{0:T(1024)}, u32[]{:S(2)}) copy-start(f32[4928]{0:T(1024)} %param.26) | copy-start | bytes 59140
  595.1 18.7 %copy-start.163 = (f32[4928]{0:T(1024)S(1)}, f32[4928]{0:T(1024)}, u32[]{:S(2)}) copy-start(f32[4928]{0:T(1024)} %param.30) | copy-start | bytes 59140
  595.1 18.7 %copy-start.164 = (f32[4928]{0:T(1024)S(1)}, f32[4928]{0:T(1024)}, u32[]{:S(2)}) copy-start(f32[4928]{0:T(1024)} %param.34) | copy-start | bytes 59140
  599.6 17.9 %copy-start.75 = (f32[2,32,4096]{2,1,0:T(8,128)S(1)}, f32[2,32,4096]{2,1,0:T(8,128)}, u32[]{:S(2)}) copy-start(f32[2,32,4096]{2,1,0:T(8,128)} %param.28) | copy-start | bytes 3145732
  (243 other events, 1213.2 us)
Sparse Core Ops, SparseCore 0:
  10.9 103.1 all-gather.5
  416.2 86.3 reduce-scatter.1

commit v4 on v3

--- a/solution.py
+++ b/solution.py
@@ -408,13 +408,14 @@
 
 
 SPLITS = 4
-
-
-def start_kernel(shard_rows, room, *refs):
-    packet_ref, vec_ref, attn_ref, ffn_ref, word_ref = refs[:5]
-    packet_out, vec_out, weight_out, rows_out = refs[5:9]
-    table, rows_held = refs[9:11]
-    packet_sem, vec_sem, row_sem, z_sem, y_sem, x_sem, d_sem = refs[11:]
+WINDOW = 3
+
+
+def start_kernel(shard_rows, room, pair_rows, *refs):
+    column_ref, row_ref, packet_ref, vec_ref, attn_ref, ffn_ref, word_ref = refs[:7]
+    place_out, packet_out, vec_out, weight_out, rows_out = refs[7:12]
+    table, rows_held, packet, slots, locals_ = refs[12:17]
+    packet_sem, vec_sem, row_sem, z_sem, y_sem, x_sem, d_sem, e_sem, own_sem = refs[17:]
 
     d = lax.axis_index("dp")
     z = lax.axis_index("zero")
@@ -424,8 +425,14 @@
     line = z // 4
     sibling = z + 1 - 2 * core
     across = z + 2 - 4 * col
-    width = attn_ref.shape[1]
-    part = width // SPLITS
+    layers = attn_ref.shape[0]
+    width = attn_ref.shape[2]
+    whole = 3 * width
+    plane = 7 * whole // 12
+    part = plane // SPLITS
+    alone = whole - plane
+    x_parts = -(-alone // part)
+    total = layers * SPLITS
 
     def everyone(k):
         p = lax.rem(me + k, 32)
@@ -438,8 +445,9 @@
         return carry
 
     lax.fori_loop(1, 32, greet, 0)
-    weight_out[z, :, 0:width] = attn_ref[...].astype(jnp.bfloat16)
-    weight_out[z, :, width : 3 * width] = ffn_ref[...].astype(jnp.bfloat16)
+    for layer in range(layers):
+        weight_out[layer, z, :, 0:width] = attn_ref[layer].astype(jnp.bfloat16)
+        weight_out[layer, z, :, width:whole] = ffn_ref[layer].astype(jnp.bfloat16)
     pl.semaphore_wait(barrier, 31)
 
     def remote(src, dst, sems, at, to):
@@ -453,7 +461,7 @@
         )
 
     def packet_copy(k, slot):
-        return remote(packet_ref, packet_out.at[slot], packet_sem, (k,), everyone(k))
+        return remote(packet, packet_out.at[slot], packet_sem, (k,), everyone(k))
 
     def vec_copy(k, slot):
         return remote(vec_ref, vec_out.at[slot], vec_sem, (k,), (d, lax.rem(z + k, 16)))
@@ -462,61 +470,128 @@
         to = lax.rem(z + k, 16)
         return remote(rows_held.at[to], rows_out.at[slot], row_sem, (k,), (d, to))
 
+    def shard(i):
+        at = lax.rem(line + i % 4, 4) * 4 + lax.rem(z, 4)
+        return at if i < 4 else at + 2 - 4 * col
+
+    def stretch(at, s, ours):
+        layer, p = s // SPLITS, s % SPLITS
+        first = ours * (whole - part * (p + 1)) + (1 - ours) * part * p
+        return weight_out.at[layer, at, :, pl.ds(pl.multiple_of(first, 128), part)]
+
+    def handed(at, s, ours):
+        layer, p = s // SPLITS, s % SPLITS
+        size = min(part, alone - part * p)
+        first = ours * (whole - part * p - size) + (1 - ours) * part * p
+        return weight_out.at[layer, at, :, pl.ds(pl.multiple_of(first, 128), size)]
+
+    def both(ref, sems, at, to):
+        return remote(ref, ref, sems, at, to)
+
+    def z_copy(s, k, at):
+        to = lax.rem(line + k, 4) * 4 + lax.rem(z, 4)
+        return both(stretch(at, s, d), z_sem, (s, k - 1), (d, to))
+
+    def y_copy(s, j, at):
+        return both(stretch(at, s, d), y_sem, (s, j), (d, across))
+
+    def x_copy(s, i, at, ours):
+        return both(handed(at, s, ours), x_sem, (s, i), (1 - d, z))
+
+    def d_copy(s, i, at):
+        return both(stretch(at, s, d), d_sem, (s, i), (d, sibling))
+
+    def e_copy(s, i, at):
+        return both(handed(at, s, 1 - d), e_sem, (s, i), (d, sibling))
+
+    def own_copy(layer, at):
+        ref = weight_out.at[layer, at]
+        return both(ref, own_sem, (layer,), (d, sibling))
+
+    def hands(s):
+        return s % SPLITS < x_parts
+
+    def spread(s, i):
+        at = shard(i)
+        if i < 4:
+            y_copy(s, i, at).start()
+        if i > 0:
+            if hands(s):
+                x_copy(s, i, at, d).start()
+            d_copy(s, i, at).start()
+
+    def open_piece(s):
+        for k in range(1, 4):
+            z_copy(s, k, z).start()
+        spread(s, 0)
+
+    for s in range(WINDOW):
+        open_piece(s)
+
+    tokens = column_ref.shape[0]
+    ids_row = row_ref[...]
+    lane = lax.broadcasted_iota(jnp.int32, (1, tokens), 1).astype(jnp.float32)
+    block = 128
+
+    def lead_of(b, least):
+        ids = column_ref[pl.ds(pl.multiple_of(b * block, block), block), :]
+        there = lax.broadcasted_iota(jnp.int32, (block, 1), 0) + b * block
+        found = jnp.where(ids == ids_row, there.astype(jnp.float32), 1e9)
+        return jnp.minimum(least, jnp.min(found, axis=0, keepdims=True))
+
+    least = lax.fori_loop(0, tokens // block, lead_of, jnp.full((1, tokens), 1e9, jnp.float32))
+    lead_ids = jnp.where(least == lane, ids_row, -1)
+
+    def place_of(b, most):
+        at = pl.ds(pl.multiple_of(b * block, block), block)
+        ids = column_ref[at, :]
+        owner = jnp.zeros_like(ids)
+        for o in range(1, 16):
+            owner = owner + (ids >= o * shard_rows).astype(jnp.int32)
+        low_id = owner * shard_rows
+        ahead = (lead_ids >= low_id) & (lead_ids < ids)
+        place = jnp.sum(jnp.where(ahead, 1.0, 0.0), axis=1, keepdims=True)
+        place_out[at, :] = place.astype(jnp.int32)
+        inside = place < room
+        slots[at, :] = jnp.where(inside, owner * 128 + place.astype(jnp.int32), -1)
+        locals_[at, :] = (ids - low_id).astype(jnp.float32)
+        return jnp.maximum(most, jnp.max(place, axis=0, keepdims=True))
+
+    most = lax.fori_loop(0, tokens // block, place_of, jnp.zeros((1, 1), jnp.float32))
+    packet[...] = packet_ref[...]
+    lane128 = lax.broadcasted_iota(jnp.int32, (1, 128), 1)
+
+    for o in range(16):
+
+        def asked_of(b, best, o=o):
+            at = pl.ds(pl.multiple_of(b * block, block), block)
+            found = jnp.where(slots[at, :] == o * 128 + lane128, locals_[at, :], -1.0)
+            return jnp.maximum(best, jnp.max(found, axis=0, keepdims=True))
+
+        best = lax.fori_loop(0, tokens // block, asked_of, jnp.full((1, 128), -1.0, jnp.float32))
+        packet[o : o + 1, :] = best.astype(jnp.int32)
+    rounds = jnp.ones((1, 1), jnp.float32)
+    for r in range(1, -(-tokens // room)):
+        rounds = rounds + (most >= r * room).astype(jnp.float32)
+    last = packet.shape[0] - 1
+    packet[last : last + 1, :] = jnp.where(
+        lane128 == pair_rows, rounds.astype(jnp.int32), packet_ref[last : last + 1, :]
+    )
+
     def send_packets(k, carry):
         packet_copy(k, me).start()
         return carry
 
     lax.fori_loop(1, 32, send_packets, 0)
 
-    def shard(i):
-        at = lax.rem(line + i % 4, 4) * 4 + lax.rem(z, 4)
-        return at if i < 4 else at + 2 - 4 * col
-
-    columns = (
-        pl.multiple_of(d * width, width),
-        2 * width,
-        pl.multiple_of((1 - d) * width, width),
-    )
-
-    def block(at, s, g):
-        first = pl.multiple_of(columns[g] + s * part, 128)
-        return weight_out.at[at, :, pl.ds(first, part)]
-
-    def z_copy(s, k, g, at):
-        to = lax.rem(line + k, 4) * 4 + lax.rem(z, 4)
-        return remote(block(at, s, g), block(at, s, g), z_sem, (s, k - 1, g), (d, to))
-
-    def y_copy(s, j, g, at):
-        return remote(block(at, s, g), block(at, s, g), y_sem, (s, j, g), (d, across))
-
-    def x_copy(s, i, g, at):
-        return remote(block(at, s, g), block(at, s, g), x_sem, (s, i), (1 - d, z))
-
-    def d_copy(s, i, g, at):
-        return remote(block(at, s, g), block(at, s, g), d_sem, (s, i, g), (d, sibling))
-
-    def spread(s, i):
-        at = shard(i)
-        if i < 4:
-            y_copy(s, i, 0, at).start()
-            y_copy(s, i, 1, at).start()
-        if i > 0:
-            x_copy(s, i, 0, at).start()
-        for g in range(2 if i > 0 else 3):
-            d_copy(s, i, g, at).start()
-
-    for s in range(SPLITS):
-        for k in range(1, 4):
-            for g in range(2):
-                z_copy(s, k, g, z).start()
-        spread(s, 0)
-
     def send_vec(k, carry):
         vec_copy(k, z).start()
         return carry
 
     lax.fori_loop(1, 16, send_vec, 0)
-    packet_out[me] = packet_ref[...]
+    for layer in range(layers):
+        own_copy(layer, z).start()
+    packet_out[me] = packet[...]
     vec_out[z] = vec_ref[...]
 
     body_rows = shard_rows // 16 * 16
@@ -533,7 +608,7 @@
     if shard_rows > body_rows:
         table[body_rows:shard_rows, :] = word_ref[body_rows:shard_rows, :].astype(jnp.bfloat16)
 
-    def answer(k):
+    def answer_one(k, carry):
         src = lax.rem(z + k, 16)
         asked = packet_out[d * 16 + src, pl.ds(z, 1), :]
         rows_at = lax.broadcasted_iota(jnp.int32, (padded, 128), 0)
@@ -541,73 +616,72 @@
         found = lax.dot_general(
             picked, table[...], (((0,), (0,)), ((), ())), preferred_element_type=jnp.float32
         )
-        return src, found[:room, :].astype(jnp.bfloat16)
+        rows_held[src] = found[:room, :].astype(jnp.bfloat16)
+        return carry
 
     def packet_in(k, carry):
         packet_copy(k, lax.rem(me + 32 - k, 32)).wait_recv()
         return carry
 
-    def answer_one(k, carry):
-        src, found = answer(k)
-        rows_held[src] = found
+    def row_start(k, carry):
         row_copy(k, z).start()
         return carry
 
     def z_phase(s):
         for k in range(1, 4):
-            at = shard(4 - k)
-            for g in range(2):
-                z_copy(s, k, g, at).wait_recv()
+            z_copy(s, k, shard(4 - k)).wait_recv()
             spread(s, 4 - k)
+        if s + WINDOW < total:
+            open_piece(s + WINDOW)
 
     def y_phase(s):
         for j in range(4):
-            at = shard(4 + j)
-            for g in range(2):
-                y_copy(s, j, g, at).wait_recv()
+            y_copy(s, j, shard(4 + j)).wait_recv()
             spread(s, 4 + j)
 
     def x_phase(s):
+        if hands(s):
+            for i in range(1, 8):
+                at = shard(i)
+                x_copy(s, i, at, 1 - d).wait_recv()
+                e_copy(s, i, at).start()
+
+    done = 0
+    for t in range(total + 2):
+        if t < total:
+            z_phase(t)
+        if t == 1:
+            lax.fori_loop(1, 32, packet_in, 0)
+        if t >= 1:
+            until = min(16, done + 4)
+            if until > done:
+                lax.fori_loop(done, until, answer_one, 0)
+            done = until
+        if t == total - 1:
+            lax.fori_loop(1, 16, row_start, 0)
+            rows_out[z] = rows_held[z]
+        if 0 <= t - 1 < total:
+            y_phase(t - 1)
+        if 0 <= t - 2 < total:
+            x_phase(t - 2)
+
+    turn = 1 - 2 * core
+    for layer in range(layers):
+        own_copy(layer, z + turn).wait_recv()
+        own_copy(layer, z).wait_send()
+    for s in range(total):
         for i in range(1, 8):
             at = shard(i)
-            x_copy(s, i, 2, at).wait_recv()
-            d_copy(s, i, 2, at).start()
-
-    lax.fori_loop(1, 32, packet_in, 0)
-    done = 1
-    for t in range(SPLITS + 2):
-        until = min(16, 1 + (t + 1) * 15 // SPLITS)
-        if until > done:
-            lax.fori_loop(done, until, answer_one, 0)
-        done = max(done, until)
-        if t < SPLITS:
-            z_phase(t)
-        if 0 <= t - 1 < SPLITS:
-            y_phase(t - 1)
-        if 0 <= t - 2 < SPLITS:
-            x_phase(t - 2)
-    _, found = answer(0)
-    rows_out[z] = found
-
-    for s in range(SPLITS):
-        for i in range(8):
-            at = shard(i)
-            there = at + 1 - 2 * core
-            for g in range(3):
-                d_copy(s, i, g, there).wait_recv()
-    for s in range(SPLITS):
+            d_copy(s, i, at + turn).wait_recv()
+            d_copy(s, i, at).wait_send()
+            if hands(s):
+                e_copy(s, i, at + turn).wait_recv()
+                e_copy(s, i, at).wait_send()
+                x_copy(s, i, at, d).wait_send()
         for k in range(1, 4):
-            for g in range(2):
-                z_copy(s, k, g, z).wait_send()
-        for i in range(8):
-            at = shard(i)
-            if i < 4:
-                y_copy(s, i, 0, at).wait_send()
-                y_copy(s, i, 1, at).wait_send()
-            if i > 0:
-                x_copy(s, i, 0, at).wait_send()
-            for g in range(3):
-                d_copy(s, i, g, at).wait_send()
+            z_copy(s, k, z).wait_send()
+        for i in range(4):
+            y_copy(s, i, shard(i)).wait_send()
 
     def finish(k, carry):
         back = lax.rem(z + 16 - k, 16)
@@ -626,40 +700,134 @@
     lax.fori_loop(1, 32, finish_packets, 0)
 
 
-def exchange_start(packet, vec_rows, attn, ffn, word_table, room, collective_id):
+def exchange_start(ids, packet, vec_rows, attn, ffn, word_table, room, pair_rows, collective_id):
     half = jnp.bfloat16
     shard_rows, features = word_table.shape
     padded = -(-shard_rows // 128) * 128
-    rows, width = attn.shape
+    layers, rows, width = attn.shape
+    tokens = ids.shape[0]
+    pieces = layers * SPLITS
     dma = pltpu.SemaphoreType.DMA
     vmem = pl.BlockSpec(memory_space=pltpu.VMEM)
     return pl.pallas_call(
-        functools.partial(start_kernel, shard_rows, room),
+        functools.partial(start_kernel, shard_rows, room, pair_rows),
         out_shape=(
+            jax.ShapeDtypeStruct((tokens, 1), jnp.int32),
             jax.ShapeDtypeStruct((32,) + packet.shape, packet.dtype),
             jax.ShapeDtypeStruct((16,) + vec_rows.shape, vec_rows.dtype),
-            jax.ShapeDtypeStruct((16, rows, 3 * width), half),
+            jax.ShapeDtypeStruct((layers, 16, rows, 3 * width), half),
             jax.ShapeDtypeStruct((16, room, features), half),
         ),
-        in_specs=[vmem] * 5,
-        out_specs=tuple([vmem] * 4),
+        in_specs=[vmem] * 7,
+        out_specs=tuple([vmem] * 5),
         scratch_shapes=[
             pltpu.VMEM((padded, features), half),
             pltpu.VMEM((16, room, features), half),
+            pltpu.VMEM(packet.shape, packet.dtype),
+            pltpu.VMEM((tokens, 1), jnp.int32),
+            pltpu.VMEM((tokens, 1), jnp.float32),
             dma((2, 32)),
             dma((2, 16)),
             dma((2, 16)),
-            dma((2, SPLITS, 3, 2)),
-            dma((2, SPLITS, 4, 2)),
-            dma((2, SPLITS, 8)),
-            dma((2, SPLITS, 8, 3)),
+            dma((2, pieces, 3)),
+            dma((2, pieces, 4)),
+            dma((2, pieces, 8)),
+            dma((2, pieces, 8)),
+            dma((2, pieces, 8)),
+            dma((2, layers)),
         ],
         compiler_params=pltpu.CompilerParams(
             collective_id=collective_id, has_side_effects=True, vmem_limit_bytes=48 * 1024 * 1024
         ),
         cost_estimate=pl.CostEstimate(flops=0, bytes_accessed=150_000_000, transcendentals=0),
         name="exchange_start",
-    )(packet, vec_rows, attn, ffn, word_table)
+    )(ids.reshape(-1, 1), ids.reshape(1, -1), packet, vec_rows, attn, ffn, word_table)
+
+
+WIDTHS = (D, D * 2 // 3, D // 3, D // 6, D // 12)
+
+
+def contrastive_kernel(pooled_ref, false_ref, pair_ref, loss_ref, grad_ref):
+    pairs = false_ref.shape[0]
+    high = lax.Precision.HIGHEST
+    columns = lax.broadcasted_iota(jnp.int32, (pairs, pairs), 1)
+    hit = columns == pair_ref[...]
+    kept = (false_ref[...] == 0) | hit
+    hits = hit.astype(jnp.float32)
+    valid = (pair_ref[...] >= 0).astype(jnp.float32)
+    inverse = 1.0 / jnp.maximum(jnp.sum(valid, axis=0, keepdims=True), 1.0)
+    weight = valid * inverse
+    named = jnp.sum(hits, axis=1, keepdims=True)
+    totals = jnp.zeros((pairs, 1), jnp.float32)
+    for first, width in enumerate(WIDTHS):
+        span = -(-width // 128) * 128
+        inside = lax.broadcasted_iota(jnp.int32, (1, span), 1) < width
+        units, scales, logs = [], [], []
+        for kind in range(2):
+            pair_units, pair_scales = [], []
+            for role in range(2):
+                rows = jnp.where(inside, pooled_ref[kind, role, :, 0:span], 0.0)
+                scale = lax.rsqrt(jnp.sum(rows * rows, axis=1, keepdims=True) + NORM_EPS)
+                pair_units.append(rows * scale)
+                pair_scales.append(scale)
+            sims = lax.dot_general(
+                pair_units[0],
+                pair_units[1],
+                (((1,), (1,)), ((), ())),
+                precision=high,
+                preferred_element_type=jnp.float32,
+            )
+            sims = jnp.where(kept, sims / SOFTMAX_TEMP, MASKED)
+            shifted = sims - jnp.max(sims, axis=1, keepdims=True)
+            logs.append(shifted - jnp.log(jnp.sum(jnp.exp(shifted), axis=1, keepdims=True)))
+            units.append(pair_units)
+            scales.append(pair_scales)
+        shallow, deep = logs
+        p_shallow, p_deep = jnp.exp(shallow), jnp.exp(deep)
+        gap = p_deep * (deep - shallow)
+        spread = jnp.sum(gap, axis=1, keepdims=True)
+        totals = totals + spread - jnp.sum(jnp.where(hit, shallow + deep, 0.0), axis=1, keepdims=True)
+        d_sims = (
+            p_shallow * (named + 1.0) - hits - p_deep,
+            gap + p_deep * (named - spread) - hits,
+        )
+        for kind in range(2):
+            d_cos = jnp.where(kept, d_sims[kind] * weight, 0.0) / SOFTMAX_TEMP
+            for role in range(2):
+                unit = units[kind][role]
+                d_unit = lax.dot_general(
+                    d_cos,
+                    units[kind][1 - role],
+                    (((1 - role,), (0,)), ((), ())),
+                    precision=high,
+                    preferred_element_type=jnp.float32,
+                )
+                along = jnp.sum(d_unit * unit, axis=1, keepdims=True)
+                d_rows = scales[kind][role] * (d_unit - unit * along)
+                if first == 0:
+                    grad_ref[kind, role] = d_rows
+                else:
+                    grad_ref[kind, role, :, 0:span] = grad_ref[kind, role, :, 0:span] + d_rows
+    loss_ref[...] = jnp.broadcast_to(
+        jnp.sum(totals * valid, axis=0, keepdims=True) * inverse, loss_ref.shape
+    )
+
+
+def contrastive(pooled_all, false_all, pair_all):
+    vmem = pl.BlockSpec(memory_space=pltpu.VMEM)
+    loss, grads = pl.pallas_call(
+        contrastive_kernel,
+        out_shape=(
+            jax.ShapeDtypeStruct((8, 128), jnp.float32),
+            jax.ShapeDtypeStruct(pooled_all.shape, jnp.float32),
+        ),
+        in_specs=[vmem] * 3,
+        out_specs=(vmem, vmem),
+        compiler_params=pltpu.CompilerParams(vmem_limit_bytes=32 * 1024 * 1024),
+        cost_estimate=pl.CostEstimate(flops=10**9, bytes_accessed=3_000_000, transcendentals=10**6),
+        name="contrastive",
+    )(pooled_all, false_all, pair_all.reshape(-1, 1))
+    return loss[0, 0], grads
 
 
 def split_vectors(vec_all):
@@ -827,18 +995,20 @@
     vec_len = vectors.shape[0]
 
     room = -(-(tokens * 9 // 8) // (nz * 8)) * 8
-    owner, place, local_row = token_plan(flat_ids.reshape(-1), shard_rows)
-    slot, asked = round_slots(owner, place, local_row, 0, room, nz)
-    rounds_here = jnp.max(place) // room + 1
-    last = jnp.concatenate([pair_index, rounds_here[None].astype(jnp.int32)])
-    packet = jnp.concatenate(
-        [
-            jnp.pad(asked.reshape(nz, room), ((0, 0), (0, 128 - room)), constant_values=-1),
-            false_neg.reshape(-1, 128),
-            jnp.pad(last, (0, 128 - last.shape[0]))[None],
-        ]
-    )
-    packet = jnp.pad(packet, ((0, -packet.shape[0] % 8), (0, 0)))
+    ids = flat_ids.reshape(-1)
+
+    def packet_of(asked, rounds_here):
+        last = jnp.concatenate([pair_index, rounds_here[None].astype(jnp.int32)])
+        lines = nz + false_neg.size // 128
+        return jnp.concatenate(
+            [
+                jnp.pad(asked.reshape(nz, room), ((0, 0), (0, 128 - room)), constant_values=-1),
+                false_neg.reshape(-1, 128),
+                jnp.zeros((7 - lines % 8, 128), jnp.int32),
+                jnp.pad(last, (0, 128 - last.shape[0]))[None],
+            ]
+        )
+
     vec_rows = pad_rows(vectors.astype(jnp.bfloat16), 16)
 
     def gather_layer(layer_index):
@@ -849,22 +1019,30 @@
         return lax.all_gather(both, "zero", axis=0, tiled=True)
 
     if by_hand:
-        packets, vec_parts, first_weights, received = exchange_start(
-            packet, vec_rows, attn_w[0], ffn_w[0], word_table, room, 0
-        )
-        layer_weights = [first_weights.reshape(-1, 4 * D + 2 * FF)]
+        packet = packet_of(jnp.zeros((nz * room,), jnp.int32), jnp.int32(0))
+        place, packets, vec_parts, gathered, received = exchange_start(
+            ids, packet, vec_rows, attn_w, ffn_w, word_table, room, pair_rows, 0
+        )
+        layer_weights = [gathered[layer].reshape(-1, 4 * D + 2 * FF) for layer in range(LAYERS)]
+        owner = ids // shard_rows
+        place, local_row = place.reshape(-1), ids - owner * shard_rows
+        slot = jnp.where(place < room, owner * room + place, -1)
     else:
+        owner, place, local_row = token_plan(ids, shard_rows)
+        slot, asked = round_slots(owner, place, local_row, 0, room, nz)
         packets, vec_parts = exchange(
-            [packet, vec_rows], ["all", "zero"], ndp, nz, 0, "gather_requests"
-        )
-        layer_weights = [gather_layer(0)]
-    for layer_index in range(1, LAYERS):
-        layer_weights.append(gather_layer(layer_index))
+            [packet_of(asked, jnp.max(place) // room + 1), vec_rows],
+            ["all", "zero"],
+            ndp,
+            nz,
+            0,
+            "gather_requests",
+        )
+        layer_weights = [gather_layer(layer_index) for layer_index in range(LAYERS)]
     asked_all = packets[:, :nz, :room]
-    at = nz + pair_rows * total_pairs // 128
-    false_all = packets[:, nz:at].reshape(total_pairs, total_pairs)
-    pair_all = packets[:, at, :pair_rows].reshape(total_pairs)
-    rounds = jnp.max(packets[:, at, pair_rows])
+    false_all = packets[:, nz : nz + false_neg.size // 128].reshape(total_pairs, total_pairs)
+    pair_all = packets[:, -1, :pair_rows].reshape(total_pairs)
+    rounds = jnp.max(packets[:, -1, pair_rows])
     vec_all = vec_parts.reshape(nz, -1)[:, :vec_len].reshape(-1).astype(jnp.float32)
 
     word_half = word_table.astype(jnp.bfloat16)
@@ -918,24 +1096,27 @@
     )
     pooled_all = pooled_all.reshape(n, 2, pair_rows, 2, D).astype(jnp.float32)
     pooled_all = pooled_all.transpose(1, 3, 0, 2, 4).reshape(2, 2, total_pairs, D)
-
-    def whole_loss(shallow_anchor, deep_anchor, shallow_pos, deep_pos):
-        return contrastive_terms(
-            shallow_anchor, deep_anchor, shallow_pos, deep_pos, false_all, pair_all
-        )
-
-    loss_total, loss_back = jax.vjp(
-        whole_loss, pooled_all[0, 0], pooled_all[1, 0], pooled_all[0, 1], pooled_all[1, 1]
-    )
-    valid_total = jnp.sum((pair_all >= 0).astype(jnp.float32))
-    inverse = 1.0 / jnp.maximum(valid_total, 1.0)
-    loss = loss_total * inverse
-    shallow_anchor_grad, deep_anchor_grad, shallow_pos_grad, deep_pos_grad = [
-        lax.dynamic_slice_in_dim(part, me * pair_rows, pair_rows, 0) for part in loss_back(inverse)
-    ]
+    if total_pairs <= 256:
+        loss, pooled_grads = contrastive(pooled_all, false_all, pair_all)
+    else:
+
+        def whole_loss(pooled_now):
+            summed = contrastive_terms(
+                pooled_now[0, 0],
+                pooled_now[1, 0],
+                pooled_now[0, 1],
+                pooled_now[1, 1],
+                false_all,
+                pair_all,
+            )
+            valid_total = jnp.sum((pair_all >= 0).astype(jnp.float32))
+            return summed / jnp.maximum(valid_total, 1.0)
+
+        loss, pooled_grads = jax.value_and_grad(whole_loss)(pooled_all)
+    pooled_grads = lax.dynamic_slice_in_dim(pooled_grads, me * pair_rows, pair_rows, 2)
+    pooled_grads = pooled_grads.transpose(0, 2, 1, 3).reshape(2, seq_rows, D)
+    shallow_back, deep_back = pooled_grads[0], pooled_grads[1]
     share = key_mask.astype(jnp.float32) / seq_lengths.astype(jnp.float32)[:, None]
-    shallow_back = jnp.stack([shallow_anchor_grad, shallow_pos_grad], axis=1).reshape(seq_rows, D)
-    deep_back = jnp.stack([deep_anchor_grad, deep_pos_grad], axis=1).reshape(seq_rows, D)
     grad_hidden = jnp.zeros_like(embedded)
     weight_parts = []
     vec_grad = jnp.zeros_like(vec_all)

time: 650 us -> 569 us (0.88)
  other arithmetic: 147 us -> 91 us
  matrix products: 175 us -> 148 us
  Pallas kernels: 212 us -> 223 us
  between operations: 27.6 us -> 21 us
    dot_general x30 -> x0, matrix products: 34.4 us -> none  [contrastive_terms(): jnp.dot(normalized_rows(anchor_vectors[:, :current_width]), normalized_ro...]
    reduce_sum x47 -> x0, other arithmetic: 21.6 us -> none  [the longest x20 10.8 us: normalized_rows(): jnp.sum(rows * rows, axis=-1, keepdims=True) + NORM_EPS]
    rsqrt x20 -> x0, other arithmetic: 11.7 us -> none  [normalized_rows(): lax.rsqrt(jnp.sum(rows * rows, axis=-1, keepdims=True) + NORM_EPS)]
    add_any x20 -> x0, other arithmetic: 9.6 us -> none  [normalized_rows(): rows * rows]
    slice x2 -> x7, local copies, waits for them, and re-layouts: 1.5 us -> 9.46 us  [the longest x1 8.86 us: body(): gathered[layer].reshape(-1, 4 * D + 2 * FF)]
    pallas_call x1 -> x2, Pallas kernels: 98.4 us -> 106 us  [the longest x1 99.9 us: exchange_start(): pl.pallas_call(functools.partial(start_kernel, shard_rows, room, pair_row...]
    dot_general x19, matrix products: 73.2 us -> 81 us  [matmul(): return jnp.dot(left, right, preferred_element_type=jnp.float32)]
    unnamed x610 -> x242, local copies, waits for them, and re-layouts: 22.5 us -> 19.7 us
  transfers between devices with their start and end apart: 2 -> 1, of which waited for: 1 -> 0; matrix products, arithmetic and copies ran while one was open for 20% -> 15% of each run, Pallas kernels for 15% -> 0%
where the time goes in v4:
time: 569 us; the launch traced here: 561 us
  Pallas kernels  223 us (39%)
  matrix products  148 us (26%)
  other arithmetic  91 us (16%)
  local copies, waits for them, and re-layouts  75.5 us (13%)
  between operations  21 us (4%)
    pallas_call x1, Pallas kernels, exchange_start(): pl.pallas_call(functools.partial(start_kernel, shard_rows, room, pair_row...  99.9 us
    pallas_call x1, Pallas kernels, exchange_gradients(): pl.pallas_call(functools.partial(gradient_kernel, tuple(chunks), len(part...  81.2 us
    dot_general x19, matrix products, matmul(): return jnp.dot(left, right, preferred_element_type=jnp.float32)  81 us
    dot_general x16, matrix products, einsum_plain(): return jnp.einsum(form, left, right, preferred_element_type=jnp.float32)  43.9 us
    pallas_call x2, Pallas kernels, exchange(): pl.pallas_call(functools.partial(exchange_kernel, tuple(modes), ndp, nz),...  35.8 us
    convert_element_type x11, other arithmetic, low_back(): return build_low_back()(value)  23.8 us
    unnamed x242, local copies, waits for them, and re-layouts  19.7 us
    sub x2, matrix products, encoder_layer(): attention = low(jax.nn.softmax(scores, axis=-1))  11.5 us
  transfers between devices with their start and end apart: 1, of which 0 were waited for; matrix products, arithmetic and copies ran while one was open for 15% of the time, Pallas kernels for 0%

profile of v4, /device:TPU:0, one launch (start us, length us, event | category | flops | bytes accessed | tf_op | source)
XLA Modules:
  0.0 560.6 jit_solution(12124115022914601877)
XLA Ops:
  11.4 3.7 convert_element_type.278
  15.2 99.9 %exchange_start.1 = (s32[1024,1]{1,0:T(8,128)S(1)}, s32[32,24,128]{2,1,0:T(8,128)S(1)}, bf16[16,48,128]{2,1,0:T(8,128)(2,1)S(1)}, bf16[2,16,32,6144]{3,2,1,0:T(8,128)(2,1)}, bf16[16,72,512]{2,1,0:T(8,128)(2,1)S(1)}) custom-call(s32[1024,1]{1,0:T(8,128)S(1)} %copy.203.refs_0_, s32[1,1024]{1,0:T(1,128)S(1)} %bitcast.278, s32[24,128]{1,0:T(8,128)S(1)} %pad_add_fusion.refs_2_, ...), custom_call_target="tpu_custom_call" | custom-call | bytes 150000000 | tf_op jit(solution)/shard_map/exchange_start/pallas_call | solution.py:712
  121.6 8.9 %fusion.121 = (bf16[1,16,32,6144]{3,2,1,0:T(8,128)(2,1)}, bf16[1,16,32,6144]{3,2,1,0:T(8,128)(2,1)S(1)}) fusion(bf16[2,16,32,6144]{3,2,1,0:T(8,128)(2,1)} %get-tuple-element.114), kind=kLoop, calls=%fused_computation.306 | loop fusion | bytes 25165824 | tf_op jit(solution)/shard_map/slice | solution.py:1026
  134.7 2.3 copy.211
  139.9 5.8 %fusion.129 = (f32[8,8,128]{2,1,0:T(8,128)S(1)}, f32[8,8,128,128]{2,3,1,0:T(8,128)}) fusion(pred[8,128]{1,0:T(8,128)(4,1)S(1)} %iota_compare_fusion.28, bf16[8,128,8,64]{1,3,2,0:T(8,128)(2,1)} %bitcast.328, bf16[8,128,8,64]{1,3,2,0:T(8,128)(2,1)} %bitcast.326), kind=kOutput, calls=%fused_computation.314 | convolution fusion | flops 138412160 | bytes 6325248 | tf_op jit(solution)/shard_map/jvp()/sub | solution.py:873
  145.7 2.8 divide_convert_fusion.1
  149.8 3.3 fusion.130
  154.0 14.4 %multiply_convert_fusion.1 = (bf16[8,128,2048]{2,1,0:T(8,128)(2,1)S(1)}, f32[8,128,2048]{2,1,0:T(8,128)}) fusion(f32[2048]{0:T(1024)S(1)} %get-tuple-element.225, bf16[8,128,512]{2,1,0:T(8,128)(2,1)S(1)} %fusion.65, bf16[512,6144]{1,0:T(8,128)(2,1)S(1)} %bitcast.324), kind=kOutput, calls=%fused_computation.59 | convolution fusion | flops 2168455168 | bytes 15736832 | tf_op jit(solution)/shard_map/jvp()/dot_general | solution.py:78
  168.5 2.7 fusion.131
  173.0 3.2 add_convert_fusion.4
  177.9 2.3 copy.216
  183.1 5.7 %fusion.132 = (f32[8,8,128]{2,1,0:T(8,128)S(1)}, f32[8,8,128,128]{2,3,1,0:T(8,128)}) fusion(pred[8,128]{1,0:T(8,128)(4,1)S(1)} %iota_compare_fusion.28, bf16[8,128,8,64]{1,3,2,0:T(8,128)(2,1)} %bitcast.332, bf16[8,128,8,64]{1,3,2,0:T(8,128)(2,1)} %bitcast.330), kind=kOutput, calls=%fused_computation.317 | convolution fusion | flops 138412160 | bytes 6325248 | tf_op jit(solution)/shard_map/jvp()/sub | solution.py:873
  188.8 2.8 divide_convert_fusion
  192.9 3.2 fusion.133
  197.0 6.4 %multiply_convert_fusion = (bf16[8,128,2048]{2,1,0:T(8,128)(2,1)S(1)}, f32[8,128,2048]{2,1,0:T(8,128)}) fusion(f32[2048]{0:T(1024)S(1)} %get-tuple-element.224, bf16[8,128,512]{2,1,0:T(8,128)(2,1)S(1)} %fusion.66, bf16[512,6144]{1,0:T(8,128)(2,1)S(1)} %bitcast.314), kind=kOutput, calls=%fused_computation.58 | convolution fusion | flops 2168455168 | bytes 15736832 | tf_op jit(solution)/shard_map/jvp()/dot_general | solution.py:78
  203.4 2.7 fusion.134
  207.8 26.6 %gather_pooled.1 = bf16[32,64,128]{2,1,0:T(8,128)(2,1)S(1)} custom-call(bf16[64,128]{1,0:T(8,128)(2,1)S(1)} %reshape.612.refs_0_), custom_call_target="tpu_custom_call" | custom-call | bytes 10485760 | tf_op jit(solution)/shard_map/gather_pooled/pallas_call | solution.py:175
  235.9 2.5 copy.273
  240.0 6.4 %contrastive.1 = (f32[8,128]{1,0:T(8,128)S(1)}, f32[2,2,128,512]{3,2,1,0:T(8,128)S(1)}) custom-call(f32[2,2,128,512]{3,2,1,0:T(8,128)S(1)} %reshape.638.pooled_ref, s32[128,128]{1,0:T(8,128)S(1)} %bitcast.280, s32[128,1]{1,0:T(8,128)S(1)} %reshape_reshape_squeeze.4.pair_ref), custom_call_target="tpu_custom_call" | custom-call | flops 1000000000 | bytes 3000000 | tf_op jit(solution)/shard_map/contrastive/pallas_call | solution.py:818
  246.5 2.3 fusion.51
  251.6 4.4 convolution_bitcast_fusion.5
  256.0 4.1 convolution_convert_fusion.1
  260.1 6.5 %fusion.19 = bf16[8,128,2048]{2,1,0:T(8,128)(2,1)S(1)} fusion(bf16[8,128,2048]{2,1,0:T(8,128)(2,1)S(1)} %convolution_convert_fusion.1, f32[8,128,2048]{2,1,0:T(8,128)S(1)} %bitcast.305, f32[2048]{0:T(1024)S(1)} %get-tuple-element.224), kind=kLoop, calls=%fused_computation.36 | loop fusion | flops 46137344 | bytes 16785408 | tf_op jit(solution)/shard_map/transpose(jvp())/convert_element_type | solution.py:70
  266.7 7.0 %multiply_reduce_fusion.8 = (f32[512]{0:T(512)}, f32[8,128]{1,0:T(8,128)S(1)}, f32[512]{0:T(512)}, f32[8,128,512]{2,1,0:T(8,128)S(1)}) fusion(f32[8,128,512]{2,1,0:T(8,128)S(1)} %copy-done.23, f32[8,128]{1,0:T(8,128)S(1)} %fusion.98, f32[8,128]{1,0:T(8,128)S(1)} %broadcast_multiply_fusion.1, f32[512]{0:T(512)S(1)} %get-tuple-element.210, ...), kind=kOutput, calls=%fused_computation.130 | convolution fusion | flops 2156394496 | bytes 12640256 | tf_op jit(solution)/shard_map/transpose(jvp())/dot_general | solution.py:78
  273.7 4.4 convolution_bitcast_fusion.4
  282.7 2.8 convolution_convert_fusion.5
  287.1 4.6 fusion.135
  296.0 2.9 fusion.42
  298.9 2.9 copy.227
  301.8 2.9 copy.229
  304.7 2.9 copy.231
  307.7 3.4 add_convert_fusion.3
  311.1 5.7 %add_add_fusion.11 = f32[8,128,512]{2,1,0:T(8,128)} fusion(f32[8,128,512]{2,1,0:T(8,128)S(1)} %copy-done.46, bf16[8,128,1536]{2,1,0:T(8,128)(2,1)S(1)} %add_convert_fusion.3, bf16[512,6144]{1,0:T(8,128)(2,1)} %bitcast.311, f32[8,128]{1,0:T(8,128)S(1)} %negate_multiply_fusion.3), kind=kOutput, calls=%fused_computation.169 | convolution fusion | flops 1611661312 | bytes 8916992 | tf_op jit(solution)/shard_map/transpose(jvp())/dot_general | solution.py:78
  316.9 3.5 convolution_bitcast_fusion.1
  320.4 2.9 add_convert_fusion.1
  323.3 2.2 add_convert_fusion.7
  325.5 3.1 pad_maximum_fusion
  330.3 2.4 convert_reduce_fusion.3
  333.4 3.0 multiply_reduce_fusion.7
  337.8 4.7 convolution_convert_fusion
  342.5 6.8 %fusion.24 = bf16[8,128,2048]{2,1,0:T(8,128)(2,1)S(1)} fusion(bf16[8,128,2048]{2,1,0:T(8,128)(2,1)S(1)} %convolution_convert_fusion, f32[8,128,2048]{2,1,0:T(8,128)S(1)} %bitcast.303, f32[2048]{0:T(1024)S(1)} %get-tuple-element.225), kind=kLoop, calls=%fused_computation.41 | loop fusion | flops 46137344 | bytes 16785408 | tf_op jit(solution)/shard_map/transpose(jvp())/convert_element_type | solution.py:70
  349.3 6.9 %multiply_reduce_fusion.6 = (f32[512]{0:T(512)}, f32[8,128]{1,0:T(8,128)S(1)}, f32[512]{0:T(512)}, f32[8,128,512]{2,1,0:T(8,128)S(1)}) fusion(f32[8,128,512]{2,1,0:T(8,128)S(1)} %copy-done.28, f32[8,128]{1,0:T(8,128)S(1)} %fusion.96, f32[8,128]{1,0:T(8,128)S(1)} %broadcast_multiply_fusion.3, f32[512]{0:T(512)S(1)} %get-tuple-element.218, ...), kind=kOutput, calls=%fused_computation.126 | convolution fusion | flops 2152724480 | bytes 12605440 | tf_op jit(solution)/shard_map/transpose(jvp())/dot_general | solution.py:78
  358.4 3.2 convolution_convert_fusion.4
  363.3 3.3 multiply_reduce_fusion
  368.3 2.9 fusion.136
  371.1 3.0 copy.238
  374.1 2.9 fusion.40
  377.0 3.0 copy.240
  380.0 2.0 fusion.39
  382.0 3.1 copy.242
  385.1 2.4 add_convert_fusion.2
  392.5 5.5 multiply_reduce_fusion.5
  406.5 2.1 convolution_bitcast_fusion.6
  412.0 2.7 fusion.46
  414.7 2.4 convolution_bitcast_fusion.3
  417.2 2.4 convolution_bitcast_fusion.2
  419.7 2.8 add_convert_fusion
  424.7 81.2 %exchange_gradients.1 = (f32[32,2048]{1,0:T(8,128)S(1)}, f32[32,4096]{1,0:T(8,128)S(1)}, f32[40,128]{1,0:T(8,128)S(1)}, bf16[2,16,72,512]{3,2,1,0:T(8,128)(2,1)}, f32[32,6144]{1,0:T(8,128)S(1)}) custom-call(bf16[4,2,2,32,2048]{4,3,2,1,0:T(8,128)(2,1)S(1)} %bitcast.266, bf16[4,2,2,32,4096]{4,3,2,1,0:T(8,128)(2,1)} %bitcast.285, ...), custom_call_target="tpu_custom_call" | custom-call | bytes 200000000 | tf_op jit(solution)/shard_map/exchange_gradients/pallas_call | solution.py:396
  506.7 9.0 %fusion.15 = f32[1908,512]{1,0:T(8,128)} fusion(bf16[2304,512]{1,0:T(8,128)(2,1)} %bitcast.349, s32[2304]{0:T(1024)S(1)} %copy-done.98), kind=kOutput, calls=%fused_computation.24 | convolution fusion | flops 4505932800 | bytes 6276096 | tf_op jit(solution)/shard_map/dot_general | solution.py:1154
  516.7 3.8 multiply_reduce_fusion.3
  524.7 9.2 %gather_squares.1 = f32[16,8,128]{2,1,0:T(8,128)S(1)} custom-call(f32[8,128]{1,0:T(8,128)S(1)} %broadcast_in_dim.161.refs_0_), custom_call_target="tpu_custom_call" | custom-call | bytes 1310720 | tf_op jit(solution)/shard_map/gather_squares/pallas_call | solution.py:175
  536.5 2.7 fusion.112
  539.3 2.5 fusion.110
  543.9 8.3 %fusion.116 = (bf16[1908,512]{1,0:T(8,128)(2,1)}, f32[1908,512]{1,0:T(8,128)}, f32[1908,512]{1,0:T(8,128)}, f32[1908,512]{1,0:T(8,128)}) fusion(f32[1908,512]{1,0:T(8,128)S(1)} %copy-done.21, f32[1908,512]{1,0:T(8,128)S(1)} %copy-done.32, f32[]{:T(128)S(6)} %min.3, f32[1908,512]{1,0:T(8,128)} %param.28, f32[1908,512]{1,0:T(8,128)} %param.32), kind=kLoop, calls=%fused_computation.302 | loop fusion | flops 15630336 | bytes 29306884 | tf_op jit(solution)/shard_map/convert_element_type | solution.py:1240
  (395 shorter events, 81.5 us)
Async XLA Ops:
  7.2 415.3 %reduce-scatter.2.cloned.1.call-start = ((), (), s32[]{:S(2)}) async-start(), calls=%async_computation.5 | async-start | bytes 6684672 | tf_op jit(solution)/shard_map/reduce_scatter | solution.py:1137
  11.3 3.8 copy-start.110
  11.3 3.9 copy-start
  11.4 3.9 copy-start.2
  11.4 3.9 copy-start.8
  116.2 33.6 %copy-start.96 = (f32[512]{0:T(512)}, f32[512]{0:T(512)S(1)}, u32[]{:S(2)}) copy-start(f32[512]{0:T(512)S(1)} %get-tuple-element.223) | copy-start | bytes 6148
  116.9 32.9 %copy-start.48 = (f32[128,512]{1,0:T(8,128)}, f32[128,512]{1,0:T(8,128)S(1)}, u32[]{:S(2)}) copy-start(f32[128,512]{1,0:T(8,128)S(1)} %slice_convert_fusion) | copy-start | bytes 786436
  120.1 29.7 %copy-start.30 = (bf16[1024,512]{1,0:T(8,128)(2,1)}, bf16[1024,512]{1,0:T(8,128)(2,1)S(1)}, u32[]{:S(2)}) copy-start(bf16[1024,512]{1,0:T(8,128)(2,1)S(1)} %get-tuple-element.112) | copy-start | bytes 3145732
  120.4 29.4 %copy-start.90 = (f32[8,128]{1,0:T(8,128)}, f32[8,128]{1,0:T(8,128)S(1)}, u32[]{:S(2)}) copy-start(f32[8,128]{1,0:T(8,128)S(1)} %get-tuple-element.230) | copy-start | bytes 12292
  121.0 9.4 %copy-start.88 = (f32[1024]{0:T(1024)}, f32[1024]{0:T(1024)S(1)}, u32[]{:S(2)}) copy-start(f32[1024]{0:T(1024)S(1)} %multiply_reduce_fusion.18) | copy-start | bytes 12292
  121.0 28.8 %copy-start.92 = (f32[8,128]{1,0:T(8,128)}, f32[8,128]{1,0:T(8,128)S(1)}, u32[]{:S(2)}) copy-start(f32[8,128]{1,0:T(8,128)S(1)} %bitcast_rsqrt_fusion) | copy-start | bytes 12292
  121.5 8.9 %copy-start.50 = (bf16[8,128,512]{2,1,0:T(8,128)(2,1)}, bf16[8,128,512]{2,1,0:T(8,128)(2,1)S(1)}, u32[]{:S(2)}) copy-start(bf16[8,128,512]{2,1,0:T(8,128)(2,1)S(1)} %fusion.64) | copy-start | bytes 3145732
  139.9 8.6 %copy-start.38 = (bf16[8,128,512]{1,2,0:T(8,128)(2,1)}, bf16[8,128,512]{1,2,0:T(8,128)(2,1)S(1)}, u32[]{:S(2)}) copy-start(bf16[8,128,512]{1,2,0:T(8,128)(2,1)S(1)} %copy.208) | copy-start | bytes 3145732
  148.5 5.5 slice-start.6
  149.8 3.4 copy-start.75
  149.8 4.2 slice-start.7
  153.1 15.3 %copy-start.27 = (f32[8,128,512]{2,1,0:T(8,128)}, f32[8,128,512]{2,1,0:T(8,128)S(1)}, u32[]{:S(2)}) copy-start(f32[8,128,512]{2,1,0:T(8,128)S(1)} %get-tuple-element.239) | copy-start | bytes 6291460
  154.0 14.5 %copy-start.55 = (bf16[8,128,512]{2,1,0:T(8,128)(2,1)}, bf16[8,128,512]{2,1,0:T(8,128)(2,1)S(1)}, u32[]{:S(2)}) copy-start(bf16[8,128,512]{2,1,0:T(8,128)(2,1)S(1)} %fusion.65) | copy-start | bytes 3145732
  183.1 8.5 %copy-start.40 = (bf16[8,128,512]{1,2,0:T(8,128)(2,1)}, bf16[8,128,512]{1,2,0:T(8,128)(2,1)S(1)}, u32[]{:S(2)}) copy-start(bf16[8,128,512]{1,2,0:T(8,128)(2,1)S(1)} %copy.214) | copy-start | bytes 3145732
  191.6 5.4 slice-start.4
  192.9 4.0 slice-start.5
  196.1 7.3 %copy-start.22 = (f32[8,128,512]{2,1,0:T(8,128)}, f32[8,128,512]{2,1,0:T(8,128)S(1)}, u32[]{:S(2)}) copy-start(f32[8,128,512]{2,1,0:T(8,128)S(1)} %get-tuple-element.247) | copy-start | bytes 6291460
  196.9 6.4 %copy-start.61 = (bf16[8,128,512]{2,1,0:T(8,128)(2,1)}, bf16[8,128,512]{2,1,0:T(8,128)(2,1)S(1)}, u32[]{:S(2)}) copy-start(bf16[8,128,512]{2,1,0:T(8,128)(2,1)S(1)} %fusion.66) | copy-start | bytes 3145732
  251.6 4.4 copy-start.33
  251.6 8.5 %slice-start.2 = ((s8[8388608]{0:T(1024)(128)(4,1)}), s8[4194304]{0:T(1024)(128)(4,1)S(1)}, s32[]{:S(2)}) async-start(s8[8388608]{0:T(1024)(128)(4,1)} %bitcast.304), calls=%async_computation.9 | async-start | bytes 8388608
  256.0 4.1 slice-start.3
  260.1 6.5 %copy-start.23 = (f32[8,128,512]{2,1,0:T(8,128)S(1)}, f32[8,128,512]{2,1,0:T(8,128)}, u32[]{:S(2)}) copy-start(f32[8,128,512]{2,1,0:T(8,128)} %copy-done.22) | copy-start | bytes 6291460
  266.7 7.1 %copy-start.16 = (bf16[8,128,2048]{2,1,0:T(8,128)(2,1)}, bf16[8,128,2048]{2,1,0:T(8,128)(2,1)S(1)}, u32[]{:S(2)}) copy-start(bf16[8,128,2048]{2,1,0:T(8,128)(2,1)S(1)} %fusion.19) | copy-start | bytes 12582916
  266.7 7.1 %copy-start.62 = (bf16[8,128,512]{2,1,0:T(8,128)(2,1)S(1)}, bf16[8,128,512]{2,1,0:T(8,128)(2,1)}, u32[]{:S(2)}) copy-start(bf16[8,128,512]{2,1,0:T(8,128)(2,1)} %copy-done.61) | copy-start | bytes 3145732
  279.0 3.7 copy-start.45
  287.1 4.7 copy-start.15
  287.1 4.7 copy-start.41
  307.7 3.5 copy-start.46
  311.1 5.7 %copy-start.13 = (bf16[8,128,1536]{2,1,0:T(8,128)(2,1)}, bf16[8,128,1536]{2,1,0:T(8,128)(2,1)S(1)}, u32[]{:S(2)}) copy-start(bf16[8,128,1536]{2,1,0:T(8,128)(2,1)S(1)} %add_convert_fusion.3) | copy-start | bytes 9437188
  311.1 5.7 %copy-start.53 = (bf16[8,128,512]{2,1,0:T(8,128)(2,1)S(1)}, bf16[8,128,512]{2,1,0:T(8,128)(2,1)}, u32[]{:S(2)}) copy-start(bf16[8,128,512]{2,1,0:T(8,128)(2,1)} %copy-done.52) | copy-start | bytes 3145732
  316.9 3.5 copy-start.29
  332.7 3.7 copy-start.86
  336.4 6.1 %slice-start = ((s8[8388608]{0:T(1024)(128)(4,1)}), s8[4194304]{0:T(1024)(128)(4,1)S(1)}, s32[]{:S(2)}) async-start(s8[8388608]{0:T(1024)(128)(4,1)} %bitcast.302), calls=%async_computation.7 | async-start | bytes 8388608
  337.8 4.7 copy-start.35
  337.8 4.7 slice-start.1
  342.5 6.8 %copy-start.28 = (f32[8,128,512]{2,1,0:T(8,128)S(1)}, f32[8,128,512]{2,1,0:T(8,128)}, u32[]{:S(2)}) copy-start(f32[8,128,512]{2,1,0:T(8,128)} %copy-done.27) | copy-start | bytes 6291460
  349.3 6.9 %copy-start.18 = (bf16[8,128,2048]{2,1,0:T(8,128)(2,1)}, bf16[8,128,2048]{2,1,0:T(8,128)(2,1)S(1)}, u32[]{:S(2)}) copy-start(bf16[8,128,2048]{2,1,0:T(8,128)(2,1)S(1)} %fusion.24) | copy-start | bytes 12582916
  358.4 4.8 copy-start.69
  358.4 4.8 copy-start.39
  363.2 3.5 copy-start.14
  385.1 7.4 %copy-start.49 = (f32[128,512]{1,0:T(8,128)S(1)}, f32[128,512]{1,0:T(8,128)}, u32[]{:S(2)}) copy-start(f32[128,512]{1,0:T(8,128)} %copy-done.48) | copy-start | bytes 786436
  389.2 3.3 copy-start.93
  389.2 3.3 copy-start.97
  389.7 8.3 %copy-start.87 = (f32[1536]{0:T(1024)}, f32[1536]{0:T(1024)S(1)}, u32[]{:S(2)}) copy-start(f32[1536]{0:T(1024)S(1)} %convert_reduce_fusion.2) | copy-start | bytes 18436
  392.5 5.5 copy-start.89
  424.7 82.0 %copy-start.98 = (s32[2304]{0:T(1024)S(1)}, s32[2304]{0:T(1024)}, u32[]{:S(2)}) copy-start(s32[2304]{0:T(1024)} %eq.69) | copy-start | bytes 27652
  506.7 9.0 %copy-start.77 = (bf16[8,128,512]{2,1,0:T(8,128)(2,1)S(1)}, bf16[8,128,512]{2,1,0:T(8,128)(2,1)}, u32[]{:S(2)}) copy-start(bf16[8,128,512]{2,1,0:T(8,128)(2,1)} %get-tuple-element.202) | copy-start | bytes 3145732
  506.7 9.0 %copy-start.80 = (s32[1024]{0:T(1024)S(1)}, s32[1024]{0:T(1024)}, u32[]{:S(2)}) copy-start(s32[1024]{0:T(1024)} %copy-done.79) | copy-start | bytes 12292
  506.7 9.0 %copy-start.82 = (s32[1024]{0:T(1024)S(1)}, s32[1024]{0:T(1024)}, u32[]{:S(2)}) copy-start(s32[1024]{0:T(1024)} %copy-done.81) | copy-start | bytes 12292
  506.7 9.0 %copy-start.84 = (s32[1024]{0:T(1024)S(1)}, s32[1024]{0:T(1024)}, u32[]{:S(2)}) copy-start(s32[1024]{0:T(1024)} %copy-done.83) | copy-start | bytes 12292
  516.6 19.2 %copy-start.85 = (f32[4928]{0:T(1024)S(1)}, f32[4928]{0:T(1024)}, u32[]{:S(2)}) copy-start(f32[4928]{0:T(1024)} %param.25) | copy-start | bytes 59140
  516.6 19.2 %copy-start.94 = (f32[4928]{0:T(1024)S(1)}, f32[4928]{0:T(1024)}, u32[]{:S(2)}) copy-start(f32[4928]{0:T(1024)} %param.29) | copy-start | bytes 59140
  516.6 19.2 %copy-start.95 = (f32[4928]{0:T(1024)S(1)}, f32[4928]{0:T(1024)}, u32[]{:S(2)}) copy-start(f32[4928]{0:T(1024)} %param.33) | copy-start | bytes 59140
  516.7 19.8 %copy-start.3 = (f32[2,32,2048]{2,1,0:T(8,128)S(1)}, f32[2,32,2048]{2,1,0:T(8,128)}, u32[]{:S(2)}) copy-start(f32[2,32,2048]{2,1,0:T(8,128)} %refs_4_.1) | copy-start | bytes 1572868
  522.0 17.2 %copy-start.1 = (f32[2,32,4096]{2,1,0:T(8,128)S(1)}, f32[2,32,4096]{2,1,0:T(8,128)}, u32[]{:S(2)}) copy-start(f32[2,32,4096]{2,1,0:T(8,128)} %refs_5_.1) | copy-start | bytes 3145732
  535.3 4.0 copy-start.73
  535.3 4.0 copy-start.74
  539.2 3.4 copy-start.21
  539.2 4.6 copy-start.32
  (60 other events, 108.9 us)
Sparse Core Ops, SparseCore 0:
  328.7 87.0 reduce-scatter.1

commit v5 on v4

--- a/solution.py
+++ b/solution.py
@@ -369,7 +369,7 @@
 def exchange_gradients(parts, sums, near, collective_id):
     chunks = []
     for index, part in enumerate(parts):
-        width = min(part.shape[4], 1024)
+        width = part.shape[4] // -(-part.shape[4] // 1024)
         for start in range(0, part.shape[4], width):
             chunks.append((index, start, width))
     half = jnp.bfloat16
@@ -409,13 +409,14 @@
 
 SPLITS = 4
 WINDOW = 3
-
-
-def start_kernel(shard_rows, room, pair_rows, *refs):
+LAG = 3
+
+
+def start_kernel(shard_rows, room, *refs):
     column_ref, row_ref, packet_ref, vec_ref, attn_ref, ffn_ref, word_ref = refs[:7]
-    place_out, packet_out, vec_out, weight_out, rows_out = refs[7:12]
-    table, rows_held, packet, slots, locals_ = refs[12:17]
-    packet_sem, vec_sem, row_sem, z_sem, y_sem, x_sem, d_sem, e_sem, own_sem = refs[17:]
+    place_out, packet_out, asked_out, weight_out, rows_out = refs[7:12]
+    table, rows_held, asked, slots, locals_ = refs[12:17]
+    packet_sem, asked_sem, row_sem, z_sem, y_sem, x_sem, d_sem, e_sem, own_sem = refs[17:]
 
     d = lax.axis_index("dp")
     z = lax.axis_index("zero")
@@ -427,11 +428,9 @@
     across = z + 2 - 4 * col
     layers = attn_ref.shape[0]
     width = attn_ref.shape[2]
-    whole = 3 * width
-    plane = 7 * whole // 12
-    part = plane // SPLITS
-    alone = whole - plane
-    x_parts = -(-alone // part)
+    whole = weight_out.shape[3]
+    unit = whole // 128 // SPLITS
+    hand = unit * 5 // 12
     total = layers * SPLITS
 
     def everyone(k):
@@ -447,7 +446,8 @@
     lax.fori_loop(1, 32, greet, 0)
     for layer in range(layers):
         weight_out[layer, z, :, 0:width] = attn_ref[layer].astype(jnp.bfloat16)
-        weight_out[layer, z, :, width:whole] = ffn_ref[layer].astype(jnp.bfloat16)
+        weight_out[layer, z, :, width : 3 * width] = ffn_ref[layer].astype(jnp.bfloat16)
+        weight_out[layer, z, :, 3 * width : whole] = vec_ref[layer]
     pl.semaphore_wait(barrier, 31)
 
     def remote(src, dst, sems, at, to):
@@ -461,10 +461,11 @@
         )
 
     def packet_copy(k, slot):
-        return remote(packet, packet_out.at[slot], packet_sem, (k,), everyone(k))
-
-    def vec_copy(k, slot):
-        return remote(vec_ref, vec_out.at[slot], vec_sem, (k,), (d, lax.rem(z + k, 16)))
+        return remote(packet_ref, packet_out.at[slot], packet_sem, (k,), everyone(k))
+
+    def asked_copy(k, slot):
+        to = everyone(k)
+        return remote(asked.at[to[1]], asked_out.at[slot], asked_sem, (k,), to)
 
     def row_copy(k, slot):
         to = lax.rem(z + k, 16)
@@ -474,16 +475,24 @@
         at = lax.rem(line + i % 4, 4) * 4 + lax.rem(z, 4)
         return at if i < 4 else at + 2 - 4 * col
 
+    def piece(s):
+        layer, p = s // SPLITS, s % SPLITS
+        size = unit if p < SPLITS - 1 else whole // 128 - p * unit
+        return layer, p * unit, size
+
+    def columns_of(at, s, first, size):
+        layer, base, _ = piece(s)
+        return weight_out.at[
+            layer, at, :, pl.ds(pl.multiple_of((base + first) * 128, 128), size * 128)
+        ]
+
     def stretch(at, s, ours):
-        layer, p = s // SPLITS, s % SPLITS
-        first = ours * (whole - part * (p + 1)) + (1 - ours) * part * p
-        return weight_out.at[layer, at, :, pl.ds(pl.multiple_of(first, 128), part)]
+        size = piece(s)[2]
+        return columns_of(at, s, ours * hand, size - hand)
 
     def handed(at, s, ours):
-        layer, p = s // SPLITS, s % SPLITS
-        size = min(part, alone - part * p)
-        first = ours * (whole - part * p - size) + (1 - ours) * part * p
-        return weight_out.at[layer, at, :, pl.ds(pl.multiple_of(first, 128), size)]
+        size = piece(s)[2]
+        return columns_of(at, s, ours * (size - hand), hand)
 
     def both(ref, sems, at, to):
         return remote(ref, ref, sems, at, to)
@@ -507,17 +516,13 @@
     def own_copy(layer, at):
         ref = weight_out.at[layer, at]
         return both(ref, own_sem, (layer,), (d, sibling))
-
-    def hands(s):
-        return s % SPLITS < x_parts
 
     def spread(s, i):
         at = shard(i)
         if i < 4:
             y_copy(s, i, at).start()
         if i > 0:
-            if hands(s):
-                x_copy(s, i, at, d).start()
+            x_copy(s, i, at, d).start()
             d_copy(s, i, at).start()
 
     def open_piece(s):
@@ -558,7 +563,9 @@
         return jnp.maximum(most, jnp.max(place, axis=0, keepdims=True))
 
     most = lax.fori_loop(0, tokens // block, place_of, jnp.zeros((1, 1), jnp.float32))
-    packet[...] = packet_ref[...]
+    rounds = jnp.ones((1, 1), jnp.float32)
+    for r in range(1, -(-tokens // room)):
+        rounds = rounds + (most >= r * room).astype(jnp.float32)
     lane128 = lax.broadcasted_iota(jnp.int32, (1, 128), 1)
 
     for o in range(16):
@@ -569,30 +576,18 @@
             return jnp.maximum(best, jnp.max(found, axis=0, keepdims=True))
 
         best = lax.fori_loop(0, tokens // block, asked_of, jnp.full((1, 128), -1.0, jnp.float32))
-        packet[o : o + 1, :] = best.astype(jnp.int32)
-    rounds = jnp.ones((1, 1), jnp.float32)
-    for r in range(1, -(-tokens // room)):
-        rounds = rounds + (most >= r * room).astype(jnp.float32)
-    last = packet.shape[0] - 1
-    packet[last : last + 1, :] = jnp.where(
-        lane128 == pair_rows, rounds.astype(jnp.int32), packet_ref[last : last + 1, :]
-    )
+        asked[o] = jnp.where(lane128 == 127, rounds, best).astype(jnp.int32)
 
     def send_packets(k, carry):
+        asked_copy(k, me).start()
         packet_copy(k, me).start()
         return carry
 
     lax.fori_loop(1, 32, send_packets, 0)
-
-    def send_vec(k, carry):
-        vec_copy(k, z).start()
-        return carry
-
-    lax.fori_loop(1, 16, send_vec, 0)
     for layer in range(layers):
         own_copy(layer, z).start()
-    packet_out[me] = packet[...]
-    vec_out[z] = vec_ref[...]
+    asked_out[me] = asked[z]
+    packet_out[me] = packet_ref[...]
 
     body_rows = shard_rows // 16 * 16
     step = 112 if body_rows % 112 == 0 else 16
@@ -610,9 +605,8 @@
 
     def answer_one(k, carry):
         src = lax.rem(z + k, 16)
-        asked = packet_out[d * 16 + src, pl.ds(z, 1), :]
         rows_at = lax.broadcasted_iota(jnp.int32, (padded, 128), 0)
-        picked = (rows_at == asked).astype(jnp.bfloat16)
+        picked = (rows_at == asked_out[d * 16 + src]).astype(jnp.bfloat16)
         found = lax.dot_general(
             picked, table[...], (((0,), (0,)), ((), ())), preferred_element_type=jnp.float32
         )
@@ -620,7 +614,7 @@
         return carry
 
     def packet_in(k, carry):
-        packet_copy(k, lax.rem(me + 32 - k, 32)).wait_recv()
+        asked_copy(k, lax.rem(me + 32 - k, 32)).wait_recv()
         return carry
 
     def row_start(k, carry):
@@ -640,14 +634,13 @@
             spread(s, 4 + j)
 
     def x_phase(s):
-        if hands(s):
-            for i in range(1, 8):
-                at = shard(i)
-                x_copy(s, i, at, 1 - d).wait_recv()
-                e_copy(s, i, at).start()
+        for i in range(1, 8):
+            at = shard(i)
+            x_copy(s, i, at, 1 - d).wait_recv()
+            e_copy(s, i, at).start()
 
     done = 0
-    for t in range(total + 2):
+    for t in range(total + LAG):
         if t < total:
             z_phase(t)
         if t == 1:
@@ -662,8 +655,8 @@
             rows_out[z] = rows_held[z]
         if 0 <= t - 1 < total:
             y_phase(t - 1)
-        if 0 <= t - 2 < total:
-            x_phase(t - 2)
+        if 0 <= t - LAG < total:
+            x_phase(t - LAG)
 
     turn = 1 - 2 * core
     for layer in range(layers):
@@ -674,10 +667,9 @@
             at = shard(i)
             d_copy(s, i, at + turn).wait_recv()
             d_copy(s, i, at).wait_send()
-            if hands(s):
-                e_copy(s, i, at + turn).wait_recv()
-                e_copy(s, i, at).wait_send()
-                x_copy(s, i, at, d).wait_send()
+            e_copy(s, i, at + turn).wait_recv()
+            e_copy(s, i, at).wait_send()
+            x_copy(s, i, at, d).wait_send()
         for k in range(1, 4):
             z_copy(s, k, z).wait_send()
         for i in range(4):
@@ -687,20 +679,20 @@
         back = lax.rem(z + 16 - k, 16)
         row_copy(k, back).wait_recv()
         row_copy(k, z).wait_send()
-        vec_copy(k, back).wait_recv()
-        vec_copy(k, z).wait_send()
         return carry
 
     lax.fori_loop(1, 16, finish, 0)
 
     def finish_packets(k, carry):
+        packet_copy(k, lax.rem(me + 32 - k, 32)).wait_recv()
         packet_copy(k, me).wait_send()
+        asked_copy(k, me).wait_send()
         return carry
 
     lax.fori_loop(1, 32, finish_packets, 0)
 
 
-def exchange_start(ids, packet, vec_rows, attn, ffn, word_table, room, pair_rows, collective_id):
+def exchange_start(ids, packet, vec_rows, attn, ffn, word_table, room, collective_id):
     half = jnp.bfloat16
     shard_rows, features = word_table.shape
     padded = -(-shard_rows // 128) * 128
@@ -710,12 +702,12 @@
     dma = pltpu.SemaphoreType.DMA
     vmem = pl.BlockSpec(memory_space=pltpu.VMEM)
     return pl.pallas_call(
-        functools.partial(start_kernel, shard_rows, room, pair_rows),
+        functools.partial(start_kernel, shard_rows, room),
         out_shape=(
             jax.ShapeDtypeStruct((tokens, 1), jnp.int32),
             jax.ShapeDtypeStruct((32,) + packet.shape, packet.dtype),
-            jax.ShapeDtypeStruct((16,) + vec_rows.shape, vec_rows.dtype),
-            jax.ShapeDtypeStruct((layers, 16, rows, 3 * width), half),
+            jax.ShapeDtypeStruct((32, 1, 128), jnp.int32),
+            jax.ShapeDtypeStruct((layers, 16, rows, 3 * width + vec_rows.shape[2]), half),
             jax.ShapeDtypeStruct((16, room, features), half),
         ),
         in_specs=[vmem] * 7,
@@ -723,11 +715,11 @@
         scratch_shapes=[
             pltpu.VMEM((padded, features), half),
             pltpu.VMEM((16, room, features), half),
-            pltpu.VMEM(packet.shape, packet.dtype),
+            pltpu.VMEM((16, 1, 128), jnp.int32),
             pltpu.VMEM((tokens, 1), jnp.int32),
             pltpu.VMEM((tokens, 1), jnp.float32),
             dma((2, 32)),
-            dma((2, 16)),
+            dma((2, 32)),
             dma((2, 16)),
             dma((2, pieces, 3)),
             dma((2, pieces, 4)),
@@ -830,6 +822,121 @@
     return loss[0, 0], grads
 
 
+def head_lanes():
+    lane = lax.broadcasted_iota(jnp.int32, (1, 2 * HD), 1)
+    return lane < HD, lane >= HD
+
+
+def probabilities(queries, keys, valid):
+    scores = lax.dot_general(
+        queries, keys, (((1,), (1,)), ((), ())), preferred_element_type=jnp.float32
+    )
+    scores = jnp.where(valid, scores * HD ** (-0.5), MASKED)
+    raised = jnp.exp(scores - jnp.max(scores, axis=1, keepdims=True))
+    return raised / jnp.sum(raised, axis=1, keepdims=True)
+
+
+def attention_kernel(mask_ref, packed_ref, context_ref):
+    valid = mask_ref[0] > 0.0
+    sides = head_lanes()
+    for pair in range(HEADS // 2):
+        at = pair * 2 * HD
+        queries = packed_ref[0, :, at : at + 2 * HD]
+        keys = packed_ref[0, :, D + at : D + at + 2 * HD]
+        values = packed_ref[0, :, 2 * D + at : 2 * D + at + 2 * HD]
+        mixed = []
+        for side in sides:
+            probs = probabilities(jnp.where(side, queries, 0), keys, valid).astype(jnp.bfloat16)
+            mixed.append(jnp.dot(probs, values, preferred_element_type=jnp.float32))
+        context_ref[0, :, at : at + 2 * HD] = jnp.where(sides[0], mixed[0], mixed[1]).astype(
+            jnp.bfloat16
+        )
+
+
+def attention_back_kernel(mask_ref, packed_ref, grad_ref, out_ref):
+    valid = mask_ref[0] > 0.0
+    sides = head_lanes()
+    for pair in range(HEADS // 2):
+        at = pair * 2 * HD
+        queries = packed_ref[0, :, at : at + 2 * HD]
+        keys = packed_ref[0, :, D + at : D + at + 2 * HD]
+        values = packed_ref[0, :, 2 * D + at : 2 * D + at + 2 * HD]
+        grad = grad_ref[0, :, at : at + 2 * HD]
+        d_queries, d_keys, d_values = [], [], []
+        for side in sides:
+            probs = probabilities(jnp.where(side, queries, 0), keys, valid)
+            d_probs = lax.dot_general(
+                jnp.where(side, grad, 0),
+                values,
+                (((1,), (1,)), ((), ())),
+                preferred_element_type=jnp.float32,
+            )
+            d_values.append(
+                lax.dot_general(
+                    probs.astype(jnp.bfloat16),
+                    grad,
+                    (((0,), (0,)), ((), ())),
+                    preferred_element_type=jnp.float32,
+                )
+            )
+            shared = jnp.sum(d_probs * probs, axis=1, keepdims=True)
+            d_scores = jnp.where(valid, probs * (d_probs - shared), 0.0).astype(jnp.bfloat16)
+            d_queries.append(jnp.dot(d_scores, keys, preferred_element_type=jnp.float32))
+            d_keys.append(
+                lax.dot_general(
+                    d_scores, queries, (((0,), (0,)), ((), ())), preferred_element_type=jnp.float32
+                )
+            )
+        for third, parts in enumerate((d_queries, d_keys, d_values)):
+            both = jnp.where(sides[0], parts[0], parts[1])
+            if third < 2:
+                both = both * HD ** (-0.5)
+            out_ref[0, :, third * D + at : third * D + at + 2 * HD] = both.astype(jnp.bfloat16)
+
+
+def attention_call(kernel, mask, operands, features, name):
+    count = operands[0].shape[0]
+
+    def spec(last):
+        return pl.BlockSpec((1, SEQ, last), lambda i: (i, 0, 0))
+
+    return pl.pallas_call(
+        kernel,
+        grid=(count,),
+        out_shape=jax.ShapeDtypeStruct((count, SEQ, features), jnp.bfloat16),
+        in_specs=[pl.BlockSpec((1, 1, SEQ), lambda i: (i, 0, 0))]
+        + [spec(operand.shape[2]) for operand in operands],
+        out_specs=spec(features),
+        compiler_params=pltpu.CompilerParams(vmem_limit_bytes=32 * 1024 * 1024),
+        cost_estimate=pl.CostEstimate(
+            flops=10**9, bytes_accessed=count * SEQ * D * 10, transcendentals=10**6
+        ),
+        name=name,
+    )(mask, *operands)
+
+
+@jax.custom_vjp
+def attend(packed, mask):
+    return attend_forward(packed, mask)[0]
+
+
+def attend_forward(packed, mask):
+    half = packed.astype(jnp.bfloat16)
+    context = attention_call(attention_kernel, mask, [half], D, "attention")
+    return context.astype(jnp.float32), (half, mask)
+
+
+def attend_backward(kept, grad):
+    half, mask = kept
+    d_packed = attention_call(
+        attention_back_kernel, mask, [half, grad.astype(jnp.bfloat16)], 3 * D, "attention_back"
+    )
+    return d_packed.astype(jnp.float32), jnp.zeros_like(mask)
+
+
+attend.defvjp(attend_forward, attend_backward)
+
+
 def split_vectors(vec_all):
     offset = SEQ * D
     position = vec_all[:offset].reshape(SEQ, D)
@@ -852,33 +959,23 @@
     return center * lax.rsqrt(spread + NORM_EPS) * gain + shift
 
 
-def embed_tokens(rows, vec_all):
-    position, emb_gain, emb_shift, layer_parts = split_vectors(vec_all)
+def embed_tokens(rows, position, emb_gain, emb_shift):
     return layer_norm(low_back(rows) + position[None], emb_gain, emb_shift)
 
 
-def encoder_layer(hidden, attn_weights, ffn_weights, vec_all, key_mask, layer_index):
+def encoder_layer(hidden, weights, vectors, mask):
+    in_weights, out_weights, up_weights, down_weights = weights
     q_bias, v_bias, o_bias, gain_one, shift_one, up_bias, down_bias, gain_two, second_shift = (
-        split_vectors(vec_all)[3][layer_index]
+        vectors
     )
-    sequence_count = hidden.shape[0]
-    packed = matmul(low(hidden), attn_weights[:, : 3 * D])
-    packed = rounded(packed + jnp.concatenate([q_bias, jnp.zeros_like(q_bias), v_bias]))
-    heads_shape = (sequence_count, SEQ, HEADS, HD)
-    queries = packed[..., :D].reshape(heads_shape)
-    key_rows = packed[..., D : 2 * D].reshape(heads_shape)
-    value_rows = packed[..., 2 * D :].reshape(heads_shape)
-    scores = low_back(einsum_plain("nqhd,nkhd->nhqk", queries, key_rows) * HD ** (-0.5))
-    scores = jnp.where(key_mask[:, None, None, :], scores, MASKED)
-    attention = low(jax.nn.softmax(scores, axis=-1))
-    context = rounded(
-        einsum_plain("nhqk,nkhd->nqhd", attention, value_rows).reshape(sequence_count, SEQ, D)
-    )
-    attended = low_back(matmul(context, attn_weights[:, 3 * D :]) + o_bias)
+    packed = matmul(low(hidden), in_weights)
+    packed = packed + jnp.concatenate([q_bias, jnp.zeros_like(q_bias), v_bias])
+    context = attend(packed, mask)
+    attended = low_back(matmul(context, out_weights) + o_bias)
     first_out = layer_norm(hidden + attended, gain_one, shift_one)
-    upward = low_back(matmul(low(first_out), ffn_weights[:, :FF]) + up_bias)
+    upward = low_back(matmul(low(first_out), up_weights) + up_bias)
     active = rounded(jax.nn.gelu(upward, approximate=True))
-    downward = low_back(einsum_plain("nsf,df->nsd", active, ffn_weights[:, FF:]) + down_bias)
+    downward = low_back(einsum_plain("nsf,df->nsd", active, down_weights) + down_bias)
     return layer_norm(first_out + downward, gain_two, second_shift)
 
 
@@ -980,7 +1077,7 @@
     ndp = lax.axis_size("dp")
     nz = lax.axis_size("zero")
     n = ndp * nz
-    by_hand = (ndp, nz) == (2, 16)
+    by_hand = (ndp, nz) == (2, 16) and token_ids.shape[0] * ndp * nz <= 256
     my_dp = lax.axis_index("dp")
     my_zero = lax.axis_index("zero")
     me = my_dp * nz + my_zero
@@ -1009,8 +1106,6 @@
             ]
         )
 
-    vec_rows = pad_rows(vectors.astype(jnp.bfloat16), 16)
-
     def gather_layer(layer_index):
         both = jnp.concatenate(
             [attn_w[layer_index].astype(jnp.bfloat16), ffn_w[layer_index].astype(jnp.bfloat16)],
@@ -1019,11 +1114,27 @@
         return lax.all_gather(both, "zero", axis=0, tiled=True)
 
     if by_hand:
-        packet = packet_of(jnp.zeros((nz * room,), jnp.int32), jnp.int32(0))
-        place, packets, vec_parts, gathered, received = exchange_start(
-            ids, packet, vec_rows, attn_w, ffn_w, word_table, room, pair_rows, 0
-        )
-        layer_weights = [gathered[layer].reshape(-1, 4 * D + 2 * FF) for layer in range(LAYERS)]
+        packet = pad_rows(jnp.concatenate([false_neg.reshape(-1), pair_index]), 8)
+        vec_rows = jnp.pad(vectors, (0, LAYERS * 32 * 128 - vec_len)).astype(jnp.bfloat16)
+        place, packets, asked_mine, gathered, received = exchange_start(
+            ids,
+            packet.astype(jnp.bfloat16),
+            vec_rows.reshape(LAYERS, 32, 128),
+            attn_w,
+            ffn_w,
+            word_table,
+            room,
+            0,
+        )
+        columns = 4 * D + 2 * FF
+        gathered = gathered.reshape(LAYERS, D, -1)
+        layer_weights = [gathered[layer, :, :columns] for layer in range(LAYERS)]
+        vec_parts = gathered[:, :, columns:].reshape(LAYERS, nz, -1).transpose(1, 0, 2)
+        rounds = jnp.max(asked_mine[:, 0, 127])
+        asked_mine = asked_mine[:, 0, :room]
+        packets = packets.reshape(n, -1).astype(jnp.int32)
+        false_all = packets[:, : false_neg.size].reshape(total_pairs, total_pairs)
+        pair_all = packets[:, false_neg.size : false_neg.size + pair_rows].reshape(total_pairs)
         owner = ids // shard_rows
         place, local_row = place.reshape(-1), ids - owner * shard_rows
         slot = jnp.where(place < room, owner * room + place, -1)
@@ -1031,7 +1142,10 @@
         owner, place, local_row = token_plan(ids, shard_rows)
         slot, asked = round_slots(owner, place, local_row, 0, room, nz)
         packets, vec_parts = exchange(
-            [packet_of(asked, jnp.max(place) // room + 1), vec_rows],
+            [
+                packet_of(asked, jnp.max(place) // room + 1),
+                pad_rows(vectors.astype(jnp.bfloat16), 16),
+            ],
             ["all", "zero"],
             ndp,
             nz,
@@ -1039,14 +1153,13 @@
             "gather_requests",
         )
         layer_weights = [gather_layer(layer_index) for layer_index in range(LAYERS)]
-    asked_all = packets[:, :nz, :room]
-    false_all = packets[:, nz : nz + false_neg.size // 128].reshape(total_pairs, total_pairs)
-    pair_all = packets[:, -1, :pair_rows].reshape(total_pairs)
-    rounds = jnp.max(packets[:, -1, pair_rows])
+        asked_mine = lax.dynamic_index_in_dim(packets[:, :nz, :room], my_zero, 1, keepdims=False)
+        false_all = packets[:, nz : nz + false_neg.size // 128].reshape(total_pairs, total_pairs)
+        pair_all = packets[:, -1, :pair_rows].reshape(total_pairs)
+        rounds = jnp.max(packets[:, -1, pair_rows])
     vec_all = vec_parts.reshape(nz, -1)[:, :vec_len].reshape(-1).astype(jnp.float32)
 
     word_half = word_table.astype(jnp.bfloat16)
-    asked_mine = lax.dynamic_index_in_dim(asked_all, my_zero, 1, keepdims=False)
     asked_near = lax.dynamic_slice_in_dim(asked_mine, my_dp * nz, nz, 0)
 
     def rows_for(wanted):
@@ -1073,19 +1186,20 @@
     _, rows = lax.while_loop(lambda state: state[0] < rounds, more_rows, (jnp.int32(1), rows))
     rows = rows.reshape(seq_rows, SEQ, D).astype(jnp.float32)
 
-    embedded, embed_back = jax.vjp(embed_tokens, rows, vec_all)
+    position, emb_gain, emb_shift, layer_vectors = split_vectors(vec_all)
+    embedded, embed_back = jax.vjp(embed_tokens, rows, position, emb_gain, emb_shift)
     hidden = embedded
+    mask = key_mask.astype(jnp.float32)[:, None, :]
     saved = []
     pooled = []
     for layer_index in range(LAYERS):
-        layer_fn = functools.partial(encoder_layer, key_mask=key_mask, layer_index=layer_index)
         weights = layer_weights[layer_index]
+        edges = (0, 3 * D, 4 * D, 4 * D + FF, 4 * D + 2 * FF)
+        parts = [
+            weights[:, first:last].astype(jnp.float32) for first, last in zip(edges, edges[1:])
+        ]
         output, layer_back = jax.vjp(
-            layer_fn,
-            hidden,
-            weights[:, : 4 * D].astype(jnp.float32),
-            weights[:, 4 * D :].astype(jnp.float32),
-            vec_all,
+            functools.partial(encoder_layer, mask=mask), hidden, parts, layer_vectors[layer_index]
         )
         saved.append(layer_back)
         hidden = output
@@ -1119,28 +1233,27 @@
     share = key_mask.astype(jnp.float32) / seq_lengths.astype(jnp.float32)[:, None]
     grad_hidden = jnp.zeros_like(embedded)
     weight_parts = []
-    vec_grad = jnp.zeros_like(vec_all)
+    vec_grads = [None] * LAYERS
     for layer_index in range(LAYERS - 1, -1, -1):
         if layer_index == LAYERS - 1:
             grad_hidden = grad_hidden + deep_back[:, None, :] * share[:, :, None]
         if layer_index == 0:
             grad_hidden = grad_hidden + shallow_back[:, None, :] * share[:, :, None]
         layer_back = saved[layer_index]
-        grad_hidden, attn_grad, ffn_grad, vec_layer_grad = layer_back(grad_hidden)
+        grad_hidden, part_grads, vec_grads[layer_index] = layer_back(grad_hidden)
+        part_grads = [part.astype(jnp.bfloat16) for part in part_grads]
         if by_hand and layer_index == 0:
-            weight_parts.insert(0, (attn_grad.astype(jnp.bfloat16), ffn_grad.astype(jnp.bfloat16)))
+            weight_parts.insert(0, part_grads)
         else:
-            both = jnp.concatenate(
-                [attn_grad.astype(jnp.bfloat16), ffn_grad.astype(jnp.bfloat16)], axis=1
-            )
+            both = jnp.concatenate(part_grads, axis=1)
             both, grad_hidden = lax.optimization_barrier((both, grad_hidden))
             weight_parts.insert(0, lax.psum_scatter(both, "zero", scatter_dimension=0, tiled=True))
-        vec_grad = vec_grad + vec_layer_grad
-    rows_grad, vec_embed_grad = embed_back(grad_hidden)
-    vec_grad = vec_grad + vec_embed_grad
-    down_local = jnp.stack(
-        [split_vectors(vec_grad)[3][layer_index][6] for layer_index in range(LAYERS)]
-    )
+    rows_grad, *embed_grads = embed_back(grad_hidden)
+    vec_pieces = [part.reshape(-1) for part in embed_grads]
+    for layer_index in range(LAYERS):
+        vec_pieces += list(vec_grads[layer_index])
+    vec_grad = jnp.concatenate(vec_pieces)
+    down_local = jnp.stack([vec_grads[layer_index][6] for layer_index in range(LAYERS)])
 
     rows_grad = rows_grad.reshape(tokens, D).astype(jnp.bfloat16)
 
@@ -1165,19 +1278,15 @@
     vec_blocks = jnp.pad(vec_blocks, ((0, 0), (0, lines * 128 - vec_blocks.shape[1])))
     sums = slot_sums(slot).reshape(nz, room, D)
     if by_hand:
-        attn_part, ffn_part = weight_parts[0]
-        attn_near, ffn_near, vec_near, sums_all, other_near = exchange_gradients(
-            [
-                attn_part.reshape(4, 2, 2, -1, 4 * D),
-                ffn_part.reshape(4, 2, 2, -1, 2 * FF),
-                vec_blocks.reshape(4, 2, 2, lines, 128),
-            ],
+        *near, vec_near, sums_all, other_near = exchange_gradients(
+            [part.reshape(4, 2, 2, -1, part.shape[1]) for part in weight_parts[0]]
+            + [vec_blocks.reshape(4, 2, 2, lines, 128)],
             sums,
             weight_parts[1],
             3,
         )
-        attn_shard = jnp.stack([attn_near, other_near[:, : 4 * D]])
-        ffn_shard = jnp.stack([ffn_near, other_near[:, 4 * D :]])
+        attn_shard = jnp.stack([jnp.concatenate(near[:2], axis=1), other_near[:, : 4 * D]])
+        ffn_shard = jnp.stack([jnp.concatenate(near[2:], axis=1), other_near[:, 4 * D :]])
         vec_sum = vec_near.reshape(-1)
     else:
         sums_all, vec_shares = exchange(

time: 569 us -> 575 us (1.011)
  Pallas kernels: 223 us -> 313 us
  matrix products: 148 us -> 87.2 us
  other arithmetic: 91 us -> 74.5 us
  local copies, waits for them, and re-layouts: 75.5 us -> 67.8 us
    pallas_call x1 -> x5, Pallas kernels: 99.9 us -> 193 us  [the longest x1 92.1 us: exchange_start(): pl.pallas_call(functools.partial(start_kernel, shard_rows, room), out_sha...]
    dot_general x16 -> x6, matrix products: 43.9 us -> 18.9 us  [einsum_plain(): return jnp.einsum(form, left, right, preferred_element_type=jnp.float32)]
    dot_general x19, matrix products: 81 us -> 56.6 us  [matmul(): return jnp.dot(left, right, preferred_element_type=jnp.float32)]
    slice x12 -> x4, local copies, waits for them, and re-layouts: 23.2 us -> 1.02 us  [the longest x1 0.97 us: body(): gathered[:, :, columns:].reshape(LAYERS, nz, -1).transpose(1, 0, 2)]
    unnamed x242 -> x271, local copies, waits for them, and re-layouts: 19.7 us -> 41.8 us
    reshape x10 -> x5, local copies, waits for them, and re-layouts: 19 us -> 0.4 us  [the longest x2 0.39 us: body(): gathered[:, :, columns:].reshape(LAYERS, nz, -1).transpose(1, 0, 2)]
    sub x2 -> x0, matrix products: 11.5 us -> none  [encoder_layer(): attention = low(jax.nn.softmax(scores, axis=-1))]
    squeeze x0 -> x1, local copies, waits for them, and re-layouts: none -> 10.6 us  [body(): layer_weights = [gathered[layer, :, :columns] for layer in range(LAYERS)]]
  transfers between devices with their start and end apart: 1 -> 1, of which waited for: 0 -> 0; matrix products, arithmetic and copies ran while one was open for 15% -> 15% of each run, Pallas kernels for 0% -> 5%
where the time goes in v5:
time: 575 us; the launch traced here: 565 us
  Pallas kernels  313 us (54%)
  matrix products  87.2 us (15%)
  other arithmetic  74.5 us (13%)
  local copies, waits for them, and re-layouts  67.8 us (12%)
  between operations  20.8 us (4%)
    pallas_call x1, Pallas kernels, exchange_start(): pl.pallas_call(functools.partial(start_kernel, shard_rows, room), out_sha...  92.1 us
    pallas_call x1, Pallas kernels, exchange_gradients(): pl.pallas_call(functools.partial(gradient_kernel, tuple(chunks), len(part...  86.5 us
    dot_general x19, matrix products, matmul(): return jnp.dot(left, right, preferred_element_type=jnp.float32)  56.6 us
    pallas_call x2, Pallas kernels, encoder_layer(): context = attend(packed, mask)  54.8 us
    pallas_call x2, Pallas kernels, attention_call(): pl.pallas_call(kernel, grid=(count,), out_shape=jax.ShapeDtypeStruct((cou...  45.7 us
    unnamed x271, local copies, waits for them, and re-layouts  41.8 us
    pallas_call x2, Pallas kernels, exchange(): pl.pallas_call(functools.partial(exchange_kernel, tuple(modes), ndp, nz),...  27.7 us
    dot_general x6, matrix products, einsum_plain(): return jnp.einsum(form, left, right, preferred_element_type=jnp.float32)  18.9 us
  transfers between devices with their start and end apart: 1, of which 0 were waited for; matrix products, arithmetic and copies ran while one was open for 15% of the time, Pallas kernels for 5%

profile of v5, /device:TPU:0, one launch (start us, length us, event | category | flops | bytes accessed | tf_op | source)
XLA Modules:
  0.0 565.2 jit_solution(6342804453040293773)
XLA Ops:
  12.4 3.7 convert_element_type.263
  16.2 92.1 %exchange_start.1 = (s32[1024,1]{1,0:T(8,128)S(1)}, bf16[32,8,128]{2,1,0:T(8,128)(2,1)S(1)}, s32[32,1,128]{2,1,0:T(1,128)S(1)}, bf16[2,16,32,6272]{3,2,1,0:T(8,128)(2,1)}, bf16[16,72,512]{2,1,0:T(8,128)(2,1)S(1)}) custom-call(s32[1024,1]{1,0:T(8,128)S(1)} %copy.104.refs_0_, s32[1,1024]{1,0:T(1,128)S(1)} %bitcast.233, bf16[8,128]{1,0:T(8,128)(2,1)S(1)} %fusion.85.refs_2_, ...), custom_call_target="tpu_custom_call" | custom-call | bytes 150000000 | tf_op jit(solution)/shard_map/exchange_start/pallas_call | solution.py:704
  109.3 10.6 %slice_bitcast_fusion = (bf16[512,6144]{1,0:T(8,128)(2,1)}, bf16[512,6144]{1,0:T(8,128)(2,1)}) fusion(bf16[2,512,6272]{2,1,0:T(8,128)(2,1)} %bitcast.244), kind=kLoop, calls=%fused_computation.56 | loop fusion | bytes 25165824 | tf_op jit(solution)/shard_map/squeeze | solution.py:1131
  124.0 1.6 fusion.57
  129.0 3.3 add_convert_fusion.1.packed_ref
  132.4 24.1 %jvp_attention_.2 = bf16[8,128,512]{2,1,0:T(8,128)(2,1)S(1)} custom-call(f32[8,1,128]{2,1,0:T(1,128)S(1)} %compare_convert_fusion.mask_ref, bf16[8,128,1536]{2,1,0:T(8,128)(2,1)S(1)} %add_convert_fusion.1.packed_ref), custom_call_target="tpu_custom_call" | custom-call | flops 1000000000 | bytes 5242880 | tf_op jit(solution)/shard_map/jvp(attention)/pallas_call | solution.py:903
  158.9 6.0 %multiply_convert_fusion.1 = (bf16[8,128,2048]{2,1,0:T(8,128)(2,1)S(1)}, f32[8,128,2048]{2,1,0:T(8,128)}) fusion(f32[2048]{0:T(1024)S(1)} %copy-done.82, bf16[8,128,512]{2,1,0:T(8,128)(2,1)S(1)} %fusion.49, bf16[512,6144]{1,0:T(8,128)(2,1)S(1)} %bitcast.250), kind=kOutput, calls=%fused_computation.55 | convolution fusion | flops 2168455168 | bytes 15736832 | tf_op jit(solution)/shard_map/jvp()/dot_general | solution.py:78
  165.0 2.7 fusion.104
  169.0 1.8 add_convert_fusion.packed_ref
  170.8 21.6 %jvp_attention_.3 = bf16[8,128,512]{2,1,0:T(8,128)(2,1)S(1)} custom-call(f32[8,1,128]{2,1,0:T(1,128)S(1)} %compare_convert_fusion.mask_ref, bf16[8,128,1536]{2,1,0:T(8,128)(2,1)S(1)} %add_convert_fusion.packed_ref), custom_call_target="tpu_custom_call" | custom-call | flops 1000000000 | bytes 5242880 | tf_op jit(solution)/shard_map/jvp(attention)/pallas_call | solution.py:903
  194.7 6.2 %multiply_convert_fusion = (bf16[8,128,2048]{2,1,0:T(8,128)(2,1)S(1)}, f32[8,128,2048]{2,1,0:T(8,128)}) fusion(f32[2048]{0:T(1024)S(1)} %copy-done.83, bf16[8,128,512]{2,1,0:T(8,128)(2,1)S(1)} %fusion.50, bf16[512,6144]{1,0:T(8,128)(2,1)S(1)} %bitcast.252), kind=kOutput, calls=%fused_computation.54 | convolution fusion | flops 2168455168 | bytes 15736832 | tf_op jit(solution)/shard_map/jvp()/dot_general | solution.py:78
  200.9 2.7 fusion.106
  205.6 19.2 %gather_pooled.1 = bf16[32,64,128]{2,1,0:T(8,128)(2,1)S(1)} custom-call(bf16[64,128]{1,0:T(8,128)(2,1)S(1)} %reshape.565.refs_0_), custom_call_target="tpu_custom_call" | custom-call | bytes 10485760 | tf_op jit(solution)/shard_map/gather_pooled/pallas_call | solution.py:175
  225.6 2.5 reshape.589
  228.1 2.5 copy.142
  230.6 2.6 reshape.585.pooled_ref
  234.4 6.5 %contrastive.1 = (f32[8,128]{1,0:T(8,128)S(1)}, f32[2,2,128,512]{3,2,1,0:T(8,128)S(1)}) custom-call(f32[2,2,128,512]{3,2,1,0:T(8,128)S(1)} %copy-done.15, s32[128,128]{1,0:T(8,128)S(1)} %reshape.568.false_ref, s32[128,1]{1,0:T(8,128)S(1)} %reshape_reshape.8.pair_ref), custom_call_target="tpu_custom_call" | custom-call | flops 1000000000 | bytes 3000000 | tf_op jit(solution)/shard_map/contrastive/pallas_call | solution.py:810
  240.9 2.4 fusion.45
  245.6 2.4 bitcast_convert_fusion.2
  248.0 2.4 convolution_convert_fusion.1
  250.4 6.7 %fusion.17 = bf16[8,128,2048]{2,1,0:T(8,128)(2,1)S(1)} fusion(bf16[8,128,2048]{2,1,0:T(8,128)(2,1)S(1)} %convolution_convert_fusion.1, f32[8,128,2048]{2,1,0:T(8,128)S(1)} %bitcast.248, f32[2048]{0:T(1024)S(1)} %copy-done.83), kind=kLoop, calls=%fused_computation.34 | loop fusion | flops 46137344 | bytes 16785408 | tf_op jit(solution)/shard_map/transpose(jvp())/convert_element_type | solution.py:70
  257.2 3.1 multiply_reduce_fusion.2
  260.3 2.4 bitcast_convert_fusion.3
  267.0 27.2 %transpose_jvp_attention_back__.2 = bf16[8,128,1536]{2,1,0:T(8,128)(2,1)S(1)} custom-call(f32[8,1,128]{2,1,0:T(1,128)S(1)} %compare_convert_fusion.mask_ref, bf16[8,128,1536]{2,1,0:T(8,128)(2,1)S(1)} %copy-done.3, bf16[8,128,512]{2,1,0:T(8,128)(2,1)S(1)} %convolution_convert_fusion.3.grad_ref), custom_call_target="tpu_custom_call" | custom-call | flops 1000000000 | bytes 5242880 | tf_op jit(solution)/shard_map/transpose(jvp(attention_back))/pallas_call | solution.py:973
  294.3 3.2 add_add_fusion.11
  297.4 1.8 fusion.38
  299.3 4.2 pad_maximum_fusion
  303.5 1.4 convert_reduce_fusion.4
  304.9 2.4 convert_reduce_fusion.2
  307.4 2.9 multiply_reduce_fusion.3
  312.4 4.9 convolution_convert_fusion
  317.3 6.3 %fusion.22 = bf16[8,128,2048]{2,1,0:T(8,128)(2,1)S(1)} fusion(bf16[8,128,2048]{2,1,0:T(8,128)(2,1)S(1)} %convolution_convert_fusion, f32[8,128,2048]{2,1,0:T(8,128)S(1)} %bitcast.246, f32[2048]{0:T(1024)S(1)} %copy-done.82), kind=kLoop, calls=%fused_computation.39 | loop fusion | flops 46137344 | bytes 16785408 | tf_op jit(solution)/shard_map/transpose(jvp())/convert_element_type | solution.py:70
  323.7 6.2 %multiply_reduce_fusion.4 = (f32[512]{0:T(512)S(1)}, f32[8,128]{1,0:T(8,128)S(1)}, f32[512]{0:T(512)S(1)}, f32[8,128,512]{2,1,0:T(8,128)S(1)}) fusion(f32[8,128,512]{2,1,0:T(8,128)S(1)} %copy-done.35, f32[8,128]{1,0:T(8,128)S(1)} %fusion.80, f32[8,128]{1,0:T(8,128)S(1)} %broadcast_multiply_fusion.3, f32[512]{0:T(512)S(1)} %copy-done.90, ...), kind=kOutput, calls=%fused_computation.106 | convolution fusion | flops 2152724480 | bytes 12605440 | tf_op jit(solution)/shard_map/transpose(jvp())/dot_general | solution.py:78
  334.2 2.1 convolution_convert_fusion.2.grad_ref
  336.3 27.6 %transpose_jvp_attention_back__.3 = bf16[8,128,1536]{2,1,0:T(8,128)(2,1)S(1)} custom-call(f32[8,1,128]{2,1,0:T(1,128)S(1)} %compare_convert_fusion.mask_ref, bf16[8,128,1536]{2,1,0:T(8,128)(2,1)S(1)} %add_convert_fusion.1.packed_ref, bf16[8,128,512]{2,1,0:T(8,128)(2,1)S(1)} %convolution_convert_fusion.2.grad_ref), custom_call_target="tpu_custom_call" | custom-call | flops 1000000000 | bytes 5242880 | tf_op jit(solution)/shard_map/transpose(jvp(attention_back))/pallas_call | solution.py:973
  364.0 5.1 multiply_reduce_fusion.5
  369.8 1.3 copy-done.38
  371.4 3.0 add_convert_fusion.2
  375.7 1.6 constant_dynamic-update-slice_fusion.19
  377.3 1.3 constant_dynamic-update-slice_fusion.18
  378.6 1.3 constant_dynamic-update-slice_fusion.17
  380.1 1.4 constant_dynamic-update-slice_fusion.16
  381.5 1.3 constant_dynamic-update-slice_fusion.15
  382.8 1.3 constant_dynamic-update-slice_fusion.14
  384.1 1.3 constant_dynamic-update-slice_fusion.13
  386.1 1.6 constant_dynamic-update-slice_fusion.12
  387.7 1.3 constant_dynamic-update-slice_fusion.11
  389.0 1.3 constant_dynamic-update-slice_fusion.10
  390.3 1.3 constant_dynamic-update-slice_fusion.9
  391.6 1.3 constant_dynamic-update-slice_fusion.8
  393.1 1.3 constant_dynamic-update-slice_fusion.7
  399.0 1.3 constant_dynamic-update-slice_fusion.3
  405.4 3.2 fusion.60
  408.6 2.7 fusion.40
  411.3 3.0 fusion.39
  414.3 3.8 bitcast_convert_fusion
  418.1 4.0 bitcast_convert_fusion.1
  424.1 86.5 %exchange_gradients.1 = (f32[32,1536]{1,0:T(8,128)S(1)}, f32[32,512]{1,0:T(8,128)S(1)}, f32[32,2048]{1,0:T(8,128)S(1)}, f32[32,2048]{1,0:T(8,128)S(1)}, f32[40,1...) custom-call(bf16[4,2,2,32,1536]{4,3,2,1,0:T(8,128)(2,1)S(1)} %bitcast.225, ...), custom_call_target="tpu_custom_call" | custom-call | bytes 200000000 | tf_op jit(solution)/shard_map/exchange_gradients/pallas_call | solution.py:396
  512.2 9.0 %fusion.13 = f32[1908,512]{1,0:T(8,128)} fusion(bf16[2304,512]{1,0:T(8,128)(2,1)} %bitcast.271, s32[2304]{0:T(1024)S(1)} %eq.69), kind=kOutput, calls=%fused_computation.22 | convolution fusion | flops 4505932800 | bytes 6276096 | tf_op jit(solution)/shard_map/dot_general | solution.py:1267
  522.1 3.8 multiply_reduce_fusion.1
  530.3 8.5 %gather_squares.1 = f32[16,8,128]{2,1,0:T(8,128)S(1)} custom-call(f32[8,128]{1,0:T(8,128)S(1)} %broadcast_in_dim.64.refs_0_), custom_call_target="tpu_custom_call" | custom-call | bytes 1310720 | tf_op jit(solution)/shard_map/gather_squares/pallas_call | solution.py:175
  541.4 2.7 fusion.90
  544.1 2.5 fusion.88
  548.7 8.2 %fusion.94 = (bf16[1908,512]{1,0:T(8,128)(2,1)}, f32[1908,512]{1,0:T(8,128)}, f32[1908,512]{1,0:T(8,128)}, f32[1908,512]{1,0:T(8,128)}) fusion(f32[1908,512]{1,0:T(8,128)S(1)} %copy-done.33, f32[1908,512]{1,0:T(8,128)S(1)} %copy-done.47, f32[]{:T(128)S(6)} %min.3, f32[1908,512]{1,0:T(8,128)} %param.28, f32[1908,512]{1,0:T(8,128)} %param.32), kind=kLoop, calls=%fused_computation.282 | loop fusion | flops 15630336 | bytes 29306884 | tf_op jit(solution)/shard_map/convert_element_type | solution.py:1349
  (382 shorter events, 59.0 us)
Async XLA Ops:
  7.2 414.9 %reduce-scatter.2.cloned.1.call-start = ((), (), s32[]{:S(2)}) async-start(), calls=%async_computation.5 | async-start | bytes 6684672 | tf_op jit(solution)/shard_map/reduce_scatter | solution.py:1250
  12.4 3.8 copy-start.24
  108.3 14.0 %copy-start.25 = (s32[32,1,128]{2,1,0:T(1,128)}, s32[32,1,128]{2,1,0:T(1,128)S(1)}, u32[]{:S(2)}) copy-start(s32[32,1,128]{2,1,0:T(1,128)S(1)} %get-tuple-element.113) | copy-start | bytes 49156
  121.9 5.5 copy-start.87
  121.9 5.5 copy-start.96
  123.4 33.1 %copy-start.51 = (f32[128,512]{1,0:T(8,128)}, f32[128,512]{1,0:T(8,128)S(1)}, u32[]{:S(2)}) copy-start(f32[128,512]{1,0:T(8,128)S(1)} %slice_convert_fusion) | copy-start | bytes 786436
  126.8 29.7 %copy-start.78 = (f32[8,128]{1,0:T(8,128)}, f32[8,128]{1,0:T(8,128)S(1)}, u32[]{:S(2)}) copy-start(f32[8,128]{1,0:T(8,128)S(1)} %get-tuple-element.226) | copy-start | bytes 12292
  127.5 29.1 %copy-start.80 = (f32[8,128]{1,0:T(8,128)}, f32[8,128]{1,0:T(8,128)S(1)}, u32[]{:S(2)}) copy-start(f32[8,128]{1,0:T(8,128)S(1)} %bitcast_rsqrt_fusion) | copy-start | bytes 12292
  127.5 29.1 %slice-start.4 = ((s8[6291456]{0:T(1024)(128)(4,1)}), s8[4194304]{0:T(1024)(128)(4,1)S(1)}, s32[]{:S(2)}) async-start(s8[6291456]{0:T(1024)(128)(4,1)} %bitcast.249), calls=%async_computation.11 | async-start | bytes 8388608
  129.0 27.5 %slice-start.5 = ((s8[6291456]{0:T(1024)(128)(4,1)}), s8[2097152]{0:T(1024)(128)(4,1)S(1)}, s32[]{:S(2)}) async-start(s8[6291456]{0:T(1024)(128)(4,1)} %bitcast.249), calls=%async_computation.12 | async-start | bytes 4194304
  132.4 24.2 %copy-start.40 = (bf16[1024,512]{1,0:T(8,128)(2,1)S(1)}, bf16[1024,512]{1,0:T(8,128)(2,1)}, u32[]{:S(2)}) copy-start(bf16[1024,512]{1,0:T(8,128)(2,1)} %copy-done.39) | copy-start | bytes 3145732
  132.4 24.2 %copy-start.88 = (f32[512]{0:T(512)S(1)}, f32[512]{0:T(512)}, u32[]{:S(2)}) copy-start(f32[512]{0:T(512)} %copy-done.87) | copy-start | bytes 6148
  132.4 24.2 %copy-start.97 = (f32[512]{0:T(512)S(1)}, f32[512]{0:T(512)}, u32[]{:S(2)}) copy-start(f32[512]{0:T(512)} %copy-done.96) | copy-start | bytes 6148
  132.4 24.2 %copy-start.107 = (f32[512]{0:T(512)S(1)}, f32[512]{0:T(512)}, u32[]{:S(2)}) copy-start(f32[512]{0:T(512)} %get-tuple-element.215) | copy-start | bytes 6148
  157.7 7.2 %copy-start.34 = (f32[8,128,512]{2,1,0:T(8,128)}, f32[8,128,512]{2,1,0:T(8,128)S(1)}, u32[]{:S(2)}) copy-start(f32[8,128,512]{2,1,0:T(8,128)S(1)} %get-tuple-element.233) | copy-start | bytes 6291460
  158.9 6.1 %copy-start.63 = (bf16[8,128,512]{2,1,0:T(8,128)(2,1)}, bf16[8,128,512]{2,1,0:T(8,128)(2,1)S(1)}, u32[]{:S(2)}) copy-start(bf16[8,128,512]{2,1,0:T(8,128)(2,1)S(1)} %fusion.49) | copy-start | bytes 3145732
  158.9 6.0 %copy-start.106 = (f32[512]{0:T(512)S(1)}, f32[512]{0:T(512)}, u32[]{:S(2)}) copy-start(f32[512]{0:T(512)} %get-tuple-element.212) | copy-start | bytes 6148
  158.9 10.0 %slice-start.6 = ((s8[6291456]{0:T(1024)(128)(4,1)}), s8[4194304]{0:T(1024)(128)(4,1)S(1)}, s32[]{:S(2)}) async-start(s8[6291456]{0:T(1024)(128)(4,1)} %bitcast.251), calls=%async_computation.13 | async-start | bytes 8388608
  165.0 4.0 slice-start.7
  167.7 36.4 %copy-start.29 = (f32[8,128,512]{2,1,0:T(8,128)}, f32[8,128,512]{2,1,0:T(8,128)S(1)}, u32[]{:S(2)}) copy-start(f32[8,128,512]{2,1,0:T(8,128)S(1)} %get-tuple-element.237) | copy-start | bytes 6291460
  170.8 21.6 %copy-start.2 = (bf16[8,128,1536]{2,1,0:T(8,128)(2,1)}, bf16[8,128,1536]{2,1,0:T(8,128)(2,1)S(1)}, u32[]{:S(2)}) copy-start(bf16[8,128,1536]{2,1,0:T(8,128)(2,1)S(1)} %add_convert_fusion.packed_ref) | copy-start | bytes 9437188
  170.8 21.6 %copy-start.105 = (f32[512]{0:T(512)S(1)}, f32[512]{0:T(512)}, u32[]{:S(2)}) copy-start(f32[512]{0:T(512)} %get-tuple-element.207) | copy-start | bytes 6148
  193.5 7.4 %copy-start.36 = (f32[8,128,512]{2,1,0:T(8,128)}, f32[8,128,512]{2,1,0:T(8,128)S(1)}, u32[]{:S(2)}) copy-start(f32[8,128,512]{2,1,0:T(8,128)S(1)} %get-tuple-element.239) | copy-start | bytes 6291460
  194.6 6.2 %copy-start.67 = (bf16[8,128,512]{2,1,0:T(8,128)(2,1)}, bf16[8,128,512]{2,1,0:T(8,128)(2,1)S(1)}, u32[]{:S(2)}) copy-start(bf16[8,128,512]{2,1,0:T(8,128)(2,1)S(1)} %fusion.50) | copy-start | bytes 3145732
  194.7 6.2 %copy-start.104 = (f32[512]{0:T(512)S(1)}, f32[512]{0:T(512)}, u32[]{:S(2)}) copy-start(f32[512]{0:T(512)} %get-tuple-element.202) | copy-start | bytes 6148
  243.3 4.7 slice-start.8
  245.5 4.8 slice-start.2
  250.4 6.7 %copy-start.37 = (f32[8,128,512]{2,1,0:T(8,128)S(1)}, f32[8,128,512]{2,1,0:T(8,128)}, u32[]{:S(2)}) copy-start(f32[8,128,512]{2,1,0:T(8,128)} %copy-done.36) | copy-start | bytes 6291460
  312.0 5.3 slice-start
  312.2 5.1 copy-start.55
  312.4 4.9 slice-start.1
  317.3 6.3 %copy-start.35 = (f32[8,128,512]{2,1,0:T(8,128)S(1)}, f32[8,128,512]{2,1,0:T(8,128)}, u32[]{:S(2)}) copy-start(f32[8,128,512]{2,1,0:T(8,128)} %copy-done.34) | copy-start | bytes 6291460
  323.7 6.2 %copy-start.44 = (bf16[8,128,2048]{2,1,0:T(8,128)(2,1)}, bf16[8,128,2048]{2,1,0:T(8,128)(2,1)S(1)}, u32[]{:S(2)}) copy-start(bf16[8,128,2048]{2,1,0:T(8,128)(2,1)S(1)} %fusion.22) | copy-start | bytes 12582916
  333.9 30.0 %copy-start.92 = (f32[1,1,1536]{2,1,0:T(1,128)}, f32[1,1,1536]{2,1,0:T(1,128)S(1)}, u32[]{:S(2)}) copy-start(f32[1,1,1536]{2,1,0:T(1,128)S(1)} %reshape.575) | copy-start | bytes 18436
  336.3 27.7 %copy-start.41 = (bf16[1024,512]{1,0:T(8,128)(2,1)S(1)}, bf16[1024,512]{1,0:T(8,128)(2,1)}, u32[]{:S(2)}) copy-start(bf16[1024,512]{1,0:T(8,128)(2,1)} %copy-done.39) | copy-start | bytes 3145732
  336.3 27.7 %copy-start.50 = (f32[8,128,512]{2,1,0:T(8,128)S(1)}, f32[8,128,512]{2,1,0:T(8,128)}, u32[]{:S(2)}) copy-start(f32[8,128,512]{2,1,0:T(8,128)} %copy-done.49) | copy-start | bytes 6291460
  336.3 27.7 %copy-start.52 = (f32[128,512]{1,0:T(8,128)S(1)}, f32[128,512]{1,0:T(8,128)}, u32[]{:S(2)}) copy-start(f32[128,512]{1,0:T(8,128)} %copy-done.51) | copy-start | bytes 786436
  336.3 27.7 %copy-start.79 = (f32[8,128]{1,0:T(8,128)S(1)}, f32[8,128]{1,0:T(8,128)}, u32[]{:S(2)}) copy-start(f32[8,128]{1,0:T(8,128)} %copy-done.78) | copy-start | bytes 12292
  336.3 27.7 %copy-start.81 = (f32[8,128]{1,0:T(8,128)S(1)}, f32[8,128]{1,0:T(8,128)}, u32[]{:S(2)}) copy-start(f32[8,128]{1,0:T(8,128)} %copy-done.80) | copy-start | bytes 12292
  336.3 27.7 %copy-start.89 = (f32[512]{0:T(512)S(1)}, f32[512]{0:T(512)}, u32[]{:S(2)}) copy-start(f32[512]{0:T(512)} %copy-done.87) | copy-start | bytes 6148
  364.0 5.1 copy-start
  374.4 5.6 copy-start.57
  374.4 11.0 %copy-start.45 = (bf16[8,128,2048]{2,1,0:T(8,128)(2,1)S(1)}, bf16[8,128,2048]{2,1,0:T(8,128)(2,1)}, u32[]{:S(2)}) copy-start(bf16[8,128,2048]{2,1,0:T(8,128)(2,1)} %copy-done.44) | copy-start | bytes 12582916
  379.9 11.7 %slice-start.10 = ((f32[1,1,1536]{2,1,0:T(1,128)}), f32[1,1,512]{2,1,0:T(1,128)S(1)}, s32[]{:S(2)}) async-start(f32[1,1,1536]{2,1,0:T(1,128)} %copy-done.92), calls=%async_computation.17 | async-start | bytes 4096 | tf_op jit(solution)/shard_map/transpose(jvp())/split | solution.py:972
  379.9 13.0 %copy-start.54 = (bf16[8,128,512]{2,1,0:T(8,128)(2,1)S(1)}, bf16[8,128,512]{2,1,0:T(8,128)(2,1)}, u32[]{:S(2)}) copy-start(bf16[8,128,512]{2,1,0:T(8,128)(2,1)} %copy-done.53) | copy-start | bytes 3145732
  385.4 12.9 %copy-start.43 = (bf16[8,128,2048]{2,1,0:T(8,128)(2,1)S(1)}, bf16[8,128,2048]{2,1,0:T(8,128)(2,1)}, u32[]{:S(2)}) copy-start(bf16[8,128,2048]{2,1,0:T(8,128)(2,1)} %copy-done.42) | copy-start | bytes 12582916
  418.1 4.0 copy-start.10
  418.1 4.0 copy-start.11
  512.2 9.0 %copy-start.70 = (bf16[8,128,512]{2,1,0:T(8,128)(2,1)S(1)}, bf16[8,128,512]{2,1,0:T(8,128)(2,1)}, u32[]{:S(2)}) copy-start(bf16[8,128,512]{2,1,0:T(8,128)(2,1)} %get-tuple-element.200) | copy-start | bytes 3145732
  512.2 9.0 %copy-start.72 = (s32[1024]{0:T(1024)S(1)}, s32[1024]{0:T(1024)}, u32[]{:S(2)}) copy-start(s32[1024]{0:T(1024)} %copy-done.71) | copy-start | bytes 12292
  512.2 9.0 %copy-start.74 = (s32[1024]{0:T(1024)S(1)}, s32[1024]{0:T(1024)}, u32[]{:S(2)}) copy-start(s32[1024]{0:T(1024)} %copy-done.73) | copy-start | bytes 12292
  512.2 9.0 %copy-start.76 = (s32[1024]{0:T(1024)S(1)}, s32[1024]{0:T(1024)}, u32[]{:S(2)}) copy-start(s32[1024]{0:T(1024)} %copy-done.75) | copy-start | bytes 12292
  522.1 3.8 copy-start.23
  522.1 3.8 copy-start.28
  522.1 4.6 copy-start.19
  522.1 4.6 copy-start.21
  525.9 14.8 %copy-start.77 = (f32[4928]{0:T(1024)S(1)}, f32[4928]{0:T(1024)}, u32[]{:S(2)}) copy-start(f32[4928]{0:T(1024)} %param.25) | copy-start | bytes 59140
  525.9 14.8 %copy-start.84 = (f32[4928]{0:T(1024)S(1)}, f32[4928]{0:T(1024)}, u32[]{:S(2)}) copy-start(f32[4928]{0:T(1024)} %param.29) | copy-start | bytes 59140
  525.9 14.8 %copy-start.85 = (f32[4928]{0:T(1024)S(1)}, f32[4928]{0:T(1024)}, u32[]{:S(2)}) copy-start(f32[4928]{0:T(1024)} %param.33) | copy-start | bytes 59140
  525.9 15.5 %copy-start.8 = (f32[2,32,2048]{2,1,0:T(8,128)S(1)}, f32[2,32,2048]{2,1,0:T(8,128)}, u32[]{:S(2)}) copy-start(f32[2,32,2048]{2,1,0:T(8,128)} %refs_4_.1) | copy-start | bytes 1572868
  527.6 16.5 %copy-start.6 = (f32[2,32,4096]{2,1,0:T(8,128)S(1)}, f32[2,32,4096]{2,1,0:T(8,128)}, u32[]{:S(2)}) copy-start(f32[2,32,4096]{2,1,0:T(8,128)} %refs_5_.1) | copy-start | bytes 3145732
  540.1 4.0 copy-start.59
  540.1 4.0 copy-start.60
  544.1 4.6 copy-start.47
  (61 other events, 115.1 us)
Sparse Core Ops, SparseCore 0:
  303.6 86.8 reduce-scatter.1

commit v6 on v5

--- a/solution.py
+++ b/solution.py
@@ -414,9 +414,10 @@
 
 def start_kernel(shard_rows, room, *refs):
     column_ref, row_ref, packet_ref, vec_ref, attn_ref, ffn_ref, word_ref = refs[:7]
-    place_out, packet_out, asked_out, weight_out, rows_out = refs[7:12]
-    table, rows_held, asked, slots, locals_ = refs[12:17]
-    packet_sem, asked_sem, row_sem, z_sem, y_sem, x_sem, d_sem, e_sem, own_sem = refs[17:]
+    place_out, packet_out, asked_out, vec_out, rows_out, *weight_outs = refs[7:14]
+    table, rows_held, asked, slots, locals_ = refs[14:19]
+    packet_sem, asked_sem, vec_sem, row_sem = refs[19:23]
+    z_sem, y_sem, x_sem, d_sem, e_sem, own_sem = refs[23:]
 
     d = lax.axis_index("dp")
     z = lax.axis_index("zero")
@@ -428,7 +429,7 @@
     across = z + 2 - 4 * col
     layers = attn_ref.shape[0]
     width = attn_ref.shape[2]
-    whole = weight_out.shape[3]
+    whole = 3 * width
     unit = whole // 128 // SPLITS
     hand = unit * 5 // 12
     total = layers * SPLITS
@@ -445,9 +446,8 @@
 
     lax.fori_loop(1, 32, greet, 0)
     for layer in range(layers):
-        weight_out[layer, z, :, 0:width] = attn_ref[layer].astype(jnp.bfloat16)
-        weight_out[layer, z, :, width : 3 * width] = ffn_ref[layer].astype(jnp.bfloat16)
-        weight_out[layer, z, :, 3 * width : whole] = vec_ref[layer]
+        weight_outs[layer][z, :, 0:width] = attn_ref[layer].astype(jnp.bfloat16)
+        weight_outs[layer][z, :, width:whole] = ffn_ref[layer].astype(jnp.bfloat16)
     pl.semaphore_wait(barrier, 31)
 
     def remote(src, dst, sems, at, to):
@@ -467,6 +467,9 @@
         to = everyone(k)
         return remote(asked.at[to[1]], asked_out.at[slot], asked_sem, (k,), to)
 
+    def vec_copy(k, slot):
+        return remote(vec_ref, vec_out.at[slot], vec_sem, (k,), (d, lax.rem(z + k, 16)))
+
     def row_copy(k, slot):
         to = lax.rem(z + k, 16)
         return remote(rows_held.at[to], rows_out.at[slot], row_sem, (k,), (d, to))
@@ -482,8 +485,8 @@
 
     def columns_of(at, s, first, size):
         layer, base, _ = piece(s)
-        return weight_out.at[
-            layer, at, :, pl.ds(pl.multiple_of((base + first) * 128, 128), size * 128)
+        return weight_outs[layer].at[
+            at, :, pl.ds(pl.multiple_of((base + first) * 128, 128), size * 128)
         ]
 
     def stretch(at, s, ours):
@@ -514,7 +517,7 @@
         return both(handed(at, s, 1 - d), e_sem, (s, i), (d, sibling))
 
     def own_copy(layer, at):
-        ref = weight_out.at[layer, at]
+        ref = weight_outs[layer].at[at]
         return both(ref, own_sem, (layer,), (d, sibling))
 
     def spread(s, i):
@@ -584,8 +587,15 @@
         return carry
 
     lax.fori_loop(1, 32, send_packets, 0)
+
+    def send_vec(k, carry):
+        vec_copy(k, z).start()
+        return carry
+
+    lax.fori_loop(1, 16, send_vec, 0)
     for layer in range(layers):
         own_copy(layer, z).start()
+    vec_out[z] = vec_ref[...]
     asked_out[me] = asked[z]
     packet_out[me] = packet_ref[...]
 
@@ -679,6 +689,8 @@
         back = lax.rem(z + 16 - k, 16)
         row_copy(k, back).wait_recv()
         row_copy(k, z).wait_send()
+        vec_copy(k, back).wait_recv()
+        vec_copy(k, z).wait_send()
         return carry
 
     lax.fori_loop(1, 16, finish, 0)
@@ -707,11 +719,12 @@
             jax.ShapeDtypeStruct((tokens, 1), jnp.int32),
             jax.ShapeDtypeStruct((32,) + packet.shape, packet.dtype),
             jax.ShapeDtypeStruct((32, 1, 128), jnp.int32),
-            jax.ShapeDtypeStruct((layers, 16, rows, 3 * width + vec_rows.shape[2]), half),
+            jax.ShapeDtypeStruct((16,) + vec_rows.shape, vec_rows.dtype),
             jax.ShapeDtypeStruct((16, room, features), half),
-        ),
+        )
+        + (jax.ShapeDtypeStruct((16, rows, 3 * width), half),) * layers,
         in_specs=[vmem] * 7,
-        out_specs=tuple([vmem] * 5),
+        out_specs=tuple([vmem] * (5 + layers)),
         scratch_shapes=[
             pltpu.VMEM((padded, features), half),
             pltpu.VMEM((16, room, features), half),
@@ -720,6 +733,7 @@
             pltpu.VMEM((tokens, 1), jnp.float32),
             dma((2, 32)),
             dma((2, 32)),
+            dma((2, 16)),
             dma((2, 16)),
             dma((2, pieces, 3)),
             dma((2, pieces, 4)),
@@ -739,7 +753,98 @@
 WIDTHS = (D, D * 2 // 3, D // 3, D // 6, D // 12)
 
 
-def contrastive_kernel(pooled_ref, false_ref, pair_ref, loss_ref, grad_ref):
+def gather_rows(block_ref, all_ref, z_sem, near_sem):
+    d = lax.axis_index("dp")
+    z = lax.axis_index("zero")
+    line, spot = z // 4, lax.rem(z, 4)
+
+    def at_line(k):
+        return lax.rem(line + k, 4) * 4 + spot
+
+    def near_by(j):
+        across = j // 4
+        return lax.rem(d + across, 2), line * 4 + lax.rem(spot + j % 4, 4)
+
+    barrier = pltpu.get_barrier_semaphore()
+    for k in range(1, 4):
+        pl.semaphore_signal(barrier, inc=1, device_id=(d, at_line(k)), device_id_type=MESH)
+    for j in range(1, 8):
+        pl.semaphore_signal(barrier, inc=1, device_id=near_by(j), device_id_type=MESH)
+    pl.semaphore_wait(barrier, 10)
+
+    def z_copy(k):
+        return pltpu.make_async_remote_copy(
+            src_ref=block_ref,
+            dst_ref=all_ref.at[d * 16 + z],
+            send_sem=z_sem.at[0, k],
+            recv_sem=z_sem.at[1, k],
+            device_id=(d, at_line(k)),
+            device_id_type=MESH,
+        )
+
+    def z_arrival(k):
+        ref = all_ref.at[d * 16 + at_line(4 - k)]
+        return pltpu.make_async_remote_copy(
+            src_ref=ref,
+            dst_ref=ref,
+            send_sem=z_sem.at[0, k],
+            recv_sem=z_sem.at[1, k],
+            device_id=(d, at_line(k)),
+            device_id_type=MESH,
+        )
+
+    def near_copy(i, j, from_d, from_z):
+        ref = all_ref.at[from_d * 16 + from_z]
+        return pltpu.make_async_remote_copy(
+            src_ref=ref,
+            dst_ref=ref,
+            send_sem=near_sem.at[0, i, j],
+            recv_sem=near_sem.at[1, i, j],
+            device_id=near_by(j),
+            device_id_type=MESH,
+        )
+
+    for k in range(1, 4):
+        z_copy(k).start()
+    all_ref[d * 16 + z] = block_ref[...]
+    for j in range(1, 8):
+        near_copy(0, j, d, z).start()
+    for k in range(1, 4):
+        z_arrival(k).wait_recv()
+        for j in range(1, 8):
+            near_copy(4 - k, j, d, at_line(4 - k)).start()
+    for i in range(4):
+        for j in range(1, 8):
+            back = lax.rem(line + i, 4) * 4 + lax.rem(spot + 4 - j % 4, 4)
+            near_copy(i, j, lax.rem(d + j // 4, 2), back).wait_recv()
+            near_copy(i, j, d, at_line(i)).wait_send()
+    for k in range(1, 4):
+        z_copy(k).wait_send()
+
+
+def contrastive_kernel(
+    block_ref, false_ref, pair_ref, loss_ref, own_ref, all_ref, pooled_ref, grad_ref, z_sem, near_sem
+):
+    me = lax.axis_index("dp") * 16 + lax.axis_index("zero")
+    gather_rows(block_ref, all_ref, z_sem, near_sem)
+    upper = lax.broadcasted_iota(jnp.int32, (8, 1), 0) < 4
+    for kind in range(2):
+        for two in range(all_ref.shape[0] // 2):
+            even = all_ref[2 * two, kind].astype(jnp.float32)
+            odd = all_ref[2 * two + 1, kind].astype(jnp.float32)
+            at = slice(8 * two, 8 * two + 8)
+            pooled_ref[kind, 0, at, :] = jnp.where(upper, even, pltpu.roll(odd, 4, 0))
+            pooled_ref[kind, 1, at, :] = jnp.where(upper, pltpu.roll(even, 4, 0), odd)
+    contrastive_math(pooled_ref, false_ref, pair_ref, loss_ref, grad_ref)
+    first = pl.multiple_of(me // 2 * 8, 8)
+    swap = lax.rem(me, 2) == 1
+    for kind in range(2):
+        for role in range(2):
+            rows = grad_ref[kind, role, pl.ds(first, 8), :]
+            own_ref[kind, role] = jnp.where(swap, pltpu.roll(rows, 4, 0), rows)
+
+
+def contrastive_math(pooled_ref, false_ref, pair_ref, loss_ref, grad_ref):
     pairs = false_ref.shape[0]
     high = lax.Precision.HIGHEST
     columns = lax.broadcasted_iota(jnp.int32, (pairs, pairs), 1)
@@ -805,93 +910,100 @@
     )
 
 
-def contrastive(pooled_all, false_all, pair_all):
+def contrastive(block, false_all, pair_all, collective_id):
     vmem = pl.BlockSpec(memory_space=pltpu.VMEM)
+    pairs = false_all.shape[0]
+    dma = pltpu.SemaphoreType.DMA
+    whole = pltpu.VMEM((2, 2, pairs, D), jnp.float32)
     loss, grads = pl.pallas_call(
         contrastive_kernel,
         out_shape=(
             jax.ShapeDtypeStruct((8, 128), jnp.float32),
-            jax.ShapeDtypeStruct(pooled_all.shape, jnp.float32),
+            jax.ShapeDtypeStruct((2, 2, 8, D), jnp.float32),
         ),
         in_specs=[vmem] * 3,
         out_specs=(vmem, vmem),
-        compiler_params=pltpu.CompilerParams(vmem_limit_bytes=32 * 1024 * 1024),
+        scratch_shapes=[
+            pltpu.VMEM((32,) + block.shape, block.dtype),
+            whole,
+            whole,
+            dma((2, 4)),
+            dma((2, 4, 8)),
+        ],
+        compiler_params=pltpu.CompilerParams(
+            collective_id=collective_id, has_side_effects=True, vmem_limit_bytes=32 * 1024 * 1024
+        ),
         cost_estimate=pl.CostEstimate(flops=10**9, bytes_accessed=3_000_000, transcendentals=10**6),
         name="contrastive",
-    )(pooled_all, false_all, pair_all.reshape(-1, 1))
+    )(block, false_all, pair_all.reshape(-1, 1))
     return loss[0, 0], grads
 
 
-def head_lanes():
+PAIRS_OF_HEADS = HEADS // 2
+
+
+def by_side(rows):
     lane = lax.broadcasted_iota(jnp.int32, (1, 2 * HD), 1)
-    return lane < HD, lane >= HD
-
-
-def probabilities(queries, keys, valid):
-    scores = lax.dot_general(
-        queries, keys, (((1,), (1,)), ((), ())), preferred_element_type=jnp.float32
+    zero = jnp.zeros_like(rows)
+    return jnp.concatenate([jnp.where(lane < HD, rows, zero), jnp.where(lane < HD, zero, rows)])
+
+
+def join_sides(stacked):
+    lane = lax.broadcasted_iota(jnp.int32, (1, 2 * HD), 1)
+    return jnp.where(lane < HD, stacked[:SEQ], stacked[SEQ:])
+
+
+def contract(left, right, left_dim, right_dim):
+    return lax.dot_general(
+        left, right, (((left_dim,), (right_dim,)), ((), ())), preferred_element_type=jnp.float32
     )
+
+
+def thirds(packed_ref):
+    for pair in range(PAIRS_OF_HEADS):
+        at = pair * 2 * HD
+        yield [packed_ref[0, :, t * D + at : t * D + at + 2 * HD] for t in range(3)]
+
+
+def probabilities(scores, valid):
     scores = jnp.where(valid, scores * HD ** (-0.5), MASKED)
     raised = jnp.exp(scores - jnp.max(scores, axis=1, keepdims=True))
-    return raised / jnp.sum(raised, axis=1, keepdims=True)
+    return raised * (1.0 / jnp.sum(raised, axis=1, keepdims=True))
 
 
 def attention_kernel(mask_ref, packed_ref, context_ref):
     valid = mask_ref[0] > 0.0
-    sides = head_lanes()
-    for pair in range(HEADS // 2):
+    parts = list(thirds(packed_ref))
+    scores = [contract(by_side(queries), keys, 1, 1) for queries, keys, _ in parts]
+    probs = [probabilities(now, valid).astype(jnp.bfloat16) for now in scores]
+    for pair in range(PAIRS_OF_HEADS):
+        mixed = contract(probs[pair], parts[pair][2], 1, 0)
         at = pair * 2 * HD
-        queries = packed_ref[0, :, at : at + 2 * HD]
-        keys = packed_ref[0, :, D + at : D + at + 2 * HD]
-        values = packed_ref[0, :, 2 * D + at : 2 * D + at + 2 * HD]
-        mixed = []
-        for side in sides:
-            probs = probabilities(jnp.where(side, queries, 0), keys, valid).astype(jnp.bfloat16)
-            mixed.append(jnp.dot(probs, values, preferred_element_type=jnp.float32))
-        context_ref[0, :, at : at + 2 * HD] = jnp.where(sides[0], mixed[0], mixed[1]).astype(
-            jnp.bfloat16
-        )
+        context_ref[0, :, at : at + 2 * HD] = join_sides(mixed).astype(jnp.bfloat16)
 
 
 def attention_back_kernel(mask_ref, packed_ref, grad_ref, out_ref):
     valid = mask_ref[0] > 0.0
-    sides = head_lanes()
-    for pair in range(HEADS // 2):
-        at = pair * 2 * HD
-        queries = packed_ref[0, :, at : at + 2 * HD]
-        keys = packed_ref[0, :, D + at : D + at + 2 * HD]
-        values = packed_ref[0, :, 2 * D + at : 2 * D + at + 2 * HD]
-        grad = grad_ref[0, :, at : at + 2 * HD]
-        d_queries, d_keys, d_values = [], [], []
-        for side in sides:
-            probs = probabilities(jnp.where(side, queries, 0), keys, valid)
-            d_probs = lax.dot_general(
-                jnp.where(side, grad, 0),
-                values,
-                (((1,), (1,)), ((), ())),
-                preferred_element_type=jnp.float32,
-            )
-            d_values.append(
-                lax.dot_general(
-                    probs.astype(jnp.bfloat16),
-                    grad,
-                    (((0,), (0,)), ((), ())),
-                    preferred_element_type=jnp.float32,
-                )
-            )
-            shared = jnp.sum(d_probs * probs, axis=1, keepdims=True)
-            d_scores = jnp.where(valid, probs * (d_probs - shared), 0.0).astype(jnp.bfloat16)
-            d_queries.append(jnp.dot(d_scores, keys, preferred_element_type=jnp.float32))
-            d_keys.append(
-                lax.dot_general(
-                    d_scores, queries, (((0,), (0,)), ((), ())), preferred_element_type=jnp.float32
-                )
-            )
-        for third, parts in enumerate((d_queries, d_keys, d_values)):
-            both = jnp.where(sides[0], parts[0], parts[1])
-            if third < 2:
-                both = both * HD ** (-0.5)
-            out_ref[0, :, third * D + at : third * D + at + 2 * HD] = both.astype(jnp.bfloat16)
+    parts = list(thirds(packed_ref))
+    queries = [by_side(part[0]) for part in parts]
+    grads = [
+        by_side(grad_ref[0, :, pair * 2 * HD : (pair + 1) * 2 * HD])
+        for pair in range(PAIRS_OF_HEADS)
+    ]
+    scores = [contract(now, part[1], 1, 1) for now, part in zip(queries, parts)]
+    d_probs = [contract(now, part[2], 1, 1) for now, part in zip(grads, parts)]
+    probs = [probabilities(now, valid) for now in scores]
+    d_scores = []
+    for now, d_now in zip(probs, d_probs):
+        shared = jnp.sum(d_now * now, axis=1, keepdims=True)
+        d_scores.append(jnp.where(valid, now * (d_now - shared), 0.0).astype(jnp.bfloat16))
+    for pair in range(PAIRS_OF_HEADS):
+        d_queries = join_sides(contract(d_scores[pair], parts[pair][1], 1, 0)) * HD ** (-0.5)
+        d_keys = contract(d_scores[pair], queries[pair], 0, 0) * HD ** (-0.5)
+        d_values = contract(probs[pair].astype(jnp.bfloat16), grads[pair], 0, 0)
+        for third, now in enumerate((d_queries, d_keys, d_values)):
+            at = third * D + pair * 2 * HD
+            out_ref[0, :, at : at + 2 * HD] = now.astype(jnp.bfloat16)
 
 
 def attention_call(kernel, mask, operands, features, name):
@@ -937,20 +1049,12 @@
 attend.defvjp(attend_forward, attend_backward)
 
 
-def split_vectors(vec_all):
-    offset = SEQ * D
-    position = vec_all[:offset].reshape(SEQ, D)
-    emb_gain = vec_all[offset : offset + D]
-    emb_shift = vec_all[offset + D : offset + 2 * D]
-    offset = offset + 2 * D
-    layer_parts = []
-    for layer_index in range(LAYERS):
-        pieces = []
-        for length_now in (D, D, D, D, D, FF, D, D, D):
-            pieces.append(vec_all[offset : offset + length_now])
-            offset = offset + length_now
-        layer_parts.append(pieces)
-    return (position, emb_gain, emb_shift, layer_parts)
+LAYER_ROWS = 8 + FF // D
+
+
+def layer_vectors(rows):
+    up = 5 + FF // D
+    return [rows[i] for i in range(5)] + [rows[5:up].reshape(FF)] + [rows[up + i] for i in range(3)]
 
 
 def layer_norm(values, gain, shift):
@@ -959,14 +1063,14 @@
     return center * lax.rsqrt(spread + NORM_EPS) * gain + shift
 
 
-def embed_tokens(rows, position, emb_gain, emb_shift):
-    return layer_norm(low_back(rows) + position[None], emb_gain, emb_shift)
+def embed_tokens(rows, vectors):
+    return layer_norm(low_back(rows) + vectors[None, :SEQ], vectors[SEQ], vectors[SEQ + 1])
 
 
 def encoder_layer(hidden, weights, vectors, mask):
     in_weights, out_weights, up_weights, down_weights = weights
     q_bias, v_bias, o_bias, gain_one, shift_one, up_bias, down_bias, gain_two, second_shift = (
-        vectors
+        layer_vectors(vectors)
     )
     packed = matmul(low(hidden), in_weights)
     packed = packed + jnp.concatenate([q_bias, jnp.zeros_like(q_bias), v_bias])
@@ -1115,21 +1219,17 @@
 
     if by_hand:
         packet = pad_rows(jnp.concatenate([false_neg.reshape(-1), pair_index]), 8)
-        vec_rows = jnp.pad(vectors, (0, LAYERS * 32 * 128 - vec_len)).astype(jnp.bfloat16)
-        place, packets, asked_mine, gathered, received = exchange_start(
+        place, packets, asked_mine, vec_parts, received, *gathered = exchange_start(
             ids,
             packet.astype(jnp.bfloat16),
-            vec_rows.reshape(LAYERS, 32, 128),
+            pad_rows(vectors.astype(jnp.bfloat16), 16),
             attn_w,
             ffn_w,
             word_table,
             room,
             0,
         )
-        columns = 4 * D + 2 * FF
-        gathered = gathered.reshape(LAYERS, D, -1)
-        layer_weights = [gathered[layer, :, :columns] for layer in range(LAYERS)]
-        vec_parts = gathered[:, :, columns:].reshape(LAYERS, nz, -1).transpose(1, 0, 2)
+        layer_weights = [part.reshape(D, -1) for part in gathered]
         rounds = jnp.max(asked_mine[:, 0, 127])
         asked_mine = asked_mine[:, 0, :room]
         packets = packets.reshape(n, -1).astype(jnp.int32)
@@ -1159,11 +1259,12 @@
         rounds = jnp.max(packets[:, -1, pair_rows])
     vec_all = vec_parts.reshape(nz, -1)[:, :vec_len].reshape(-1).astype(jnp.float32)
 
-    word_half = word_table.astype(jnp.bfloat16)
     asked_near = lax.dynamic_slice_in_dim(asked_mine, my_dp * nz, nz, 0)
 
     def rows_for(wanted):
-        return matmul(one_hot(wanted.reshape(-1), shard_rows), word_half).astype(jnp.bfloat16)
+        table, wanted = lax.optimization_barrier((word_table, wanted))
+        picked = one_hot(wanted.reshape(-1), shard_rows)
+        return matmul(picked, table.astype(jnp.bfloat16)).astype(jnp.bfloat16)
 
     def rows_from(slot_now, received):
         return matmul(one_hot(slot_now, nz * room), received.reshape(nz * room, D)).astype(
@@ -1186,8 +1287,10 @@
     _, rows = lax.while_loop(lambda state: state[0] < rounds, more_rows, (jnp.int32(1), rows))
     rows = rows.reshape(seq_rows, SEQ, D).astype(jnp.float32)
 
-    position, emb_gain, emb_shift, layer_vectors = split_vectors(vec_all)
-    embedded, embed_back = jax.vjp(embed_tokens, rows, position, emb_gain, emb_shift)
+    vec_rows = vec_all.reshape(-1, D)
+    edges = [0] + [SEQ + 2 + i * LAYER_ROWS for i in range(LAYERS + 1)]
+    vec_parts = [vec_rows[first:last] for first, last in zip(edges, edges[1:])]
+    embedded, embed_back = jax.vjp(embed_tokens, rows, vec_parts[0])
     hidden = embedded
     mask = key_mask.astype(jnp.float32)[:, None, :]
     saved = []
@@ -1199,20 +1302,22 @@
             weights[:, first:last].astype(jnp.float32) for first, last in zip(edges, edges[1:])
         ]
         output, layer_back = jax.vjp(
-            functools.partial(encoder_layer, mask=mask), hidden, parts, layer_vectors[layer_index]
+            functools.partial(encoder_layer, mask=mask), hidden, parts, vec_parts[1 + layer_index]
         )
         saved.append(layer_back)
         hidden = output
         pooled.append(pool_rows(hidden, key_mask, seq_lengths).astype(jnp.bfloat16))
 
-    (pooled_all,) = exchange(
-        [jnp.stack(pooled).reshape(-1, 128)], ["all"], ndp, nz, 2, "gather_pooled"
-    )
-    pooled_all = pooled_all.reshape(n, 2, pair_rows, 2, D).astype(jnp.float32)
-    pooled_all = pooled_all.transpose(1, 3, 0, 2, 4).reshape(2, 2, total_pairs, D)
-    if total_pairs <= 256:
-        loss, pooled_grads = contrastive(pooled_all, false_all, pair_all)
+    if by_hand and pair_rows == 4:
+        block = jnp.stack(pooled).reshape(2, pair_rows, 2, D).transpose(0, 2, 1, 3)
+        loss, pooled_grads = contrastive(block.reshape(2, 2 * pair_rows, D), false_all, pair_all, 2)
+        pooled_grads = pooled_grads[:, :, :pair_rows]
     else:
+        (pooled_all,) = exchange(
+            [jnp.stack(pooled).reshape(-1, 128)], ["all"], ndp, nz, 2, "gather_pooled"
+        )
+        pooled_all = pooled_all.reshape(n, 2, pair_rows, 2, D).astype(jnp.float32)
+        pooled_all = pooled_all.transpose(1, 3, 0, 2, 4).reshape(2, 2, total_pairs, D)
 
         def whole_loss(pooled_now):
             summed = contrastive_terms(
@@ -1227,7 +1332,7 @@
             return summed / jnp.maximum(valid_total, 1.0)
 
         loss, pooled_grads = jax.value_and_grad(whole_loss)(pooled_all)
-    pooled_grads = lax.dynamic_slice_in_dim(pooled_grads, me * pair_rows, pair_rows, 2)
+        pooled_grads = lax.dynamic_slice_in_dim(pooled_grads, me * pair_rows, pair_rows, 2)
     pooled_grads = pooled_grads.transpose(0, 2, 1, 3).reshape(2, seq_rows, D)
     shallow_back, deep_back = pooled_grads[0], pooled_grads[1]
     share = key_mask.astype(jnp.float32) / seq_lengths.astype(jnp.float32)[:, None]
@@ -1248,12 +1353,9 @@
             both = jnp.concatenate(part_grads, axis=1)
             both, grad_hidden = lax.optimization_barrier((both, grad_hidden))
             weight_parts.insert(0, lax.psum_scatter(both, "zero", scatter_dimension=0, tiled=True))
-    rows_grad, *embed_grads = embed_back(grad_hidden)
-    vec_pieces = [part.reshape(-1) for part in embed_grads]
-    for layer_index in range(LAYERS):
-        vec_pieces += list(vec_grads[layer_index])
-    vec_grad = jnp.concatenate(vec_pieces)
-    down_local = jnp.stack([vec_grads[layer_index][6] for layer_index in range(LAYERS)])
+    rows_grad, embed_grads = embed_back(grad_hidden)
+    vec_grad = jnp.concatenate([embed_grads] + vec_grads, axis=0)
+    down_local = jnp.stack([part[5 + FF // D] for part in vec_grads])
 
     rows_grad = rows_grad.reshape(tokens, D).astype(jnp.bfloat16)
 

time: 575 us -> 461 us (0.80)
  Pallas kernels: 313 us -> 239 us
  local copies, waits for them, and re-layouts: 67.8 us -> 23.3 us
  other arithmetic: 74.5 us -> 80.7 us
    pallas_call x2, Pallas kernels: 54.8 us -> 19.1 us  [encoder_layer(): context = attend(packed, mask)]
    pallas_call x2, Pallas kernels: 45.7 us -> 12.6 us  [attention_call(): pl.pallas_call(kernel, grid=(count,), out_shape=jax.ShapeDtypeStruct((cou...]
    unnamed x271 -> x250, local copies, waits for them, and re-layouts: 41.8 us -> 17.4 us
    pallas_call x2 -> x1, Pallas kernels: 27.7 us -> 8.4 us  [exchange(): pl.pallas_call(functools.partial(exchange_kernel, tuple(modes), ndp, nz),...]
    pallas_call x1, Pallas kernels: 6.46 us -> 23.6 us  [contrastive(): pl.pallas_call(contrastive_kernel, out_shape=(jax.ShapeDtypeStruct((8, 12...]
    squeeze x1 -> x0, local copies, waits for them, and re-layouts: 10.6 us -> none  [body(): layer_weights = [gathered[layer, :, :columns] for layer in range(LAYERS)]]
    reshape x6 -> x4, local copies, waits for them, and re-layouts: 7.94 us -> 0.04 us  [the longest x2 0.02 us: layer_vectors(): rows[5:up].reshape(FF)]
  transfers between devices with their start and end apart: 1 -> 1, of which waited for: 0 -> 0; matrix products, arithmetic and copies ran while one was open for 15% -> 15% of each run, Pallas kernels for 5% -> 2%
where the time goes in v6:
time: 461 us; the launch traced here: 453 us
  Pallas kernels  239 us (52%)
  matrix products  87.9 us (19%)
  other arithmetic  80.7 us (18%)
  local copies, waits for them, and re-layouts  23.3 us (5%)
  between operations  20.8 us (5%)
    pallas_call x1, Pallas kernels, exchange_start(): pl.pallas_call(functools.partial(start_kernel, shard_rows, room), out_sha...  92.3 us
    pallas_call x1, Pallas kernels, exchange_gradients(): pl.pallas_call(functools.partial(gradient_kernel, tuple(chunks), len(part...  82.7 us
    dot_general x19, matrix products, matmul(): return jnp.dot(left, right, preferred_element_type=jnp.float32)  57.6 us
    pallas_call x1, Pallas kernels, contrastive(): pl.pallas_call(contrastive_kernel, out_shape=(jax.ShapeDtypeStruct((8, 12...  23.6 us
    pallas_call x2, Pallas kernels, encoder_layer(): context = attend(packed, mask)  19.1 us
    convert_element_type x7, other arithmetic, low_back(): return build_low_back()(value)  19 us
    dot_general x6, matrix products, einsum_plain(): return jnp.einsum(form, left, right, preferred_element_type=jnp.float32)  18.6 us
    unnamed x250, local copies, waits for them, and re-layouts  17.4 us
  transfers between devices with their start and end apart: 1, of which 0 were waited for; matrix products, arithmetic and copies ran while one was open for 15% of the time, Pallas kernels for 2%

profile of v6, /device:TPU:0, one launch (start us, length us, event | category | flops | bytes accessed | tf_op | source)
XLA Modules:
  0.0 453.1 jit_solution(1016481043122351296)
XLA Ops:
  12.4 3.7 convert.19
  16.2 92.3 %exchange_start.1 = (s32[1024,1]{1,0:T(8,128)S(1)}, bf16[32,8,128]{2,1,0:T(8,128)(2,1)S(1)}, s32[32,1,128]{2,1,0:T(1,128)S(1)}, bf16[16,48,128]{2,1,0:T(8,128)(2...) custom-call(s32[1024,1]{1,0:T(8,128)S(1)} %copy.121.refs_0_, ...), custom_call_target="tpu_custom_call" | custom-call | bytes 150000000 | tf_op jit(solution)/shard_map/exchange_start/pallas_call | solution.py:716
  112.2 1.6 fusion.58
  116.3 0.9 copy-done.59
  117.2 3.3 add_convert_fusion.1.packed_ref
  120.6 7.4 %jvp_attention_.2 = bf16[8,128,512]{2,1,0:T(8,128)(2,1)S(1)} custom-call(f32[8,1,128]{2,1,0:T(1,128)S(1)} %compare_convert_fusion.mask_ref, bf16[8,128,1536]{2,1,0:T(8,128)(2,1)S(1)} %add_convert_fusion.1.packed_ref), custom_call_target="tpu_custom_call" | custom-call | flops 1000000000 | bytes 5242880 | tf_op jit(solution)/shard_map/jvp(attention)/pallas_call | solution.py:1015
  128.1 1.1 fusion.104
  130.4 6.0 %multiply_convert_fusion.1 = (bf16[8,128,2048]{2,1,0:T(8,128)(2,1)S(1)}, f32[8,128,2048]{2,1,0:T(8,128)}) fusion(f32[2048]{0:T(1024)S(1)} %copy-done.82, bf16[8,128,512]{2,1,0:T(8,128)(2,1)S(1)} %fusion.50, bf16[512,6144]{1,0:T(8,128)(2,1)S(1)} %bitcast.290), kind=kOutput, calls=%fused_computation.56 | convolution fusion | flops 2168455168 | bytes 15736832 | tf_op jit(solution)/shard_map/jvp()/dot_general | solution.py:78
  136.5 2.7 fusion.105
  140.4 1.0 copy-done.63
  141.5 1.8 add_convert_fusion.packed_ref
  143.3 5.2 %jvp_attention_.3 = bf16[8,128,512]{2,1,0:T(8,128)(2,1)S(1)} custom-call(f32[8,1,128]{2,1,0:T(1,128)S(1)} %compare_convert_fusion.mask_ref, bf16[8,128,1536]{2,1,0:T(8,128)(2,1)S(1)} %add_convert_fusion.packed_ref), custom_call_target="tpu_custom_call" | custom-call | flops 1000000000 | bytes 5242880 | tf_op jit(solution)/shard_map/jvp(attention)/pallas_call | solution.py:1015
  148.6 1.0 fusion.106
  150.8 6.2 %multiply_convert_fusion = (bf16[8,128,2048]{2,1,0:T(8,128)(2,1)S(1)}, f32[8,128,2048]{2,1,0:T(8,128)}) fusion(f32[2048]{0:T(1024)S(1)} %copy-done.83, bf16[8,128,512]{2,1,0:T(8,128)(2,1)S(1)} %fusion.51, bf16[512,6144]{1,0:T(8,128)(2,1)S(1)} %bitcast.296), kind=kOutput, calls=%fused_computation.55 | convolution fusion | flops 2168455168 | bytes 15736832 | tf_op jit(solution)/shard_map/jvp()/dot_general | solution.py:78
  157.0 2.7 fusion.107
  160.5 1.2 multiply_reduce_fusion.13
  161.8 23.6 %contrastive.1 = (f32[8,128]{1,0:T(8,128)S(1)}, f32[2,2,8,512]{3,2,1,0:T(8,128)S(1)}) custom-call(bf16[2,8,512]{2,1,0:T(8,128)(2,1)S(1)} %reshape.633.block_ref, s32[128,128]{1,0:T(8,128)S(1)} %reshape.634.false_ref, s32[128,1]{1,0:T(8,128)S(1)} %reshape_reshape.8.pair_ref), custom_call_target="tpu_custom_call" | custom-call | flops 1000000000 | bytes 3000000 | tf_op jit(solution)/shard_map/contrastive/pallas_call | solution.py:918
  185.5 2.4 fusion.46
  187.9 1.3 fusion.47
  190.1 2.5 bitcast_convert_fusion.2
  192.6 2.4 convolution_convert_fusion.1
  195.1 6.7 %fusion.18 = bf16[8,128,2048]{2,1,0:T(8,128)(2,1)S(1)} fusion(bf16[8,128,2048]{2,1,0:T(8,128)(2,1)S(1)} %convolution_convert_fusion.1, f32[8,128,2048]{2,1,0:T(8,128)S(1)} %bitcast.256, f32[2048]{0:T(1024)S(1)} %copy-done.83), kind=kLoop, calls=%fused_computation.35 | loop fusion | flops 46137344 | bytes 16785408 | tf_op jit(solution)/shard_map/transpose(jvp())/convert_element_type | solution.py:70
  201.8 3.1 multiply_reduce_fusion.2
  205.0 2.4 bitcast_convert_fusion.3
  208.4 1.0 copy-done.14
  211.6 9.6 %transpose_jvp_attention_back__.2 = bf16[8,128,1536]{2,1,0:T(8,128)(2,1)S(1)} custom-call(f32[8,1,128]{2,1,0:T(1,128)S(1)} %compare_convert_fusion.mask_ref, bf16[8,128,1536]{2,1,0:T(8,128)(2,1)S(1)} %copy-done.3, bf16[8,128,512]{2,1,0:T(8,128)(2,1)S(1)} %convolution_convert_fusion.3.grad_ref), custom_call_target="tpu_custom_call" | custom-call | flops 1000000000 | bytes 5242880 | tf_op jit(solution)/shard_map/transpose(jvp(attention_back))/pallas_call | solution.py:1077
  221.3 3.2 add_add_fusion.11
  224.4 1.8 fusion.39
  226.3 4.0 pad_maximum_fusion
  230.4 2.9 multiply_reduce_fusion.4
  234.1 1.0 fusion.98
  235.2 1.3 copy-done.44
  236.7 4.6 %convolution_convert_fusion = bf16[8,128,2048]{2,1,0:T(8,128)(2,1)S(1)} fusion(bf16[8,128,512]{2,1,0:T(8,128)(2,1)S(1)} %add_convert_fusion.4, bf16[512,6144]{1,0:T(8,128)(2,1)} %bitcast.283), kind=kOutput, calls=%fused_computation.77 | convolution fusion | flops 2149580800 | bytes 7340032 | tf_op jit(solution)/shard_map/transpose(jvp(nsf,df->nsd))/dot_general | solution.py:82
  241.3 7.8 %fusion.23 = bf16[8,128,2048]{2,1,0:T(8,128)(2,1)} fusion(bf16[8,128,2048]{2,1,0:T(8,128)(2,1)S(1)} %convolution_convert_fusion, f32[8,128,2048]{2,1,0:T(8,128)S(1)} %bitcast.254, f32[2048]{0:T(1024)S(1)} %copy-done.82), kind=kLoop, calls=%fused_computation.40 | loop fusion | flops 46137344 | bytes 16785408 | tf_op jit(solution)/shard_map/transpose(jvp())/convert_element_type | solution.py:70
  249.7 7.2 %multiply_reduce_fusion.3 = (f32[512]{0:T(512)S(1)}, f32[8,128]{1,0:T(8,128)S(1)}, f32[512]{0:T(512)S(1)}, f32[8,128,512]{2,1,0:T(8,128)S(1)}) fusion(f32[8,128,512]{2,1,0:T(8,128)} %copy-done.33, f32[8,128]{1,0:T(8,128)S(1)} %fusion.81, f32[8,128]{1,0:T(8,128)S(1)} %broadcast_multiply_fusion.3, f32[512]{0:T(512)S(1)} %copy-done.90, ...), kind=kOutput, calls=%fused_computation.104 | convolution fusion | flops 2152724480 | bytes 12605440 | tf_op jit(solution)/shard_map/transpose(jvp())/dot_general | solution.py:78
  257.9 1.1 copy-done.45
  259.0 1.0 copy-done.53
  260.0 1.8 convolution_convert_fusion.2.grad_ref
  261.7 9.5 %transpose_jvp_attention_back__.3 = bf16[8,128,1536]{2,1,0:T(8,128)(2,1)S(1)} custom-call(f32[8,1,128]{2,1,0:T(1,128)S(1)} %compare_convert_fusion.mask_ref, bf16[8,128,1536]{2,1,0:T(8,128)(2,1)S(1)} %add_convert_fusion.1.packed_ref, bf16[8,128,512]{2,1,0:T(8,128)(2,1)S(1)} %convolution_convert_fusion.2.grad_ref), custom_call_target="tpu_custom_call" | custom-call | flops 1000000000 | bytes 5242880 | tf_op jit(solution)/shard_map/transpose(jvp(attention_back))/pallas_call | solution.py:1077
  271.2 1.7 copy-done
  274.8 3.0 convert_reduce_fusion
  278.6 3.3 convert_reduce_fusion.1
  282.1 5.7 %multiply_reduce_fusion.6 = (f32[512]{0:T(512)S(1)}, f32[8,128]{1,0:T(8,128)S(1)}, f32[512]{0:T(512)S(1)}, f32[8,128,512]{2,1,0:T(8,128)S(1)}) fusion(f32[8,128]{1,0:T(8,128)S(1)} %copy-done.81, f32[8,128]{1,0:T(8,128)S(1)} %copy-done.79, f32[128,512]{1,0:T(8,128)S(1)} %copy-done.47, bf16[1024,512]{1,0:T(8,128)(2,1)} %copy-done.37, f32[512]{0:T(512)S(1)} %copy-done.89, ...), kind=kOutput, calls=%fused_computation.108 | convolution fusion | flops 1618475008 | bytes 11294720 | tf_op jit(solution)/shard_map/transpose(jvp())/dot_general | solution.py:78
  287.8 2.0 add_add_fusion
  289.7 1.8 reduce_sum.442
  291.6 3.0 add_convert_fusion.2
  295.4 0.9 reshape.643
  296.3 1.1 fusion.70
  297.5 3.2 fusion.61
  300.6 2.7 fusion.41
  303.4 3.0 fusion.40
  306.4 3.8 bitcast_convert_fusion
  310.2 3.8 bitcast_convert_fusion.1
  313.9 1.0 copy-done.15
  315.0 1.0 copy-done.16
  316.0 82.7 %exchange_gradients.1 = (f32[32,1536]{1,0:T(8,128)S(1)}, f32[32,512]{1,0:T(8,128)S(1)}, f32[32,2048]{1,0:T(8,128)S(1)}, f32[32,2048]{1,0:T(8,128)S(1)}, f32[40,1...) custom-call(bf16[4,2,2,32,1536]{4,3,2,1,0:T(8,128)(2,1)S(1)} %bitcast.235, ...), custom_call_target="tpu_custom_call" | custom-call | bytes 200000000 | tf_op jit(solution)/shard_map/exchange_gradients/pallas_call | solution.py:396
  400.2 8.9 %fusion.14 = f32[1908,512]{1,0:T(8,128)} fusion(bf16[2304,512]{1,0:T(8,128)(2,1)} %bitcast.305, s32[2304]{0:T(1024)S(1)} %copy-done.92), kind=kOutput, calls=%fused_computation.23 | convolution fusion | flops 4505932800 | bytes 6276096 | tf_op jit(solution)/shard_map/dot_general | solution.py:1369
  410.1 3.8 multiply_reduce_fusion.1
  418.3 8.4 %gather_squares.1 = f32[16,8,128]{2,1,0:T(8,128)S(1)} custom-call(f32[8,128]{1,0:T(8,128)S(1)} %broadcast_in_dim.173.refs_0_), custom_call_target="tpu_custom_call" | custom-call | bytes 1310720 | tf_op jit(solution)/shard_map/gather_squares/pallas_call | solution.py:175
  429.3 2.7 fusion.91
  432.1 2.5 fusion.89
  434.5 1.0 copy-done.32
  435.5 1.2 copy-done.42
  436.7 8.2 %fusion.95 = (bf16[1908,512]{1,0:T(8,128)(2,1)}, f32[1908,512]{1,0:T(8,128)}, f32[1908,512]{1,0:T(8,128)}, f32[1908,512]{1,0:T(8,128)}) fusion(f32[1908,512]{1,0:T(8,128)S(1)} %copy-done.32, f32[1908,512]{1,0:T(8,128)S(1)} %copy-done.42, f32[]{:T(128)S(6)} %min.3, f32[1908,512]{1,0:T(8,128)} %param.28, f32[1908,512]{1,0:T(8,128)} %param.32), kind=kLoop, calls=%fused_computation.265 | loop fusion | flops 15630336 | bytes 29306884 | tf_op jit(solution)/shard_map/convert_element_type | solution.py:1451
  (366 shorter events, 31.8 us)
Async XLA Ops:
  7.2 306.7 %reduce-scatter.2.cloned.1.call-start = ((), (), s32[]{:S(2)}) async-start(), calls=%async_computation.5 | async-start | bytes 6684672 | tf_op jit(solution)/shard_map/reduce_scatter | solution.py:1355
  12.4 3.8 copy-start.6
  12.4 3.8 copy-start.8
  12.4 3.8 copy-start.27
  108.5 3.7 copy-start.23
  110.1 5.6 %copy-start.87 = (f32[512]{0:T(512)}, f32[512]{0:T(512)S(1)}, u32[]{:S(2)}) copy-start(f32[512]{0:T(512)S(1)} %get-tuple-element.223) | copy-start | bytes 6148
  110.1 5.6 %copy-start.96 = (f32[512]{0:T(512)}, f32[512]{0:T(512)S(1)}, u32[]{:S(2)}) copy-start(f32[512]{0:T(512)S(1)} %get-tuple-element.222) | copy-start | bytes 6148
  111.5 16.5 %copy-start.46 = (f32[128,512]{1,0:T(8,128)}, f32[128,512]{1,0:T(8,128)S(1)}, u32[]{:S(2)}) copy-start(f32[128,512]{1,0:T(8,128)S(1)} %slice_convert_fusion) | copy-start | bytes 786436
  115.0 13.0 %copy-start.78 = (f32[8,128]{1,0:T(8,128)}, f32[8,128]{1,0:T(8,128)S(1)}, u32[]{:S(2)}) copy-start(f32[8,128]{1,0:T(8,128)S(1)} %get-tuple-element.230) | copy-start | bytes 12292
  115.6 12.4 %copy-start.80 = (f32[8,128]{1,0:T(8,128)}, f32[8,128]{1,0:T(8,128)S(1)}, u32[]{:S(2)}) copy-start(f32[8,128]{1,0:T(8,128)S(1)} %bitcast_rsqrt_fusion) | copy-start | bytes 12292
  115.7 12.4 %slice-start.6 = ((s8[6291456]{0:T(1024)(128)(4,1)}), s8[4194304]{0:T(1024)(128)(4,1)S(1)}, s32[]{:S(2)}) async-start(s8[6291456]{0:T(1024)(128)(4,1)} %bitcast.287), calls=%async_computation.13 | async-start | bytes 8388608
  117.2 10.8 %slice-start.7 = ((s8[6291456]{0:T(1024)(128)(4,1)}), s8[2097152]{0:T(1024)(128)(4,1)S(1)}, s32[]{:S(2)}) async-start(s8[6291456]{0:T(1024)(128)(4,1)} %bitcast.287), calls=%async_computation.14 | async-start | bytes 4194304
  120.6 7.5 %copy-start.38 = (bf16[1024,512]{1,0:T(8,128)(2,1)S(1)}, bf16[1024,512]{1,0:T(8,128)(2,1)}, u32[]{:S(2)}) copy-start(bf16[1024,512]{1,0:T(8,128)(2,1)} %copy-done.37) | copy-start | bytes 3145732
  120.6 7.5 %copy-start.88 = (f32[512]{0:T(512)S(1)}, f32[512]{0:T(512)}, u32[]{:S(2)}) copy-start(f32[512]{0:T(512)} %copy-done.87) | copy-start | bytes 6148
  120.6 7.5 %copy-start.97 = (f32[512]{0:T(512)S(1)}, f32[512]{0:T(512)}, u32[]{:S(2)}) copy-start(f32[512]{0:T(512)} %copy-done.96) | copy-start | bytes 6148
  120.6 7.5 %copy-start.107 = (f32[512]{0:T(512)S(1)}, f32[512]{0:T(512)}, u32[]{:S(2)}) copy-start(f32[512]{0:T(512)} %get-tuple-element.219) | copy-start | bytes 6148
  129.2 7.2 %copy-start.33 = (f32[8,128,512]{2,1,0:T(8,128)}, f32[8,128,512]{2,1,0:T(8,128)S(1)}, u32[]{:S(2)}) copy-start(f32[8,128,512]{2,1,0:T(8,128)S(1)} %get-tuple-element.237) | copy-start | bytes 6291460
  130.3 6.2 %copy-start.61 = (bf16[8,128,512]{2,1,0:T(8,128)(2,1)}, bf16[8,128,512]{2,1,0:T(8,128)(2,1)S(1)}, u32[]{:S(2)}) copy-start(bf16[8,128,512]{2,1,0:T(8,128)(2,1)S(1)} %fusion.50) | copy-start | bytes 3145732
  130.4 6.0 %copy-start.106 = (f32[512]{0:T(512)S(1)}, f32[512]{0:T(512)}, u32[]{:S(2)}) copy-start(f32[512]{0:T(512)} %get-tuple-element.216) | copy-start | bytes 6148
  130.4 11.1 %slice-start.8 = ((s8[6291456]{0:T(1024)(128)(4,1)}), s8[4194304]{0:T(1024)(128)(4,1)S(1)}, s32[]{:S(2)}) async-start(s8[6291456]{0:T(1024)(128)(4,1)} %bitcast.292), calls=%async_computation.15 | async-start | bytes 8388608
  136.5 5.0 %slice-start.9 = ((s8[6291456]{0:T(1024)(128)(4,1)}), s8[2097152]{0:T(1024)(128)(4,1)S(1)}, s32[]{:S(2)}) async-start(s8[6291456]{0:T(1024)(128)(4,1)} %bitcast.292), calls=%async_computation.16 | async-start | bytes 4194304
  139.2 21.0 %copy-start.28 = (f32[8,128,512]{2,1,0:T(8,128)}, f32[8,128,512]{2,1,0:T(8,128)S(1)}, u32[]{:S(2)}) copy-start(f32[8,128,512]{2,1,0:T(8,128)S(1)} %get-tuple-element.241) | copy-start | bytes 6291460
  143.3 5.2 %copy-start.2 = (bf16[8,128,1536]{2,1,0:T(8,128)(2,1)}, bf16[8,128,1536]{2,1,0:T(8,128)(2,1)S(1)}, u32[]{:S(2)}) copy-start(bf16[8,128,1536]{2,1,0:T(8,128)(2,1)S(1)} %add_convert_fusion.packed_ref) | copy-start | bytes 9437188
  143.3 5.3 %copy-start.105 = (f32[512]{0:T(512)S(1)}, f32[512]{0:T(512)}, u32[]{:S(2)}) copy-start(f32[512]{0:T(512)} %get-tuple-element.211) | copy-start | bytes 6148
  149.6 7.4 %copy-start.35 = (f32[8,128,512]{2,1,0:T(8,128)}, f32[8,128,512]{2,1,0:T(8,128)S(1)}, u32[]{:S(2)}) copy-start(f32[8,128,512]{2,1,0:T(8,128)S(1)} %get-tuple-element.243) | copy-start | bytes 6291460
  150.7 6.3 %copy-start.65 = (bf16[8,128,512]{2,1,0:T(8,128)(2,1)}, bf16[8,128,512]{2,1,0:T(8,128)(2,1)S(1)}, u32[]{:S(2)}) copy-start(bf16[8,128,512]{2,1,0:T(8,128)(2,1)S(1)} %fusion.51) | copy-start | bytes 3145732
  150.8 6.2 %copy-start.104 = (f32[512]{0:T(512)S(1)}, f32[512]{0:T(512)}, u32[]{:S(2)}) copy-start(f32[512]{0:T(512)} %get-tuple-element.206) | copy-start | bytes 6148
  187.9 4.7 %slice-start.10 = ((s8[6291456]{0:T(1024)(128)(4,1)}), s8[4194304]{0:T(1024)(128)(4,1)S(1)}, s32[]{:S(2)}) async-start(s8[6291456]{0:T(1024)(128)(4,1)} %bitcast.298), calls=%async_computation.17 | async-start | bytes 8388608
  190.1 4.9 %slice-start.2 = ((s8[8388608]{0:T(1024)(128)(4,1)}), s8[4194304]{0:T(1024)(128)(4,1)S(1)}, s32[]{:S(2)}) async-start(s8[8388608]{0:T(1024)(128)(4,1)} %bitcast.255), calls=%async_computation.9 | async-start | bytes 8388608
  195.1 6.7 %copy-start.36 = (f32[8,128,512]{2,1,0:T(8,128)S(1)}, f32[8,128,512]{2,1,0:T(8,128)}, u32[]{:S(2)}) copy-start(f32[8,128,512]{2,1,0:T(8,128)} %copy-done.35) | copy-start | bytes 6291460
  230.4 3.7 copy-start.43
  234.1 7.2 %slice-start = ((s8[8388608]{0:T(1024)(128)(4,1)}), s8[4194304]{0:T(1024)(128)(4,1)S(1)}, s32[]{:S(2)}) async-start(s8[8388608]{0:T(1024)(128)(4,1)} %bitcast.253), calls=%async_computation.7 | async-start | bytes 8388608
  236.7 4.6 %copy-start.48 = (bf16[8,128,512]{2,1,0:T(8,128)(2,1)}, bf16[8,128,512]{2,1,0:T(8,128)(2,1)S(1)}, u32[]{:S(2)}) copy-start(bf16[8,128,512]{2,1,0:T(8,128)(2,1)S(1)} %add_convert_fusion.4) | copy-start | bytes 3145732
  236.7 4.6 %slice-start.1 = ((s8[8388608]{0:T(1024)(128)(4,1)}), s8[4194304]{0:T(1024)(128)(4,1)S(1)}, s32[]{:S(2)}) async-start(s8[8388608]{0:T(1024)(128)(4,1)} %bitcast.253), calls=%async_computation.8 | async-start | bytes 8388608
  241.3 7.8 %copy-start.5 = (bf16[8,128,1536]{2,1,0:T(8,128)(2,1)S(1)}, bf16[8,128,1536]{2,1,0:T(8,128)(2,1)}, u32[]{:S(2)}) copy-start(bf16[8,128,1536]{2,1,0:T(8,128)(2,1)} %copy-done.4) | copy-start | bytes 9437188
  249.6 7.2 %copy-start.76 = (f32[1536]{0:T(1024)}, f32[1536]{0:T(1024)S(1)}, u32[]{:S(2)}) copy-start(f32[1536]{0:T(1024)S(1)} %convert_reduce_fusion.2) | copy-start | bytes 18436
  249.7 7.2 %copy-start.34 = (f32[8,128,512]{2,1,0:T(8,128)S(1)}, f32[8,128,512]{2,1,0:T(8,128)}, u32[]{:S(2)}) copy-start(f32[8,128,512]{2,1,0:T(8,128)} %copy-done.33) | copy-start | bytes 6291460
  273.4 4.4 copy-start.77
  278.6 3.5 copy-start.1
  278.6 3.5 copy-start.47
  278.6 3.4 copy-start.79
  282.0 5.7 %copy-start.39 = (bf16[1024,512]{1,0:T(8,128)(2,1)S(1)}, bf16[1024,512]{1,0:T(8,128)(2,1)}, u32[]{:S(2)}) copy-start(bf16[1024,512]{1,0:T(8,128)(2,1)} %copy-done.37) | copy-start | bytes 3145732
  291.6 3.5 slice-start.5
  306.4 3.8 copy-start.40
  306.4 3.8 copy-start.62
  310.1 3.8 copy-start.10
  310.1 3.8 copy-start.11
  316.0 84.2 %copy-start.92 = (s32[2304]{0:T(1024)S(1)}, s32[2304]{0:T(1024)}, u32[]{:S(2)}) copy-start(s32[2304]{0:T(1024)} %eq.69) | copy-start | bytes 27652
  400.2 9.0 %copy-start.68 = (bf16[8,128,512]{2,1,0:T(8,128)(2,1)S(1)}, bf16[8,128,512]{2,1,0:T(8,128)(2,1)}, u32[]{:S(2)}) copy-start(bf16[8,128,512]{2,1,0:T(8,128)(2,1)} %get-tuple-element.204) | copy-start | bytes 3145732
  400.2 9.0 %copy-start.70 = (s32[1024]{0:T(1024)S(1)}, s32[1024]{0:T(1024)}, u32[]{:S(2)}) copy-start(s32[1024]{0:T(1024)} %copy-done.69) | copy-start | bytes 12292
  400.2 9.0 %copy-start.72 = (s32[1024]{0:T(1024)S(1)}, s32[1024]{0:T(1024)}, u32[]{:S(2)}) copy-start(s32[1024]{0:T(1024)} %copy-done.71) | copy-start | bytes 12292
  400.2 9.0 %copy-start.74 = (s32[1024]{0:T(1024)S(1)}, s32[1024]{0:T(1024)}, u32[]{:S(2)}) copy-start(s32[1024]{0:T(1024)} %copy-done.73) | copy-start | bytes 12292
  410.1 3.8 copy-start.22
  410.1 3.8 copy-start.26
  410.1 4.6 %copy-start.18 = (f32[32,2048]{1,0:T(8,128)S(1)}, f32[32,2048]{1,0:T(8,128)}, u32[]{:S(2)}) copy-start(f32[32,2048]{1,0:T(8,128)} %copy-done.17) | copy-start | bytes 786436
  410.1 4.6 %copy-start.20 = (f32[32,2048]{1,0:T(8,128)S(1)}, f32[32,2048]{1,0:T(8,128)}, u32[]{:S(2)}) copy-start(f32[32,2048]{1,0:T(8,128)} %copy-done.19) | copy-start | bytes 786436
  413.9 14.7 %copy-start.75 = (f32[4928]{0:T(1024)S(1)}, f32[4928]{0:T(1024)}, u32[]{:S(2)}) copy-start(f32[4928]{0:T(1024)} %param.25) | copy-start | bytes 59140
  413.9 14.7 %copy-start.84 = (f32[4928]{0:T(1024)S(1)}, f32[4928]{0:T(1024)}, u32[]{:S(2)}) copy-start(f32[4928]{0:T(1024)} %param.29) | copy-start | bytes 59140
  413.9 14.7 %copy-start.85 = (f32[4928]{0:T(1024)S(1)}, f32[4928]{0:T(1024)}, u32[]{:S(2)}) copy-start(f32[4928]{0:T(1024)} %param.33) | copy-start | bytes 59140
  413.9 15.4 %copy-start.9 = (f32[2,32,2048]{2,1,0:T(8,128)S(1)}, f32[2,32,2048]{2,1,0:T(8,128)}, u32[]{:S(2)}) copy-start(f32[2,32,2048]{2,1,0:T(8,128)} %refs_4_.1) | copy-start | bytes 1572868
  415.6 16.4 %copy-start.7 = (f32[2,32,4096]{2,1,0:T(8,128)S(1)}, f32[2,32,4096]{2,1,0:T(8,128)}, u32[]{:S(2)}) copy-start(f32[2,32,4096]{2,1,0:T(8,128)} %refs_5_.1) | copy-start | bytes 3145732
  428.1 4.0 copy-start.57
  428.1 4.0 copy-start.58
  432.0 4.6 %copy-start.42 = (f32[1908,512]{1,0:T(8,128)S(1)}, f32[1908,512]{1,0:T(8,128)}, u32[]{:S(2)}) copy-start(f32[1908,512]{1,0:T(8,128)} %get-tuple-element.128) | copy-start | bytes 11722756
  (62 other events, 111.5 us)
Sparse Core Ops, SparseCore 0:
  230.5 82.8 reduce-scatter.1

commit v7 on v6

--- a/solution.py
+++ b/solution.py
@@ -186,16 +186,18 @@
     )(*arrays)
 
 
-def gradient_kernel(chunks, count, *refs):
+def gradient_kernel(chunks, matrices, vec_len, *refs):
     take = iter(refs)
-    parts = [next(take) for _ in range(count)]
-    sums_ref, near_ref = next(take), next(take)
-    totals = [next(take) for _ in range(count)]
-    rows_ref, near_out = next(take), next(take)
+    pairs = [(next(take), next(take)) for _ in range(matrices)]
+    vec_ref, sums_ref, near_ref, asked_ref, extra_ref = [next(take) for _ in range(5)]
+    attn_out, ffn_out, word_out, vec_out, stats_out = [next(take) for _ in range(5)]
+    held = [None if m is None else next(take) for m, _, _ in chunks]
     bufs = [[next(take) for _ in range(5)] for _ in chunks]
-    near_buf = next(take)
+    near_buf, rows_ref, added, square_ref, squares_ref = [next(take) for _ in range(5)]
     send_a, recv_a, send_y, recv_y, send_z, recv_z, send_x, recv_x = [next(take) for _ in range(8)]
-    row_send, row_recv, pass_send, pass_recv, near_sem = [next(take) for _ in range(5)]
+    row_send, row_recv, pass_send, pass_recv, near_sem, extra_sem, square_sem = [
+        next(take) for _ in range(7)
+    ]
 
     d = lax.axis_index("dp")
     z = lax.axis_index("zero")
@@ -204,6 +206,7 @@
     line = z // 4
     sibling = z + 1 - 2 * core
     across = z + 2 - 4 * col
+    attn_width = attn_out.shape[2]
 
     def along(k):
         return lax.rem(line + k, 4) * 4 + lax.rem(z, 4)
@@ -230,9 +233,11 @@
             device_id_type=MESH,
         )
 
+    def part_of(i):
+        return vec_ref if held[i] is None else held[i]
+
     def copy_a(i):
-        part, start, width = chunks[i]
-        src = parts[part].at[:, :, 1 - core, :, pl.ds(start, width)]
+        src = part_of(i).at[:, :, 1 - core]
         return remote(src, bufs[i][0], send_a.at[i], recv_a.at[i], (d, sibling))
 
     def copy_y(i):
@@ -259,10 +264,10 @@
         )
 
     near = remote(near_ref, near_buf, near_sem.at[0], near_sem.at[1], (1 - d, z))
+    extra = pltpu.make_async_copy(extra_ref, word_out, extra_sem)
+    extra.start()
 
     total = len(chunks)
-    for i in range(total):
-        copy_a(i).start()
 
     def push(k, carry):
         row_push(k).start()
@@ -273,15 +278,32 @@
     rows_ref[d, z] = sums_ref[z]
     row_pass(0).start()
 
+    def compute(i):
+        matrix, start, width = chunks[i]
+        if matrix is not None:
+            left, right = pairs[matrix]
+
+            def rows_of(j, carry):
+                at = pl.ds(pl.multiple_of(j * 128, 128), 128)
+                found = lax.dot_general(
+                    left[:, at],
+                    right[:, start : start + width],
+                    (((0,), (0,)), ((), ())),
+                    preferred_element_type=jnp.float32,
+                )
+                held[i][j] = found.astype(jnp.bfloat16).reshape(2, 2, 32, width)
+                return carry
+
+            lax.fori_loop(0, 4, rows_of, 0)
+        copy_a(i).start()
+
     def stage_a(i):
-        part, start, width = chunks[i]
         copy_a(i).wait_recv()
-
         buf = bufs[i][0]
 
         def add_block(b, carry):
             line_at, col_at = b // 2, lax.rem(b, 2)
-            mine = parts[part][line_at, col_at, core, :, pl.ds(start, width)].astype(jnp.float32)
+            mine = part_of(i)[line_at, col_at, core].astype(jnp.float32)
             got = buf[line_at, col_at].astype(jnp.float32)
             buf[line_at, col_at] = (mine + got).astype(buf.dtype)
             return carry
@@ -312,18 +334,44 @@
         copy_x(i).start()
 
     def stage_x(i):
-        part, start, width = chunks[i]
+        matrix, start, width = chunks[i]
         copy_x(i).wait_recv()
-        totals[part][:, pl.ds(start, width)] = bufs[i][3][...].astype(jnp.float32) + bufs[i][4][
-            ...
-        ].astype(jnp.float32)
+        value = bufs[i][3][...].astype(jnp.float32) + bufs[i][4][...].astype(jnp.float32)
+        if matrix is None:
+            vec_out[...] = value
+        else:
+            first = start + sum(pairs[m][1].shape[1] for m in range(matrix))
+            if first < attn_width:
+                attn_out[0, :, first : first + width] = value
+            else:
+                ffn_out[0, :, first - attn_width : first - attn_width + width] = value
 
     def pass_on(k):
         row_push(k).wait_recv()
         row_pass(k).start()
 
+    tiles = added.shape[0] // 128
+    spots = rows_ref.shape[1] * rows_ref.shape[2]
+
+    def into_rows(plane, tile):
+        lane = lax.broadcasted_iota(jnp.int32, (1, 128), 1) + tile * 128
+        picked = (asked_ref[plane] == lane).astype(jnp.bfloat16)
+        return lax.dot_general(
+            picked,
+            rows_ref[plane].reshape(spots, rows_ref.shape[3]),
+            (((0,), (0,)), ((), ())),
+            preferred_element_type=jnp.float32,
+        )
+
+    def own_plane(tile, carry):
+        added[pl.ds(pl.multiple_of(tile * 128, 128), 128), :] = into_rows(d, tile)
+        return carry
+
+    compute(0)
     passed = 1
     for t in range(total + 3):
+        if t + 1 < total:
+            compute(t + 1)
         if t < total:
             stage_a(t)
         if 0 <= t - 1 < total:
@@ -332,15 +380,82 @@
             stage_z(t - 2)
         if 0 <= t - 3 < total:
             stage_x(t - 3)
-        until = min(16, 1 + (t + 1) * 15 // (total + 3))
+        until = min(16, 1 + (t + 1) * 15 // (total - 1))
         for k in range(passed, until):
             pass_on(k)
         passed = until
-    for k in range(passed, 16):
-        pass_on(k)
+        if t == total - 1:
+            lax.fori_loop(0, tiles, own_plane, 0)
 
     near.wait()
-    near_out[...] = near_ref[...].astype(jnp.float32) + near_buf[...].astype(jnp.float32)
+    attn_out[1] = near_ref[:, :attn_width].astype(jnp.float32) + near_buf[:, :attn_width].astype(
+        jnp.float32
+    )
+    ffn_out[1] = near_ref[:, attn_width:].astype(jnp.float32) + near_buf[:, attn_width:].astype(
+        jnp.float32
+    )
+
+    def arrived(k, carry):
+        at = lax.rem(z + 16 - k, 16)
+        ref = rows_ref.at[1 - d, at]
+        remote(ref, ref, pass_send.at[k], pass_recv.at[k], (1 - d, z)).wait_recv()
+        return carry
+
+    lax.fori_loop(0, 16, arrived, 0)
+    extra.wait()
+    features = word_out.shape[1]
+
+    def add_rows(tile, count, first):
+        at = pl.ds(first, count)
+        value = (added[at, :] + into_rows(1 - d, tile)[:count]) + word_out[at, :]
+        word_out[at, :] = value
+        return jnp.sum(value * value, axis=0, keepdims=True)
+
+    full = word_out.shape[0] // 128
+
+    def other_plane(tile, carry):
+        return carry + add_rows(tile, 128, pl.multiple_of(tile * 128, 128))
+
+    squares = lax.fori_loop(0, full, other_plane, jnp.zeros((1, features), jnp.float32))
+    if word_out.shape[0] % 128:
+        squares = squares + add_rows(full, word_out.shape[0] % 128, full * 128)
+    square = jnp.sum(squares, axis=1, keepdims=True)
+    for out in (attn_out, ffn_out):
+
+        def of_rows(r, carry, out=out):
+            at = pl.ds(pl.multiple_of(r * 8, 8), 8)
+            for layer in range(out.shape[0]):
+                value = out[layer, at, :]
+                carry = carry + jnp.sum(value * value, axis=0, keepdims=True)
+            return carry
+
+        found = lax.fori_loop(
+            0, out.shape[1] // 8, of_rows, jnp.zeros((1, out.shape[2]), jnp.float32)
+        )
+        square = square + jnp.sum(found, axis=1, keepdims=True)
+    place = lax.broadcasted_iota(jnp.int32, vec_out.shape, 0) * 128 + lax.broadcasted_iota(
+        jnp.int32, vec_out.shape, 1
+    )
+    value = jnp.where(place < vec_len, vec_out[...], 0.0)
+    found = jnp.sum(value * value, axis=0, keepdims=True)
+    square = square + jnp.sum(found, axis=1, keepdims=True)
+    square_ref[...] = jnp.broadcast_to(square, square_ref.shape)
+
+    def square_copy(k, slot):
+        return remote(
+            square_ref,
+            squares_ref.at[slot],
+            square_sem.at[0, k],
+            square_sem.at[1, k],
+            (d, lax.rem(z + k, 16)),
+        )
+
+    def send_square(k, carry):
+        square_copy(k, z).start()
+        return carry
+
+    lax.fori_loop(1, 16, send_square, 0)
+    squares_ref[z] = square_ref[...]
 
     for i in range(total):
         copy_a(i).wait_send()
@@ -351,60 +466,81 @@
 
     def finish(k, carry):
         row_push(k).wait_send()
+        square_copy(k, lax.rem(z + 16 - k, 16)).wait_recv()
+        square_copy(k, z).wait_send()
         return carry
 
     lax.fori_loop(1, 16, finish, 0)
 
     def finish_pass(k, carry):
         row_pass(k).wait_send()
-        at = lax.rem(z + 16 - k, 16)
-        remote(
-            rows_ref.at[1 - d, at], rows_ref.at[1 - d, at], pass_send.at[k], pass_recv.at[k], (1 - d, z)
-        ).wait_recv()
         return carry
 
     lax.fori_loop(0, 16, finish_pass, 0)
-
-
-def exchange_gradients(parts, sums, near, collective_id):
-    chunks = []
-    for index, part in enumerate(parts):
-        width = part.shape[4] // -(-part.shape[4] // 1024)
-        for start in range(0, part.shape[4], width):
+    norm = squares_ref[0]
+    for slot in range(1, 16):
+        norm = norm + squares_ref[slot]
+    norm = jnp.sqrt(norm)
+    stats_out[0:1, :] = norm
+    stats_out[1:2, :] = jnp.minimum(1.0, CLIP_NORM / (norm + 1e-06))
+
+
+def exchange_gradients(pairs, vec_parts, sums, near, asked, extra, vec_len, collective_id):
+    chunks = [(None, 0, 128)]
+    for index in (3, 2, 0, 1):
+        columns = pairs[index][1].shape[1]
+        width = columns // -(-columns // 1024)
+        for start in range(0, columns, width):
             chunks.append((index, start, width))
     half = jnp.bfloat16
-    scratch = []
+    held, bufs = [], []
     for index, start, width in chunks:
-        r = parts[index].shape[3]
-        scratch += [
-            pltpu.VMEM((4, 2, r, width), parts[index].dtype),
-            pltpu.VMEM((4, r, width), parts[index].dtype),
-            pltpu.VMEM((3, r, width), parts[index].dtype),
-            pltpu.VMEM((r, width), parts[index].dtype),
-            pltpu.VMEM((r, width), parts[index].dtype),
+        kind = vec_parts.dtype if index is None else half
+        r = vec_parts.shape[3] if index is None else 32
+        if index is not None:
+            held.append(pltpu.VMEM((4, 2, 2, r, width), kind))
+        bufs += [
+            pltpu.VMEM((4, 2, r, width), kind),
+            pltpu.VMEM((4, r, width), kind),
+            pltpu.VMEM((3, r, width), kind),
+            pltpu.VMEM((r, width), kind),
+            pltpu.VMEM((r, width), kind),
         ]
-    scratch += [pltpu.VMEM(near.shape, half)]
+    shard_rows, features = extra.shape
     dma = pltpu.SemaphoreType.DMA
     count = len(chunks)
+    scratch = held + bufs
+    scratch += [
+        pltpu.VMEM(near.shape, half),
+        pltpu.VMEM((2,) + sums.shape, half),
+        pltpu.VMEM((-(-shard_rows // 128) * 128, features), jnp.float32),
+        pltpu.VMEM((1, 128), jnp.float32),
+        pltpu.VMEM((16, 1, 128), jnp.float32),
+    ]
     scratch += [dma((count,)) for _ in range(4)] + [dma((count, 3)) for _ in range(2)]
     scratch += [dma((count,)) for _ in range(2)]
-    scratch += [dma((16,)) for _ in range(4)] + [dma((2,))]
-    outs = [jax.ShapeDtypeStruct(part.shape[3:], jnp.float32) for part in parts]
-    outs += [jax.ShapeDtypeStruct((2,) + sums.shape, sums.dtype)]
-    outs += [jax.ShapeDtypeStruct(near.shape, jnp.float32)]
+    scratch += [dma((16,)) for _ in range(4)] + [dma((2,)), dma, dma((2, 16))]
+    rows = near.shape[0]
+    outs = [
+        jax.ShapeDtypeStruct((2, rows, 4 * D), jnp.float32),
+        jax.ShapeDtypeStruct((2, rows, 2 * FF), jnp.float32),
+        jax.ShapeDtypeStruct(extra.shape, jnp.float32),
+        jax.ShapeDtypeStruct(vec_parts.shape[3:], jnp.float32),
+        jax.ShapeDtypeStruct((8, 128), jnp.float32),
+    ]
     vmem = pl.BlockSpec(memory_space=pltpu.VMEM)
     return pl.pallas_call(
-        functools.partial(gradient_kernel, tuple(chunks), len(parts)),
+        functools.partial(gradient_kernel, tuple(chunks), len(pairs), vec_len),
         out_shape=tuple(outs),
-        in_specs=[vmem] * (len(parts) + 2),
+        in_specs=[vmem] * (2 * len(pairs) + 4) + [pl.BlockSpec(memory_space=pl.ANY)],
         out_specs=tuple([vmem] * len(outs)),
         scratch_shapes=scratch,
         compiler_params=pltpu.CompilerParams(
-            collective_id=collective_id, has_side_effects=True, vmem_limit_bytes=48 * 1024 * 1024
+            collective_id=collective_id, has_side_effects=True, vmem_limit_bytes=58 * 1024 * 1024
         ),
         cost_estimate=pl.CostEstimate(flops=0, bytes_accessed=200_000_000, transcendentals=0),
         name="exchange_gradients",
-    )(*parts, sums, near)
+    )(*[array for pair in pairs for array in pair], vec_parts, sums, near, asked, extra)
 
 
 SPLITS = 4
@@ -414,10 +550,10 @@
 
 def start_kernel(shard_rows, room, *refs):
     column_ref, row_ref, packet_ref, vec_ref, attn_ref, ffn_ref, word_ref = refs[:7]
-    place_out, packet_out, asked_out, vec_out, rows_out, *weight_outs = refs[7:14]
-    table, rows_held, asked, slots, locals_ = refs[14:19]
-    packet_sem, asked_sem, vec_sem, row_sem = refs[19:23]
-    z_sem, y_sem, x_sem, d_sem, e_sem, own_sem = refs[23:]
+    place_out, slot_out, packet_out, asked_out, vec_out, rows_out, *weight_outs = refs[7:15]
+    table, rows_held, asked, slots, locals_ = refs[15:20]
+    packet_sem, asked_sem, vec_sem, row_sem = refs[20:24]
+    z_sem, y_sem, x_sem, d_sem, e_sem, own_sem = refs[24:]
 
     d = lax.axis_index("dp")
     z = lax.axis_index("zero")
@@ -562,6 +698,7 @@
         place_out[at, :] = place.astype(jnp.int32)
         inside = place < room
         slots[at, :] = jnp.where(inside, owner * 128 + place.astype(jnp.int32), -1)
+        slot_out[at, :] = jnp.where(inside, owner * room + place.astype(jnp.int32), -1)
         locals_[at, :] = (ids - low_id).astype(jnp.float32)
         return jnp.maximum(most, jnp.max(place, axis=0, keepdims=True))
 
@@ -717,6 +854,7 @@
         functools.partial(start_kernel, shard_rows, room),
         out_shape=(
             jax.ShapeDtypeStruct((tokens, 1), jnp.int32),
+            jax.ShapeDtypeStruct((tokens, 1), jnp.int32),
             jax.ShapeDtypeStruct((32,) + packet.shape, packet.dtype),
             jax.ShapeDtypeStruct((32, 1, 128), jnp.int32),
             jax.ShapeDtypeStruct((16,) + vec_rows.shape, vec_rows.dtype),
@@ -724,7 +862,7 @@
         )
         + (jax.ShapeDtypeStruct((16, rows, 3 * width), half),) * layers,
         in_specs=[vmem] * 7,
-        out_specs=tuple([vmem] * (5 + layers)),
+        out_specs=tuple([vmem] * (6 + layers)),
         scratch_shapes=[
             pltpu.VMEM((padded, features), half),
             pltpu.VMEM((16, room, features), half),
@@ -1027,28 +1165,6 @@
     )(mask, *operands)
 
 
-@jax.custom_vjp
-def attend(packed, mask):
-    return attend_forward(packed, mask)[0]
-
-
-def attend_forward(packed, mask):
-    half = packed.astype(jnp.bfloat16)
-    context = attention_call(attention_kernel, mask, [half], D, "attention")
-    return context.astype(jnp.float32), (half, mask)
-
-
-def attend_backward(kept, grad):
-    half, mask = kept
-    d_packed = attention_call(
-        attention_back_kernel, mask, [half, grad.astype(jnp.bfloat16)], 3 * D, "attention_back"
-    )
-    return d_packed.astype(jnp.float32), jnp.zeros_like(mask)
-
-
-attend.defvjp(attend_forward, attend_backward)
-
-
 LAYER_ROWS = 8 + FF // D
 
 
@@ -1067,20 +1183,115 @@
     return layer_norm(low_back(rows) + vectors[None, :SEQ], vectors[SEQ], vectors[SEQ + 1])
 
 
-def encoder_layer(hidden, weights, vectors, mask):
+def norm_forward(values, gain, shift):
+    center = values - jnp.mean(values, axis=-1, keepdims=True)
+    inverse = lax.rsqrt(jnp.mean(center * center, axis=-1, keepdims=True) + NORM_EPS)
+    normal = center * inverse
+    return normal * gain + shift, normal, inverse
+
+
+def norm_back(grad, normal, inverse, gain):
+    scaled = grad * gain
+    mean = jnp.mean(scaled, axis=-1, keepdims=True)
+    along = jnp.mean(scaled * normal, axis=-1, keepdims=True)
+    return (
+        (scaled - mean - normal * along) * inverse,
+        jnp.sum(grad * normal, axis=(0, 1)),
+        jnp.sum(grad, axis=(0, 1)),
+    )
+
+
+GELU_SCALE = 0.7978845608028654
+
+
+def gelu(value):
+    bent = jnp.tanh(GELU_SCALE * (value + 0.044715 * value * value * value))
+    return 0.5 * value * (1.0 + bent)
+
+
+def gelu_slope(value):
+    square = value * value
+    bent = jnp.tanh(GELU_SCALE * (value + 0.044715 * square * value))
+    inner = GELU_SCALE * (1.0 + 3.0 * 0.044715 * square)
+    return 0.5 * (1.0 + bent) + 0.5 * value * (1.0 - bent * bent) * inner
+
+
+def layer_forward(hidden, weights, vectors, mask):
     in_weights, out_weights, up_weights, down_weights = weights
     q_bias, v_bias, o_bias, gain_one, shift_one, up_bias, down_bias, gain_two, second_shift = (
         layer_vectors(vectors)
     )
-    packed = matmul(low(hidden), in_weights)
-    packed = packed + jnp.concatenate([q_bias, jnp.zeros_like(q_bias), v_bias])
-    context = attend(packed, mask)
-    attended = low_back(matmul(context, out_weights) + o_bias)
-    first_out = layer_norm(hidden + attended, gain_one, shift_one)
-    upward = low_back(matmul(low(first_out), up_weights) + up_bias)
-    active = rounded(jax.nn.gelu(upward, approximate=True))
-    downward = low_back(einsum_plain("nsf,df->nsd", active, down_weights) + down_bias)
-    return layer_norm(first_out + downward, gain_two, second_shift)
+    half = jnp.bfloat16
+    entry = hidden.astype(half)
+    bias = jnp.concatenate([q_bias, jnp.zeros_like(q_bias), v_bias])
+    packed = (matmul(entry, in_weights) + bias).astype(half)
+    context = attention_call(attention_kernel, mask, [packed], D, "attention")
+    attended = matmul(context, out_weights) + o_bias
+    first, normal_one, inverse_one = norm_forward(hidden + attended, gain_one, shift_one)
+    middle = first.astype(half)
+    upward = matmul(middle, up_weights) + up_bias
+    active = gelu(upward).astype(half)
+    downward = einsum_plain("nsf,df->nsd", active, down_weights) + down_bias
+    output, normal_two, inverse_two = norm_forward(first + downward, gain_two, second_shift)
+    kept = (
+        entry, packed, context, middle, upward, active,
+        normal_one, inverse_one, normal_two, inverse_two,
+    )
+    return output, kept
+
+
+def layer_backward(kept, weights, vectors, mask, grad):
+    in_weights, out_weights, up_weights, down_weights = weights
+    entry, packed, context, middle, upward, active = kept[:6]
+    normal_one, inverse_one, normal_two, inverse_two = kept[6:]
+    gain_one, gain_two = layer_vectors(vectors)[3], layer_vectors(vectors)[7]
+    half = jnp.bfloat16
+
+    def total(value):
+        return jnp.sum(value.astype(jnp.float32), axis=(0, 1))
+
+    d_second, d_gain_two, d_shift_two = norm_back(grad, normal_two, inverse_two, gain_two)
+    d_down = d_second.astype(half)
+    d_active = jnp.einsum("nsd,df->nsf", d_down, down_weights, preferred_element_type=jnp.float32)
+    d_active = d_active.astype(half).astype(jnp.float32)
+    d_up = (d_active * gelu_slope(upward)).astype(half)
+    d_first = d_second + jnp.einsum(
+        "nsf,df->nsd", d_up, up_weights, preferred_element_type=jnp.float32
+    )
+    d_middle, d_gain_one, d_shift_one = norm_back(d_first, normal_one, inverse_one, gain_one)
+    d_attended = d_middle.astype(half)
+    d_context = jnp.einsum(
+        "nsd,ed->nse", d_attended, out_weights, preferred_element_type=jnp.float32
+    ).astype(half)
+    d_packed = attention_call(
+        attention_back_kernel, mask, [packed, d_context], 3 * D, "attention_back"
+    )
+    d_hidden = d_middle + jnp.einsum(
+        "nsp,dp->nsd", d_packed, in_weights, preferred_element_type=jnp.float32
+    )
+    packed_total = total(d_packed)
+    pieces = [
+        packed_total[:D], packed_total[2 * D :], total(d_attended), d_gain_one, d_shift_one,
+        total(d_up), total(d_down), d_gain_two, d_shift_two,
+    ]
+    d_vectors, at = jnp.zeros((LAYER_ROWS, D), jnp.float32), 0
+    for piece in pieces:
+        rows = piece.reshape(-1, D)
+        d_vectors = d_vectors + jnp.pad(rows, ((at, LAYER_ROWS - at - rows.shape[0]), (0, 0)))
+        at = at + rows.shape[0]
+    flat = [
+        (left.reshape(-1, left.shape[2]), right.reshape(-1, right.shape[2]))
+        for left, right in (
+            (entry, d_packed), (context, d_attended), (middle, d_up), (d_down, active)
+        )
+    ]
+    return d_hidden, flat, d_vectors
+
+
+def weight_gradient(left, right):
+    return lax.dot_general(
+        left, right, (((0,), (0,)), ((), ())), preferred_element_type=jnp.float32
+    ).astype(jnp.bfloat16)
 
 
 def pool_rows(hidden, key_mask, seq_lengths):
@@ -1219,7 +1430,7 @@
 
     if by_hand:
         packet = pad_rows(jnp.concatenate([false_neg.reshape(-1), pair_index]), 8)
-        place, packets, asked_mine, vec_parts, received, *gathered = exchange_start(
+        place, slot, packets, asked_mine, vec_parts, received, *gathered = exchange_start(
             ids,
             packet.astype(jnp.bfloat16),
             pad_rows(vectors.astype(jnp.bfloat16), 16),
@@ -1235,9 +1446,7 @@
         packets = packets.reshape(n, -1).astype(jnp.int32)
         false_all = packets[:, : false_neg.size].reshape(total_pairs, total_pairs)
         pair_all = packets[:, false_neg.size : false_neg.size + pair_rows].reshape(total_pairs)
-        owner = ids // shard_rows
-        place, local_row = place.reshape(-1), ids - owner * shard_rows
-        slot = jnp.where(place < room, owner * room + place, -1)
+        place, slot = place.reshape(-1), slot.reshape(-1)
     else:
         owner, place, local_row = token_plan(ids, shard_rows)
         slot, asked = round_slots(owner, place, local_row, 0, room, nz)
@@ -1262,9 +1471,8 @@
     asked_near = lax.dynamic_slice_in_dim(asked_mine, my_dp * nz, nz, 0)
 
     def rows_for(wanted):
-        table, wanted = lax.optimization_barrier((word_table, wanted))
         picked = one_hot(wanted.reshape(-1), shard_rows)
-        return matmul(picked, table.astype(jnp.bfloat16)).astype(jnp.bfloat16)
+        return matmul(picked, word_table.astype(jnp.bfloat16)).astype(jnp.bfloat16)
 
     def rows_from(slot_now, received):
         return matmul(one_hot(slot_now, nz * room), received.reshape(nz * room, D)).astype(
@@ -1277,14 +1485,29 @@
         )
     rows = rows_from(slot, received)
 
+    def round_of(round_index):
+        owner = ids // shard_rows
+        local_row = ids - owner * shard_rows
+        return round_slots(owner, place, local_row, round_index, room, nz)
+
     def more_rows(state):
         round_index, rows_now = state
-        slot_now, asked_now = round_slots(owner, place, local_row, round_index, room, nz)
+        slot_now, asked_now = round_of(round_index)
         wanted = lax.all_to_all(asked_now.reshape(nz, room), "zero", 0, 0, tiled=True)
         got = lax.all_to_all(rows_for(wanted).reshape(nz, room, D), "zero", 0, 0, tiled=True)
         return round_index + 1, rows_now + rows_from(slot_now, got)
 
-    _, rows = lax.while_loop(lambda state: state[0] < rounds, more_rows, (jnp.int32(1), rows))
+    def further(step, value):
+        return lax.cond(
+            rounds > 1,
+            lambda now: lax.while_loop(
+                lambda state: state[0] < rounds, step, (jnp.int32(1), now)
+            )[1],
+            lambda now: now,
+            value,
+        )
+
+    rows = further(more_rows, rows)
     rows = rows.reshape(seq_rows, SEQ, D).astype(jnp.float32)
 
     vec_rows = vec_all.reshape(-1, D)
@@ -1294,18 +1517,15 @@
     hidden = embedded
     mask = key_mask.astype(jnp.float32)[:, None, :]
     saved = []
+    layer_parts = []
     pooled = []
     for layer_index in range(LAYERS):
         weights = layer_weights[layer_index]
         edges = (0, 3 * D, 4 * D, 4 * D + FF, 4 * D + 2 * FF)
-        parts = [
-            weights[:, first:last].astype(jnp.float32) for first, last in zip(edges, edges[1:])
-        ]
-        output, layer_back = jax.vjp(
-            functools.partial(encoder_layer, mask=mask), hidden, parts, vec_parts[1 + layer_index]
-        )
-        saved.append(layer_back)
-        hidden = output
+        parts = [weights[:, first:last] for first, last in zip(edges, edges[1:])]
+        layer_parts.append(parts)
+        hidden, kept = layer_forward(hidden, parts, vec_parts[1 + layer_index], mask)
+        saved.append(kept)
         pooled.append(pool_rows(hidden, key_mask, seq_lengths).astype(jnp.bfloat16))
 
     if by_hand and pair_rows == 4:
@@ -1344,13 +1564,17 @@
             grad_hidden = grad_hidden + deep_back[:, None, :] * share[:, :, None]
         if layer_index == 0:
             grad_hidden = grad_hidden + shallow_back[:, None, :] * share[:, :, None]
-        layer_back = saved[layer_index]
-        grad_hidden, part_grads, vec_grads[layer_index] = layer_back(grad_hidden)
-        part_grads = [part.astype(jnp.bfloat16) for part in part_grads]
+        grad_hidden, pairs, vec_grads[layer_index] = layer_backward(
+            saved[layer_index],
+            layer_parts[layer_index],
+            vec_parts[1 + layer_index],
+            mask,
+            grad_hidden,
+        )
         if by_hand and layer_index == 0:
-            weight_parts.insert(0, part_grads)
+            weight_parts.insert(0, pairs)
         else:
-            both = jnp.concatenate(part_grads, axis=1)
+            both = jnp.concatenate([weight_gradient(*pair) for pair in pairs], axis=1)
             both, grad_hidden = lax.optimization_barrier((both, grad_hidden))
             weight_parts.insert(0, lax.psum_scatter(both, "zero", scatter_dimension=0, tiled=True))
     rows_grad, embed_grads = embed_back(grad_hidden)
@@ -1379,17 +1603,30 @@
     lines = -(-vec_blocks.shape[1] // 1024) * 8
     vec_blocks = jnp.pad(vec_blocks, ((0, 0), (0, lines * 128 - vec_blocks.shape[1])))
     sums = slot_sums(slot).reshape(nz, room, D)
+
+    def more_sums(state):
+        round_index, grad_now = state
+        slot_now, asked_now = round_of(round_index)
+        wanted = lax.all_to_all(asked_now.reshape(nz, room), "zero", 0, 0, tiled=True)
+        got = lax.all_to_all(slot_sums(slot_now).reshape(nz, room, D), "zero", 0, 0, tiled=True)
+        wanted = lax.all_gather(wanted, "dp", axis=0, tiled=True)
+        got = lax.all_gather(got, "dp", axis=0, tiled=True)
+        return round_index + 1, grad_now + into_rows(wanted, got)
+
     if by_hand:
-        *near, vec_near, sums_all, other_near = exchange_gradients(
-            [part.reshape(4, 2, 2, -1, part.shape[1]) for part in weight_parts[0]]
-            + [vec_blocks.reshape(4, 2, 2, lines, 128)],
+        extra = further(more_sums, jnp.zeros((shard_rows, D), jnp.float32))
+        attn_shard, ffn_shard, word_grad, vec_sum, stats = exchange_gradients(
+            weight_parts[0],
+            vec_blocks.reshape(4, 2, 2, lines, 128),
             sums,
             weight_parts[1],
+            asked_mine.reshape(ndp, nz * room, 1),
+            extra,
+            vec_len,
             3,
         )
-        attn_shard = jnp.stack([jnp.concatenate(near[:2], axis=1), other_near[:, : 4 * D]])
-        ffn_shard = jnp.stack([jnp.concatenate(near[2:], axis=1), other_near[:, 4 * D :]])
-        vec_sum = vec_near.reshape(-1)
+        vec_sum = vec_sum.reshape(-1)
+        grad_norm, factor = stats[0, 0], stats[1, 0]
     else:
         sums_all, vec_shares = exchange(
             [sums, vec_blocks.reshape(nz, lines, 128)],
@@ -1404,31 +1641,19 @@
         weight_sum = jnp.sum(weight_all.astype(jnp.float32), axis=0)
         attn_shard = weight_sum[:, :, : 4 * D]
         ffn_shard = weight_sum[:, :, 4 * D :]
-    word_grad = into_rows(asked_mine, sums_all)
-
-    def more_sums(state):
-        round_index, grad_now = state
-        slot_now, asked_now = round_slots(owner, place, local_row, round_index, room, nz)
-        wanted = lax.all_to_all(asked_now.reshape(nz, room), "zero", 0, 0, tiled=True)
-        got = lax.all_to_all(slot_sums(slot_now).reshape(nz, room, D), "zero", 0, 0, tiled=True)
-        wanted = lax.all_gather(wanted, "dp", axis=0, tiled=True)
-        got = lax.all_gather(got, "dp", axis=0, tiled=True)
-        return round_index + 1, grad_now + into_rows(wanted, got)
-
-    _, word_grad = lax.while_loop(
-        lambda state: state[0] < rounds, more_sums, (jnp.int32(1), word_grad)
-    )
+        word_grad = further(more_sums, into_rows(asked_mine, sums_all))
     vec_shard = vec_sum[:vec_len]
     down_shard = vec_sum[vec_len : vec_len + down_len].reshape(LAYERS, -1)
 
-    square_local = jnp.sum(word_grad * word_grad) + jnp.sum(vec_shard * vec_shard)
-    square_local = square_local + jnp.sum(attn_shard * attn_shard) + jnp.sum(ffn_shard * ffn_shard)
-    (squares,) = exchange(
-        [jnp.broadcast_to(square_local, (8, 128))], ["zero"], ndp, nz, 5, "gather_squares"
-    )
-    square_total = jnp.sum(squares[:, 0, 0])
-    grad_norm = jnp.sqrt(square_total)
-    factor = jnp.minimum(1.0, CLIP_NORM / (grad_norm + 1e-06))
+    if not by_hand:
+        square_local = jnp.sum(word_grad * word_grad) + jnp.sum(vec_shard * vec_shard)
+        square_local = square_local + jnp.sum(attn_shard * attn_shard)
+        square_local = square_local + jnp.sum(ffn_shard * ffn_shard)
+        (squares,) = exchange(
+            [jnp.broadcast_to(square_local, (8, 128))], ["zero"], ndp, nz, 5, "gather_squares"
+        )
+        grad_norm = jnp.sqrt(jnp.sum(squares[:, 0, 0]))
+        factor = jnp.minimum(1.0, CLIP_NORM / (grad_norm + 1e-06))
     word_new, word_first_new, word_second_new = adam_update(
         word_table, word_grad * factor, word_first, word_second, LEARN_RATE
     )

time: 461 us -> 509 us (1.10)
  waiting for transfers between devices: 0.02 us -> 75.6 us
  other arithmetic: 80.7 us -> 54.5 us
  Pallas kernels: 239 us -> 253 us
  matrix products: 87.9 us -> 74.7 us
  loops' own time: 1.73 us -> 12.1 us
  local copies, waits for them, and re-layouts: 23.3 us -> 15.4 us
    reduce_scatter x1, waiting for transfers between devices: 0.01 us -> 75 us  [body(): lax.psum_scatter(both, 'zero', scatter_dimension=0, tiled=True)]
    dot_general x19 -> x7, matrix products: 57.6 us -> 18.2 us  [matmul(): return jnp.dot(left, right, preferred_element_type=jnp.float32)]
    dot_general x1 -> x12, matrix products: 8.94 us -> 47.4 us  [the longest x2 19.8 us: layer_backward(): jnp.einsum('nsd,df->nsf', d_down, down_weights, preferred_element_type=jn...]
    pallas_call x2 -> x4, Pallas kernels: 12.6 us -> 30.1 us  [attention_call(): pl.pallas_call(kernel, grid=(count,), out_shape=jax.ShapeDtypeStruct((cou...]
    convert_element_type x7 -> x1, other arithmetic: 19 us -> 3.53 us  [low_back(): return build_low_back()(value)]
    dot_general x6 -> x2, matrix products: 18.6 us -> 6.4 us  [einsum_plain(): return jnp.einsum(form, left, right, preferred_element_type=jnp.float32)]
    unnamed x250 -> x134, local copies, waits for them, and re-layouts: 17.4 us -> 6.89 us
    another operation x2, loops' own time: 1.73 us -> 12.1 us  [further(): lax.cond(rounds > 1, lambda now: lax.while_loop(lambda state: state[0] <...]
  transfers between devices with their start and end apart: 1 -> 1, of which waited for: 0 -> 1; matrix products, arithmetic and copies ran while one was open for 15% -> 2% of each run, Pallas kernels for 2% -> 0%
where the time goes in v7:
time: 509 us; the launch traced here: 502 us
  Pallas kernels  253 us (50%)
  waiting for transfers between devices  75.6 us (15%)
  matrix products  74.7 us (15%)
  other arithmetic  54.5 us (11%)
  between operations  16.6 us (3%)
  local copies, waits for them, and re-layouts  15.4 us (3%)
  loops' own time  12.1 us (2%)
    pallas_call x1, Pallas kernels, exchange_gradients(): pl.pallas_call(functools.partial(gradient_kernel, tuple(chunks), len(pair...  107 us
    pallas_call x1, Pallas kernels, exchange_start(): pl.pallas_call(functools.partial(start_kernel, shard_rows, room), out_sha...  92.3 us
    reduce_scatter x1, waiting for transfers between devices, body(): lax.psum_scatter(both, 'zero', scatter_dimension=0, tiled=True)  75 us
    pallas_call x4, Pallas kernels, attention_call(): pl.pallas_call(kernel, grid=(count,), out_shape=jax.ShapeDtypeStruct((cou...  30.1 us
    pallas_call x1, Pallas kernels, contrastive(): pl.pallas_call(contrastive_kernel, out_shape=(jax.ShapeDtypeStruct((8, 12...  23.6 us
    dot_general x2, matrix products, layer_backward(): jnp.einsum('nsd,df->nsf', d_down, down_weights, preferred_element_type=jn...  19.8 us
    dot_general x7, matrix products, matmul(): return jnp.dot(left, right, preferred_element_type=jnp.float32)  18.2 us
    dot_general x4, matrix products, weight_gradient(): lax.dot_general(left, right, (((0,), (0,)), ((), ())), preferred_element_...  12.7 us
  transfers between devices with their start and end apart: 1, of which 1 were waited for; matrix products, arithmetic and copies ran while one was open for 2% of the time, Pallas kernels for 0%

profile of v7, /device:TPU:0, one launch (start us, length us, event | category | flops | bytes accessed | tf_op | source)
XLA Modules:
  0.0 501.7 jit_solution(5936547210042902552)
XLA Ops:
  7.2 0.9 copy.80.refs_0_
  8.1 0.7 convert.15
  8.8 0.7 convert_bitcast_fusion
  9.4 0.7 convert_element_type.285
  10.2 1.2 copy-done.5
  11.4 1.0 copy-done.7
  12.5 92.3 %exchange_start.1 = (s32[1024,1]{1,0:T(8,128)S(1)}, s32[1024,1]{1,0:T(8,128)S(1)}, bf16[32,8,128]{2,1,0:T(8,128)(2,1)S(1)}, s32[32,1,128]{2,1,0:T(1,128)S(1)}, b...) custom-call(s32[1024,1]{1,0:T(8,128)S(1)} %copy.80.refs_0_, ...), custom_call_target="tpu_custom_call" | custom-call | bytes 150000000 | tf_op jit(solution)/shard_map/exchange_start/pallas_call | solution.py:853
  105.5 0.7 slice_reduce_fusion.1
  107.6 1.6 fusion.57
  109.2 8.3 %conditional.2 = (bf16[1024,512]{1,0:T(8,128)(2,1)S(1)}) conditional(s32[]{:T(128)} %convert_element_type.286, bf16[1024,512]{1,0:T(8,128)(2,1)S(1)} %fusion.57, (s32[1024]{0:T(1024)S(1)}, f32[1908,512]{1,0:T(8,128)}, s32[]{:T(128)}, s32[1024]{0:T(1024)S(1)}, bf16[1024,512]{1,0:T(8,128)(2,1)S(1)}) %tuple.161), branch_computations={%region_1.2_spmd, %region_2.6_spmd} | conditional | flops 3468276224 | bytes 15899929 | solution.py:1501
  118.5 4.0 add_convert_fusion.1.packed_ref
  122.6 5.2 %attention.2 = bf16[8,128,512]{2,1,0:T(8,128)(2,1)S(1)} custom-call(f32[8,1,128]{2,1,0:T(1,128)S(1)} %compare_convert_fusion.mask_ref, bf16[8,128,1536]{2,1,0:T(8,128)(2,1)S(1)} %add_convert_fusion.1.packed_ref), custom_call_target="tpu_custom_call" | custom-call | flops 1000000000 | bytes 5242880 | tf_op jit(solution)/shard_map/attention/pallas_call | solution.py:1153
  127.9 1.1 fusion.110
  129.9 6.1 %fusion.19 = (bf16[8,128,2048]{2,1,0:T(8,128)(2,1)S(1)}, f32[8,128,2048]{2,1,0:T(8,128)}) fusion(f32[2048]{0:T(1024)S(1)} %get-tuple-element.391, bf16[8,128,512]{2,1,0:T(8,128)(2,1)S(1)} %fusion.45, bf16[512,6144]{1,0:T(8,128)(2,1)S(1)} %bitcast.258), kind=kOutput, calls=%fused_computation.39 | convolution fusion | flops 2168455168 | bytes 15736832 | tf_op jit(solution)/shard_map/dot_general | solution.py:78
  136.0 2.7 fusion.111
  139.7 1.4 slice-done.5
  141.1 1.9 add_convert_fusion.packed_ref
  143.0 5.7 %attention.3 = bf16[8,128,512]{2,1,0:T(8,128)(2,1)S(1)} custom-call(f32[8,1,128]{2,1,0:T(1,128)S(1)} %compare_convert_fusion.mask_ref, bf16[8,128,1536]{2,1,0:T(8,128)(2,1)S(1)} %add_convert_fusion.packed_ref), custom_call_target="tpu_custom_call" | custom-call | flops 1000000000 | bytes 5242880 | tf_op jit(solution)/shard_map/attention/pallas_call | solution.py:1153
  148.7 1.0 fusion.112
  150.2 2.4 fusion.53
  152.6 3.7 fusion.113
  156.8 1.4 multiply_reduce_fusion.12
  158.4 23.6 %contrastive.1 = (f32[8,128]{1,0:T(8,128)S(1)}, f32[2,2,8,512]{3,2,1,0:T(8,128)S(1)}) custom-call(bf16[2,8,512]{2,1,0:T(8,128)(2,1)S(1)} %reshape.651.block_ref, s32[128,128]{1,0:T(8,128)S(1)} %reshape.652.false_ref, s32[128,1]{1,0:T(8,128)S(1)} %reshape_reshape.8.pair_ref), custom_call_target="tpu_custom_call" | custom-call | flops 1000000000 | bytes 3000000 | tf_op jit(solution)/shard_map/contrastive/pallas_call | solution.py:1056
  182.1 3.2 fusion.42
  185.2 1.5 convert_reduce_fusion.4
  186.7 7.3 %bitcast_convert_fusion = bf16[512,2048]{1,0:T(8,128)(2,1)S(1)} fusion(bf16[8,128,512]{2,1,0:T(8,128)(2,1)S(1)} %get-tuple-element.383, f32[8,128,2048]{2,1,0:T(8,128)} %copy-done.56, f32[2048]{0:T(1024)S(1)} %get-tuple-element.390), kind=kOutput, calls=%fused_computation.63 | convolution fusion | flops 2169503744 | bytes 11542528 | tf_op jit(solution)/shard_map/dot_general | solution.py:1292
  194.1 9.7 %convert_reduce_fusion = (f32[2048]{0:T(1024)}, bf16[8,128,2048]{2,1,0:T(8,128)(2,1)S(1)}) fusion(f32[8,128,2048]{2,1,0:T(8,128)} %copy-done.56, f32[2048]{0:T(1024)S(1)} %get-tuple-element.390, bf16[8,128,512]{2,1,0:T(8,128)(2,1)S(1)} %get-tuple-element.383, bf16[512,6144]{1,0:T(8,128)(2,1)S(1)} %bitcast.273), kind=kOutput, calls=%fused_computation.49 | convolution fusion | flops 2195716096 | bytes 15745024 | tf_op jit(solution)/shard_map/nsd,df->nsf/dot_general | solution.py:1255
  203.9 2.6 bitcast_convert_fusion.1
  206.5 3.4 multiply_reduce_fusion.1
  209.9 0.8 convert_reduce_fusion.5
  211.1 0.7 fusion.58
  211.9 0.7 convolution_convert_fusion.1.grad_ref
  212.6 9.8 %attention_back.2 = bf16[8,128,1536]{2,1,0:T(8,128)(2,1)S(1)} custom-call(f32[8,1,128]{2,1,0:T(1,128)S(1)} %compare_convert_fusion.mask_ref, bf16[8,128,1536]{2,1,0:T(8,128)(2,1)S(1)} %add_convert_fusion.packed_ref, bf16[8,128,512]{2,1,0:T(8,128)(2,1)S(1)} %convolution_convert_fusion.1.grad_ref), custom_call_target="tpu_custom_call" | custom-call | flops 1000000000 | bytes 5242880 | tf_op jit(solution)/shard_map/attention_back/pallas_call | solution.py:1153
  222.5 2.0 fusion.35
  224.5 3.4 convolution_add_fusion.1
  227.9 4.0 pad_maximum_fusion
  232.0 2.7 multiply_reduce_fusion.2
  234.7 1.0 convert_reduce_fusion.6
  235.8 10.1 %convert_reduce_fusion.1 = (f32[2048]{0:T(1024)S(1)}, bf16[8,128,2048]{2,1,0:T(8,128)(2,1)S(1)}) fusion(f32[8,128,2048]{2,1,0:T(8,128)} %get-tuple-element.427, f32[2048]{0:T(1024)S(1)} %get-tuple-element.391, bf16[8,128,512]{2,1,0:T(8,128)(2,1)S(1)} %get-tuple-element.379, bf16[512,6144]{1,0:T(8,128)(2,1)} %bitcast.254), kind=kOutput, calls=%fused_computation.50 | convolution fusion | flops 2195716096 | bytes 15745024 | tf_op jit(solution)/shard_map/nsd,df->nsf/dot_general | solution.py:1255
  245.9 3.7 multiply_reduce_fusion.3
  249.6 1.0 convert_reduce_fusion.7
  250.6 1.0 copy-done.31
  251.5 0.7 convolution_convert_fusion.grad_ref
  252.3 9.5 %attention_back.3 = bf16[8,128,1536]{2,1,0:T(8,128)(2,1)S(1)} custom-call(f32[8,1,128]{2,1,0:T(1,128)S(1)} %compare_convert_fusion.mask_ref, bf16[8,128,1536]{2,1,0:T(8,128)(2,1)S(1)} %copy-done.3, bf16[8,128,512]{2,1,0:T(8,128)(2,1)S(1)} %convolution_convert_fusion.grad_ref), custom_call_target="tpu_custom_call" | custom-call | flops 1000000000 | bytes 5242880 | tf_op jit(solution)/shard_map/attention_back/pallas_call | solution.py:1153
  261.8 2.9 multiply_reduce_fusion.5
  264.8 2.0 add_add_fusion
  266.7 1.8 reduce_sum.412
  268.5 3.5 add_convert_fusion.3
  272.1 6.1 %conditional.3 = (f32[1908,512]{1,0:T(8,128)}) conditional(s32[]{:T(128)} %convert_element_type.286, () %tuple.53, (s32[1024]{0:T(1024)S(1)}, s32[]{:T(128)}, s32[1024]{0:T(1024)S(1)}, bf16[1024,512]{1,0:T(8,128)(2,1)}) %tuple.162), branch_computations={%region_48.49_spmd, %region_49.53_spmd} | conditional | flops 5720194048 | bytes 29424452 | solution.py:1501
  272.1 2.4 broadcast_in_dim.48
  279.5 2.7 add_convert_fusion.2.refs_0_
  282.3 2.4 convert_reduce_fusion.2
  286.0 0.8 copy.101
  286.8 1.4 reshape_squeeze.4.refs_11_
  288.2 2.7 fusion.36
  290.9 75.0 %reduce-scatter.2.cloned.1.call-done.refs_10_ = bf16[32,6144]{1,0:T(8,128)(2,1)} async-done(((bf16[512,6144]{1,0:T(8,128)(2,1)}), bf16[32,6144]{1,0:T(8,128)(2,1)}) %reduce-scatter.2.cloned.1.call-update) | async-done | bytes 393232 | tf_op jit(solution)/shard_map/reduce_scatter | solution.py:1579
  365.9 106.7 %exchange_gradients.1 = (f32[2,32,2048]{2,1,0:T(8,128)}, f32[2,32,4096]{2,1,0:T(8,128)}, f32[1908,512]{1,0:T(8,128)}, f32[40,128]{1,0:T(8,128)}, f32[8,128]{1,0:T(8,128)}) custom-call(bf16[1024,512]{1,0:T(8,128)(2,1)} %add_convert_fusion.2.refs_0_, bf16[1024,1536]{1,0:T(8,128)(2,1)} %bitcast.205, bf16[1024,512]{1,0:T(8,128)(2,1)} %bitcast.206, ...), custom_call_target="tpu_custom_call" | custom-call | bytes 200000000 | tf_op jit(solution)/shard_map/exchange_gradients/pallas_call | solution.py:532
  472.6 1.3 fusion.109
  474.0 0.8 slice.253
  474.8 1.2 slice_multiply_fusion.1
  476.1 11.5 %fusion.97 = (bf16[1908,512]{1,0:T(8,128)(2,1)}, f32[1908,512]{1,0:T(8,128)}, f32[1908,512]{1,0:T(8,128)}, f32[1908,512]{1,0:T(8,128)}) fusion(f32[1908,512]{1,0:T(8,128)} %refs_6_.1, f32[1908,512]{1,0:T(8,128)} %get-tuple-element.307, f32[]{:T(128)} %bitcast.63, f32[1908,512]{1,0:T(8,128)} %param.32, f32[1908,512]{1,0:T(8,128)} %param.36), kind=kLoop, calls=%fused_computation.238 | loop fusion | flops 15630336 | bytes 29306884 | tf_op jit(solution)/shard_map/convert_element_type | solution.py:1676
  487.6 1.4 fusion.95
  489.0 2.2 fusion.93
  491.2 3.1 fusion.91
  (213 shorter events, 8.2 us)
Async XLA Ops:
  10.2 1.2 copy-start.5
  11.4 1.0 copy-start.7
  12.5 92.6 %copy-start.55 = (s32[4,2]{0,1:T(2,128)S(1)}, s32[4,2]{0,1:T(2,128)}, u32[]{:S(2)}) copy-start(s32[4,2]{0,1:T(2,128)} %param.25) | copy-start | bytes 100
  104.8 2.8 copy-start.11
  105.1 22.8 %copy-start.47 = (f32[512]{0:T(512)}, f32[512]{0:T(512)S(1)}, u32[]{:S(2)}) copy-start(f32[512]{0:T(512)S(1)} %get-tuple-element.408) | copy-start | bytes 6148
  107.1 2.1 copy-start.53
  107.6 20.3 %copy-start.25 = (f32[128,512]{1,0:T(8,128)}, f32[128,512]{1,0:T(8,128)S(1)}, u32[]{:S(2)}) copy-start(f32[128,512]{1,0:T(8,128)S(1)} %slice_convert_fusion) | copy-start | bytes 786436
  107.6 1.6 copy-start.37
  117.6 10.3 %copy-start.20 = (bf16[1024,512]{1,0:T(8,128)(2,1)}, bf16[1024,512]{1,0:T(8,128)(2,1)S(1)}, u32[]{:S(2)}) copy-start(bf16[1024,512]{1,0:T(8,128)(2,1)S(1)} %get-tuple-element.599) | copy-start | bytes 3145732
  117.6 10.3 %slice-start = ((s8[6291456]{0:T(1024)(128)(4,1)}), s8[4194304]{0:T(1024)(128)(4,1)S(1)}, s32[]{:S(2)}) async-start(s8[6291456]{0:T(1024)(128)(4,1)} %bitcast.255), calls=%async_computation.7 | async-start | bytes 8388608
  117.9 4.7 copy-start.43
  118.5 9.4 %slice-start.1 = ((s8[6291456]{0:T(1024)(128)(4,1)}), s8[2097152]{0:T(1024)(128)(4,1)S(1)}, s32[]{:S(2)}) async-start(s8[6291456]{0:T(1024)(128)(4,1)} %bitcast.255), calls=%async_computation.8 | async-start | bytes 4194304
  122.6 5.2 %copy-start.2 = (bf16[8,128,1536]{2,1,0:T(8,128)(2,1)}, bf16[8,128,1536]{2,1,0:T(8,128)(2,1)S(1)}, u32[]{:S(2)}) copy-start(bf16[8,128,1536]{2,1,0:T(8,128)(2,1)S(1)} %add_convert_fusion.1.packed_ref) | copy-start | bytes 9437188
  127.8 1.2 copy-start.4
  129.0 6.9 %copy-start.18 = (f32[8,128,512]{2,1,0:T(8,128)}, f32[8,128,512]{2,1,0:T(8,128)S(1)}, u32[]{:S(2)}) copy-start(f32[8,128,512]{2,1,0:T(8,128)S(1)} %get-tuple-element.425) | copy-start | bytes 6291460
  129.9 6.1 %copy-start.30 = (bf16[8,128,512]{2,1,0:T(8,128)(2,1)}, bf16[8,128,512]{2,1,0:T(8,128)(2,1)S(1)}, u32[]{:S(2)}) copy-start(bf16[8,128,512]{2,1,0:T(8,128)(2,1)S(1)} %fusion.45) | copy-start | bytes 3145732
  136.0 2.8 copy-start.27
  136.0 3.7 slice-start.4
  136.0 5.1 %slice-start.5 = ((s8[6291456]{0:T(1024)(128)(4,1)}), s8[2097152]{0:T(1024)(128)(4,1)S(1)}, s32[]{:S(2)}) async-start(s8[6291456]{0:T(1024)(128)(4,1)} %bitcast.265), calls=%async_computation.12 | async-start | bytes 4194304
  138.7 18.1 %copy-start.13 = (f32[8,128,512]{2,1,0:T(8,128)}, f32[8,128,512]{2,1,0:T(8,128)S(1)}, u32[]{:S(2)}) copy-start(f32[8,128,512]{2,1,0:T(8,128)S(1)} %get-tuple-element.429) | copy-start | bytes 6291460
  148.7 1.0 copy-start.9
  149.7 2.9 copy-start.23
  152.6 3.7 copy-start.56
  156.3 1.9 copy-start.16
  182.1 3.2 copy-start.17
  182.1 12.0 %slice-start.6 = ((s8[6291456]{0:T(1024)(128)(4,1)}), s8[4194304]{0:T(1024)(128)(4,1)S(1)}, s32[]{:S(2)}) async-start(s8[6291456]{0:T(1024)(128)(4,1)} %bitcast.271), calls=%async_computation.13 | async-start | bytes 8388608
  186.7 7.4 %slice-start.7 = ((s8[6291456]{0:T(1024)(128)(4,1)}), s8[2097152]{0:T(1024)(128)(4,1)S(1)}, s32[]{:S(2)}) async-start(s8[6291456]{0:T(1024)(128)(4,1)} %bitcast.271), calls=%async_computation.14 | async-start | bytes 4194304
  194.1 9.8 %copy-start.24 = (f32[8,128,512]{2,1,0:T(8,128)S(1)}, f32[8,128,512]{2,1,0:T(8,128)}, u32[]{:S(2)}) copy-start(f32[8,128,512]{2,1,0:T(8,128)} %copy-done.23) | copy-start | bytes 6291460
  209.9 1.2 copy-start.10
  212.6 9.8 %copy-start.14 = (f32[8,128,512]{2,1,0:T(8,128)S(1)}, f32[8,128,512]{2,1,0:T(8,128)}, u32[]{:S(2)}) copy-start(f32[8,128,512]{2,1,0:T(8,128)} %copy-done.13) | copy-start | bytes 6291460
  222.4 2.0 copy-start.1
  227.9 4.1 copy-start.15
  232.0 2.8 copy-start.22
  234.7 11.1 %slice-start.2 = ((s8[6291456]{0:T(1024)(128)(4,1)}), s8[4194304]{0:T(1024)(128)(4,1)S(1)}, s32[]{:S(2)}) async-start(s8[6291456]{0:T(1024)(128)(4,1)} %bitcast.260), calls=%async_computation.9 | async-start | bytes 8388608
  235.7 10.1 %copy-start.29 = (bf16[8,128,512]{2,1,0:T(8,128)(2,1)}, bf16[8,128,512]{2,1,0:T(8,128)(2,1)S(1)}, u32[]{:S(2)}) copy-start(bf16[8,128,512]{2,1,0:T(8,128)(2,1)S(1)} %get-tuple-element.379) | copy-start | bytes 3145732
  235.8 10.1 %copy-start.19 = (f32[8,128,512]{2,1,0:T(8,128)S(1)}, f32[8,128,512]{2,1,0:T(8,128)}, u32[]{:S(2)}) copy-start(f32[8,128,512]{2,1,0:T(8,128)} %copy-done.18) | copy-start | bytes 6291460
  235.8 10.1 %slice-start.3 = ((s8[6291456]{0:T(1024)(128)(4,1)}), s8[2097152]{0:T(1024)(128)(4,1)S(1)}, s32[]{:S(2)}) async-start(s8[6291456]{0:T(1024)(128)(4,1)} %bitcast.260), calls=%async_computation.10 | async-start | bytes 4194304
  245.9 3.7 copy-start.28
  249.6 2.7 copy-start.3
  252.3 9.5 %copy-start.21 = (bf16[1024,512]{1,0:T(8,128)(2,1)S(1)}, bf16[1024,512]{1,0:T(8,128)(2,1)}, u32[]{:S(2)}) copy-start(bf16[1024,512]{1,0:T(8,128)(2,1)} %copy-done.20) | copy-start | bytes 3145732
  252.3 9.5 %copy-start.26 = (f32[128,512]{1,0:T(8,128)S(1)}, f32[128,512]{1,0:T(8,128)}, u32[]{:S(2)}) copy-start(f32[128,512]{1,0:T(8,128)} %copy-done.25) | copy-start | bytes 786436
  261.8 23.0 %copy-start = (bf16[8,128,1536]{2,1,0:T(8,128)(2,1)}, bf16[8,128,1536]{2,1,0:T(8,128)(2,1)S(1)}, u32[]{:S(2)}) copy-start(bf16[8,128,1536]{2,1,0:T(8,128)(2,1)S(1)} %attention_back.3) | copy-start | bytes 9437188
  278.2 87.7 %reduce-scatter.2.cloned.1.call-start = ((), (), s32[]{:S(2)}) async-start(), calls=%async_computation.5 | async-start | bytes 6684672 | tf_op jit(solution)/shard_map/reduce_scatter | solution.py:1579
  278.3 1.2 copy-start.44
  278.3 1.2 copy-start.48
  279.0 3.3 copy-start.52
  282.3 2.4 copy-start.49
  282.3 2.4 copy-start.50
  282.3 2.5 copy-start.51
  285.3 1.5 copy-start.12
  285.6 2.6 copy-start.35
  285.6 2.6 copy-start.54
  476.0 11.6 %copy-start.41 = (f32[4928]{0:T(1024)S(1)}, f32[4928]{0:T(1024)}, u32[]{:S(2)}) copy-start(f32[4928]{0:T(1024)} %param.29) | copy-start | bytes 59140
  476.0 11.6 %copy-start.42 = (f32[40,128]{1,0:T(8,128)S(1)}, f32[40,128]{1,0:T(8,128)}, u32[]{:S(2)}) copy-start(f32[40,128]{1,0:T(8,128)} %get-tuple-element.308) | copy-start | bytes 61444
  476.0 11.6 %copy-start.45 = (f32[4928]{0:T(1024)S(1)}, f32[4928]{0:T(1024)}, u32[]{:S(2)}) copy-start(f32[4928]{0:T(1024)} %param.33) | copy-start | bytes 59140
  476.0 11.6 %copy-start.46 = (f32[4928]{0:T(1024)S(1)}, f32[4928]{0:T(1024)}, u32[]{:S(2)}) copy-start(f32[4928]{0:T(1024)} %param.37) | copy-start | bytes 59140
  476.0 13.0 %copy-start.8 = (f32[2,32,2048]{2,1,0:T(8,128)S(1)}, f32[2,32,2048]{2,1,0:T(8,128)}, u32[]{:S(2)}) copy-start(f32[2,32,2048]{2,1,0:T(8,128)} %refs_4_.1) | copy-start | bytes 1572868
  476.0 13.0 %copy-start.38 = (f32[2,32,2048]{2,1,0:T(8,128)S(1)}, f32[2,32,2048]{2,1,0:T(8,128)}, u32[]{:S(2)}) copy-start(f32[2,32,2048]{2,1,0:T(8,128)} %param.34) | copy-start | bytes 1572868
  476.0 13.0 %copy-start.39 = (f32[2,32,2048]{2,1,0:T(8,128)S(1)}, f32[2,32,2048]{2,1,0:T(8,128)}, u32[]{:S(2)}) copy-start(f32[2,32,2048]{2,1,0:T(8,128)} %param.38) | copy-start | bytes 1572868
  476.0 13.0 %copy-start.40 = (f32[2,32,2048]{2,1,0:T(8,128)S(1)}, f32[2,32,2048]{2,1,0:T(8,128)}, u32[]{:S(2)}) copy-start(f32[2,32,2048]{2,1,0:T(8,128)} %get-tuple-element.309) | copy-start | bytes 1572868
  476.0 15.1 %copy-start.34 = (f32[2,32,4096]{2,1,0:T(8,128)S(1)}, f32[2,32,4096]{2,1,0:T(8,128)}, u32[]{:S(2)}) copy-start(f32[2,32,4096]{2,1,0:T(8,128)} %get-tuple-element.310) | copy-start | bytes 3145732
  487.5 3.7 copy-start.6
  487.5 3.7 copy-start.32
  487.5 3.7 copy-start.33
  (2 other events, 1.9 us)
Sparse Core Ops, SparseCore 0:
  283.0 82.8 reduce-scatter.1

commit v8 on v7

--- a/solution.py
+++ b/solution.py
@@ -186,17 +186,22 @@
     )(*arrays)
 
 
+CHUNK = 1024
+LAG_Z = 3
+REST_EACH = 4
+
+
 def gradient_kernel(chunks, matrices, vec_len, *refs):
     take = iter(refs)
     pairs = [(next(take), next(take)) for _ in range(matrices)]
-    vec_ref, sums_ref, near_ref, asked_ref, extra_ref = [next(take) for _ in range(5)]
+    vec_ref, sums_ref, near_ref, asked_ref = [next(take) for _ in range(4)]
     attn_out, ffn_out, word_out, vec_out, stats_out = [next(take) for _ in range(5)]
     held = [None if m is None else next(take) for m, _, _ in chunks]
     bufs = [[next(take) for _ in range(5)] for _ in chunks]
-    near_buf, rows_ref, added, square_ref, squares_ref = [next(take) for _ in range(5)]
+    near_buf, rows_ref, sum_ref, square_ref, squares_ref = [next(take) for _ in range(5)]
     send_a, recv_a, send_y, recv_y, send_z, recv_z, send_x, recv_x = [next(take) for _ in range(8)]
-    row_send, row_recv, pass_send, pass_recv, near_sem, extra_sem, square_sem = [
-        next(take) for _ in range(7)
+    row_send, row_recv, pass_send, pass_recv, near_sem, square_sem = [
+        next(take) for _ in range(6)
     ]
 
     d = lax.axis_index("dp")
@@ -264,8 +269,6 @@
         )
 
     near = remote(near_ref, near_buf, near_sem.at[0], near_sem.at[1], (1 - d, z))
-    extra = pltpu.make_async_copy(extra_ref, word_out, extra_sem)
-    extra.start()
 
     total = len(chunks)
 
@@ -350,42 +353,61 @@
         row_push(k).wait_recv()
         row_pass(k).start()
 
-    tiles = added.shape[0] // 128
+    shard_rows, features = word_out.shape
+    tiles = -(-shard_rows // 128)
     spots = rows_ref.shape[1] * rows_ref.shape[2]
-
-    def into_rows(plane, tile):
-        lane = lax.broadcasted_iota(jnp.int32, (1, 128), 1) + tile * 128
-        picked = (asked_ref[plane] == lane).astype(jnp.bfloat16)
-        return lax.dot_general(
-            picked,
-            rows_ref[plane].reshape(spots, rows_ref.shape[3]),
-            (((0,), (0,)), ((), ())),
-            preferred_element_type=jnp.float32,
-        )
-
-    def own_plane(tile, carry):
-        added[pl.ds(pl.multiple_of(tile * 128, 128), 128), :] = into_rows(d, tile)
-        return carry
+    sum_ref[...] = jnp.zeros_like(sum_ref)
+
+    def into_rows(plane, first, count):
+        row = lax.broadcasted_iota(jnp.int32, (128, 1), 0) + first
+        picked = (asked_ref[plane] == row).astype(jnp.bfloat16)
+        return jnp.dot(
+            picked, rows_ref[plane].reshape(spots, features), preferred_element_type=jnp.float32
+        )[:count]
+
+    def own_rows(tile):
+        first, count = tile * 128, min(128, shard_rows - tile * 128)
+        word_out[first : first + count, :] = into_rows(d, first, count)
+
+    def all_arrived():
+        def arrived(k, carry):
+            ref = rows_ref.at[1 - d, lax.rem(z + 16 - k, 16)]
+            remote(ref, ref, pass_send.at[k], pass_recv.at[k], (1 - d, z)).wait_recv()
+            return carry
+
+        lax.fori_loop(0, 16, arrived, 0)
+
+    def other_rows(tile):
+        first, count = tile * 128, min(128, shard_rows - tile * 128)
+        value = word_out[first : first + count, :] + into_rows(1 - d, first, count)
+        word_out[first : first + count, :] = value
+        sum_ref[...] = sum_ref[...] + jnp.sum(value * value, axis=0, keepdims=True)
+
+    rest = [functools.partial(own_rows, tile) for tile in range(tiles)]
+    rest += [all_arrived] + [functools.partial(other_rows, tile) for tile in range(tiles)]
 
     compute(0)
     passed = 1
-    for t in range(total + 3):
+    for t in range(total + LAG_Z + 2):
         if t + 1 < total:
             compute(t + 1)
         if t < total:
             stage_a(t)
         if 0 <= t - 1 < total:
             stage_y(t - 1)
-        if 0 <= t - 2 < total:
-            stage_z(t - 2)
-        if 0 <= t - 3 < total:
-            stage_x(t - 3)
-        until = min(16, 1 + (t + 1) * 15 // (total - 1))
+        if 0 <= t - 1 - LAG_Z < total:
+            stage_z(t - 1 - LAG_Z)
+        if 0 <= t - 2 - LAG_Z < total:
+            stage_x(t - 2 - LAG_Z)
+        until = min(16, 1 + (t + 1) * 15 // (total - 2))
         for k in range(passed, until):
             pass_on(k)
         passed = until
-        if t == total - 1:
-            lax.fori_loop(0, tiles, own_plane, 0)
+        if t >= total - 2:
+            for _ in range(min(len(rest), REST_EACH)):
+                rest.pop(0)()
+    while rest:
+        rest.pop(0)()
 
     near.wait()
     attn_out[1] = near_ref[:, :attn_width].astype(jnp.float32) + near_buf[:, :attn_width].astype(
@@ -394,31 +416,7 @@
     ffn_out[1] = near_ref[:, attn_width:].astype(jnp.float32) + near_buf[:, attn_width:].astype(
         jnp.float32
     )
-
-    def arrived(k, carry):
-        at = lax.rem(z + 16 - k, 16)
-        ref = rows_ref.at[1 - d, at]
-        remote(ref, ref, pass_send.at[k], pass_recv.at[k], (1 - d, z)).wait_recv()
-        return carry
-
-    lax.fori_loop(0, 16, arrived, 0)
-    extra.wait()
-    features = word_out.shape[1]
-
-    def add_rows(tile, count, first):
-        at = pl.ds(first, count)
-        value = (added[at, :] + into_rows(1 - d, tile)[:count]) + word_out[at, :]
-        word_out[at, :] = value
-        return jnp.sum(value * value, axis=0, keepdims=True)
-
-    full = word_out.shape[0] // 128
-
-    def other_plane(tile, carry):
-        return carry + add_rows(tile, 128, pl.multiple_of(tile * 128, 128))
-
-    squares = lax.fori_loop(0, full, other_plane, jnp.zeros((1, features), jnp.float32))
-    if word_out.shape[0] % 128:
-        squares = squares + add_rows(full, word_out.shape[0] % 128, full * 128)
+    squares = sum_ref[...]
     square = jnp.sum(squares, axis=1, keepdims=True)
     for out in (attn_out, ffn_out):
 
@@ -480,16 +478,14 @@
     norm = squares_ref[0]
     for slot in range(1, 16):
         norm = norm + squares_ref[slot]
-    norm = jnp.sqrt(norm)
-    stats_out[0:1, :] = norm
-    stats_out[1:2, :] = jnp.minimum(1.0, CLIP_NORM / (norm + 1e-06))
-
-
-def exchange_gradients(pairs, vec_parts, sums, near, asked, extra, vec_len, collective_id):
+    stats_out[...] = jnp.broadcast_to(norm, stats_out.shape)
+
+
+def exchange_gradients(pairs, vec_parts, sums, near, asked, shard_rows, vec_len, collective_id):
     chunks = [(None, 0, 128)]
     for index in (3, 2, 0, 1):
         columns = pairs[index][1].shape[1]
-        width = columns // -(-columns // 1024)
+        width = columns // -(-columns // CHUNK)
         for start in range(0, columns, width):
             chunks.append((index, start, width))
     half = jnp.bfloat16
@@ -506,25 +502,25 @@
             pltpu.VMEM((r, width), kind),
             pltpu.VMEM((r, width), kind),
         ]
-    shard_rows, features = extra.shape
+    features = sums.shape[2]
     dma = pltpu.SemaphoreType.DMA
     count = len(chunks)
     scratch = held + bufs
     scratch += [
         pltpu.VMEM(near.shape, half),
         pltpu.VMEM((2,) + sums.shape, half),
-        pltpu.VMEM((-(-shard_rows // 128) * 128, features), jnp.float32),
+        pltpu.VMEM((1, features), jnp.float32),
         pltpu.VMEM((1, 128), jnp.float32),
         pltpu.VMEM((16, 1, 128), jnp.float32),
     ]
     scratch += [dma((count,)) for _ in range(4)] + [dma((count, 3)) for _ in range(2)]
     scratch += [dma((count,)) for _ in range(2)]
-    scratch += [dma((16,)) for _ in range(4)] + [dma((2,)), dma, dma((2, 16))]
+    scratch += [dma((16,)) for _ in range(4)] + [dma((2,)), dma((2, 16))]
     rows = near.shape[0]
     outs = [
         jax.ShapeDtypeStruct((2, rows, 4 * D), jnp.float32),
         jax.ShapeDtypeStruct((2, rows, 2 * FF), jnp.float32),
-        jax.ShapeDtypeStruct(extra.shape, jnp.float32),
+        jax.ShapeDtypeStruct((shard_rows, features), jnp.float32),
         jax.ShapeDtypeStruct(vec_parts.shape[3:], jnp.float32),
         jax.ShapeDtypeStruct((8, 128), jnp.float32),
     ]
@@ -532,7 +528,7 @@
     return pl.pallas_call(
         functools.partial(gradient_kernel, tuple(chunks), len(pairs), vec_len),
         out_shape=tuple(outs),
-        in_specs=[vmem] * (2 * len(pairs) + 4) + [pl.BlockSpec(memory_space=pl.ANY)],
+        in_specs=[vmem] * (2 * len(pairs) + 4),
         out_specs=tuple([vmem] * len(outs)),
         scratch_shapes=scratch,
         compiler_params=pltpu.CompilerParams(
@@ -540,7 +536,7 @@
         ),
         cost_estimate=pl.CostEstimate(flops=0, bytes_accessed=200_000_000, transcendentals=0),
         name="exchange_gradients",
-    )(*[array for pair in pairs for array in pair], vec_parts, sums, near, asked, extra)
+    )(*[array for pair in pairs for array in pair], vec_parts, sums, near, asked)
 
 
 SPLITS = 4
@@ -1222,15 +1218,15 @@
         layer_vectors(vectors)
     )
     half = jnp.bfloat16
-    entry = hidden.astype(half)
+    entry = lax.optimization_barrier(hidden.astype(half))
     bias = jnp.concatenate([q_bias, jnp.zeros_like(q_bias), v_bias])
     packed = (matmul(entry, in_weights) + bias).astype(half)
     context = attention_call(attention_kernel, mask, [packed], D, "attention")
     attended = matmul(context, out_weights) + o_bias
     first, normal_one, inverse_one = norm_forward(hidden + attended, gain_one, shift_one)
-    middle = first.astype(half)
+    middle = lax.optimization_barrier(first.astype(half))
     upward = matmul(middle, up_weights) + up_bias
-    active = gelu(upward).astype(half)
+    active = lax.optimization_barrier(gelu(upward).astype(half))
     downward = einsum_plain("nsf,df->nsd", active, down_weights) + down_bias
     output, normal_two, inverse_two = norm_forward(first + downward, gain_two, second_shift)
     kept = (
@@ -1251,15 +1247,15 @@
         return jnp.sum(value.astype(jnp.float32), axis=(0, 1))
 
     d_second, d_gain_two, d_shift_two = norm_back(grad, normal_two, inverse_two, gain_two)
-    d_down = d_second.astype(half)
+    d_down = lax.optimization_barrier(d_second.astype(half))
     d_active = jnp.einsum("nsd,df->nsf", d_down, down_weights, preferred_element_type=jnp.float32)
-    d_active = d_active.astype(half).astype(jnp.float32)
-    d_up = (d_active * gelu_slope(upward)).astype(half)
+    d_active = lax.optimization_barrier(d_active.astype(half)).astype(jnp.float32)
+    d_up = lax.optimization_barrier((d_active * gelu_slope(upward)).astype(half))
     d_first = d_second + jnp.einsum(
         "nsf,df->nsd", d_up, up_weights, preferred_element_type=jnp.float32
     )
     d_middle, d_gain_one, d_shift_one = norm_back(d_first, normal_one, inverse_one, gain_one)
-    d_attended = d_middle.astype(half)
+    d_attended = lax.optimization_barrier(d_middle.astype(half))
     d_context = jnp.einsum(
         "nsd,ed->nse", d_attended, out_weights, preferred_element_type=jnp.float32
     ).astype(half)
@@ -1471,8 +1467,8 @@
     asked_near = lax.dynamic_slice_in_dim(asked_mine, my_dp * nz, nz, 0)
 
     def rows_for(wanted):
-        picked = one_hot(wanted.reshape(-1), shard_rows)
-        return matmul(picked, word_table.astype(jnp.bfloat16)).astype(jnp.bfloat16)
+        picked = one_hot(wanted.reshape(-1), shard_rows, jnp.float32)
+        return jnp.dot(picked, word_table, precision=lax.Precision.HIGHEST).astype(jnp.bfloat16)
 
     def rows_from(slot_now, received):
         return matmul(one_hot(slot_now, nz * room), received.reshape(nz * room, D)).astype(
@@ -1497,17 +1493,10 @@
         got = lax.all_to_all(rows_for(wanted).reshape(nz, room, D), "zero", 0, 0, tiled=True)
         return round_index + 1, rows_now + rows_from(slot_now, got)
 
-    def further(step, value):
-        return lax.cond(
-            rounds > 1,
-            lambda now: lax.while_loop(
-                lambda state: state[0] < rounds, step, (jnp.int32(1), now)
-            )[1],
-            lambda now: now,
-            value,
-        )
-
-    rows = further(more_rows, rows)
+    def further(step, *value):
+        return lax.while_loop(lambda state: state[0] < rounds, step, (jnp.int32(1), *value))[1:]
+
+    (rows,) = further(more_rows, rows)
     rows = rows.reshape(seq_rows, SEQ, D).astype(jnp.float32)
 
     vec_rows = vec_all.reshape(-1, D)
@@ -1605,28 +1594,29 @@
     sums = slot_sums(slot).reshape(nz, room, D)
 
     def more_sums(state):
-        round_index, grad_now = state
+        round_index, grad_now, square_now = state
         slot_now, asked_now = round_of(round_index)
         wanted = lax.all_to_all(asked_now.reshape(nz, room), "zero", 0, 0, tiled=True)
         got = lax.all_to_all(slot_sums(slot_now).reshape(nz, room, D), "zero", 0, 0, tiled=True)
         wanted = lax.all_gather(wanted, "dp", axis=0, tiled=True)
         got = lax.all_gather(got, "dp", axis=0, tiled=True)
-        return round_index + 1, grad_now + into_rows(wanted, got)
+        grad_next = grad_now + into_rows(wanted, got)
+        grown = jnp.sum(grad_next * grad_next) - jnp.sum(grad_now * grad_now)
+        return round_index + 1, grad_next, square_now + lax.psum(grown, "zero")
 
     if by_hand:
-        extra = further(more_sums, jnp.zeros((shard_rows, D), jnp.float32))
-        attn_shard, ffn_shard, word_grad, vec_sum, stats = exchange_gradients(
+        attn_shard, ffn_shard, word_grad, vec_sum, squares = exchange_gradients(
             weight_parts[0],
             vec_blocks.reshape(4, 2, 2, lines, 128),
             sums,
             weight_parts[1],
-            asked_mine.reshape(ndp, nz * room, 1),
-            extra,
+            asked_mine.reshape(ndp, 1, nz * room),
+            shard_rows,
             vec_len,
             3,
         )
         vec_sum = vec_sum.reshape(-1)
-        grad_norm, factor = stats[0, 0], stats[1, 0]
+        square_total = squares[0, 0]
     else:
         sums_all, vec_shares = exchange(
             [sums, vec_blocks.reshape(nz, lines, 128)],
@@ -1641,7 +1631,7 @@
         weight_sum = jnp.sum(weight_all.astype(jnp.float32), axis=0)
         attn_shard = weight_sum[:, :, : 4 * D]
         ffn_shard = weight_sum[:, :, 4 * D :]
-        word_grad = further(more_sums, into_rows(asked_mine, sums_all))
+        word_grad = into_rows(asked_mine, sums_all)
     vec_shard = vec_sum[:vec_len]
     down_shard = vec_sum[vec_len : vec_len + down_len].reshape(LAYERS, -1)
 
@@ -1652,8 +1642,10 @@
         (squares,) = exchange(
             [jnp.broadcast_to(square_local, (8, 128))], ["zero"], ndp, nz, 5, "gather_squares"
         )
-        grad_norm = jnp.sqrt(jnp.sum(squares[:, 0, 0]))
-        factor = jnp.minimum(1.0, CLIP_NORM / (grad_norm + 1e-06))
+        square_total = jnp.sum(squares[:, 0, 0])
+    word_grad, square_total = further(more_sums, word_grad, square_total)
+    grad_norm = jnp.sqrt(square_total)
+    factor = jnp.minimum(1.0, CLIP_NORM / (grad_norm + 1e-06))
     word_new, word_first_new, word_second_new = adam_update(
         word_table, word_grad * factor, word_first, word_second, LEARN_RATE
     )

time: 509 us -> 439 us (0.86)
  waiting for transfers between devices: 75.6 us -> 20.8 us
  Pallas kernels: 253 us -> 233 us
  loops' own time: 12.1 us -> 1.82 us
  other arithmetic: 54.5 us -> 63.6 us
    reduce_scatter x1, waiting for transfers between devices: 75 us -> 20.8 us  [body(): lax.psum_scatter(both, 'zero', scatter_dimension=0, tiled=True)]
    pallas_call x1, Pallas kernels: 107 us -> 85.2 us  [exchange_gradients(): pl.pallas_call(functools.partial(gradient_kernel, tuple(chunks), len(pair...]
    convert_element_type x2 -> x10, other arithmetic: 3.14 us -> 16.6 us  [the longest x2 11.6 us: layer_backward(): (d_active * gelu_slope(upward)).astype(half)]
    dot_general x2, matrix products: 19.8 us -> 9.21 us  [layer_backward(): jnp.einsum('nsd,df->nsf', d_down, down_weights, preferred_element_type=jn...]
    another operation x2, loops' own time: 12.1 us -> 1.82 us  [further(): lax.while_loop(lambda state: state[0] < rounds, step, (jnp.int32(1), *val...]
    dot_general x2, matrix products: 7.06 us -> 13.8 us  [layer_backward(): jnp.einsum('nsf,df->nsd', d_up, up_weights, preferred_element_type=jnp.fl...]
    unnamed x134 -> x136, local copies, waits for them, and re-layouts: 6.89 us -> 12.5 us
  transfers between devices with their start and end apart: 1 -> 1, of which waited for: 1 -> 1; matrix products, arithmetic and copies ran while one was open for 2% -> 11% of each run, Pallas kernels for 0% -> 2%
where the time goes in v8:
time: 439 us; the launch traced here: 432 us
  Pallas kernels  233 us (53%)
  matrix products  77.7 us (18%)
  other arithmetic  63.6 us (14%)
  waiting for transfers between devices  20.8 us (5%)
  between operations  17.6 us (4%)
  local copies, waits for them, and re-layouts  17 us (4%)
    pallas_call x1, Pallas kernels, exchange_start(): pl.pallas_call(functools.partial(start_kernel, shard_rows, room), out_sha...  92.3 us
    pallas_call x1, Pallas kernels, exchange_gradients(): pl.pallas_call(functools.partial(gradient_kernel, tuple(chunks), len(pair...  85.2 us
    pallas_call x4, Pallas kernels, attention_call(): pl.pallas_call(kernel, grid=(count,), out_shape=jax.ShapeDtypeStruct((cou...  32.3 us
    pallas_call x1, Pallas kernels, contrastive(): pl.pallas_call(contrastive_kernel, out_shape=(jax.ShapeDtypeStruct((8, 12...  23.6 us
    dot_general x7, matrix products, matmul(): return jnp.dot(left, right, preferred_element_type=jnp.float32)  21.6 us
    reduce_scatter x1, waiting for transfers between devices, body(): lax.psum_scatter(both, 'zero', scatter_dimension=0, tiled=True)  20.8 us
    dot_general x2, matrix products, layer_backward(): jnp.einsum('nsf,df->nsd', d_up, up_weights, preferred_element_type=jnp.fl...  13.8 us
    unnamed x136, local copies, waits for them, and re-layouts  12.5 us
  transfers between devices with their start and end apart: 1, of which 1 were waited for; matrix products, arithmetic and copies ran while one was open for 11% of the time, Pallas kernels for 2%

profile of v8, /device:TPU:0, one launch (start us, length us, event | category | flops | bytes accessed | tf_op | source)
XLA Modules:
  0.0 431.9 jit_solution(12911326061483037796)
XLA Ops:
  7.2 0.8 copy.80
  8.9 0.9 copy.79.refs_0_
  11.1 0.7 convert_element_type.269
  11.9 1.2 copy-done.6
  13.1 1.0 copy-done.8
  14.1 92.3 %exchange_start.1 = (s32[1024,1]{1,0:T(8,128)S(1)}, s32[1024,1]{1,0:T(8,128)S(1)}, bf16[32,8,128]{2,1,0:T(8,128)(2,1)S(1)}, s32[32,1,128]{2,1,0:T(1,128)S(1)}, b...) custom-call(s32[1024,1]{1,0:T(8,128)S(1)} %copy.79.refs_0_, ...), custom_call_target="tpu_custom_call" | custom-call | bytes 150000000 | tf_op jit(solution)/shard_map/exchange_start/pallas_call | solution.py:849
  106.8 0.7 slice_reduce_fusion.1
  108.4 1.6 fusion.56
  110.0 0.9 while.28
  112.3 3.9 add_convert_fusion.1.packed_ref
  116.2 7.9 %attention.2 = bf16[8,128,512]{2,1,0:T(8,128)(2,1)S(1)} custom-call(f32[8,1,128]{2,1,0:T(1,128)S(1)} %compare_convert_fusion.mask_ref, bf16[8,128,1536]{2,1,0:T(8,128)(2,1)S(1)} %add_convert_fusion.1.packed_ref), custom_call_target="tpu_custom_call" | custom-call | flops 1000000000 | bytes 5242880 | tf_op jit(solution)/shard_map/attention/pallas_call | solution.py:1149
  124.2 1.1 fusion.91
  126.2 6.0 %fusion.19 = (bf16[8,128,2048]{2,1,0:T(8,128)(2,1)S(1)}, f32[8,128,2048]{2,1,0:T(8,128)}) fusion(f32[2048]{0:T(1024)S(1)} %get-tuple-element.443, bf16[8,128,512]{2,1,0:T(8,128)(2,1)S(1)} %fusion.44, bf16[512,6144]{1,0:T(8,128)(2,1)S(1)} %bitcast.264), kind=kOutput, calls=%fused_computation.40 | convolution fusion | flops 2168455168 | bytes 15736832 | tf_op jit(solution)/shard_map/dot_general | solution.py:78
  132.2 2.7 fusion.92
  135.8 1.0 copy-done.44
  136.8 1.8 add_convert_fusion.packed_ref
  138.6 5.2 %attention.3 = bf16[8,128,512]{2,1,0:T(8,128)(2,1)S(1)} custom-call(f32[8,1,128]{2,1,0:T(1,128)S(1)} %compare_convert_fusion.mask_ref, bf16[8,128,1536]{2,1,0:T(8,128)(2,1)S(1)} %add_convert_fusion.packed_ref), custom_call_target="tpu_custom_call" | custom-call | flops 1000000000 | bytes 5242880 | tf_op jit(solution)/shard_map/attention/pallas_call | solution.py:1149
  143.8 1.0 fusion.93
  145.7 6.2 %fusion.24 = (bf16[8,128,2048]{2,1,0:T(8,128)(2,1)S(1)}, f32[8,128,2048]{2,1,0:T(8,128)}) fusion(f32[2048]{0:T(1024)S(1)} %get-tuple-element.442, bf16[8,128,512]{2,1,0:T(8,128)(2,1)S(1)} %fusion.45, bf16[512,6144]{1,0:T(8,128)(2,1)S(1)} %bitcast.274), kind=kOutput, calls=%fused_computation.45 | convolution fusion | flops 2168455168 | bytes 15736832 | tf_op jit(solution)/shard_map/dot_general | solution.py:78
  152.0 2.7 fusion.94
  155.2 1.2 multiply_reduce_fusion.14
  156.6 23.6 %contrastive.1 = (f32[8,128]{1,0:T(8,128)S(1)}, f32[2,2,8,512]{3,2,1,0:T(8,128)S(1)}) custom-call(bf16[2,8,512]{2,1,0:T(8,128)(2,1)S(1)} %reshape.656.block_ref, s32[128,128]{1,0:T(8,128)S(1)} %reshape.657.false_ref, s32[128,1]{1,0:T(8,128)S(1)} %reshape_reshape.8.pair_ref), custom_call_target="tpu_custom_call" | custom-call | flops 1000000000 | bytes 3000000 | tf_op jit(solution)/shard_map/contrastive/pallas_call | solution.py:1052
  180.2 2.8 fusion.42
  183.0 0.9 fusion.59
  184.0 5.0 %bitcast_convert_fusion = bf16[512,2048]{1,0:T(8,128)(2,1)S(1)} fusion(bf16[8,128,512]{2,1,0:T(8,128)(2,1)S(1)} %fusion.59, bf16[8,128,2048]{2,1,0:T(8,128)(2,1)} %copy-done.57), kind=kOutput, calls=%fused_computation.64 | convolution fusion | flops 2148532224 | bytes 7340032 | tf_op jit(solution)/shard_map/dot_general | solution.py:1288
  189.0 4.1 convolution_convert_fusion.1
  193.2 6.0 %multiply_convert_fusion.1 = bf16[8,128,2048]{2,1,0:T(8,128)(2,1)S(1)} fusion(bf16[8,128,2048]{2,1,0:T(8,128)(2,1)S(1)} %convolution_convert_fusion.1, f32[8,128,2048]{2,1,0:T(8,128)S(1)} %bitcast.221, f32[2048]{0:T(1024)S(1)} %get-tuple-element.442), kind=kLoop, calls=%fused_computation.53 | loop fusion | flops 41943040 | bytes 16785408 | tf_op jit(solution)/shard_map/convert_element_type | solution.py:1253
  199.2 6.6 %multiply_reduce_fusion.3 = (f32[512]{0:T(512)S(1)}, f32[8,128]{1,0:T(8,128)S(1)}, f32[8,128]{1,0:T(8,128)S(1)}, f32[512]{0:T(512)S(1)}, f32[8,128,512]{2,1,0:T(8,128)S(1)}) fusion(f32[8,128,512]{2,1,0:T(8,128)S(1)} %copy-done.20, f32[8,128]{1,0:T(8,128)S(1)} %add_rsqrt_fusion.1, f32[8,128]{1,0:T(8,128)S(1)} %broadcast_multiply_fusion.9, ...), kind=kOutput, calls=%fused_computation.93 | convolution fusion | flops 2156917760 | bytes 12644352 | tf_op jit(solution)/shard_map/nsf,df->nsd/dot_general | solution.py:1254
  205.8 2.5 bitcast_convert_fusion.1
  208.3 0.8 fusion.63
  209.6 0.7 fusion.57
  210.5 1.8 convolution_convert_fusion.3.grad_ref
  212.3 9.4 %attention_back.2 = bf16[8,128,1536]{2,1,0:T(8,128)(2,1)S(1)} custom-call(f32[8,1,128]{2,1,0:T(1,128)S(1)} %compare_convert_fusion.mask_ref, bf16[8,128,1536]{2,1,0:T(8,128)(2,1)S(1)} %add_convert_fusion.packed_ref, bf16[8,128,512]{2,1,0:T(8,128)(2,1)S(1)} %convolution_convert_fusion.3.grad_ref), custom_call_target="tpu_custom_call" | custom-call | flops 1000000000 | bytes 5242880 | tf_op jit(solution)/shard_map/attention_back/pallas_call | solution.py:1149
  221.7 5.9 %convolution_add_fusion.1 = f32[8,128,512]{2,1,0:T(8,128)} fusion(bf16[8,128,1536]{2,1,0:T(8,128)(2,1)S(1)} %attention_back.2, bf16[512,6144]{1,0:T(8,128)(2,1)} %bitcast.269, f32[8,128]{1,0:T(8,128)S(1)} %broadcast_multiply_fusion.4, f32[8,128]{1,0:T(8,128)S(1)} %add_rsqrt_fusion.1, f32[8,128,512]{2,1,0:T(8,128)S(1)} %copy-done.20, ...), kind=kOutput, calls=%fused_computation.149 | convolution fusion | flops 1614807040 | bytes 11028480 | tf_op jit(solution)/shard_map/nsp,dp->nsd/dot_general | solution.py:1265
  227.7 1.8 fusion.35
  229.5 4.2 pad_maximum_fusion
  233.8 1.1 copy-done.39
  235.2 3.2 convert_reduce_fusion
  240.9 2.8 multiply_reduce_fusion.4
  243.7 0.9 fusion.76
  244.7 5.1 %convolution_convert_fusion = bf16[8,128,2048]{2,1,0:T(8,128)(2,1)S(1)} fusion(bf16[8,128,512]{2,1,0:T(8,128)(2,1)S(1)} %fusion.76, bf16[512,6144]{1,0:T(8,128)(2,1)} %bitcast.257), kind=kOutput, calls=%fused_computation.72 | convolution fusion | flops 2149580800 | bytes 7340032 | tf_op jit(solution)/shard_map/nsd,df->nsf/dot_general | solution.py:1251
  249.8 5.6 %multiply_convert_fusion = bf16[8,128,2048]{2,1,0:T(8,128)(2,1)S(1)} fusion(bf16[8,128,2048]{2,1,0:T(8,128)(2,1)S(1)} %convolution_convert_fusion, f32[8,128,2048]{2,1,0:T(8,128)S(1)} %bitcast.219, f32[2048]{0:T(1024)S(1)} %get-tuple-element.443), kind=kLoop, calls=%fused_computation.52 | loop fusion | flops 41943040 | bytes 16785408 | tf_op jit(solution)/shard_map/convert_element_type | solution.py:1253
  255.5 2.0 copy-done.14
  258.1 7.2 %multiply_reduce_fusion.5 = (f32[512]{0:T(512)S(1)}, f32[8,128]{1,0:T(8,128)S(1)}, f32[8,128]{1,0:T(8,128)S(1)}, f32[512]{0:T(512)S(1)}, f32[8,128,512]{2,1,0:T(8,128)S(1)}) fusion(f32[8,128,512]{2,1,0:T(8,128)} %copy-done.17, f32[8,128]{1,0:T(8,128)S(1)} %add_rsqrt_fusion.3, f32[8,128]{1,0:T(8,128)S(1)} %broadcast_multiply_fusion.11, ...), kind=kOutput, calls=%fused_computation.97 | convolution fusion | flops 2157442048 | bytes 14741504 | tf_op jit(solution)/shard_map/nsf,df->nsd/dot_general | solution.py:1254
  265.3 0.7 fusion.64
  266.1 1.0 copy-done.27
  267.1 1.8 convolution_convert_fusion.2.grad_ref
  268.9 9.9 %attention_back.3 = bf16[8,128,1536]{2,1,0:T(8,128)(2,1)S(1)} custom-call(f32[8,1,128]{2,1,0:T(1,128)S(1)} %compare_convert_fusion.mask_ref, bf16[8,128,1536]{2,1,0:T(8,128)(2,1)S(1)} %copy-done.2, bf16[8,128,512]{2,1,0:T(8,128)(2,1)S(1)} %convolution_convert_fusion.2.grad_ref), custom_call_target="tpu_custom_call" | custom-call | flops 1000000000 | bytes 5242880 | tf_op jit(solution)/shard_map/attention_back/pallas_call | solution.py:1149
  278.8 5.3 %multiply_reduce_fusion.7 = (f32[512]{0:T(512)S(1)}, f32[8,128]{1,0:T(8,128)S(1)}, f32[512]{0:T(512)S(1)}, f32[8,128,512]{2,1,0:T(8,128)S(1)}) fusion(f32[8,128]{1,0:T(8,128)S(1)} %bitcast_rsqrt_fusion, f32[8,128]{1,0:T(8,128)S(1)} %get-tuple-element.452, f32[128,512]{1,0:T(8,128)S(1)} %copy-done.33, bf16[1024,512]{1,0:T(8,128)(2,1)S(1)} %copy-done.22, ...), kind=kOutput, calls=%fused_computation.100 | convolution fusion | flops 1621620736 | bytes 13406208 | tf_op jit(solution)/shard_map/nsp,dp->nsd/dot_general | solution.py:1265
  284.1 1.9 add_add_fusion
  286.1 1.8 reduce_sum.438
  287.9 3.0 add_convert_fusion.2
  292.5 0.8 copy.99
  293.3 2.7 fusion.36
  296.0 20.8 %reduce-scatter.2.cloned.1.call-done.refs_10_ = bf16[32,6144]{1,0:T(8,128)(2,1)} async-done(((bf16[512,6144]{1,0:T(8,128)(2,1)}), bf16[32,6144]{1,0:T(8,128)(2,1)}) %reduce-scatter.2.cloned.1.call-update) | async-done | bytes 393232 | tf_op jit(solution)/shard_map/reduce_scatter | solution.py:1568
  316.8 85.2 %exchange_gradients.1 = (f32[2,32,2048]{2,1,0:T(8,128)}, f32[2,32,4096]{2,1,0:T(8,128)}, f32[1908,512]{1,0:T(8,128)S(1)}, f32[40,128]{1,0:T(8,128)}, f32[8,128]{1,0:T(8,128)}) custom-call(bf16[1024,512]{1,0:T(8,128)(2,1)} %bitcast.222, bf16[1024,1536]{1,0:T(8,128)(2,1)} %bitcast.205, bf16[1024,512]{1,0:T(8,128)(2,1)} %bitcast.206, ...), custom_call_target="tpu_custom_call" | custom-call | bytes 200000000 | tf_op jit(solution)/shard_map/exchange_gradients/pallas_call | solution.py:528
  402.0 1.8 multiply_reduce_fusion.2
  403.8 1.2 slice.247
  405.0 1.0 while.29
  408.1 2.7 fusion.79
  410.8 2.5 fusion.77
  413.3 1.0 copy-done.24
  414.2 1.2 copy-done.26
  415.4 8.2 %fusion.83 = (bf16[1908,512]{1,0:T(8,128)(2,1)}, f32[1908,512]{1,0:T(8,128)}, f32[1908,512]{1,0:T(8,128)}, f32[1908,512]{1,0:T(8,128)}) fusion(f32[1908,512]{1,0:T(8,128)S(1)} %copy-done.24, f32[1908,512]{1,0:T(8,128)S(1)} %copy-done.26, f32[]{:T(128)S(6)} %min.3, f32[1908,512]{1,0:T(8,128)} %param.28, f32[1908,512]{1,0:T(8,128)} %param.32), kind=kLoop, calls=%fused_computation.234 | loop fusion | flops 15630336 | bytes 29306884 | tf_op jit(solution)/shard_map/convert_element_type | solution.py:1668
  (225 shorter events, 14.8 us)
Async XLA Ops:
  7.2 309.6 %reduce-scatter.2.cloned.1.call-start = ((), (), s32[]{:S(2)}) async-start(), calls=%async_computation.5 | async-start | bytes 6684672 | tf_op jit(solution)/shard_map/reduce_scatter | solution.py:1568
  11.9 1.2 copy-start.6
  13.1 1.0 copy-start.8
  107.8 2.2 copy-start.55
  108.4 15.8 %copy-start.32 = (f32[128,512]{1,0:T(8,128)}, f32[128,512]{1,0:T(8,128)S(1)}, u32[]{:S(2)}) copy-start(f32[128,512]{1,0:T(8,128)S(1)} %slice_convert_fusion) | copy-start | bytes 786436
  108.4 1.6 copy-start.49
  110.9 13.3 %copy-start.21 = (bf16[1024,512]{1,0:T(8,128)(2,1)}, bf16[1024,512]{1,0:T(8,128)(2,1)S(1)}, u32[]{:S(2)}) copy-start(bf16[1024,512]{1,0:T(8,128)(2,1)S(1)} %get-tuple-element.275) | copy-start | bytes 3145732
  111.8 12.4 %slice-start.4 = ((s8[6291456]{0:T(1024)(128)(4,1)}), s8[4194304]{0:T(1024)(128)(4,1)S(1)}, s32[]{:S(2)}) async-start(s8[6291456]{0:T(1024)(128)(4,1)} %bitcast.261), calls=%async_computation.11 | async-start | bytes 8388608
  112.3 3.9 copy-start.34
  112.3 11.8 %slice-start.5 = ((s8[6291456]{0:T(1024)(128)(4,1)}), s8[2097152]{0:T(1024)(128)(4,1)S(1)}, s32[]{:S(2)}) async-start(s8[6291456]{0:T(1024)(128)(4,1)} %bitcast.261), calls=%async_computation.12 | async-start | bytes 4194304
  116.2 7.9 %copy-start.1 = (bf16[8,128,1536]{2,1,0:T(8,128)(2,1)}, bf16[8,128,1536]{2,1,0:T(8,128)(2,1)S(1)}, u32[]{:S(2)}) copy-start(bf16[8,128,1536]{2,1,0:T(8,128)(2,1)S(1)} %add_convert_fusion.1.packed_ref) | copy-start | bytes 9437188
  124.1 1.2 copy-start.5
  125.3 6.9 %copy-start.17 = (f32[8,128,512]{2,1,0:T(8,128)}, f32[8,128,512]{2,1,0:T(8,128)S(1)}, u32[]{:S(2)}) copy-start(f32[8,128,512]{2,1,0:T(8,128)S(1)} %get-tuple-element.457) | copy-start | bytes 6291460
  126.2 6.1 %copy-start.35 = (bf16[8,128,512]{2,1,0:T(8,128)(2,1)}, bf16[8,128,512]{2,1,0:T(8,128)(2,1)S(1)}, u32[]{:S(2)}) copy-start(bf16[8,128,512]{2,1,0:T(8,128)(2,1)S(1)} %fusion.44) | copy-start | bytes 3145732
  126.2 10.6 %slice-start.6 = ((s8[6291456]{0:T(1024)(128)(4,1)}), s8[4194304]{0:T(1024)(128)(4,1)S(1)}, s32[]{:S(2)}) async-start(s8[6291456]{0:T(1024)(128)(4,1)} %bitcast.270), calls=%async_computation.13 | async-start | bytes 8388608
  132.2 2.7 copy-start.40
  132.2 4.6 %slice-start.7 = ((s8[6291456]{0:T(1024)(128)(4,1)}), s8[2097152]{0:T(1024)(128)(4,1)S(1)}, s32[]{:S(2)}) async-start(s8[6291456]{0:T(1024)(128)(4,1)} %bitcast.270), calls=%async_computation.14 | async-start | bytes 4194304
  135.0 20.3 %copy-start.12 = (f32[8,128,512]{2,1,0:T(8,128)}, f32[8,128,512]{2,1,0:T(8,128)S(1)}, u32[]{:S(2)}) copy-start(f32[8,128,512]{2,1,0:T(8,128)S(1)} %get-tuple-element.461) | copy-start | bytes 6291460
  143.8 1.0 copy-start.10
  144.9 7.1 %copy-start.19 = (f32[8,128,512]{2,1,0:T(8,128)}, f32[8,128,512]{2,1,0:T(8,128)S(1)}, u32[]{:S(2)}) copy-start(f32[8,128,512]{2,1,0:T(8,128)S(1)} %get-tuple-element.463) | copy-start | bytes 6291460
  145.7 6.2 %copy-start.46 = (bf16[8,128,512]{2,1,0:T(8,128)(2,1)}, bf16[8,128,512]{2,1,0:T(8,128)(2,1)S(1)}, u32[]{:S(2)}) copy-start(bf16[8,128,512]{2,1,0:T(8,128)(2,1)S(1)} %fusion.45) | copy-start | bytes 3145732
  151.9 2.7 copy-start.57
  154.7 1.8 copy-start.15
  180.2 2.8 copy-start.16
  183.9 5.0 %copy-start.38 = (bf16[8,128,512]{2,1,0:T(8,128)(2,1)}, bf16[8,128,512]{2,1,0:T(8,128)(2,1)S(1)}, u32[]{:S(2)}) copy-start(bf16[8,128,512]{2,1,0:T(8,128)(2,1)S(1)} %fusion.59) | copy-start | bytes 3145732
  184.0 9.2 %slice-start.2 = ((s8[8388608]{0:T(1024)(128)(4,1)}), s8[4194304]{0:T(1024)(128)(4,1)S(1)}, s32[]{:S(2)}) async-start(s8[8388608]{0:T(1024)(128)(4,1)} %bitcast.220), calls=%async_computation.9 | async-start | bytes 8388608
  189.0 4.1 slice-start.3
  193.1 6.0 %copy-start.20 = (f32[8,128,512]{2,1,0:T(8,128)S(1)}, f32[8,128,512]{2,1,0:T(8,128)}, u32[]{:S(2)}) copy-start(f32[8,128,512]{2,1,0:T(8,128)} %copy-done.19) | copy-start | bytes 6291460
  199.2 6.6 %copy-start.23 = (bf16[8,128,2048]{2,1,0:T(8,128)(2,1)}, bf16[8,128,2048]{2,1,0:T(8,128)(2,1)S(1)}, u32[]{:S(2)}) copy-start(bf16[8,128,2048]{2,1,0:T(8,128)(2,1)S(1)} %multiply_convert_fusion.1) | copy-start | bytes 12582916
  199.2 6.6 %copy-start.47 = (bf16[8,128,512]{2,1,0:T(8,128)(2,1)S(1)}, bf16[8,128,512]{2,1,0:T(8,128)(2,1)}, u32[]{:S(2)}) copy-start(bf16[8,128,512]{2,1,0:T(8,128)(2,1)} %copy-done.46) | copy-start | bytes 3145732
  208.3 1.2 copy-start.11
  221.7 6.0 %copy-start.3 = (bf16[8,128,1536]{2,1,0:T(8,128)(2,1)}, bf16[8,128,1536]{2,1,0:T(8,128)(2,1)S(1)}, u32[]{:S(2)}) copy-start(bf16[8,128,1536]{2,1,0:T(8,128)(2,1)S(1)} %attention_back.2) | copy-start | bytes 9437188
  221.7 6.0 %copy-start.45 = (bf16[8,128,512]{2,1,0:T(8,128)(2,1)S(1)}, bf16[8,128,512]{2,1,0:T(8,128)(2,1)}, u32[]{:S(2)}) copy-start(bf16[8,128,512]{2,1,0:T(8,128)(2,1)} %copy-done.44) | copy-start | bytes 3145732
  233.8 1.2 copy-start.39
  235.2 3.3 copy-start.37
  235.2 3.8 copy-start.4
  238.5 2.4 copy-start.13
  240.8 2.9 copy-start.31
  243.7 6.1 %slice-start = ((s8[8388608]{0:T(1024)(128)(4,1)}), s8[4194304]{0:T(1024)(128)(4,1)S(1)}, s32[]{:S(2)}) async-start(s8[8388608]{0:T(1024)(128)(4,1)} %bitcast.218), calls=%async_computation.7 | async-start | bytes 8388608
  244.7 5.1 %copy-start.29 = (bf16[8,128,512]{2,1,0:T(8,128)(2,1)}, bf16[8,128,512]{2,1,0:T(8,128)(2,1)S(1)}, u32[]{:S(2)}) copy-start(bf16[8,128,512]{2,1,0:T(8,128)(2,1)S(1)} %fusion.76) | copy-start | bytes 3145732
  244.7 5.1 %slice-start.1 = ((s8[8388608]{0:T(1024)(128)(4,1)}), s8[4194304]{0:T(1024)(128)(4,1)S(1)}, s32[]{:S(2)}) async-start(s8[8388608]{0:T(1024)(128)(4,1)} %bitcast.218), calls=%async_computation.8 | async-start | bytes 8388608
  255.4 2.0 copy-start.14
  258.1 7.2 %copy-start.18 = (f32[8,128,512]{2,1,0:T(8,128)S(1)}, f32[8,128,512]{2,1,0:T(8,128)}, u32[]{:S(2)}) copy-start(f32[8,128,512]{2,1,0:T(8,128)} %copy-done.17) | copy-start | bytes 6291460
  265.3 3.5 copy-start.2
  268.9 9.9 %copy-start.22 = (bf16[1024,512]{1,0:T(8,128)(2,1)S(1)}, bf16[1024,512]{1,0:T(8,128)(2,1)}, u32[]{:S(2)}) copy-start(bf16[1024,512]{1,0:T(8,128)(2,1)} %copy-done.21) | copy-start | bytes 3145732
  268.9 9.9 %copy-start.33 = (f32[128,512]{1,0:T(8,128)S(1)}, f32[128,512]{1,0:T(8,128)}, u32[]{:S(2)}) copy-start(f32[128,512]{1,0:T(8,128)} %copy-done.32) | copy-start | bytes 786436
  278.8 12.6 %copy-start = (bf16[8,128,1536]{2,1,0:T(8,128)(2,1)}, bf16[8,128,1536]{2,1,0:T(8,128)(2,1)S(1)}, u32[]{:S(2)}) copy-start(bf16[8,128,1536]{2,1,0:T(8,128)(2,1)S(1)} %attention_back.3) | copy-start | bytes 9437188
  287.9 3.0 copy-start.30
  287.9 3.2 copy-start.28
  291.9 1.4 copy-start.48
  291.9 1.4 copy-start.56
  402.0 3.0 copy-start.25
  405.0 1.7 copy-start.52
  405.0 2.4 copy-start.51
  405.0 2.4 copy-start.53
  405.0 2.4 copy-start.54
  405.0 3.1 copy-start.9
  405.0 3.1 copy-start.50
  406.7 4.1 copy-start.7
  406.7 4.1 copy-start.41
  406.8 4.0 copy-start.42
  406.8 4.0 copy-start.43
  410.8 3.4 copy-start.24
  410.8 4.6 %copy-start.26 = (f32[1908,512]{1,0:T(8,128)S(1)}, f32[1908,512]{1,0:T(8,128)}, u32[]{:S(2)}) copy-start(f32[1908,512]{1,0:T(8,128)} %get-tuple-element.287) | copy-start | bytes 11722756
  (3 other events, 2.9 us)
Sparse Core Ops, SparseCore 0:
  233.9 82.8 reduce-scatter.1

commit v9 on v8

--- a/solution.py
+++ b/solution.py
@@ -189,6 +189,7 @@
 CHUNK = 1024
 LAG_Z = 3
 REST_EACH = 4
+HALVED = (2,)
 
 
 def gradient_kernel(chunks, matrices, vec_len, *refs):
@@ -196,10 +197,11 @@
     pairs = [(next(take), next(take)) for _ in range(matrices)]
     vec_ref, sums_ref, near_ref, asked_ref = [next(take) for _ in range(4)]
     attn_out, ffn_out, word_out, vec_out, stats_out = [next(take) for _ in range(5)]
-    held = [None if m is None else next(take) for m, _, _ in chunks]
-    bufs = [[next(take) for _ in range(5)] for _ in chunks]
+    held = [None if chunk[1] is None else next(take) for chunk in chunks]
+    bufs = [[next(take) for _ in range(6 if chunk[4] else 5)] for chunk in chunks]
     near_buf, rows_ref, sum_ref, square_ref, squares_ref = [next(take) for _ in range(5)]
     send_a, recv_a, send_y, recv_y, send_z, recv_z, send_x, recv_x = [next(take) for _ in range(8)]
+    send_h, recv_h = next(take), next(take)
     row_send, row_recv, pass_send, pass_recv, near_sem, square_sem = [
         next(take) for _ in range(6)
     ]
@@ -241,22 +243,35 @@
     def part_of(i):
         return vec_ref if held[i] is None else held[i]
 
+    def halves(i):
+        return chunks[i][4]
+
+    def after_y(i):
+        return bufs[i][1 + halves(i)]
+
+    def half_rows(i, which):
+        rows = bufs[i][0].shape[2] // 2
+        return pl.ds(pl.multiple_of(which * rows, 16), rows)
+
     def copy_a(i):
         src = part_of(i).at[:, :, 1 - core]
         return remote(src, bufs[i][0], send_a.at[i], recv_a.at[i], (d, sibling))
 
+    def copy_h(i):
+        src = bufs[i][0].at[:, :, half_rows(i, 1 - d)]
+        return remote(src, bufs[i][1], send_h.at[i], recv_h.at[i], (1 - d, z))
+
     def copy_y(i):
-        src = bufs[i][0].at[:, 1 - col]
-        return remote(src, bufs[i][1], send_y.at[i], recv_y.at[i], (d, across))
+        src = bufs[i][halves(i)].at[:, 1 - col]
+        return remote(src, after_y(i), send_y.at[i], recv_y.at[i], (d, across))
 
     def copy_z(i, k):
-        src = bufs[i][1].at[lax.rem(line + k, 4)]
-        return remote(
-            src, bufs[i][2].at[k - 1], send_z.at[i, k - 1], recv_z.at[i, k - 1], (d, along(k))
-        )
+        src = after_y(i).at[lax.rem(line + k, 4)]
+        into = bufs[i][-3].at[k - 1]
+        return remote(src, into, send_z.at[i, k - 1], recv_z.at[i, k - 1], (d, along(k)))
 
     def copy_x(i):
-        return remote(bufs[i][3], bufs[i][4], send_x.at[i], recv_x.at[i], (1 - d, z))
+        return remote(bufs[i][-2], bufs[i][-1], send_x.at[i], recv_x.at[i], (1 - d, z))
 
     def row_push(k):
         to = lax.rem(z + k, 16)
@@ -282,7 +297,7 @@
     row_pass(0).start()
 
     def compute(i):
-        matrix, start, width = chunks[i]
+        _, matrix, start, width, _ = chunks[i]
         if matrix is not None:
             left, right = pairs[matrix]
 
@@ -300,54 +315,71 @@
             lax.fori_loop(0, 4, rows_of, 0)
         copy_a(i).start()
 
+    def add_into(buf, count, place, mine):
+        def add_block(b, carry):
+            at = place(b)
+            value = mine(b).astype(jnp.float32) + buf[at].astype(jnp.float32)
+            buf[at] = value.astype(buf.dtype)
+            return carry
+
+        lax.fori_loop(0, count, add_block, 0)
+
     def stage_a(i):
         copy_a(i).wait_recv()
-        buf = bufs[i][0]
-
-        def add_block(b, carry):
-            line_at, col_at = b // 2, lax.rem(b, 2)
-            mine = part_of(i)[line_at, col_at, core].astype(jnp.float32)
-            got = buf[line_at, col_at].astype(jnp.float32)
-            buf[line_at, col_at] = (mine + got).astype(buf.dtype)
-            return carry
-
-        lax.fori_loop(0, 8, add_block, 0)
+        add_into(
+            bufs[i][0],
+            8,
+            lambda b: (b // 2, lax.rem(b, 2)),
+            lambda b: part_of(i)[b // 2, lax.rem(b, 2), core],
+        )
+        (copy_h if halves(i) else copy_y)(i).start()
+
+    def stage_h(i):
+        copy_h(i).wait_recv()
+        add_into(
+            bufs[i][1],
+            8,
+            lambda b: (b // 2, lax.rem(b, 2)),
+            lambda b: bufs[i][0][b // 2, lax.rem(b, 2), half_rows(i, d), :],
+        )
         copy_y(i).start()
 
     def stage_y(i):
         copy_y(i).wait_recv()
-        buf = bufs[i][1]
-
-        def add_block(b, carry):
-            mine = bufs[i][0][b, col].astype(jnp.float32)
-            buf[b] = (mine + buf[b].astype(jnp.float32)).astype(buf.dtype)
-            return carry
-
-        lax.fori_loop(0, 4, add_block, 0)
+        add_into(after_y(i), 4, lambda b: b, lambda b: bufs[i][halves(i)][b, col])
         for k in range(1, 4):
             copy_z(i, k).start()
 
     def stage_z(i):
         for k in range(1, 4):
             copy_z(i, k).wait_recv()
-        value = bufs[i][1][line].astype(jnp.float32)
+        value = after_y(i)[line].astype(jnp.float32)
         for k in range(3):
-            value = value + bufs[i][2][k].astype(jnp.float32)
-        bufs[i][3][...] = value.astype(bufs[i][3].dtype)
+            value = value + bufs[i][-3][k].astype(jnp.float32)
+        bufs[i][-2][...] = value.astype(bufs[i][-2].dtype)
         copy_x(i).start()
 
     def stage_x(i):
-        matrix, start, width = chunks[i]
+        target, _, start, width, _ = chunks[i]
         copy_x(i).wait_recv()
-        value = bufs[i][3][...].astype(jnp.float32) + bufs[i][4][...].astype(jnp.float32)
-        if matrix is None:
-            vec_out[...] = value
+        mine, other = bufs[i][-2][...].astype(jnp.float32), bufs[i][-1][...].astype(jnp.float32)
+        if target is None:
+            vec_out[...] = mine + other
+            return
+        layer, first = target[0], target[1] + start
+        out, first = (attn_out, first) if first < attn_width else (ffn_out, first - attn_width)
+        if halves(i):
+            out[layer, half_rows(i, d), first : first + width] = mine
+            out[layer, half_rows(i, 1 - d), first : first + width] = other
         else:
-            first = start + sum(pairs[m][1].shape[1] for m in range(matrix))
-            if first < attn_width:
-                attn_out[0, :, first : first + width] = value
-            else:
-                ffn_out[0, :, first - attn_width : first - attn_width + width] = value
+            out[layer, :, first : first + width] = mine + other
+
+    def steps_of(i):
+        if halves(i):
+            order = ((stage_a, 0), (stage_h, 1), (stage_y, 2), (stage_z, 2 + LAG_Z), (stage_x, 3 + LAG_Z))
+        else:
+            order = ((stage_a, 0), (stage_y, 1), (stage_z, 1 + LAG_Z), (stage_x, 2 + LAG_Z))
+        return [(i + later, now) for now, later in order]
 
     def pass_on(k):
         row_push(k).wait_recv()
@@ -388,17 +420,13 @@
 
     compute(0)
     passed = 1
-    for t in range(total + LAG_Z + 2):
+    for t in range(total + LAG_Z + 3):
         if t + 1 < total:
             compute(t + 1)
-        if t < total:
-            stage_a(t)
-        if 0 <= t - 1 < total:
-            stage_y(t - 1)
-        if 0 <= t - 1 - LAG_Z < total:
-            stage_z(t - 1 - LAG_Z)
-        if 0 <= t - 2 - LAG_Z < total:
-            stage_x(t - 2 - LAG_Z)
+        for i in range(total - 1, -1, -1):
+            for at, now in steps_of(i):
+                if at == t:
+                    now(i)
         until = min(16, 1 + (t + 1) * 15 // (total - 2))
         for k in range(passed, until):
             pass_on(k)
@@ -410,12 +438,7 @@
         rest.pop(0)()
 
     near.wait()
-    attn_out[1] = near_ref[:, :attn_width].astype(jnp.float32) + near_buf[:, :attn_width].astype(
-        jnp.float32
-    )
-    ffn_out[1] = near_ref[:, attn_width:].astype(jnp.float32) + near_buf[:, attn_width:].astype(
-        jnp.float32
-    )
+    ffn_out[1] = near_ref[...].astype(jnp.float32) + near_buf[...].astype(jnp.float32)
     squares = sum_ref[...]
     square = jnp.sum(squares, axis=1, keepdims=True)
     for out in (attn_out, ffn_out):
@@ -457,6 +480,8 @@
 
     for i in range(total):
         copy_a(i).wait_send()
+        if halves(i):
+            copy_h(i).wait_send()
         copy_y(i).wait_send()
         for k in range(1, 4):
             copy_z(i, k).wait_send()
@@ -482,21 +507,32 @@
 
 
 def exchange_gradients(pairs, vec_parts, sums, near, asked, shard_rows, vec_len, collective_id):
-    chunks = [(None, 0, 128)]
-    for index in (3, 2, 0, 1):
-        columns = pairs[index][1].shape[1]
+    spans = []
+    for index, (_, right) in enumerate(pairs):
+        layer, matrix = index // 4, index % 4
+        columns = right.shape[1]
         width = columns // -(-columns // CHUNK)
+        offset = sum(pairs[m][1].shape[1] for m in range(matrix))
         for start in range(0, columns, width):
-            chunks.append((index, start, width))
+            spans.append(((layer, offset), index, start, width, index in HALVED))
+    plain = [chunk for chunk in spans if not chunk[4]]
+    halved = [chunk for chunk in spans if chunk[4]]
+    chunks = [(None, None, 0, 128, False)]
+    while plain or halved:
+        chunks += halved[:1] + plain[:1]
+        halved, plain = halved[1:], plain[1:]
     half = jnp.bfloat16
     held, bufs = [], []
-    for index, start, width in chunks:
+    for _, index, _, width, halves in chunks:
         kind = vec_parts.dtype if index is None else half
         r = vec_parts.shape[3] if index is None else 32
         if index is not None:
             held.append(pltpu.VMEM((4, 2, 2, r, width), kind))
+        bufs.append(pltpu.VMEM((4, 2, r, width), kind))
+        if halves:
+            r = r // 2
+            bufs.append(pltpu.VMEM((4, 2, r, width), kind))
         bufs += [
-            pltpu.VMEM((4, 2, r, width), kind),
             pltpu.VMEM((4, r, width), kind),
             pltpu.VMEM((3, r, width), kind),
             pltpu.VMEM((r, width), kind),
@@ -514,7 +550,7 @@
         pltpu.VMEM((16, 1, 128), jnp.float32),
     ]
     scratch += [dma((count,)) for _ in range(4)] + [dma((count, 3)) for _ in range(2)]
-    scratch += [dma((count,)) for _ in range(2)]
+    scratch += [dma((count,)) for _ in range(4)]
     scratch += [dma((16,)) for _ in range(4)] + [dma((2,)), dma((2, 16))]
     rows = near.shape[0]
     outs = [
@@ -1161,6 +1197,64 @@
     )(mask, *operands)
 
 
+GELU_SCALE = 0.7978845608028654
+
+
+def feed_back_kernel(middle_ref, down_ref, up_weights, down_weights, bias_ref, *outs):
+    active_ref, d_up_ref, d_first_ref, total_ref = outs
+    middle, d_down = middle_ref[...], down_ref[...]
+    tile = FF // 4
+    d_first = jnp.zeros(d_first_ref.shape, jnp.float32)
+    for start in range(0, FF, tile):
+        at = slice(start, start + tile)
+        upward = contract(middle, up_weights[:, at], 1, 0) + bias_ref[:, at]
+        d_active = contract(d_down, down_weights[:, at], 1, 0).astype(jnp.bfloat16)
+        square = upward * upward
+        bent = jnp.tanh(GELU_SCALE * (upward + 0.044715 * (square * upward)))
+        share = 0.5 * (1.0 + bent)
+        inner = GELU_SCALE * (1.0 + 3.0 * 0.044715 * square)
+        slope = share + 0.5 * upward * (1.0 - bent * bent) * inner
+        active_ref[:, at] = (upward * share).astype(jnp.bfloat16)
+        d_up = (d_active.astype(jnp.float32) * slope).astype(jnp.bfloat16)
+        d_up_ref[:, at] = d_up
+        d_first = d_first + contract(d_up, up_weights[:, at], 1, 1)
+        found = jnp.sum(d_up.astype(jnp.float32), axis=0, keepdims=True)
+        before = jnp.where(pl.program_id(0) == 0, 0.0, total_ref[:, at])
+        total_ref[:, at] = before + found
+    d_first_ref[...] = d_first
+
+
+def feed_back(middle, d_down, weights, up_bias):
+    tokens = middle.shape[0]
+    rows = 256
+    half = jnp.bfloat16
+
+    def by_rows(columns):
+        return pl.BlockSpec((rows, columns), lambda i: (i, 0))
+
+    def matrix(which):
+        return pl.BlockSpec((D, FF), lambda i: (0, which))
+
+    whole = pl.BlockSpec((1, FF), lambda i: (0, 0))
+    return pl.pallas_call(
+        feed_back_kernel,
+        grid=(tokens // rows,),
+        out_shape=(
+            jax.ShapeDtypeStruct((tokens, FF), half),
+            jax.ShapeDtypeStruct((tokens, FF), half),
+            jax.ShapeDtypeStruct((tokens, D), jnp.float32),
+            jax.ShapeDtypeStruct((1, FF), jnp.float32),
+        ),
+        in_specs=[by_rows(D), by_rows(D), matrix(1), matrix(2), whole],
+        out_specs=(by_rows(FF), by_rows(FF), by_rows(D), whole),
+        compiler_params=pltpu.CompilerParams(vmem_limit_bytes=40 * 1024 * 1024),
+        cost_estimate=pl.CostEstimate(
+            flops=6 * tokens * D * FF, bytes_accessed=24 * tokens * D, transcendentals=tokens * FF
+        ),
+        name="feed_back",
+    )(middle, d_down, weights, weights, up_bias.reshape(1, FF))
+
+
 LAYER_ROWS = 8 + FF // D
 
 
@@ -1197,23 +1291,20 @@
     )
 
 
-GELU_SCALE = 0.7978845608028654
-
-
 def gelu(value):
     bent = jnp.tanh(GELU_SCALE * (value + 0.044715 * value * value * value))
     return 0.5 * value * (1.0 + bent)
 
 
-def gelu_slope(value):
-    square = value * value
-    bent = jnp.tanh(GELU_SCALE * (value + 0.044715 * square * value))
-    inner = GELU_SCALE * (1.0 + 3.0 * 0.044715 * square)
-    return 0.5 * (1.0 + bent) + 0.5 * value * (1.0 - bent * bent) * inner
+EDGES = (0, 3 * D, 4 * D, 4 * D + FF, 4 * D + 2 * FF)
+
+
+def four_matrices(weights):
+    return [weights[:, first:last] for first, last in zip(EDGES, EDGES[1:])]
 
 
 def layer_forward(hidden, weights, vectors, mask):
-    in_weights, out_weights, up_weights, down_weights = weights
+    in_weights, out_weights, up_weights, down_weights = four_matrices(weights)
     q_bias, v_bias, o_bias, gain_one, shift_one, up_bias, down_bias, gain_two, second_shift = (
         layer_vectors(vectors)
     )
@@ -1230,16 +1321,16 @@
     downward = einsum_plain("nsf,df->nsd", active, down_weights) + down_bias
     output, normal_two, inverse_two = norm_forward(first + downward, gain_two, second_shift)
     kept = (
-        entry, packed, context, middle, upward, active,
+        entry, packed, context, middle,
         normal_one, inverse_one, normal_two, inverse_two,
     )
     return output, kept
 
 
-def layer_backward(kept, weights, vectors, mask, grad):
-    in_weights, out_weights, up_weights, down_weights = weights
-    entry, packed, context, middle, upward, active = kept[:6]
-    normal_one, inverse_one, normal_two, inverse_two = kept[6:]
+def layer_backward(kept, weights, vectors, mask, grad, midway):
+    in_weights, out_weights, _, _ = four_matrices(weights)
+    entry, packed, context, middle = kept[:4]
+    normal_one, inverse_one, normal_two, inverse_two = kept[4:]
     gain_one, gain_two = layer_vectors(vectors)[3], layer_vectors(vectors)[7]
     half = jnp.bfloat16
 
@@ -1248,12 +1339,12 @@
 
     d_second, d_gain_two, d_shift_two = norm_back(grad, normal_two, inverse_two, gain_two)
     d_down = lax.optimization_barrier(d_second.astype(half))
-    d_active = jnp.einsum("nsd,df->nsf", d_down, down_weights, preferred_element_type=jnp.float32)
-    d_active = lax.optimization_barrier(d_active.astype(half)).astype(jnp.float32)
-    d_up = lax.optimization_barrier((d_active * gelu_slope(upward)).astype(half))
-    d_first = d_second + jnp.einsum(
-        "nsf,df->nsd", d_up, up_weights, preferred_element_type=jnp.float32
+    flat_middle, flat_down = middle.reshape(-1, D), d_down.reshape(-1, D)
+    active, d_up, d_first, d_up_bias = feed_back(
+        flat_middle, flat_down, weights, layer_vectors(vectors)[5]
     )
+    feed_pairs = [(flat_middle, d_up), (flat_down, active)]
+    d_first = midway(feed_pairs, d_second + d_first.reshape(d_second.shape))
     d_middle, d_gain_one, d_shift_one = norm_back(d_first, normal_one, inverse_one, gain_one)
     d_attended = lax.optimization_barrier(d_middle.astype(half))
     d_context = jnp.einsum(
@@ -1268,7 +1359,7 @@
     packed_total = total(d_packed)
     pieces = [
         packed_total[:D], packed_total[2 * D :], total(d_attended), d_gain_one, d_shift_one,
-        total(d_up), total(d_down), d_gain_two, d_shift_two,
+        d_up_bias, total(d_down), d_gain_two, d_shift_two,
     ]
     d_vectors, at = jnp.zeros((LAYER_ROWS, D), jnp.float32), 0
     for piece in pieces:
@@ -1277,11 +1368,9 @@
         at = at + rows.shape[0]
     flat = [
         (left.reshape(-1, left.shape[2]), right.reshape(-1, right.shape[2]))
-        for left, right in (
-            (entry, d_packed), (context, d_attended), (middle, d_up), (d_down, active)
-        )
+        for left, right in ((entry, d_packed), (context, d_attended))
     ]
-    return d_hidden, flat, d_vectors
+    return d_hidden, flat + feed_pairs, d_vectors
 
 
 def weight_gradient(left, right):
@@ -1506,14 +1595,10 @@
     hidden = embedded
     mask = key_mask.astype(jnp.float32)[:, None, :]
     saved = []
-    layer_parts = []
     pooled = []
     for layer_index in range(LAYERS):
         weights = layer_weights[layer_index]
-        edges = (0, 3 * D, 4 * D, 4 * D + FF, 4 * D + 2 * FF)
-        parts = [weights[:, first:last] for first, last in zip(edges, edges[1:])]
-        layer_parts.append(parts)
-        hidden, kept = layer_forward(hidden, parts, vec_parts[1 + layer_index], mask)
+        hidden, kept = layer_forward(hidden, weights, vec_parts[1 + layer_index], mask)
         saved.append(kept)
         pooled.append(pool_rows(hidden, key_mask, seq_lengths).astype(jnp.bfloat16))
 
@@ -1546,26 +1631,34 @@
     shallow_back, deep_back = pooled_grads[0], pooled_grads[1]
     share = key_mask.astype(jnp.float32) / seq_lengths.astype(jnp.float32)[:, None]
     grad_hidden = jnp.zeros_like(embedded)
-    weight_parts = []
+    weight_parts, layer_pairs = [], []
     vec_grads = [None] * LAYERS
     for layer_index in range(LAYERS - 1, -1, -1):
         if layer_index == LAYERS - 1:
             grad_hidden = grad_hidden + deep_back[:, None, :] * share[:, :, None]
         if layer_index == 0:
             grad_hidden = grad_hidden + shallow_back[:, None, :] * share[:, :, None]
+        by_scatter = []
+
+        def scatter(pairs, after):
+            both = jnp.concatenate([weight_gradient(*pair) for pair in pairs], axis=1)
+            both, after = lax.optimization_barrier((both, after))
+            by_scatter.append(lax.psum_scatter(both, "zero", scatter_dimension=0, tiled=True))
+            return after
+
+        early = by_hand and layer_index == LAYERS - 1
         grad_hidden, pairs, vec_grads[layer_index] = layer_backward(
             saved[layer_index],
-            layer_parts[layer_index],
+            layer_weights[layer_index],
             vec_parts[1 + layer_index],
             mask,
             grad_hidden,
-        )
-        if by_hand and layer_index == 0:
-            weight_parts.insert(0, pairs)
-        else:
-            both = jnp.concatenate([weight_gradient(*pair) for pair in pairs], axis=1)
-            both, grad_hidden = lax.optimization_barrier((both, grad_hidden))
-            weight_parts.insert(0, lax.psum_scatter(both, "zero", scatter_dimension=0, tiled=True))
+            scatter if early else lambda pairs, after: after,
+        )
+        if not by_hand:
+            grad_hidden = scatter(pairs, grad_hidden)
+        layer_pairs.insert(0, pairs)
+        weight_parts = by_scatter + weight_parts
     rows_grad, embed_grads = embed_back(grad_hidden)
     vec_grad = jnp.concatenate([embed_grads] + vec_grads, axis=0)
     down_local = jnp.stack([part[5 + FF // D] for part in vec_grads])
@@ -1606,10 +1699,10 @@
 
     if by_hand:
         attn_shard, ffn_shard, word_grad, vec_sum, squares = exchange_gradients(
-            weight_parts[0],
+            layer_pairs[0] + layer_pairs[1][:2],
             vec_blocks.reshape(4, 2, 2, lines, 128),
             sums,
-            weight_parts[1],
+            weight_parts[0],
             asked_mine.reshape(ndp, 1, nz * room),
             shard_rows,
             vec_len,

time: 439 us -> 425 us (0.968)
  Pallas kernels: 233 us -> 273 us
  matrix products: 77.7 us -> 45.7 us
  waiting for transfers between devices: 20.8 us -> 0.02 us
  other arithmetic: 63.6 us -> 53.9 us
  local copies, waits for them, and re-layouts: 17 us -> 25.1 us
    pallas_call x0 -> x2, Pallas kernels: none -> 28.6 us  [feed_back(): pl.pallas_call(feed_back_kernel, grid=(tokens // rows,), out_shape=(jax.S...]
    dot_general x4 -> x0, matrix products: 23 us -> none  [the longest x2 13.8 us: layer_backward(): jnp.einsum('nsf,df->nsd', d_up, up_weights, preferred_element_type=jnp.fl...]
    reduce_scatter x1, waiting for transfers between devices: 20.8 us -> 0.01 us  [scatter(): lax.psum_scatter(both, 'zero', scatter_dimension=0, tiled=True)]
    convert_element_type x2 -> x0, other arithmetic: 11.6 us -> none  [layer_backward(): (d_active * gelu_slope(upward)).astype(half)]
    pallas_call x1, Pallas kernels: 85.2 us -> 95.9 us  [exchange_gradients(): pl.pallas_call(functools.partial(gradient_kernel, tuple(chunks), len(pair...]
    unnamed x136 -> x120, local copies, waits for them, and re-layouts: 12.5 us -> 20 us
    dot_general x4 -> x2, matrix products: 10.1 us -> 4.93 us  [weight_gradient(): lax.dot_general(left, right, (((0,), (0,)), ((), ())), preferred_element_...]
  transfers between devices with their start and end apart: 1 -> 1, of which waited for: 1 -> 0; matrix products, arithmetic and copies ran while one was open for 11% -> 10% of each run, Pallas kernels for 2% -> 8%
where the time goes in v9:
time: 425 us; the launch traced here: 417 us
  Pallas kernels  273 us (64%)
  other arithmetic  53.9 us (13%)
  matrix products  45.7 us (11%)
  local copies, waits for them, and re-layouts  25.1 us (6%)
  between operations  17.7 us (4%)
    pallas_call x1, Pallas kernels, exchange_gradients(): pl.pallas_call(functools.partial(gradient_kernel, tuple(chunks), len(pair...  95.9 us
    pallas_call x1, Pallas kernels, exchange_start(): pl.pallas_call(functools.partial(start_kernel, shard_rows, room), out_sha...  92.3 us
    pallas_call x4, Pallas kernels, attention_call(): pl.pallas_call(kernel, grid=(count,), out_shape=jax.ShapeDtypeStruct((cou...  32.6 us
    pallas_call x2, Pallas kernels, feed_back(): pl.pallas_call(feed_back_kernel, grid=(tokens // rows,), out_shape=(jax.S...  28.6 us
    pallas_call x1, Pallas kernels, contrastive(): pl.pallas_call(contrastive_kernel, out_shape=(jax.ShapeDtypeStruct((8, 12...  23.6 us
    unnamed x120, local copies, waits for them, and re-layouts  20 us
    dot_general x7, matrix products, matmul(): return jnp.dot(left, right, preferred_element_type=jnp.float32)  17.9 us
    dot_general x2, matrix products, layer_backward(): jnp.einsum('nsp,dp->nsd', d_packed, in_weights, preferred_element_type=jn...  10.1 us
  transfers between devices with their start and end apart: 1, of which 0 were waited for; matrix products, arithmetic and copies ran while one was open for 10% of the time, Pallas kernels for 8%

profile of v9, /device:TPU:0, one launch (start us, length us, event | category | flops | bytes accessed | tf_op | source)
XLA Modules:
  0.0 417.2 jit_solution(4156227611585523225)
XLA Ops:
  7.2 0.8 copy.55
  8.2 0.7 sign.30
  8.9 0.9 copy.54.refs_0_
  11.1 0.7 convert_element_type.239
  11.9 1.2 copy-done.12
  13.1 1.0 copy-done.16
  14.1 92.3 %exchange_start.1 = (s32[1024,1]{1,0:T(8,128)S(1)}, s32[1024,1]{1,0:T(8,128)S(1)}, bf16[32,8,128]{2,1,0:T(8,128)(2,1)S(1)}, s32[32,1,128]{2,1,0:T(1,128)S(1)}, b...) custom-call(s32[1024,1]{1,0:T(8,128)S(1)} %copy.54.refs_0_, ...), custom_call_target="tpu_custom_call" | custom-call | bytes 150000000 | tf_op jit(solution)/shard_map/exchange_start/pallas_call | solution.py:885
  106.8 0.7 slice_reduce_fusion.1
  108.4 1.6 fusion.45
  110.0 0.9 while.28
  112.4 3.9 add_convert_fusion.1.packed_ref
  116.2 7.9 %attention.2 = bf16[8,128,512]{2,1,0:T(8,128)(2,1)S(1)} custom-call(f32[8,1,128]{2,1,0:T(1,128)S(1)} %compare_convert_fusion.mask_ref, bf16[8,128,1536]{2,1,0:T(8,128)(2,1)S(1)} %add_convert_fusion.1.packed_ref), custom_call_target="tpu_custom_call" | custom-call | flops 1000000000 | bytes 5242880 | tf_op jit(solution)/shard_map/attention/pallas_call | solution.py:1185
  124.2 1.1 fusion.81
  126.2 4.2 fusion.19
  130.4 2.7 fusion.82
  134.0 1.0 copy-done.41
  135.0 1.8 add_convert_fusion.packed_ref
  136.8 5.2 %attention.3 = bf16[8,128,512]{2,1,0:T(8,128)(2,1)S(1)} custom-call(f32[8,1,128]{2,1,0:T(1,128)S(1)} %compare_convert_fusion.mask_ref, bf16[8,128,1536]{2,1,0:T(8,128)(2,1)S(1)} %add_convert_fusion.packed_ref), custom_call_target="tpu_custom_call" | custom-call | flops 1000000000 | bytes 5242880 | tf_op jit(solution)/shard_map/attention/pallas_call | solution.py:1185
  142.0 1.0 fusion.83
  143.9 4.3 %fusion.24 = bf16[8,128,2048]{2,1,0:T(8,128)(2,1)S(1)} fusion(f32[2048]{0:T(1024)S(1)} %get-tuple-element.459, bf16[8,128,512]{2,1,0:T(8,128)(2,1)S(1)} %fusion.42, bf16[512,6144]{1,0:T(8,128)(2,1)S(1)} %bitcast.258), kind=kOutput, calls=%fused_computation.43 | convolution fusion | flops 2168455168 | bytes 7348224 | tf_op jit(solution)/shard_map/dot_general | solution.py:78
  148.3 2.7 fusion.84
  151.6 1.2 multiply_reduce_fusion.14
  152.9 23.6 %contrastive.1 = (f32[8,128]{1,0:T(8,128)S(1)}, f32[2,2,8,512]{3,2,1,0:T(8,128)S(1)}) custom-call(bf16[2,8,512]{2,1,0:T(8,128)(2,1)S(1)} %reshape.668.block_ref, s32[128,128]{1,0:T(8,128)S(1)} %reshape.669.false_ref, s32[128,1]{1,0:T(8,128)S(1)} %reshape_reshape.16.pair_ref), custom_call_target="tpu_custom_call" | custom-call | flops 1000000000 | bytes 3000000 | tf_op jit(solution)/shard_map/contrastive/pallas_call | solution.py:1088
  176.6 1.4 fusion.37
  178.1 2.1 fusion.47
  180.2 14.3 %feed_back.2 = (bf16[1024,2048]{1,0:T(8,128)(2,1)S(1)}, bf16[1024,2048]{1,0:T(8,128)(2,1)S(1)}, f32[1024,512]{1,0:T(8,128)S(1)}, f32[1,2048]{1,0:T(1,128)S(1)}) custom-call(bf16[1024,512]{1,0:T(8,128)(2,1)S(1)} %bitcast.193, bf16[1024,512]{1,0:T(8,128)(2,1)S(1)} %bitcast.189, bf16[512,6144]{1,0:T(8,128)(2,1)} %bitcast.250, bf16[512,6144]{1,0:T(8,128)(2,1)} %bitcast.251, ...), custom_call_target="tpu_custom_call" | custom-call | flops 6442450944 | bytes 12582912 | tf_op jit(solution)/shard_map/feed_back/pallas_call | solution.py:1239
  194.5 1.9 fusion.46
  196.5 2.5 convolution_convert_fusion.1
  198.9 2.5 convolution_convert_fusion
  201.4 2.5 pad_maximum_fusion
  204.2 3.4 multiply_reduce_fusion.3
  207.8 0.8 fusion.51
  208.8 0.8 copy-done.34
  209.6 2.8 convolution_convert_fusion.3.grad_ref
  212.4 0.7 reshape_squeeze.3.refs_15_
  214.8 2.0 copy-done.5
  216.9 1.3 copy-done.18
  218.1 9.8 %attention_back.2 = bf16[8,128,1536]{2,1,0:T(8,128)(2,1)S(1)} custom-call(f32[8,1,128]{2,1,0:T(1,128)S(1)} %compare_convert_fusion.mask_ref, bf16[8,128,1536]{2,1,0:T(8,128)(2,1)S(1)} %copy-done.5, bf16[8,128,512]{2,1,0:T(8,128)(2,1)S(1)} %copy-done.18), custom_call_target="tpu_custom_call" | custom-call | flops 1000000000 | bytes 5242880 | tf_op jit(solution)/shard_map/attention_back/pallas_call | solution.py:1185
  228.5 2.2 copy-done.20
  230.7 4.7 %multiply_reduce_fusion.4 = (f32[512]{0:T(512)S(1)}, f32[8,128]{1,0:T(8,128)S(1)}, f32[8,128]{1,0:T(8,128)S(1)}, f32[512]{0:T(512)S(1)}, f32[8,128,512]{2,1,0:T(8,128)S(1)}) fusion(f32[8,128]{1,0:T(8,128)S(1)} %add_rsqrt_fusion.2, f32[8,128,512]{2,1,0:T(8,128)S(1)} %copy-done.20, f32[8,128]{1,0:T(8,128)S(1)} %broadcast_multiply_fusion.10, ...), kind=kOutput, calls=%fused_computation.83 | convolution fusion | flops 1620571136 | bytes 13168640 | tf_op jit(solution)/shard_map/nsp,dp->nsd/dot_general | solution.py:1356
  235.6 0.8 fusion.53
  237.4 14.3 %feed_back.3 = (bf16[1024,2048]{1,0:T(8,128)(2,1)S(1)}, bf16[1024,2048]{1,0:T(8,128)(2,1)S(1)}, f32[1024,512]{1,0:T(8,128)S(1)}, f32[1,2048]{1,0:T(1,128)S(1)}) custom-call(bf16[1024,512]{1,0:T(8,128)(2,1)S(1)} %bitcast.188, bf16[1024,512]{1,0:T(8,128)(2,1)S(1)} %bitcast.183, bf16[512,6144]{1,0:T(8,128)(2,1)} %bitcast.241, bf16[512,6144]{1,0:T(8,128)(2,1)} %bitcast.242, ...), custom_call_target="tpu_custom_call" | custom-call | flops 6442450944 | bytes 12582912 | tf_op jit(solution)/shard_map/feed_back/pallas_call | solution.py:1239
  251.8 2.1 copy-done.14
  253.9 2.0 copy-done.15
  256.6 4.0 multiply_reduce_fusion.5
  260.6 0.8 fusion.54
  261.4 1.0 copy-done.35
  262.4 1.8 convolution_convert_fusion.2.grad_ref
  264.2 9.6 %attention_back.3 = bf16[8,128,1536]{2,1,0:T(8,128)(2,1)S(1)} custom-call(f32[8,1,128]{2,1,0:T(1,128)S(1)} %compare_convert_fusion.mask_ref, bf16[8,128,1536]{2,1,0:T(8,128)(2,1)S(1)} %copy-done.3, bf16[8,128,512]{2,1,0:T(8,128)(2,1)S(1)} %convolution_convert_fusion.2.grad_ref), custom_call_target="tpu_custom_call" | custom-call | flops 1000000000 | bytes 5242880 | tf_op jit(solution)/shard_map/attention_back/pallas_call | solution.py:1185
  273.8 5.4 %multiply_reduce_fusion.7 = (f32[512]{0:T(512)S(1)}, f32[8,128]{1,0:T(8,128)S(1)}, f32[512]{0:T(512)S(1)}, f32[8,128,512]{2,1,0:T(8,128)S(1)}) fusion(f32[8,128]{1,0:T(8,128)S(1)} %bitcast_rsqrt_fusion, f32[8,128]{1,0:T(8,128)S(1)} %get-tuple-element.469, f32[128,512]{1,0:T(8,128)S(1)} %copy-done.39, bf16[1024,512]{1,0:T(8,128)(2,1)S(1)} %copy-done.30, ...), kind=kOutput, calls=%fused_computation.88 | convolution fusion | flops 1621620736 | bytes 13406208 | tf_op jit(solution)/shard_map/nsp,dp->nsd/dot_general | solution.py:1356
  279.2 2.0 add_add_fusion
  281.2 1.8 reduce_sum.420
  283.1 3.0 add_convert_fusion.2
  287.6 0.8 copy.63
  288.4 2.7 fusion.31
  291.1 95.9 %exchange_gradients.1 = (f32[2,32,2048]{2,1,0:T(8,128)}, f32[2,32,4096]{2,1,0:T(8,128)}, f32[1908,512]{1,0:T(8,128)S(1)}, f32[40,128]{1,0:T(8,128)}, f32[8,128]{1,0:T(8,128)}) custom-call(bf16[1024,512]{1,0:T(8,128)(2,1)} %bitcast.207, bf16[1024,1536]{1,0:T(8,128)(2,1)} %bitcast.182, bf16[1024,512]{1,0:T(8,128)(2,1)} %bitcast.185, ...), custom_call_target="tpu_custom_call" | custom-call | bytes 200000000 | tf_op jit(solution)/shard_map/exchange_gradients/pallas_call | solution.py:564
  387.0 1.8 multiply_reduce_fusion.2
  388.8 1.2 slice.253
  390.0 1.0 while.29
  393.1 2.7 fusion.68
  395.9 2.5 fusion.66
  398.4 1.0 copy-done.31
  399.3 1.2 copy-done.33
  400.5 8.2 %fusion.72 = (bf16[1908,512]{1,0:T(8,128)(2,1)}, f32[1908,512]{1,0:T(8,128)}, f32[1908,512]{1,0:T(8,128)}, f32[1908,512]{1,0:T(8,128)}) fusion(f32[1908,512]{1,0:T(8,128)S(1)} %copy-done.31, f32[1908,512]{1,0:T(8,128)S(1)} %copy-done.33, f32[]{:T(128)S(6)} %min.3, f32[1908,512]{1,0:T(8,128)} %param.28, f32[1908,512]{1,0:T(8,128)} %param.32), kind=kLoop, calls=%fused_computation.213 | loop fusion | flops 15630336 | bytes 29306884 | tf_op jit(solution)/shard_map/convert_element_type | solution.py:1761
  (204 shorter events, 15.0 us)
Async XLA Ops:
  7.2 283.9 %reduce-scatter.2.cloned.1.call-start = ((), (), s32[]{:S(2)}) async-start(), calls=%async_computation.5 | async-start | bytes 4456448 | tf_op jit(solution)/shard_map/reduce_scatter | solution.py:1646
  11.9 1.2 copy-start.12
  13.1 1.0 copy-start.16
  107.8 2.2 copy-start.52
  108.4 15.8 %copy-start.38 = (f32[128,512]{1,0:T(8,128)}, f32[128,512]{1,0:T(8,128)S(1)}, u32[]{:S(2)}) copy-start(f32[128,512]{1,0:T(8,128)S(1)} %slice_convert_fusion) | copy-start | bytes 786436
  108.4 1.6 copy-start.46
  110.9 13.3 %copy-start.29 = (bf16[1024,512]{1,0:T(8,128)(2,1)}, bf16[1024,512]{1,0:T(8,128)(2,1)S(1)}, u32[]{:S(2)}) copy-start(bf16[1024,512]{1,0:T(8,128)(2,1)S(1)} %get-tuple-element.283) | copy-start | bytes 3145732
  111.8 12.4 %slice-start = ((s8[6291456]{0:T(1024)(128)(4,1)}), s8[4194304]{0:T(1024)(128)(4,1)S(1)}, s32[]{:S(2)}) async-start(s8[6291456]{0:T(1024)(128)(4,1)} %bitcast.245), calls=%async_computation.7 | async-start | bytes 8388608
  112.3 3.9 copy-start.40
  112.3 11.8 %slice-start.1 = ((s8[6291456]{0:T(1024)(128)(4,1)}), s8[2097152]{0:T(1024)(128)(4,1)S(1)}, s32[]{:S(2)}) async-start(s8[6291456]{0:T(1024)(128)(4,1)} %bitcast.245), calls=%async_computation.8 | async-start | bytes 4194304
  116.2 7.9 %copy-start.2 = (bf16[8,128,1536]{2,1,0:T(8,128)(2,1)}, bf16[8,128,1536]{2,1,0:T(8,128)(2,1)S(1)}, u32[]{:S(2)}) copy-start(bf16[8,128,1536]{2,1,0:T(8,128)(2,1)S(1)} %add_convert_fusion.1.packed_ref) | copy-start | bytes 9437188
  124.1 1.2 copy-start.8
  125.3 5.1 %copy-start.25 = (f32[8,128,512]{2,1,0:T(8,128)}, f32[8,128,512]{2,1,0:T(8,128)S(1)}, u32[]{:S(2)}) copy-start(f32[8,128,512]{2,1,0:T(8,128)S(1)} %get-tuple-element.474) | copy-start | bytes 6291460
  126.2 4.2 %copy-start.10 = (bf16[8,128,512]{2,1,0:T(8,128)(2,1)}, bf16[8,128,512]{2,1,0:T(8,128)(2,1)S(1)}, u32[]{:S(2)}) copy-start(bf16[8,128,512]{2,1,0:T(8,128)(2,1)S(1)} %fusion.41) | copy-start | bytes 3145732
  126.2 8.8 %slice-start.2 = ((s8[6291456]{0:T(1024)(128)(4,1)}), s8[4194304]{0:T(1024)(128)(4,1)S(1)}, s32[]{:S(2)}) async-start(s8[6291456]{0:T(1024)(128)(4,1)} %bitcast.254), calls=%async_computation.9 | async-start | bytes 8388608
  130.4 4.6 %slice-start.3 = ((s8[6291456]{0:T(1024)(128)(4,1)}), s8[2097152]{0:T(1024)(128)(4,1)S(1)}, s32[]{:S(2)}) async-start(s8[6291456]{0:T(1024)(128)(4,1)} %bitcast.254), calls=%async_computation.10 | async-start | bytes 4194304
  133.1 18.4 %copy-start.19 = (f32[8,128,512]{2,1,0:T(8,128)}, f32[8,128,512]{2,1,0:T(8,128)S(1)}, u32[]{:S(2)}) copy-start(f32[8,128,512]{2,1,0:T(8,128)S(1)} %get-tuple-element.476) | copy-start | bytes 6291460
  134.0 1.0 copy-start.41
  136.8 5.2 %copy-start.4 = (bf16[8,128,1536]{2,1,0:T(8,128)(2,1)}, bf16[8,128,1536]{2,1,0:T(8,128)(2,1)S(1)}, u32[]{:S(2)}) copy-start(bf16[8,128,1536]{2,1,0:T(8,128)(2,1)S(1)} %add_convert_fusion.packed_ref) | copy-start | bytes 9437188
  142.0 1.1 copy-start.9
  143.1 5.2 %copy-start.23 = (f32[8,128,512]{2,1,0:T(8,128)}, f32[8,128,512]{2,1,0:T(8,128)S(1)}, u32[]{:S(2)}) copy-start(f32[8,128,512]{2,1,0:T(8,128)S(1)} %get-tuple-element.478) | copy-start | bytes 6291460
  151.0 25.5 %copy-start.21 = (f32[8,128,512]{2,1,0:T(8,128)}, f32[8,128,512]{2,1,0:T(8,128)S(1)}, u32[]{:S(2)}) copy-start(f32[8,128,512]{2,1,0:T(8,128)S(1)} %get-tuple-element.480) | copy-start | bytes 6291460
  180.2 14.3 %copy-start.22 = (f32[8,128,512]{2,1,0:T(8,128)S(1)}, f32[8,128,512]{2,1,0:T(8,128)}, u32[]{:S(2)}) copy-start(f32[8,128,512]{2,1,0:T(8,128)} %copy-done.21) | copy-start | bytes 6291460
  204.2 3.4 copy-start.24
  204.2 3.7 copy-start.27
  208.6 1.0 copy-start.34
  214.8 2.0 copy-start.5
  216.9 1.3 copy-start.18
  218.1 10.4 %copy-start.28 = (f32[8,128,512]{2,1,0:T(8,128)S(1)}, f32[8,128,512]{2,1,0:T(8,128)}, u32[]{:S(2)}) copy-start(f32[8,128,512]{2,1,0:T(8,128)} %fusion.46) | copy-start | bytes 6291460
  228.0 7.4 %copy-start = (bf16[8,128,1536]{2,1,0:T(8,128)(2,1)}, bf16[8,128,1536]{2,1,0:T(8,128)(2,1)S(1)}, u32[]{:S(2)}) copy-start(bf16[8,128,1536]{2,1,0:T(8,128)(2,1)S(1)} %attention_back.2) | copy-start | bytes 9437188
  228.0 2.7 copy-start.20
  235.4 1.3 copy-start.37
  235.5 1.9 copy-start.11
  236.8 15.0 %copy-start.6 = (bf16[8,128,512]{2,1,0:T(8,128)(2,1)}, bf16[8,128,512]{2,1,0:T(8,128)(2,1)S(1)}, u32[]{:S(2)}) copy-start(bf16[8,128,512]{2,1,0:T(8,128)(2,1)S(1)} %fusion.53) | copy-start | bytes 3145732
  251.8 2.1 copy-start.14
  253.9 2.0 copy-start.15
  256.6 4.0 copy-start.26
  260.6 3.5 copy-start.3
  261.4 1.0 copy-start.35
  264.2 9.7 %copy-start.30 = (bf16[1024,512]{1,0:T(8,128)(2,1)S(1)}, bf16[1024,512]{1,0:T(8,128)(2,1)}, u32[]{:S(2)}) copy-start(bf16[1024,512]{1,0:T(8,128)(2,1)} %copy-done.29) | copy-start | bytes 3145732
  264.2 9.7 %copy-start.39 = (f32[128,512]{1,0:T(8,128)S(1)}, f32[128,512]{1,0:T(8,128)}, u32[]{:S(2)}) copy-start(f32[128,512]{1,0:T(8,128)} %copy-done.38) | copy-start | bytes 786436
  273.8 12.6 %copy-start.1 = (bf16[8,128,1536]{2,1,0:T(8,128)(2,1)}, bf16[8,128,1536]{2,1,0:T(8,128)(2,1)S(1)}, u32[]{:S(2)}) copy-start(bf16[8,128,1536]{2,1,0:T(8,128)(2,1)S(1)} %attention_back.3) | copy-start | bytes 9437188
  283.0 3.0 copy-start.7
  283.0 3.2 copy-start.36
  287.0 1.4 copy-start.45
  287.0 1.4 copy-start.53
  387.0 3.0 copy-start.32
  390.0 1.8 copy-start.49
  390.0 2.5 copy-start.48
  390.0 2.5 copy-start.50
  390.0 2.5 copy-start.51
  390.0 3.1 copy-start.17
  390.0 3.1 copy-start.47
  391.8 4.1 copy-start.13
  391.8 4.1 copy-start.42
  391.9 4.0 copy-start.43
  391.9 4.0 copy-start.44
  395.9 3.4 copy-start.31
  395.9 4.6 %copy-start.33 = (f32[1908,512]{1,0:T(8,128)S(1)}, f32[1908,512]{1,0:T(8,128)}, u32[]{:S(2)}) copy-start(f32[1908,512]{1,0:T(8,128)} %get-tuple-element.303) | copy-start | bytes 11722756
Sparse Core Ops, SparseCore 0:
  204.0 70.3 reduce-scatter.1

commit v10 on v9

--- a/solution.py
+++ b/solution.py
@@ -200,6 +200,7 @@
     held = [None if chunk[1] is None else next(take) for chunk in chunks]
     bufs = [[next(take) for _ in range(6 if chunk[4] else 5)] for chunk in chunks]
     near_buf, rows_ref, sum_ref, square_ref, squares_ref = [next(take) for _ in range(5)]
+    left_buf, right_buf, fetch_sem = [next(take) for _ in range(3)]
     send_a, recv_a, send_y, recv_y, send_z, recv_z, send_x, recv_x = [next(take) for _ in range(8)]
     send_h, recv_h = next(take), next(take)
     row_send, row_recv, pass_send, pass_recv, near_sem, square_sem = [
@@ -296,16 +297,40 @@
     rows_ref[d, z] = sums_ref[z]
     row_pass(0).start()
 
+    made = [i for i in range(total) if held[i] is not None]
+
+    def fetches(i):
+        _, matrix, start, width, _ = chunks[i]
+        slot = made.index(i) % 2
+        left, right = pairs[matrix]
+        return (
+            pltpu.make_async_copy(left, left_buf.at[slot], fetch_sem.at[0, slot]),
+            pltpu.make_async_copy(
+                right.at[:, pl.ds(start, width)],
+                right_buf.at[slot, :, pl.ds(0, width)],
+                fetch_sem.at[1, slot],
+            ),
+        )
+
+    for copy in fetches(made[0]):
+        copy.start()
+
     def compute(i):
         _, matrix, start, width, _ = chunks[i]
         if matrix is not None:
-            left, right = pairs[matrix]
+            place = made.index(i)
+            slot = place % 2
+            if place + 1 < len(made):
+                for copy in fetches(made[place + 1]):
+                    copy.start()
+            for copy in fetches(i):
+                copy.wait()
 
             def rows_of(j, carry):
                 at = pl.ds(pl.multiple_of(j * 128, 128), 128)
                 found = lax.dot_general(
-                    left[:, at],
-                    right[:, start : start + width],
+                    left_buf[slot, :, at],
+                    right_buf[slot, :, 0:width],
                     (((0,), (0,)), ((), ())),
                     preferred_element_type=jnp.float32,
                 )
@@ -548,6 +573,9 @@
         pltpu.VMEM((1, features), jnp.float32),
         pltpu.VMEM((1, 128), jnp.float32),
         pltpu.VMEM((16, 1, 128), jnp.float32),
+        pltpu.VMEM((2,) + pairs[0][0].shape, half),
+        pltpu.VMEM((2, pairs[0][0].shape[0], max(chunk[3] for chunk in chunks)), half),
+        dma((2, 2)),
     ]
     scratch += [dma((count,)) for _ in range(4)] + [dma((count, 3)) for _ in range(2)]
     scratch += [dma((count,)) for _ in range(4)]
@@ -564,11 +592,11 @@
     return pl.pallas_call(
         functools.partial(gradient_kernel, tuple(chunks), len(pairs), vec_len),
         out_shape=tuple(outs),
-        in_specs=[vmem] * (2 * len(pairs) + 4),
+        in_specs=[pl.BlockSpec(memory_space=pl.ANY)] * (2 * len(pairs)) + [vmem] * 4,
         out_specs=tuple([vmem] * len(outs)),
         scratch_shapes=scratch,
         compiler_params=pltpu.CompilerParams(
-            collective_id=collective_id, has_side_effects=True, vmem_limit_bytes=58 * 1024 * 1024
+            collective_id=collective_id, has_side_effects=True, vmem_limit_bytes=40 * 1024 * 1024
         ),
         cost_estimate=pl.CostEstimate(flops=0, bytes_accessed=200_000_000, transcendentals=0),
         name="exchange_gradients",
@@ -576,16 +604,16 @@
 
 
 SPLITS = 4
-WINDOW = 3
+WINDOW = 2
 LAG = 3
 
 
 def start_kernel(shard_rows, room, *refs):
     column_ref, row_ref, packet_ref, vec_ref, attn_ref, ffn_ref, word_ref = refs[:7]
     place_out, slot_out, packet_out, asked_out, vec_out, rows_out, *weight_outs = refs[7:15]
-    table, rows_held, asked, slots, locals_ = refs[15:20]
-    packet_sem, asked_sem, vec_sem, row_sem = refs[20:24]
-    z_sem, y_sem, x_sem, d_sem, e_sem, own_sem = refs[24:]
+    table, rows_held, asked, words, own = refs[15:20]
+    packet_sem, near_sem, far_sem, vec_sem, row_sem = refs[20:25]
+    z_sem, y_sem, x_sem, d_sem, e_sem, own_sem, word_sem, self_sem = refs[25:]
 
     d = lax.axis_index("dp")
     z = lax.axis_index("zero")
@@ -613,9 +641,18 @@
         return carry
 
     lax.fori_loop(1, 32, greet, 0)
+    word_copy = pltpu.make_async_copy(word_ref, words, word_sem)
+    word_copy.start()
+
+    def self_copy(layer):
+        return pltpu.make_async_copy(own.at[layer], weight_outs[layer].at[z], self_sem.at[layer])
+
     for layer in range(layers):
-        weight_outs[layer][z, :, 0:width] = attn_ref[layer].astype(jnp.bfloat16)
-        weight_outs[layer][z, :, width:whole] = ffn_ref[layer].astype(jnp.bfloat16)
+        own[layer, :, 0:width] = attn_ref[layer].astype(jnp.bfloat16)
+        own[layer, :, width:whole] = ffn_ref[layer].astype(jnp.bfloat16)
+        self_copy(layer).start()
+    for layer in range(layers):
+        self_copy(layer).wait()
     pl.semaphore_wait(barrier, 31)
 
     def remote(src, dst, sems, at, to):
@@ -631,9 +668,13 @@
     def packet_copy(k, slot):
         return remote(packet_ref, packet_out.at[slot], packet_sem, (k,), everyone(k))
 
-    def asked_copy(k, slot):
-        to = everyone(k)
-        return remote(asked.at[to[1]], asked_out.at[slot], asked_sem, (k,), to)
+    def near_copy(k, slot):
+        to = lax.rem(z + k, 16)
+        return remote(asked.at[to], asked_out.at[slot], near_sem, (k,), (d, to))
+
+    def far_copy(k, slot):
+        to = lax.rem(z + k, 16)
+        return remote(asked.at[to], asked_out.at[slot], far_sem, (k,), (1 - d, to))
 
     def vec_copy(k, slot):
         return remote(vec_ref, vec_out.at[slot], vec_sem, (k,), (d, lax.rem(z + k, 16)))
@@ -718,40 +759,54 @@
     least = lax.fori_loop(0, tokens // block, lead_of, jnp.full((1, tokens), 1e9, jnp.float32))
     lead_ids = jnp.where(least == lane, ids_row, -1)
 
-    def place_of(b, most):
+    lane128 = lax.broadcasted_iota(jnp.int32, (1, 128), 1).astype(jnp.float32)
+
+    def place_of(b, carry):
+        most, best = carry
         at = pl.ds(pl.multiple_of(b * block, block), block)
         ids = column_ref[at, :]
-        owner = jnp.zeros_like(ids)
-        for o in range(1, 16):
-            owner = owner + (ids >= o * shard_rows).astype(jnp.int32)
-        low_id = owner * shard_rows
+        owner = jnp.floor((ids.astype(jnp.float32) + 0.5) * (1.0 / shard_rows))
+        low_id = owner.astype(jnp.int32) * shard_rows
         ahead = (lead_ids >= low_id) & (lead_ids < ids)
         place = jnp.sum(jnp.where(ahead, 1.0, 0.0), axis=1, keepdims=True)
         place_out[at, :] = place.astype(jnp.int32)
         inside = place < room
-        slots[at, :] = jnp.where(inside, owner * 128 + place.astype(jnp.int32), -1)
-        slot_out[at, :] = jnp.where(inside, owner * room + place.astype(jnp.int32), -1)
-        locals_[at, :] = (ids - low_id).astype(jnp.float32)
-        return jnp.maximum(most, jnp.max(place, axis=0, keepdims=True))
-
-    most = lax.fori_loop(0, tokens // block, place_of, jnp.zeros((1, 1), jnp.float32))
+        slot_out[at, :] = jnp.where(inside, owner * room + place, -1.0).astype(jnp.int32)
+        slot = jnp.broadcast_to(jnp.where(inside, owner * 128.0 + place, -1.0), (block, 128))
+        local = jnp.broadcast_to((ids - low_id).astype(jnp.float32), (block, 128))
+        grown = []
+        for o in range(16):
+            found = jnp.where(slot == o * 128.0 + lane128, local, -1.0)
+            found = jnp.max(found.reshape(block // 8, 8, 128), axis=0)
+            grown.append(jnp.maximum(best[o], found))
+        return jnp.maximum(most, jnp.max(place, axis=0, keepdims=True)), tuple(grown)
+
+    most, best = lax.fori_loop(
+        0,
+        tokens // block,
+        place_of,
+        (jnp.zeros((1, 1), jnp.float32), (jnp.full((8, 128), -1.0, jnp.float32),) * 16),
+    )
     rounds = jnp.ones((1, 1), jnp.float32)
     for r in range(1, -(-tokens // room)):
         rounds = rounds + (most >= r * room).astype(jnp.float32)
-    lane128 = lax.broadcasted_iota(jnp.int32, (1, 128), 1)
-
     for o in range(16):
-
-        def asked_of(b, best, o=o):
-            at = pl.ds(pl.multiple_of(b * block, block), block)
-            found = jnp.where(slots[at, :] == o * 128 + lane128, locals_[at, :], -1.0)
-            return jnp.maximum(best, jnp.max(found, axis=0, keepdims=True))
-
-        best = lax.fori_loop(0, tokens // block, asked_of, jnp.full((1, 128), -1.0, jnp.float32))
-        asked[o] = jnp.where(lane128 == 127, rounds, best).astype(jnp.int32)
+        found = jnp.max(best[o], axis=0, keepdims=True)
+        asked[o] = jnp.where(lane128 == 127.0, rounds, found).astype(jnp.int32)
+
+    def send_near(k, carry):
+        near_copy(k, me).start()
+        return carry
+
+    lax.fori_loop(1, 16, send_near, 0)
+
+    def send_far(k, carry):
+        far_copy(k, me).start()
+        return carry
+
+    lax.fori_loop(0, 16, send_far, 0)
 
     def send_packets(k, carry):
-        asked_copy(k, me).start()
         packet_copy(k, me).start()
         return carry
 
@@ -773,14 +828,15 @@
 
     def to_half(i, carry):
         at = pl.multiple_of(i * step, 16)
-        table[pl.ds(at, step), :] = word_ref[pl.ds(at, step), :].astype(jnp.bfloat16)
+        table[pl.ds(at, step), :] = words[pl.ds(at, step), :].astype(jnp.bfloat16)
         return carry
 
+    word_copy.wait()
     lax.fori_loop(0, body_rows // step, to_half, 0)
     padded = table.shape[0]
     table[body_rows:padded, :] = jnp.zeros((padded - body_rows, table.shape[1]), jnp.bfloat16)
     if shard_rows > body_rows:
-        table[body_rows:shard_rows, :] = word_ref[body_rows:shard_rows, :].astype(jnp.bfloat16)
+        table[body_rows:shard_rows, :] = words[body_rows:shard_rows, :].astype(jnp.bfloat16)
 
     def answer_one(k, carry):
         src = lax.rem(z + k, 16)
@@ -793,7 +849,7 @@
         return carry
 
     def packet_in(k, carry):
-        asked_copy(k, lax.rem(me + 32 - k, 32)).wait_recv()
+        near_copy(k, d * 16 + lax.rem(z + 16 - k, 16)).wait_recv()
         return carry
 
     def row_start(k, carry):
@@ -823,7 +879,7 @@
         if t < total:
             z_phase(t)
         if t == 1:
-            lax.fori_loop(1, 32, packet_in, 0)
+            lax.fori_loop(1, 16, packet_in, 0)
         if t >= 1:
             until = min(16, done + 4)
             if until > done:
@@ -860,6 +916,7 @@
         row_copy(k, z).wait_send()
         vec_copy(k, back).wait_recv()
         vec_copy(k, z).wait_send()
+        near_copy(k, me).wait_send()
         return carry
 
     lax.fori_loop(1, 16, finish, 0)
@@ -867,10 +924,16 @@
     def finish_packets(k, carry):
         packet_copy(k, lax.rem(me + 32 - k, 32)).wait_recv()
         packet_copy(k, me).wait_send()
-        asked_copy(k, me).wait_send()
         return carry
 
     lax.fori_loop(1, 32, finish_packets, 0)
+
+    def finish_far(k, carry):
+        far_copy(k, (1 - d) * 16 + lax.rem(z + 16 - k, 16)).wait_recv()
+        far_copy(k, me).wait_send()
+        return carry
+
+    lax.fori_loop(0, 16, finish_far, 0)
 
 
 def exchange_start(ids, packet, vec_rows, attn, ffn, word_table, room, collective_id):
@@ -882,6 +945,7 @@
     pieces = layers * SPLITS
     dma = pltpu.SemaphoreType.DMA
     vmem = pl.BlockSpec(memory_space=pltpu.VMEM)
+    anywhere = pl.BlockSpec(memory_space=pl.ANY)
     return pl.pallas_call(
         functools.partial(start_kernel, shard_rows, room),
         out_shape=(
@@ -893,16 +957,17 @@
             jax.ShapeDtypeStruct((16, room, features), half),
         )
         + (jax.ShapeDtypeStruct((16, rows, 3 * width), half),) * layers,
-        in_specs=[vmem] * 7,
-        out_specs=tuple([vmem] * (6 + layers)),
+        in_specs=[vmem] * 6 + [anywhere],
+        out_specs=tuple([vmem] * 6 + [anywhere] * layers),
         scratch_shapes=[
             pltpu.VMEM((padded, features), half),
             pltpu.VMEM((16, room, features), half),
             pltpu.VMEM((16, 1, 128), jnp.int32),
-            pltpu.VMEM((tokens, 1), jnp.int32),
-            pltpu.VMEM((tokens, 1), jnp.float32),
+            pltpu.VMEM(word_table.shape, word_table.dtype),
+            pltpu.VMEM((layers, rows, 3 * width), half),
             dma((2, 32)),
-            dma((2, 32)),
+            dma((2, 16)),
+            dma((2, 16)),
             dma((2, 16)),
             dma((2, 16)),
             dma((2, pieces, 3)),
@@ -911,6 +976,8 @@
             dma((2, pieces, 8)),
             dma((2, pieces, 8)),
             dma((2, layers)),
+            dma,
+            dma((layers,)),
         ],
         compiler_params=pltpu.CompilerParams(
             collective_id=collective_id, has_side_effects=True, vmem_limit_bytes=48 * 1024 * 1024

time: 425 us -> 411 us (0.967)
  Pallas kernels: 273 us -> 251 us
  local copies, waits for them, and re-layouts: 25.1 us -> 32.5 us
    pallas_call x1, Pallas kernels: 92.3 us -> 81.4 us  [exchange_start(): pl.pallas_call(functools.partial(start_kernel, shard_rows, room), out_sha...]
    pallas_call x1, Pallas kernels: 95.9 us -> 85.8 us  [exchange_gradients(): pl.pallas_call(functools.partial(gradient_kernel, tuple(chunks), len(pair...]
    unnamed x120 -> x142, local copies, waits for them, and re-layouts: 20 us -> 28.6 us
where the time goes in v10:
time: 411 us; the launch traced here: 404 us
  Pallas kernels  251 us (61%)
  other arithmetic  53.6 us (13%)
  matrix products  46.8 us (11%)
  local copies, waits for them, and re-layouts  32.5 us (8%)
  between operations  17.7 us (4%)
    pallas_call x1, Pallas kernels, exchange_gradients(): pl.pallas_call(functools.partial(gradient_kernel, tuple(chunks), len(pair...  85.8 us
    pallas_call x1, Pallas kernels, exchange_start(): pl.pallas_call(functools.partial(start_kernel, shard_rows, room), out_sha...  81.4 us
    pallas_call x4, Pallas kernels, attention_call(): pl.pallas_call(kernel, grid=(count,), out_shape=jax.ShapeDtypeStruct((cou...  32 us
    pallas_call x2, Pallas kernels, feed_back(): pl.pallas_call(feed_back_kernel, grid=(tokens // rows,), out_shape=(jax.S...  28.7 us
    unnamed x142, local copies, waits for them, and re-layouts  28.6 us
    pallas_call x1, Pallas kernels, contrastive(): pl.pallas_call(contrastive_kernel, out_shape=(jax.ShapeDtypeStruct((8, 12...  23 us
    dot_general x7, matrix products, matmul(): return jnp.dot(left, right, preferred_element_type=jnp.float32)  17.5 us
    dot_general x2, matrix products, layer_backward(): jnp.einsum('nsp,dp->nsd', d_packed, in_weights, preferred_element_type=jn...  10.2 us
  transfers between devices with their start and end apart: 1, of which 0 were waited for; matrix products, arithmetic and copies ran while one was open for 10% of the time, Pallas kernels for 8%

profile of v10, /device:TPU:0, one launch (start us, length us, event | category | flops | bytes accessed | tf_op | source)
XLA Modules:
  0.0 403.5 jit_solution(3854944851053728318)
XLA Ops:
  7.2 0.8 copy.55
  8.9 0.9 copy.54.refs_0_
  11.9 1.2 copy-done.25
  13.1 1.0 copy-done.29
  14.1 81.4 %exchange_start.1 = (s32[1024,1]{1,0:T(8,128)S(1)}, s32[1024,1]{1,0:T(8,128)S(1)}, bf16[32,8,128]{2,1,0:T(8,128)(2,1)S(1)}, s32[32,1,128]{2,1,0:T(1,128)S(1)}, b...) custom-call(s32[1024,1]{1,0:T(8,128)S(1)} %copy.54.refs_0_, ...), custom_call_target="tpu_custom_call" | custom-call | bytes 150000000 | tf_op jit(solution)/shard_map/exchange_start/pallas_call | solution.py:949
  97.5 1.6 fusion.45
  99.1 0.9 while.28
  101.5 3.5 add_convert_fusion.1.packed_ref
  105.0 1.0 copy-done.18
  105.9 7.3 %attention.2 = bf16[8,128,512]{2,1,0:T(8,128)(2,1)S(1)} custom-call(f32[8,1,128]{2,1,0:T(1,128)S(1)} %compare_convert_fusion.mask_ref, bf16[8,128,1536]{2,1,0:T(8,128)(2,1)S(1)} %add_convert_fusion.1.packed_ref), custom_call_target="tpu_custom_call" | custom-call | flops 1000000000 | bytes 5242880 | tf_op jit(solution)/shard_map/attention/pallas_call | solution.py:1252
  113.3 1.1 fusion.81
  115.3 4.2 %fusion.19 = bf16[8,128,2048]{2,1,0:T(8,128)(2,1)S(1)} fusion(f32[2048]{0:T(1024)S(1)} %get-tuple-element.460, bf16[8,128,512]{2,1,0:T(8,128)(2,1)S(1)} %fusion.41, bf16[512,6144]{1,0:T(8,128)(2,1)S(1)} %bitcast.248), kind=kOutput, calls=%fused_computation.38 | convolution fusion | flops 2168455168 | bytes 7348224 | tf_op jit(solution)/shard_map/dot_general | solution.py:78
  119.5 2.7 fusion.82
  123.1 1.8 add_convert_fusion.packed_ref
  125.0 1.0 copy-done.23
  126.0 5.2 %attention.3 = bf16[8,128,512]{2,1,0:T(8,128)(2,1)S(1)} custom-call(f32[8,1,128]{2,1,0:T(1,128)S(1)} %compare_convert_fusion.mask_ref, bf16[8,128,1536]{2,1,0:T(8,128)(2,1)S(1)} %add_convert_fusion.packed_ref), custom_call_target="tpu_custom_call" | custom-call | flops 1000000000 | bytes 5242880 | tf_op jit(solution)/shard_map/attention/pallas_call | solution.py:1252
  131.2 1.0 fusion.83
  133.1 4.3 %fusion.24 = bf16[8,128,2048]{2,1,0:T(8,128)(2,1)S(1)} fusion(f32[2048]{0:T(1024)S(1)} %get-tuple-element.459, bf16[8,128,512]{2,1,0:T(8,128)(2,1)S(1)} %fusion.42, bf16[512,6144]{1,0:T(8,128)(2,1)S(1)} %bitcast.258), kind=kOutput, calls=%fused_computation.43 | convolution fusion | flops 2168455168 | bytes 7348224 | tf_op jit(solution)/shard_map/dot_general | solution.py:78
  137.4 2.7 fusion.84
  140.7 1.3 multiply_reduce_fusion.14
  142.1 23.0 %contrastive.1 = (f32[8,128]{1,0:T(8,128)S(1)}, f32[2,2,8,512]{3,2,1,0:T(8,128)S(1)}) custom-call(bf16[2,8,512]{2,1,0:T(8,128)(2,1)S(1)} %reshape.668.block_ref, s32[128,128]{1,0:T(8,128)S(1)} %reshape.669.false_ref, s32[128,1]{1,0:T(8,128)S(1)} %reshape_reshape.16.pair_ref), custom_call_target="tpu_custom_call" | custom-call | flops 1000000000 | bytes 3000000 | tf_op jit(solution)/shard_map/contrastive/pallas_call | solution.py:1155
  165.2 1.5 fusion.37
  166.7 2.1 fusion.47
  168.8 14.3 %feed_back.2 = (bf16[1024,2048]{1,0:T(8,128)(2,1)S(1)}, bf16[1024,2048]{1,0:T(8,128)(2,1)S(1)}, f32[1024,512]{1,0:T(8,128)S(1)}, f32[1,2048]{1,0:T(1,128)S(1)}) custom-call(bf16[1024,512]{1,0:T(8,128)(2,1)S(1)} %bitcast.199, bf16[1024,512]{1,0:T(8,128)(2,1)S(1)} %bitcast.193, bf16[512,6144]{1,0:T(8,128)(2,1)} %bitcast.250, bf16[512,6144]{1,0:T(8,128)(2,1)} %bitcast.251, ...), custom_call_target="tpu_custom_call" | custom-call | flops 6442450944 | bytes 12582912 | tf_op jit(solution)/shard_map/feed_back/pallas_call | solution.py:1306
  183.1 1.9 fusion.46
  185.0 2.5 convolution_convert_fusion.1
  187.5 2.5 convolution_convert_fusion
  190.0 2.5 pad_maximum_fusion
  192.7 3.3 multiply_reduce_fusion.3
  196.4 0.8 fusion.51
  198.1 2.8 convolution_convert_fusion.3.grad_ref
  202.8 2.0 copy-done.5
  204.8 1.3 copy-done.34
  206.1 9.8 %attention_back.2 = bf16[8,128,1536]{2,1,0:T(8,128)(2,1)S(1)} custom-call(f32[8,1,128]{2,1,0:T(1,128)S(1)} %compare_convert_fusion.mask_ref, bf16[8,128,1536]{2,1,0:T(8,128)(2,1)S(1)} %copy-done.5, bf16[8,128,512]{2,1,0:T(8,128)(2,1)S(1)} %copy-done.34), custom_call_target="tpu_custom_call" | custom-call | flops 1000000000 | bytes 5242880 | tf_op jit(solution)/shard_map/attention_back/pallas_call | solution.py:1252
  216.5 2.2 copy-done.38
  218.7 4.9 %multiply_reduce_fusion.4 = (f32[512]{0:T(512)S(1)}, f32[8,128]{1,0:T(8,128)S(1)}, f32[8,128]{1,0:T(8,128)S(1)}, f32[512]{0:T(512)S(1)}, f32[8,128,512]{2,1,0:T(8,128)S(1)}) fusion(f32[8,128]{1,0:T(8,128)S(1)} %add_rsqrt_fusion.2, f32[8,128,512]{2,1,0:T(8,128)S(1)} %copy-done.38, f32[8,128]{1,0:T(8,128)S(1)} %broadcast_multiply_fusion.10, ...), kind=kOutput, calls=%fused_computation.83 | convolution fusion | flops 1620571136 | bytes 13168640 | tf_op jit(solution)/shard_map/nsp,dp->nsd/dot_general | solution.py:1423
  223.7 0.8 fusion.53
  225.6 14.3 %feed_back.3 = (bf16[1024,2048]{1,0:T(8,128)(2,1)S(1)}, bf16[1024,2048]{1,0:T(8,128)(2,1)S(1)}, f32[1024,512]{1,0:T(8,128)S(1)}, f32[1,2048]{1,0:T(1,128)S(1)}) custom-call(bf16[1024,512]{1,0:T(8,128)(2,1)S(1)} %bitcast.190, bf16[1024,512]{1,0:T(8,128)(2,1)S(1)} %bitcast.184, bf16[512,6144]{1,0:T(8,128)(2,1)} %bitcast.241, bf16[512,6144]{1,0:T(8,128)(2,1)} %bitcast.242, ...), custom_call_target="tpu_custom_call" | custom-call | flops 6442450944 | bytes 12582912 | tf_op jit(solution)/shard_map/feed_back/pallas_call | solution.py:1306
  239.9 1.9 copy-done.27
  241.9 2.0 copy-done.28
  244.6 4.0 multiply_reduce_fusion.5
  249.4 1.0 copy-done.11
  250.3 1.8 convolution_convert_fusion.2.grad_ref
  252.2 9.6 %attention_back.3 = bf16[8,128,1536]{2,1,0:T(8,128)(2,1)S(1)} custom-call(f32[8,1,128]{2,1,0:T(1,128)S(1)} %compare_convert_fusion.mask_ref, bf16[8,128,1536]{2,1,0:T(8,128)(2,1)S(1)} %copy-done.3, bf16[8,128,512]{2,1,0:T(8,128)(2,1)S(1)} %convolution_convert_fusion.2.grad_ref), custom_call_target="tpu_custom_call" | custom-call | flops 1000000000 | bytes 5242880 | tf_op jit(solution)/shard_map/attention_back/pallas_call | solution.py:1252
  261.8 5.4 %multiply_reduce_fusion.7 = (f32[512]{0:T(512)S(1)}, f32[8,128]{1,0:T(8,128)S(1)}, f32[512]{0:T(512)S(1)}, f32[8,128,512]{2,1,0:T(8,128)S(1)}) fusion(f32[8,128]{1,0:T(8,128)S(1)} %bitcast_rsqrt_fusion, f32[8,128]{1,0:T(8,128)S(1)} %get-tuple-element.469, f32[128,512]{1,0:T(8,128)S(1)} %copy-done.54, bf16[1024,512]{1,0:T(8,128)(2,1)S(1)} %copy-done.48, ...), kind=kOutput, calls=%fused_computation.88 | convolution fusion | flops 1621620736 | bytes 13406208 | tf_op jit(solution)/shard_map/nsp,dp->nsd/dot_general | solution.py:1423
  267.2 2.0 add_add_fusion
  269.2 1.8 reduce_sum.420
  271.0 3.0 add_convert_fusion.2
  275.7 4.1 %fusion.31 = bf16[1152,512]{1,0:T(8,128)(2,1)} fusion(bf16[1024,512]{1,0:T(8,128)(2,1)} %bitcast.212, s32[1024]{0:T(1024)S(1)} %copy-done.64), kind=kOutput, calls=%fused_computation.66 | convolution fusion | flops 1209729024 | bytes 2232320 | tf_op jit(solution)/shard_map/dot_general | solution.py:1737
  279.8 1.2 copy-done.15
  281.0 1.2 copy-done.17
  282.2 1.2 copy-done.19
  283.5 1.2 copy-done.22
  284.7 1.2 copy-done.24
  285.9 1.3 copy-done.31
  287.2 0.9 copy-done.36
  288.1 85.8 %exchange_gradients.1 = (f32[2,32,2048]{2,1,0:T(8,128)S(1)}, f32[2,32,4096]{2,1,0:T(8,128)S(1)}, f32[1908,512]{1,0:T(8,128)S(1)}, f32[40,128]{1,0:T(8,128)S(1)}, f32[8,128]{1,0:T(8,128)S(1)}) custom-call(bf16[1024,512]{1,0:T(8,128)(2,1)S(1)} %bitcast.189, bf16[1024,1536]{1,0:T(8,128)(2,1)} %bitcast.182, bf16[1024,512]{1,0:T(8,128)(2,1)S(1)} %bitcast.187, ...), custom_call_target="tpu_custom_call" | custom-call | bytes 200000000 | tf_op jit(solution)/shard_map/exchange_gradients/pallas_call | solution.py:592
  374.0 1.6 multiply_reduce_fusion.2
  376.4 1.0 while.29
  379.5 2.7 fusion.68
  382.2 2.5 fusion.66
  384.7 0.9 copy-done.49
  385.7 1.2 copy-done.51
  386.9 8.2 %fusion.72 = (bf16[1908,512]{1,0:T(8,128)(2,1)}, f32[1908,512]{1,0:T(8,128)}, f32[1908,512]{1,0:T(8,128)}, f32[1908,512]{1,0:T(8,128)}) fusion(f32[1908,512]{1,0:T(8,128)S(1)} %copy-done.49, f32[1908,512]{1,0:T(8,128)S(1)} %copy-done.51, f32[]{:T(128)S(6)} %min.3, f32[1908,512]{1,0:T(8,128)} %param.28, f32[1908,512]{1,0:T(8,128)} %param.32), kind=kLoop, calls=%fused_computation.213 | loop fusion | flops 15630336 | bytes 29306884 | tf_op jit(solution)/shard_map/convert_element_type | solution.py:1828
  (226 shorter events, 19.6 us)
Async XLA Ops:
  7.2 272.6 %reduce-scatter.2.cloned.1.call-start = ((), (), s32[]{:S(2)}) async-start(), calls=%async_computation.5 | async-start | bytes 4456448 | tf_op jit(solution)/shard_map/reduce_scatter | solution.py:1713
  11.9 1.2 copy-start.25
  13.1 1.0 copy-start.29
  96.9 2.2 copy-start.63
  97.5 15.8 %copy-start.53 = (f32[128,512]{1,0:T(8,128)}, f32[128,512]{1,0:T(8,128)S(1)}, u32[]{:S(2)}) copy-start(f32[128,512]{1,0:T(8,128)S(1)} %slice_convert_fusion) | copy-start | bytes 786436
  97.5 1.6 copy-start.58
  100.0 13.3 %copy-start.47 = (bf16[1024,512]{1,0:T(8,128)(2,1)}, bf16[1024,512]{1,0:T(8,128)(2,1)S(1)}, u32[]{:S(2)}) copy-start(bf16[1024,512]{1,0:T(8,128)(2,1)S(1)} %get-tuple-element.283) | copy-start | bytes 3145732
  100.9 12.4 %slice-start = ((s8[6291456]{0:T(1024)(128)(4,1)}), s8[4194304]{0:T(1024)(128)(4,1)S(1)}, s32[]{:S(2)}) async-start(s8[6291456]{0:T(1024)(128)(4,1)} %bitcast.245), calls=%async_computation.7 | async-start | bytes 8388608
  101.5 11.8 %slice-start.1 = ((s8[6291456]{0:T(1024)(128)(4,1)}), s8[2097152]{0:T(1024)(128)(4,1)S(1)}, s32[]{:S(2)}) async-start(s8[6291456]{0:T(1024)(128)(4,1)} %bitcast.245), calls=%async_computation.8 | async-start | bytes 4194304
  105.9 7.3 %copy-start.2 = (bf16[8,128,1536]{2,1,0:T(8,128)(2,1)}, bf16[8,128,1536]{2,1,0:T(8,128)(2,1)S(1)}, u32[]{:S(2)}) copy-start(bf16[8,128,1536]{2,1,0:T(8,128)(2,1)S(1)} %add_convert_fusion.1.packed_ref) | copy-start | bytes 9437188
  113.3 1.2 copy-start.14
  114.4 5.1 %copy-start.43 = (f32[8,128,512]{2,1,0:T(8,128)}, f32[8,128,512]{2,1,0:T(8,128)S(1)}, u32[]{:S(2)}) copy-start(f32[8,128,512]{2,1,0:T(8,128)S(1)} %get-tuple-element.474) | copy-start | bytes 6291460
  115.3 4.2 %copy-start.20 = (bf16[8,128,512]{2,1,0:T(8,128)(2,1)}, bf16[8,128,512]{2,1,0:T(8,128)(2,1)S(1)}, u32[]{:S(2)}) copy-start(bf16[8,128,512]{2,1,0:T(8,128)(2,1)S(1)} %fusion.41) | copy-start | bytes 3145732
  115.3 7.8 %slice-start.2 = ((s8[6291456]{0:T(1024)(128)(4,1)}), s8[4194304]{0:T(1024)(128)(4,1)S(1)}, s32[]{:S(2)}) async-start(s8[6291456]{0:T(1024)(128)(4,1)} %bitcast.254), calls=%async_computation.9 | async-start | bytes 8388608
  119.5 3.6 slice-start.3
  122.3 18.4 %copy-start.37 = (f32[8,128,512]{2,1,0:T(8,128)}, f32[8,128,512]{2,1,0:T(8,128)S(1)}, u32[]{:S(2)}) copy-start(f32[8,128,512]{2,1,0:T(8,128)S(1)} %get-tuple-element.476) | copy-start | bytes 6291460
  126.0 5.2 %copy-start.4 = (bf16[8,128,1536]{2,1,0:T(8,128)(2,1)}, bf16[8,128,1536]{2,1,0:T(8,128)(2,1)S(1)}, u32[]{:S(2)}) copy-start(bf16[8,128,1536]{2,1,0:T(8,128)(2,1)S(1)} %add_convert_fusion.packed_ref) | copy-start | bytes 9437188
  131.2 1.1 copy-start.16
  132.2 5.2 %copy-start.41 = (f32[8,128,512]{2,1,0:T(8,128)}, f32[8,128,512]{2,1,0:T(8,128)S(1)}, u32[]{:S(2)}) copy-start(f32[8,128,512]{2,1,0:T(8,128)S(1)} %get-tuple-element.478) | copy-start | bytes 6291460
  140.2 25.0 %copy-start.39 = (f32[8,128,512]{2,1,0:T(8,128)}, f32[8,128,512]{2,1,0:T(8,128)S(1)}, u32[]{:S(2)}) copy-start(f32[8,128,512]{2,1,0:T(8,128)S(1)} %get-tuple-element.480) | copy-start | bytes 6291460
  168.8 14.3 %copy-start.40 = (f32[8,128,512]{2,1,0:T(8,128)S(1)}, f32[8,128,512]{2,1,0:T(8,128)}, u32[]{:S(2)}) copy-start(f32[8,128,512]{2,1,0:T(8,128)} %copy-done.39) | copy-start | bytes 6291460
  192.7 3.4 copy-start.42
  192.7 3.7 copy-start.45
  202.8 2.0 copy-start.5
  204.8 1.3 copy-start.34
  206.1 10.4 %copy-start.46 = (f32[8,128,512]{2,1,0:T(8,128)S(1)}, f32[8,128,512]{2,1,0:T(8,128)}, u32[]{:S(2)}) copy-start(f32[8,128,512]{2,1,0:T(8,128)} %fusion.46) | copy-start | bytes 6291460
  216.0 7.6 %copy-start = (bf16[8,128,1536]{2,1,0:T(8,128)(2,1)}, bf16[8,128,1536]{2,1,0:T(8,128)(2,1)S(1)}, u32[]{:S(2)}) copy-start(bf16[8,128,1536]{2,1,0:T(8,128)(2,1)S(1)} %attention_back.2) | copy-start | bytes 9437188
  216.0 2.7 copy-start.38
  223.6 1.3 copy-start.52
  223.7 1.9 copy-start.21
  224.9 15.1 %copy-start.8 = (bf16[8,128,512]{2,1,0:T(8,128)(2,1)}, bf16[8,128,512]{2,1,0:T(8,128)(2,1)S(1)}, u32[]{:S(2)}) copy-start(bf16[8,128,512]{2,1,0:T(8,128)(2,1)S(1)} %fusion.53) | copy-start | bytes 3145732
  239.9 1.9 copy-start.27
  241.9 2.0 copy-start.28
  244.6 4.0 copy-start.44
  248.6 3.5 copy-start.3
  252.1 9.7 %copy-start.48 = (bf16[1024,512]{1,0:T(8,128)(2,1)S(1)}, bf16[1024,512]{1,0:T(8,128)(2,1)}, u32[]{:S(2)}) copy-start(bf16[1024,512]{1,0:T(8,128)(2,1)} %copy-done.47) | copy-start | bytes 3145732
  252.1 9.7 %copy-start.54 = (f32[128,512]{1,0:T(8,128)S(1)}, f32[128,512]{1,0:T(8,128)}, u32[]{:S(2)}) copy-start(f32[128,512]{1,0:T(8,128)} %copy-done.53) | copy-start | bytes 786436
  261.8 12.6 %copy-start.1 = (bf16[8,128,1536]{2,1,0:T(8,128)(2,1)}, bf16[8,128,1536]{2,1,0:T(8,128)(2,1)S(1)}, u32[]{:S(2)}) copy-start(bf16[8,128,1536]{2,1,0:T(8,128)(2,1)S(1)} %attention_back.3) | copy-start | bytes 9437188
  271.0 3.0 copy-start.9
  271.0 3.2 copy-start.12
  275.6 4.1 %copy-start.7 = (bf16[8,128,512]{2,1,0:T(8,128)(2,1)S(1)}, bf16[8,128,512]{2,1,0:T(8,128)(2,1)}, u32[]{:S(2)}) copy-start(bf16[8,128,512]{2,1,0:T(8,128)(2,1)} %copy-done.6) | copy-start | bytes 3145732
  275.6 4.1 %copy-start.10 = (bf16[8,128,512]{2,1,0:T(8,128)(2,1)S(1)}, bf16[8,128,512]{2,1,0:T(8,128)(2,1)}, u32[]{:S(2)}) copy-start(bf16[8,128,512]{2,1,0:T(8,128)(2,1)} %copy-done.8) | copy-start | bytes 3145732
  275.6 4.1 %copy-start.13 = (bf16[8,128,512]{2,1,0:T(8,128)(2,1)S(1)}, bf16[8,128,512]{2,1,0:T(8,128)(2,1)}, u32[]{:S(2)}) copy-start(bf16[8,128,512]{2,1,0:T(8,128)(2,1)} %copy-done.11) | copy-start | bytes 3145732
  279.8 1.2 copy-start.15
  281.0 1.2 copy-start.17
  282.2 1.2 copy-start.19
  283.5 1.2 copy-start.22
  284.7 1.2 copy-start.24
  285.9 1.3 copy-start.31
  373.9 2.3 copy-start.32
  374.0 2.3 copy-start.50
  374.0 2.4 copy-start.35
  374.0 2.3 copy-start.57
  376.4 2.4 copy-start.60
  376.4 2.4 copy-start.61
  376.4 2.4 copy-start.62
  376.4 3.1 copy-start.30
  376.4 3.1 copy-start.59
  378.1 4.1 %copy-start.26 = (f32[2,32,4096]{2,1,0:T(8,128)S(1)}, f32[2,32,4096]{2,1,0:T(8,128)}, u32[]{:S(2)}) copy-start(f32[2,32,4096]{2,1,0:T(8,128)} %refs_5_.1) | copy-start | bytes 3145732
  378.2 4.1 %copy-start.33 = (f32[2,32,4096]{2,1,0:T(8,128)S(1)}, f32[2,32,4096]{2,1,0:T(8,128)}, u32[]{:S(2)}) copy-start(f32[2,32,4096]{2,1,0:T(8,128)} %copy-done.32) | copy-start | bytes 3145732
  378.2 4.0 copy-start.55
  378.2 4.0 copy-start.56
  382.2 3.4 copy-start.49
  382.2 4.6 %copy-start.51 = (f32[1908,512]{1,0:T(8,128)S(1)}, f32[1908,512]{1,0:T(8,128)}, u32[]{:S(2)}) copy-start(f32[1908,512]{1,0:T(8,128)} %get-tuple-element.303) | copy-start | bytes 11722756
  (6 other events, 5.5 us)
Sparse Core Ops, SparseCore 0:
  192.6 69.9 reduce-scatter.1

commit v11 on v10

--- a/solution.py
+++ b/solution.py
@@ -200,7 +200,7 @@
     held = [None if chunk[1] is None else next(take) for chunk in chunks]
     bufs = [[next(take) for _ in range(6 if chunk[4] else 5)] for chunk in chunks]
     near_buf, rows_ref, sum_ref, square_ref, squares_ref = [next(take) for _ in range(5)]
-    left_buf, right_buf, fetch_sem = [next(take) for _ in range(3)]
+    left_buf, right_buf, fetch_sem, near_held, local_sem = [next(take) for _ in range(5)]
     send_a, recv_a, send_y, recv_y, send_z, recv_z, send_x, recv_x = [next(take) for _ in range(8)]
     send_h, recv_h = next(take), next(take)
     row_send, row_recv, pass_send, pass_recv, near_sem, square_sem = [
@@ -294,8 +294,10 @@
 
     lax.fori_loop(1, 16, push, 0)
     near.start()
-    rows_ref[d, z] = sums_ref[z]
-    row_pass(0).start()
+    near_copy = pltpu.make_async_copy(near_ref, near_held, local_sem.at[0])
+    near_copy.start()
+    own_copy = pltpu.make_async_copy(sums_ref.at[z], rows_ref.at[d, z], local_sem.at[1])
+    own_copy.start()
 
     made = [i for i in range(total) if held[i] is not None]
 
@@ -444,6 +446,8 @@
     rest += [all_arrived] + [functools.partial(other_rows, tile) for tile in range(tiles)]
 
     compute(0)
+    own_copy.wait()
+    row_pass(0).start()
     passed = 1
     for t in range(total + LAG_Z + 3):
         if t + 1 < total:
@@ -463,7 +467,8 @@
         rest.pop(0)()
 
     near.wait()
-    ffn_out[1] = near_ref[...].astype(jnp.float32) + near_buf[...].astype(jnp.float32)
+    near_copy.wait()
+    ffn_out[1] = near_held[...].astype(jnp.float32) + near_buf[...].astype(jnp.float32)
     squares = sum_ref[...]
     square = jnp.sum(squares, axis=1, keepdims=True)
     for out in (attn_out, ffn_out):
@@ -576,6 +581,8 @@
         pltpu.VMEM((2,) + pairs[0][0].shape, half),
         pltpu.VMEM((2, pairs[0][0].shape[0], max(chunk[3] for chunk in chunks)), half),
         dma((2, 2)),
+        pltpu.VMEM(near.shape, half),
+        dma((2,)),
     ]
     scratch += [dma((count,)) for _ in range(4)] + [dma((count, 3)) for _ in range(2)]
     scratch += [dma((count,)) for _ in range(4)]
@@ -589,14 +596,15 @@
         jax.ShapeDtypeStruct((8, 128), jnp.float32),
     ]
     vmem = pl.BlockSpec(memory_space=pltpu.VMEM)
+    hbm = pl.BlockSpec(memory_space=pltpu.HBM)
     return pl.pallas_call(
         functools.partial(gradient_kernel, tuple(chunks), len(pairs), vec_len),
         out_shape=tuple(outs),
-        in_specs=[pl.BlockSpec(memory_space=pl.ANY)] * (2 * len(pairs)) + [vmem] * 4,
+        in_specs=[hbm] * (2 * len(pairs)) + [vmem, hbm, hbm, vmem],
         out_specs=tuple([vmem] * len(outs)),
         scratch_shapes=scratch,
         compiler_params=pltpu.CompilerParams(
-            collective_id=collective_id, has_side_effects=True, vmem_limit_bytes=40 * 1024 * 1024
+            collective_id=collective_id, has_side_effects=True, vmem_limit_bytes=58 * 1024 * 1024
         ),
         cost_estimate=pl.CostEstimate(flops=0, bytes_accessed=200_000_000, transcendentals=0),
         name="exchange_gradients",
@@ -611,9 +619,9 @@
 def start_kernel(shard_rows, room, *refs):
     column_ref, row_ref, packet_ref, vec_ref, attn_ref, ffn_ref, word_ref = refs[:7]
     place_out, slot_out, packet_out, asked_out, vec_out, rows_out, *weight_outs = refs[7:15]
-    table, rows_held, asked, words, own = refs[15:20]
-    packet_sem, near_sem, far_sem, vec_sem, row_sem = refs[20:25]
-    z_sem, y_sem, x_sem, d_sem, e_sem, own_sem, word_sem, self_sem = refs[25:]
+    table, rows_held, asked, words, own, attn_held, ffn_held = refs[15:22]
+    packet_sem, near_sem, far_sem, vec_sem, row_sem = refs[22:27]
+    z_sem, y_sem, x_sem, d_sem, e_sem, own_sem, word_sem, self_sem = refs[27:]
 
     d = lax.axis_index("dp")
     z = lax.axis_index("zero")
@@ -634,6 +642,14 @@
         p = lax.rem(me + k, 32)
         return (p // 16, lax.rem(p, 16))
 
+    held_copies = [
+        pltpu.make_async_copy(attn_ref, attn_held, word_sem.at[1]),
+        pltpu.make_async_copy(ffn_ref, ffn_held, word_sem.at[2]),
+    ]
+    for copy in held_copies:
+        copy.start()
+    word_copy = pltpu.make_async_copy(word_ref, words, word_sem.at[0])
+    word_copy.start()
     barrier = pltpu.get_barrier_semaphore()
 
     def greet(k, carry):
@@ -641,15 +657,15 @@
         return carry
 
     lax.fori_loop(1, 32, greet, 0)
-    word_copy = pltpu.make_async_copy(word_ref, words, word_sem)
-    word_copy.start()
+    for copy in held_copies:
+        copy.wait()
 
     def self_copy(layer):
         return pltpu.make_async_copy(own.at[layer], weight_outs[layer].at[z], self_sem.at[layer])
 
     for layer in range(layers):
-        own[layer, :, 0:width] = attn_ref[layer].astype(jnp.bfloat16)
-        own[layer, :, width:whole] = ffn_ref[layer].astype(jnp.bfloat16)
+        own[layer, :, 0:width] = attn_held[layer].astype(jnp.bfloat16)
+        own[layer, :, width:whole] = ffn_held[layer].astype(jnp.bfloat16)
         self_copy(layer).start()
     for layer in range(layers):
         self_copy(layer).wait()
@@ -945,7 +961,7 @@
     pieces = layers * SPLITS
     dma = pltpu.SemaphoreType.DMA
     vmem = pl.BlockSpec(memory_space=pltpu.VMEM)
-    anywhere = pl.BlockSpec(memory_space=pl.ANY)
+    anywhere = pl.BlockSpec(memory_space=pltpu.HBM)
     return pl.pallas_call(
         functools.partial(start_kernel, shard_rows, room),
         out_shape=(
@@ -957,7 +973,7 @@
             jax.ShapeDtypeStruct((16, room, features), half),
         )
         + (jax.ShapeDtypeStruct((16, rows, 3 * width), half),) * layers,
-        in_specs=[vmem] * 6 + [anywhere],
+        in_specs=[vmem] * 4 + [anywhere] * 3,
         out_specs=tuple([vmem] * 6 + [anywhere] * layers),
         scratch_shapes=[
             pltpu.VMEM((padded, features), half),
@@ -965,6 +981,8 @@
             pltpu.VMEM((16, 1, 128), jnp.int32),
             pltpu.VMEM(word_table.shape, word_table.dtype),
             pltpu.VMEM((layers, rows, 3 * width), half),
+            pltpu.VMEM(attn.shape, attn.dtype),
+            pltpu.VMEM(ffn.shape, ffn.dtype),
             dma((2, 32)),
             dma((2, 16)),
             dma((2, 16)),
@@ -976,11 +994,11 @@
             dma((2, pieces, 8)),
             dma((2, pieces, 8)),
             dma((2, layers)),
-            dma,
+            dma((3,)),
             dma((layers,)),
         ],
         compiler_params=pltpu.CompilerParams(
-            collective_id=collective_id, has_side_effects=True, vmem_limit_bytes=48 * 1024 * 1024
+            collective_id=collective_id, has_side_effects=True, vmem_limit_bytes=52 * 1024 * 1024
         ),
         cost_estimate=pl.CostEstimate(flops=0, bytes_accessed=150_000_000, transcendentals=0),
         name="exchange_start",
@@ -1168,7 +1186,7 @@
             dma((2, 4, 8)),
         ],
         compiler_params=pltpu.CompilerParams(
-            collective_id=collective_id, has_side_effects=True, vmem_limit_bytes=32 * 1024 * 1024
+            collective_id=collective_id, has_side_effects=True, vmem_limit_bytes=20 * 1024 * 1024
         ),
         cost_estimate=pl.CostEstimate(flops=10**9, bytes_accessed=3_000_000, transcendentals=10**6),
         name="contrastive",
@@ -1256,7 +1274,7 @@
         in_specs=[pl.BlockSpec((1, 1, SEQ), lambda i: (i, 0, 0))]
         + [spec(operand.shape[2]) for operand in operands],
         out_specs=spec(features),
-        compiler_params=pltpu.CompilerParams(vmem_limit_bytes=32 * 1024 * 1024),
+        compiler_params=pltpu.CompilerParams(vmem_limit_bytes=14 * 1024 * 1024),
         cost_estimate=pl.CostEstimate(
             flops=10**9, bytes_accessed=count * SEQ * D * 10, transcendentals=10**6
         ),
@@ -1314,7 +1332,7 @@
         ),
         in_specs=[by_rows(D), by_rows(D), matrix(1), matrix(2), whole],
         out_specs=(by_rows(FF), by_rows(FF), by_rows(D), whole),
-        compiler_params=pltpu.CompilerParams(vmem_limit_bytes=40 * 1024 * 1024),
+        compiler_params=pltpu.CompilerParams(vmem_limit_bytes=26 * 1024 * 1024),
         cost_estimate=pl.CostEstimate(
             flops=6 * tokens * D * FF, bytes_accessed=24 * tokens * D, transcendentals=tokens * FF
         ),
@@ -1638,7 +1656,7 @@
     rows = rows_from(slot, received)
 
     def round_of(round_index):
-        owner = ids // shard_rows
+        owner = lax.div(ids, jnp.int32(shard_rows))
         local_row = ids - owner * shard_rows
         return round_slots(owner, place, local_row, round_index, room, nz)
 
@@ -1760,9 +1778,9 @@
         got = lax.all_to_all(slot_sums(slot_now).reshape(nz, room, D), "zero", 0, 0, tiled=True)
         wanted = lax.all_gather(wanted, "dp", axis=0, tiled=True)
         got = lax.all_gather(got, "dp", axis=0, tiled=True)
-        grad_next = grad_now + into_rows(wanted, got)
-        grown = jnp.sum(grad_next * grad_next) - jnp.sum(grad_now * grad_now)
-        return round_index + 1, grad_next, square_now + lax.psum(grown, "zero")
+        more = into_rows(wanted, got)
+        grown = lax.psum(jnp.sum(more * (2.0 * grad_now + more)), "zero")
+        return round_index + 1, grad_now + more, square_now + grown
 
     if by_hand:
         attn_shard, ffn_shard, word_grad, vec_sum, squares = exchange_gradients(

time: 411 us -> 400 us (0.973)
  local copies, waits for them, and re-layouts: 32.5 us -> 24.6 us
    unnamed x142 -> x122, local copies, waits for them, and re-layouts: 28.6 us -> 19.6 us
where the time goes in v11:
time: 400 us; the launch traced here: 393 us
  Pallas kernels  251 us (63%)
  other arithmetic  51.5 us (13%)
  matrix products  45.9 us (11%)
  local copies, waits for them, and re-layouts  24.6 us (6%)
  between operations  17.7 us (4%)
    pallas_call x1, Pallas kernels, exchange_gradients(): pl.pallas_call(functools.partial(gradient_kernel, tuple(chunks), len(pair...  88.6 us
    pallas_call x1, Pallas kernels, exchange_start(): pl.pallas_call(functools.partial(start_kernel, shard_rows, room), out_sha...  83.1 us
    pallas_call x4, Pallas kernels, attention_call(): pl.pallas_call(kernel, grid=(count,), out_shape=jax.ShapeDtypeStruct((cou...  32.4 us
    pallas_call x2, Pallas kernels, feed_back(): pl.pallas_call(feed_back_kernel, grid=(tokens // rows,), out_shape=(jax.S...  24.6 us
    pallas_call x1, Pallas kernels, contrastive(): pl.pallas_call(contrastive_kernel, out_shape=(jax.ShapeDtypeStruct((8, 12...  22.8 us
    unnamed x122, local copies, waits for them, and re-layouts  19.6 us
    dot_general x7, matrix products, matmul(): return jnp.dot(left, right, preferred_element_type=jnp.float32)  17.9 us
    dot_general x2, matrix products, layer_backward(): jnp.einsum('nsp,dp->nsd', d_packed, in_weights, preferred_element_type=jn...  10.3 us
  transfers between devices with their start and end apart: 1, of which 0 were waited for; matrix products, arithmetic and copies ran while one was open for 10% of the time, Pallas kernels for 8%

profile of v11, /device:TPU:0, one launch (start us, length us, event | category | flops | bytes accessed | tf_op | source)
XLA Modules:
  0.0 393.0 jit_solution(16755498940154878549)
XLA Ops:
  7.2 0.8 copy.53
  8.2 0.7 convert.15
  8.8 0.7 convert_bitcast_fusion
  9.5 0.7 convert_element_type.227
  10.3 0.9 copy.52.refs_0_
  11.2 83.1 %exchange_start.1 = (s32[1024,1]{1,0:T(8,128)S(1)}, s32[1024,1]{1,0:T(8,128)S(1)}, bf16[32,8,128]{2,1,0:T(8,128)(2,1)S(1)}, s32[32,1,128]{2,1,0:T(1,128)S(1)}, b...) custom-call(s32[1024,1]{1,0:T(8,128)S(1)} %copy.52.refs_0_, ...), custom_call_target="tpu_custom_call" | custom-call | bytes 150000000 | tf_op jit(solution)/shard_map/exchange_start/pallas_call | solution.py:965
  94.6 0.7 slice_reduce_fusion.1
  96.2 1.6 fusion.43
  97.8 0.9 while.22
  100.2 3.8 add_convert_fusion.1.packed_ref
  104.0 7.9 %attention.2 = bf16[8,128,512]{2,1,0:T(8,128)(2,1)S(1)} custom-call(f32[8,1,128]{2,1,0:T(1,128)S(1)} %compare_convert_fusion.mask_ref, bf16[8,128,1536]{2,1,0:T(8,128)(2,1)S(1)} %add_convert_fusion.1.packed_ref), custom_call_target="tpu_custom_call" | custom-call | flops 1000000000 | bytes 5242880 | tf_op jit(solution)/shard_map/attention/pallas_call | solution.py:1270
  112.0 1.1 fusion.79
  114.0 4.2 %fusion.17 = bf16[8,128,2048]{2,1,0:T(8,128)(2,1)S(1)} fusion(f32[2048]{0:T(1024)S(1)} %get-tuple-element.236, bf16[8,128,512]{2,1,0:T(8,128)(2,1)S(1)} %fusion.39, bf16[512,6144]{1,0:T(8,128)(2,1)S(1)} %bitcast.205), kind=kOutput, calls=%fused_computation.32 | convolution fusion | flops 2168455168 | bytes 7348224 | tf_op jit(solution)/shard_map/dot_general | solution.py:78
  118.2 2.7 fusion.80
  121.8 1.8 add_convert_fusion.packed_ref
  123.7 5.2 %attention.3 = bf16[8,128,512]{2,1,0:T(8,128)(2,1)S(1)} custom-call(f32[8,1,128]{2,1,0:T(1,128)S(1)} %compare_convert_fusion.mask_ref, bf16[8,128,1536]{2,1,0:T(8,128)(2,1)S(1)} %add_convert_fusion.packed_ref), custom_call_target="tpu_custom_call" | custom-call | flops 1000000000 | bytes 5242880 | tf_op jit(solution)/shard_map/attention/pallas_call | solution.py:1270
  128.9 1.0 fusion.81
  130.8 4.3 %fusion.22 = bf16[8,128,2048]{2,1,0:T(8,128)(2,1)S(1)} fusion(f32[2048]{0:T(1024)S(1)} %get-tuple-element.235, bf16[8,128,512]{2,1,0:T(8,128)(2,1)S(1)} %fusion.40, bf16[512,6144]{1,0:T(8,128)(2,1)S(1)} %bitcast.217), kind=kOutput, calls=%fused_computation.37 | convolution fusion | flops 2168455168 | bytes 7348224 | tf_op jit(solution)/shard_map/dot_general | solution.py:78
  135.2 2.7 fusion.82
  138.4 1.2 multiply_reduce_fusion.12
  139.8 22.8 %contrastive.1 = (f32[8,128]{1,0:T(8,128)S(1)}, f32[2,2,8,512]{3,2,1,0:T(8,128)S(1)}) custom-call(bf16[2,8,512]{2,1,0:T(8,128)(2,1)S(1)} %reshape.580.block_ref, s32[128,128]{1,0:T(8,128)S(1)} %reshape.581.false_ref, s32[128,1]{1,0:T(8,128)S(1)} %reshape_reshape.16.pair_ref), custom_call_target="tpu_custom_call" | custom-call | flops 1000000000 | bytes 3000000 | tf_op jit(solution)/shard_map/contrastive/pallas_call | solution.py:1173
  162.6 1.4 fusion.35
  164.1 2.1 fusion.45
  166.2 2.8 copy-done.15
  169.0 12.2 %feed_back.2 = (bf16[1024,2048]{1,0:T(8,128)(2,1)S(1)}, bf16[1024,2048]{1,0:T(8,128)(2,1)S(1)}, f32[1024,512]{1,0:T(8,128)S(1)}, f32[1,2048]{1,0:T(1,128)S(1)}) custom-call(bf16[1024,512]{1,0:T(8,128)(2,1)S(1)} %bitcast.193, bf16[1024,512]{1,0:T(8,128)(2,1)S(1)} %bitcast.189, bf16[512,6144]{1,0:T(8,128)(2,1)S(1)} %bitcast.219, ...), custom_call_target="tpu_custom_call" | custom-call | flops 6442450944 | bytes 12582912 | tf_op jit(solution)/shard_map/feed_back/pallas_call | solution.py:1324
  181.2 1.9 fusion.44
  183.1 2.5 convolution_convert_fusion.1
  185.6 2.5 convolution_convert_fusion
  188.1 2.5 pad_maximum_fusion
  190.9 3.3 multiply_reduce_fusion.1
  194.5 0.8 fusion.49
  195.5 0.8 copy-done.29
  196.2 2.8 convolution_convert_fusion.3.grad_ref
  199.0 0.7 reshape_squeeze.3.refs_15_
  200.8 0.7 reduce.23
  201.5 2.1 copy-done.5
  203.5 1.3 copy-done.14
  204.8 9.8 %attention_back.2 = bf16[8,128,1536]{2,1,0:T(8,128)(2,1)S(1)} custom-call(f32[8,1,128]{2,1,0:T(1,128)S(1)} %compare_convert_fusion.mask_ref, bf16[8,128,1536]{2,1,0:T(8,128)(2,1)S(1)} %copy-done.5, bf16[8,128,512]{2,1,0:T(8,128)(2,1)S(1)} %copy-done.14), custom_call_target="tpu_custom_call" | custom-call | flops 1000000000 | bytes 5242880 | tf_op jit(solution)/shard_map/attention_back/pallas_call | solution.py:1270
  215.1 2.2 copy-done.17
  217.3 4.9 %multiply_reduce_fusion.2 = (f32[512]{0:T(512)S(1)}, f32[8,128]{1,0:T(8,128)S(1)}, f32[8,128]{1,0:T(8,128)S(1)}, f32[512]{0:T(512)S(1)}, f32[8,128,512]{2,1,0:T(8,128)S(1)}) fusion(f32[8,128]{1,0:T(8,128)S(1)} %add_rsqrt_fusion.2, f32[8,128,512]{2,1,0:T(8,128)S(1)} %copy-done.17, f32[8,128]{1,0:T(8,128)S(1)} %broadcast_multiply_fusion.10, ...), kind=kOutput, calls=%fused_computation.76 | convolution fusion | flops 1620571136 | bytes 13168640 | tf_op jit(solution)/shard_map/nsp,dp->nsd/dot_general | solution.py:1441
  222.3 0.7 fusion.51
  224.2 12.4 %feed_back.3 = (bf16[1024,2048]{1,0:T(8,128)(2,1)S(1)}, bf16[1024,2048]{1,0:T(8,128)(2,1)S(1)}, f32[1024,512]{1,0:T(8,128)S(1)}, f32[1,2048]{1,0:T(1,128)S(1)}) custom-call(bf16[1024,512]{1,0:T(8,128)(2,1)S(1)} %bitcast.188, bf16[1024,512]{1,0:T(8,128)(2,1)S(1)} %bitcast.183, bf16[512,6144]{1,0:T(8,128)(2,1)S(1)} %bitcast.209, ...), custom_call_target="tpu_custom_call" | custom-call | flops 6442450944 | bytes 12582912 | tf_op jit(solution)/shard_map/feed_back/pallas_call | solution.py:1324
  236.7 2.1 copy-done.12
  238.7 2.0 copy-done.13
  240.8 0.7 reduce.24
  241.5 4.0 %multiply_reduce_fusion.3 = (f32[512]{0:T(512)S(1)}, f32[8,128]{1,0:T(8,128)S(1)}, f32[8,128]{1,0:T(8,128)S(1)}, f32[512]{0:T(512)S(1)}, f32[8,128,512]{2,1,0:T(8,128)S(1)}) fusion(f32[8,128,512]{2,1,0:T(8,128)} %copy-done.22, f32[8,128]{1,0:T(8,128)S(1)} %add_rsqrt_fusion.3, f32[8,128]{1,0:T(8,128)S(1)} %broadcast_multiply_fusion.11, ...), kind=kLoop, calls=%fused_computation.78 | loop fusion | flops 8909824 | bytes 10526720 | tf_op jit(solution)/shard_map/reduce_sum | solution.py:1374
  245.5 0.8 fusion.52
  246.3 1.0 copy-done.30
  247.3 1.8 convolution_convert_fusion.2.grad_ref
  249.1 9.6 %attention_back.3 = bf16[8,128,1536]{2,1,0:T(8,128)(2,1)S(1)} custom-call(f32[8,1,128]{2,1,0:T(1,128)S(1)} %compare_convert_fusion.mask_ref, bf16[8,128,1536]{2,1,0:T(8,128)(2,1)S(1)} %copy-done.3, bf16[8,128,512]{2,1,0:T(8,128)(2,1)S(1)} %convolution_convert_fusion.2.grad_ref), custom_call_target="tpu_custom_call" | custom-call | flops 1000000000 | bytes 5242880 | tf_op jit(solution)/shard_map/attention_back/pallas_call | solution.py:1270
  258.7 5.4 %multiply_reduce_fusion.5 = (f32[512]{0:T(512)S(1)}, f32[8,128]{1,0:T(8,128)S(1)}, f32[512]{0:T(512)S(1)}, f32[8,128,512]{2,1,0:T(8,128)S(1)}) fusion(f32[8,128]{1,0:T(8,128)S(1)} %bitcast_rsqrt_fusion, f32[8,128]{1,0:T(8,128)S(1)} %get-tuple-element.245, f32[128,512]{1,0:T(8,128)S(1)} %copy-done.34, bf16[1024,512]{1,0:T(8,128)(2,1)S(1)} %copy-done.27, ...), kind=kOutput, calls=%fused_computation.81 | convolution fusion | flops 1621620736 | bytes 13406208 | tf_op jit(solution)/shard_map/nsp,dp->nsd/dot_general | solution.py:1441
  264.2 2.0 add_add_fusion
  266.1 1.8 reduce_sum.403
  268.0 3.0 add_convert_fusion.2
  272.5 0.8 copy.61
  273.3 2.7 fusion.29
  276.0 88.6 %exchange_gradients.1 = (f32[2,32,2048]{2,1,0:T(8,128)}, f32[2,32,4096]{2,1,0:T(8,128)}, f32[1908,512]{1,0:T(8,128)}, f32[40,128]{1,0:T(8,128)}, f32[8,128]{1,0:T(8,128)}) custom-call(bf16[1024,512]{1,0:T(8,128)(2,1)} %bitcast.228, bf16[1024,1536]{1,0:T(8,128)(2,1)} %bitcast.182, bf16[1024,512]{1,0:T(8,128)(2,1)} %bitcast.185, bf16[1024,512]{1,0:T(8,128)(2,1)} %bitcast.227, ...), custom_call_target="tpu_custom_call" | custom-call | bytes 200000000 | tf_op jit(solution)/shard_map/exchange_gradients/pallas_call | solution.py:600
  364.7 1.2 slice.253
  365.9 1.0 while.23
  369.0 2.7 fusion.66
  371.7 2.5 fusion.64
  374.2 1.0 copy-done.28
  375.1 1.2 copy-done.38
  376.3 8.3 %fusion.70 = (bf16[1908,512]{1,0:T(8,128)(2,1)}, f32[1908,512]{1,0:T(8,128)}, f32[1908,512]{1,0:T(8,128)}, f32[1908,512]{1,0:T(8,128)}) fusion(f32[1908,512]{1,0:T(8,128)S(1)} %copy-done.28, f32[1908,512]{1,0:T(8,128)} %get-tuple-element.140, f32[]{:T(128)S(6)} %min.3, f32[1908,512]{1,0:T(8,128)S(1)} %copy-done.38, f32[1908,512]{1,0:T(8,128)} %param.32), kind=kLoop, calls=%fused_computation.206 | loop fusion | flops 15630336 | bytes 29306884 | tf_op jit(solution)/shard_map/convert_element_type | solution.py:1846
  (205 shorter events, 12.3 us)
Async XLA Ops:
  7.2 268.8 %reduce-scatter.2.cloned.1.call-start = ((), (), s32[]{:S(2)}) async-start(), calls=%async_computation.5 | async-start | bytes 4456448 | tf_op jit(solution)/shard_map/reduce_scatter | solution.py:1731
  94.3 1.9 copy-start.52
  95.6 2.2 copy-start.50
  96.2 15.8 %copy-start.33 = (f32[128,512]{1,0:T(8,128)}, f32[128,512]{1,0:T(8,128)S(1)}, u32[]{:S(2)}) copy-start(f32[128,512]{1,0:T(8,128)S(1)} %slice_convert_fusion) | copy-start | bytes 786436
  96.2 1.6 copy-start.44
  98.7 13.3 %copy-start.26 = (bf16[1024,512]{1,0:T(8,128)(2,1)}, bf16[1024,512]{1,0:T(8,128)(2,1)S(1)}, u32[]{:S(2)}) copy-start(bf16[1024,512]{1,0:T(8,128)(2,1)S(1)} %get-tuple-element.120) | copy-start | bytes 3145732
  99.6 12.4 %slice-start = ((s8[6291456]{0:T(1024)(128)(4,1)}), s8[4194304]{0:T(1024)(128)(4,1)S(1)}, s32[]{:S(2)}) async-start(s8[6291456]{0:T(1024)(128)(4,1)} %bitcast.202), calls=%async_computation.7 | async-start | bytes 8388608
  100.1 3.9 copy-start.35
  100.2 11.8 %slice-start.1 = ((s8[6291456]{0:T(1024)(128)(4,1)}), s8[2097152]{0:T(1024)(128)(4,1)S(1)}, s32[]{:S(2)}) async-start(s8[6291456]{0:T(1024)(128)(4,1)} %bitcast.202), calls=%async_computation.8 | async-start | bytes 4194304
  104.0 7.9 %copy-start.2 = (bf16[8,128,1536]{2,1,0:T(8,128)(2,1)}, bf16[8,128,1536]{2,1,0:T(8,128)(2,1)S(1)}, u32[]{:S(2)}) copy-start(bf16[8,128,1536]{2,1,0:T(8,128)(2,1)S(1)} %add_convert_fusion.1.packed_ref) | copy-start | bytes 9437188
  111.9 1.2 copy-start.8
  113.1 5.1 %copy-start.22 = (f32[8,128,512]{2,1,0:T(8,128)}, f32[8,128,512]{2,1,0:T(8,128)S(1)}, u32[]{:S(2)}) copy-start(f32[8,128,512]{2,1,0:T(8,128)S(1)} %get-tuple-element.250) | copy-start | bytes 6291460
  114.0 4.2 %copy-start.10 = (bf16[8,128,512]{2,1,0:T(8,128)(2,1)}, bf16[8,128,512]{2,1,0:T(8,128)(2,1)S(1)}, u32[]{:S(2)}) copy-start(bf16[8,128,512]{2,1,0:T(8,128)(2,1)S(1)} %fusion.39) | copy-start | bytes 3145732
  114.0 7.8 %slice-start.4 = ((s8[6291456]{0:T(1024)(128)(4,1)}), s8[2097152]{0:T(1024)(128)(4,1)S(1)}, s32[]{:S(2)}) async-start(s8[6291456]{0:T(1024)(128)(4,1)} %bitcast.213), calls=%async_computation.11 | async-start | bytes 4194304
  118.2 3.6 slice-start.5
  120.9 17.5 %copy-start.16 = (f32[8,128,512]{2,1,0:T(8,128)}, f32[8,128,512]{2,1,0:T(8,128)S(1)}, u32[]{:S(2)}) copy-start(f32[8,128,512]{2,1,0:T(8,128)S(1)} %get-tuple-element.252) | copy-start | bytes 6291460
  121.8 1.9 copy-start.36
  123.7 5.2 %copy-start.4 = (bf16[8,128,1536]{2,1,0:T(8,128)(2,1)}, bf16[8,128,1536]{2,1,0:T(8,128)(2,1)S(1)}, u32[]{:S(2)}) copy-start(bf16[8,128,1536]{2,1,0:T(8,128)(2,1)S(1)} %add_convert_fusion.packed_ref) | copy-start | bytes 9437188
  128.9 1.1 copy-start.9
  129.9 5.2 %copy-start.20 = (f32[8,128,512]{2,1,0:T(8,128)}, f32[8,128,512]{2,1,0:T(8,128)S(1)}, u32[]{:S(2)}) copy-start(f32[8,128,512]{2,1,0:T(8,128)S(1)} %get-tuple-element.254) | copy-start | bytes 6291460
  137.9 24.7 %copy-start.18 = (f32[8,128,512]{2,1,0:T(8,128)}, f32[8,128,512]{2,1,0:T(8,128)S(1)}, u32[]{:S(2)}) copy-start(f32[8,128,512]{2,1,0:T(8,128)S(1)} %get-tuple-element.256) | copy-start | bytes 6291460
  166.2 2.8 copy-start.15
  169.0 12.2 %copy-start.19 = (f32[8,128,512]{2,1,0:T(8,128)S(1)}, f32[8,128,512]{2,1,0:T(8,128)}, u32[]{:S(2)}) copy-start(f32[8,128,512]{2,1,0:T(8,128)} %copy-done.18) | copy-start | bytes 6291460
  190.9 3.4 copy-start.21
  190.9 3.6 copy-start.24
  195.3 1.0 copy-start.29
  201.5 2.1 copy-start.5
  203.5 1.3 copy-start.14
  204.8 10.3 %copy-start.25 = (f32[8,128,512]{2,1,0:T(8,128)S(1)}, f32[8,128,512]{2,1,0:T(8,128)}, u32[]{:S(2)}) copy-start(f32[8,128,512]{2,1,0:T(8,128)} %fusion.44) | copy-start | bytes 6291460
  204.8 18.8 %slice-start.2 = ((s8[6291456]{0:T(1024)(128)(4,1)}), s8[4194304]{0:T(1024)(128)(4,1)S(1)}, s32[]{:S(2)}) async-start(s8[6291456]{0:T(1024)(128)(4,1)} %bitcast.207), calls=%async_computation.9 | async-start | bytes 8388608
  214.6 7.7 %copy-start = (bf16[8,128,1536]{2,1,0:T(8,128)(2,1)}, bf16[8,128,1536]{2,1,0:T(8,128)(2,1)S(1)}, u32[]{:S(2)}) copy-start(bf16[8,128,1536]{2,1,0:T(8,128)(2,1)S(1)} %attention_back.2) | copy-start | bytes 9437188
  214.6 2.7 copy-start.17
  217.3 6.3 %slice-start.3 = ((s8[6291456]{0:T(1024)(128)(4,1)}), s8[2097152]{0:T(1024)(128)(4,1)S(1)}, s32[]{:S(2)}) async-start(s8[6291456]{0:T(1024)(128)(4,1)} %bitcast.207), calls=%async_computation.10 | async-start | bytes 4194304
  222.2 1.3 copy-start.32
  222.3 1.9 copy-start.11
  223.6 13.1 %copy-start.6 = (bf16[8,128,512]{2,1,0:T(8,128)(2,1)}, bf16[8,128,512]{2,1,0:T(8,128)(2,1)S(1)}, u32[]{:S(2)}) copy-start(bf16[8,128,512]{2,1,0:T(8,128)(2,1)S(1)} %fusion.51) | copy-start | bytes 3145732
  236.7 2.1 copy-start.12
  238.7 2.0 copy-start.13
  241.5 4.1 %copy-start.23 = (f32[8,128,512]{2,1,0:T(8,128)S(1)}, f32[8,128,512]{2,1,0:T(8,128)}, u32[]{:S(2)}) copy-start(f32[8,128,512]{2,1,0:T(8,128)} %copy-done.22) | copy-start | bytes 6291460
  245.5 3.5 copy-start.3
  246.3 1.0 copy-start.30
  249.1 9.6 %copy-start.27 = (bf16[1024,512]{1,0:T(8,128)(2,1)S(1)}, bf16[1024,512]{1,0:T(8,128)(2,1)}, u32[]{:S(2)}) copy-start(bf16[1024,512]{1,0:T(8,128)(2,1)} %copy-done.26) | copy-start | bytes 3145732
  249.1 9.6 %copy-start.34 = (f32[128,512]{1,0:T(8,128)S(1)}, f32[128,512]{1,0:T(8,128)}, u32[]{:S(2)}) copy-start(f32[128,512]{1,0:T(8,128)} %copy-done.33) | copy-start | bytes 786436
  258.7 12.7 %copy-start.1 = (bf16[8,128,1536]{2,1,0:T(8,128)(2,1)}, bf16[8,128,1536]{2,1,0:T(8,128)(2,1)S(1)}, u32[]{:S(2)}) copy-start(bf16[8,128,1536]{2,1,0:T(8,128)(2,1)S(1)} %attention_back.3) | copy-start | bytes 9437188
  267.9 3.0 copy-start.7
  267.9 3.2 copy-start.31
  271.9 1.4 copy-start.43
  271.9 1.4 copy-start.51
  365.8 1.8 copy-start.47
  365.9 2.5 copy-start.46
  365.9 2.5 copy-start.48
  365.9 2.5 copy-start.49
  365.9 3.1 copy-start.39
  365.9 3.1 copy-start.45
  367.6 4.1 %copy-start.37 = (f32[2,32,4096]{2,1,0:T(8,128)S(1)}, f32[2,32,4096]{2,1,0:T(8,128)}, u32[]{:S(2)}) copy-start(f32[2,32,4096]{2,1,0:T(8,128)} %refs_5_.1) | copy-start | bytes 3145732
  367.6 4.1 %copy-start.40 = (f32[2,32,4096]{2,1,0:T(8,128)S(1)}, f32[2,32,4096]{2,1,0:T(8,128)}, u32[]{:S(2)}) copy-start(f32[2,32,4096]{2,1,0:T(8,128)} %param.31) | copy-start | bytes 3145732
  367.7 4.0 %copy-start.41 = (f32[2,32,4096]{2,1,0:T(8,128)S(1)}, f32[2,32,4096]{2,1,0:T(8,128)}, u32[]{:S(2)}) copy-start(f32[2,32,4096]{2,1,0:T(8,128)} %param.35) | copy-start | bytes 3145732
  367.7 4.0 %copy-start.42 = (f32[2,32,4096]{2,1,0:T(8,128)S(1)}, f32[2,32,4096]{2,1,0:T(8,128)}, u32[]{:S(2)}) copy-start(f32[2,32,4096]{2,1,0:T(8,128)} %get-tuple-element.143) | copy-start | bytes 3145732
  371.7 3.4 copy-start.28
  371.7 4.6 %copy-start.38 = (f32[1908,512]{1,0:T(8,128)S(1)}, f32[1908,512]{1,0:T(8,128)}, u32[]{:S(2)}) copy-start(f32[1908,512]{1,0:T(8,128)} %param.28) | copy-start | bytes 11722756
Sparse Core Ops, SparseCore 0:
  190.7 70.2 reduce-scatter.1

commit v12 on v11

--- a/solution.py
+++ b/solution.py
@@ -1340,6 +1340,49 @@
     )(middle, d_down, weights, weights, up_bias.reshape(1, FF))
 
 
+def embed_back_kernel(grad_ref, normal_ref, inverse_ref, gain_ref, rows_ref, vec_ref):
+    grad, normal = grad_ref[0], normal_ref[0]
+    scaled = grad * gain_ref[...]
+    mean = jnp.mean(scaled, axis=1, keepdims=True)
+    along = jnp.mean(scaled * normal, axis=1, keepdims=True)
+    values = (scaled - mean - normal * along) * inverse_ref[0]
+    rows_ref[0] = values.astype(jnp.bfloat16)
+    first = pl.program_id(0) == 0
+    for start, stop, found in (
+        (0, SEQ, values),
+        (SEQ, SEQ + 1, jnp.sum(grad * normal, axis=0, keepdims=True)),
+        (SEQ + 1, SEQ + 2, jnp.sum(grad, axis=0, keepdims=True)),
+    ):
+        before = jnp.where(first, 0.0, vec_ref[start:stop, :])
+        vec_ref[start:stop, :] = before + found
+
+
+def embed_back(grad, normal, inverse, gain):
+    count = grad.shape[0]
+
+    def by_sequence(last):
+        return pl.BlockSpec((1, SEQ, last), lambda i: (i, 0, 0))
+
+    def whole(rows):
+        return pl.BlockSpec((rows, D), lambda i: (0, 0))
+
+    return pl.pallas_call(
+        embed_back_kernel,
+        grid=(count,),
+        out_shape=(
+            jax.ShapeDtypeStruct((count, SEQ, D), jnp.bfloat16),
+            jax.ShapeDtypeStruct((SEQ + 2, D), jnp.float32),
+        ),
+        in_specs=[by_sequence(D), by_sequence(D), by_sequence(1), whole(1)],
+        out_specs=(by_sequence(D), whole(SEQ + 2)),
+        compiler_params=pltpu.CompilerParams(vmem_limit_bytes=14 * 1024 * 1024),
+        cost_estimate=pl.CostEstimate(
+            flops=10 * count * SEQ * D, bytes_accessed=10 * count * SEQ * D, transcendentals=0
+        ),
+        name="embed_back",
+    )(grad, normal, inverse, gain.reshape(1, D))
+
+
 LAYER_ROWS = 8 + FF // D
 
 
@@ -1352,10 +1395,6 @@
     center = values - jnp.mean(values, axis=-1, keepdims=True)
     spread = jnp.mean(center * center, axis=-1, keepdims=True)
     return center * lax.rsqrt(spread + NORM_EPS) * gain + shift
-
-
-def embed_tokens(rows, vectors):
-    return layer_norm(low_back(rows) + vectors[None, :SEQ], vectors[SEQ], vectors[SEQ + 1])
 
 
 def norm_forward(values, gain, shift):
@@ -1676,7 +1715,10 @@
     vec_rows = vec_all.reshape(-1, D)
     edges = [0] + [SEQ + 2 + i * LAYER_ROWS for i in range(LAYERS + 1)]
     vec_parts = [vec_rows[first:last] for first, last in zip(edges, edges[1:])]
-    embedded, embed_back = jax.vjp(embed_tokens, rows, vec_parts[0])
+    first_part = vec_parts[0]
+    embedded, embed_normal, embed_inverse = norm_forward(
+        rows + first_part[None, :SEQ], first_part[SEQ], first_part[SEQ + 1]
+    )
     hidden = embedded
     mask = key_mask.astype(jnp.float32)[:, None, :]
     saved = []
@@ -1744,11 +1786,13 @@
             grad_hidden = scatter(pairs, grad_hidden)
         layer_pairs.insert(0, pairs)
         weight_parts = by_scatter + weight_parts
-    rows_grad, embed_grads = embed_back(grad_hidden)
+    rows_grad, embed_grads = embed_back(
+        grad_hidden, embed_normal, embed_inverse, first_part[SEQ]
+    )
     vec_grad = jnp.concatenate([embed_grads] + vec_grads, axis=0)
     down_local = jnp.stack([part[5 + FF // D] for part in vec_grads])
 
-    rows_grad = rows_grad.reshape(tokens, D).astype(jnp.bfloat16)
+    rows_grad = rows_grad.reshape(tokens, D)
 
     def slot_sums(slot_now):
         picked = one_hot(slot_now, nz * room)

time: 400 us -> 388 us (0.970)
  local copies, waits for them, and re-layouts: 24.6 us -> 16.2 us
  other arithmetic: 51.5 us -> 45.6 us
    unnamed x122 -> x116, local copies, waits for them, and re-layouts: 19.6 us -> 10.1 us
  transfers between devices with their start and end apart: 1 -> 1, of which waited for: 0 -> 0; matrix products, arithmetic and copies ran while one was open for 10% -> 9% of each run, Pallas kernels for 8% -> 9%
where the time goes in v12:
time: 388 us; the launch traced here: 381 us
  Pallas kernels  253 us (65%)
  matrix products  46.8 us (12%)
  other arithmetic  45.6 us (12%)
  between operations  17.4 us (4%)
  local copies, waits for them, and re-layouts  16.2 us (4%)
    pallas_call x1, Pallas kernels, exchange_gradients(): pl.pallas_call(functools.partial(gradient_kernel, tuple(chunks), len(pair...  89.8 us
    pallas_call x1, Pallas kernels, exchange_start(): pl.pallas_call(functools.partial(start_kernel, shard_rows, room), out_sha...  83.1 us
    pallas_call x4, Pallas kernels, attention_call(): pl.pallas_call(kernel, grid=(count,), out_shape=jax.ShapeDtypeStruct((cou...  30.8 us
    pallas_call x2, Pallas kernels, feed_back(): pl.pallas_call(feed_back_kernel, grid=(tokens // rows,), out_shape=(jax.S...  24.5 us
    pallas_call x1, Pallas kernels, contrastive(): pl.pallas_call(contrastive_kernel, out_shape=(jax.ShapeDtypeStruct((8, 12...  22.7 us
    dot_general x7, matrix products, matmul(): return jnp.dot(left, right, preferred_element_type=jnp.float32)  19.7 us
    convert_element_type x1, other arithmetic, body(): word_new.astype(jnp.bfloat16)  10.9 us
    unnamed x116, local copies, waits for them, and re-layouts  10.1 us
  transfers between devices with their start and end apart: 1, of which 0 were waited for; matrix products, arithmetic and copies ran while one was open for 9% of the time, Pallas kernels for 9%

profile of v12, /device:TPU:0, one launch (start us, length us, event | category | flops | bytes accessed | tf_op | source)
XLA Modules:
  0.0 380.5 jit_solution(6761293553503435196)
XLA Ops:
  7.2 0.9 copy.54.refs_0_
  8.1 0.7 convert.15
  8.8 0.7 convert_bitcast_fusion
  9.5 0.7 convert_element_type.219
  10.3 83.1 %exchange_start.1 = (s32[1024,1]{1,0:T(8,128)S(1)}, s32[1024,1]{1,0:T(8,128)S(1)}, bf16[32,8,128]{2,1,0:T(8,128)(2,1)S(1)}, s32[32,1,128]{2,1,0:T(1,128)S(1)}, b...) custom-call(s32[1024,1]{1,0:T(8,128)S(1)} %copy.54.refs_0_, ...), custom_call_target="tpu_custom_call" | custom-call | bytes 150000000 | tf_op jit(solution)/shard_map/exchange_start/pallas_call | solution.py:965
  94.0 0.7 slice_reduce_fusion.1
  95.5 2.8 fusion.43
  98.3 1.2 while.22
  99.8 0.6 multiply_reduce_fusion.13
  101.0 4.6 %add_convert_fusion.1.packed_ref = bf16[8,128,1536]{2,1,0:T(8,128)(2,1)S(1)} fusion(bf16[8,128,512]{2,1,0:T(8,128)(2,1)S(1)} %get-tuple-element.209, f32[1536]{0:T(1024)S(1)} %get-tuple-element.251, bf16[512,6144]{1,0:T(8,128)(2,1)} %bitcast.185), kind=kOutput, calls=%fused_computation.41 | convolution fusion | flops 1613758464 | bytes 5773312 | tf_op jit(solution)/shard_map/dot_general | solution.py:78
  105.7 6.6 %attention.2 = bf16[8,128,512]{2,1,0:T(8,128)(2,1)S(1)} custom-call(f32[8,1,128]{2,1,0:T(1,128)S(1)} %compare_convert_fusion.mask_ref, bf16[8,128,1536]{2,1,0:T(8,128)(2,1)S(1)} %add_convert_fusion.1.packed_ref), custom_call_target="tpu_custom_call" | custom-call | flops 1000000000 | bytes 5242880 | tf_op jit(solution)/shard_map/attention/pallas_call | solution.py:1270
  112.3 0.9 fusion.78
  114.2 4.2 %fusion.17 = bf16[8,128,2048]{2,1,0:T(8,128)(2,1)S(1)} fusion(f32[2048]{0:T(1024)S(1)} %get-tuple-element.237, bf16[8,128,512]{2,1,0:T(8,128)(2,1)S(1)} %fusion.40, bf16[512,6144]{1,0:T(8,128)(2,1)S(1)} %bitcast.191), kind=kOutput, calls=%fused_computation.32 | convolution fusion | flops 2168455168 | bytes 7348224 | tf_op jit(solution)/shard_map/dot_general | solution.py:78
  118.4 2.7 fusion.79
  122.0 1.8 add_convert_fusion.packed_ref
  123.8 5.2 %attention.3 = bf16[8,128,512]{2,1,0:T(8,128)(2,1)S(1)} custom-call(f32[8,1,128]{2,1,0:T(1,128)S(1)} %compare_convert_fusion.mask_ref, bf16[8,128,1536]{2,1,0:T(8,128)(2,1)S(1)} %add_convert_fusion.packed_ref), custom_call_target="tpu_custom_call" | custom-call | flops 1000000000 | bytes 5242880 | tf_op jit(solution)/shard_map/attention/pallas_call | solution.py:1270
  129.1 1.0 fusion.80
  131.0 4.4 %fusion.22 = bf16[8,128,2048]{2,1,0:T(8,128)(2,1)S(1)} fusion(f32[2048]{0:T(1024)S(1)} %get-tuple-element.236, bf16[8,128,512]{2,1,0:T(8,128)(2,1)S(1)} %fusion.41, bf16[512,6144]{1,0:T(8,128)(2,1)S(1)} %bitcast.203), kind=kOutput, calls=%fused_computation.37 | convolution fusion | flops 2168455168 | bytes 7348224 | tf_op jit(solution)/shard_map/dot_general | solution.py:78
  135.4 2.7 fusion.81
  138.5 1.2 multiply_reduce_fusion.10
  139.9 22.7 %contrastive.1 = (f32[8,128]{1,0:T(8,128)S(1)}, f32[2,2,8,512]{3,2,1,0:T(8,128)S(1)}) custom-call(bf16[2,8,512]{2,1,0:T(8,128)(2,1)S(1)} %reshape.574.block_ref, s32[128,128]{1,0:T(8,128)S(1)} %reshape.575.false_ref, s32[128,1]{1,0:T(8,128)S(1)} %reshape_reshape.16.pair_ref), custom_call_target="tpu_custom_call" | custom-call | flops 1000000000 | bytes 3000000 | tf_op jit(solution)/shard_map/contrastive/pallas_call | solution.py:1173
  162.7 1.6 fusion.35
  164.4 0.9 fusion.45
  165.3 3.2 copy-done.20
  168.5 12.2 %feed_back.2 = (bf16[1024,2048]{1,0:T(8,128)(2,1)S(1)}, bf16[1024,2048]{1,0:T(8,128)(2,1)S(1)}, f32[1024,512]{1,0:T(8,128)S(1)}, f32[1,2048]{1,0:T(1,128)S(1)}) custom-call(bf16[1024,512]{1,0:T(8,128)(2,1)S(1)} %bitcast.178, bf16[1024,512]{1,0:T(8,128)(2,1)S(1)} %bitcast.174, bf16[512,6144]{1,0:T(8,128)(2,1)S(1)} %bitcast.205, ...), custom_call_target="tpu_custom_call" | custom-call | flops 6442450944 | bytes 12582912 | tf_op jit(solution)/shard_map/feed_back/pallas_call | solution.py:1324
  180.7 2.4 convolution_convert_fusion
  183.1 2.4 convolution_convert_fusion.1
  185.5 1.9 fusion.44
  187.3 2.5 pad_maximum_fusion
  189.8 0.5 slice.245
  190.4 1.0 copy-done.24
  191.4 2.7 multiply_reduce_fusion.1
  194.2 0.8 fusion.49
  195.0 1.0 copy-done.29
  196.0 1.9 convolution_convert_fusion.3.grad_ref
  198.0 9.6 %attention_back.2 = bf16[8,128,1536]{2,1,0:T(8,128)(2,1)S(1)} custom-call(f32[8,1,128]{2,1,0:T(1,128)S(1)} %compare_convert_fusion.mask_ref, bf16[8,128,1536]{2,1,0:T(8,128)(2,1)S(1)} %copy-done.5, bf16[8,128,512]{2,1,0:T(8,128)(2,1)S(1)} %convolution_convert_fusion.3.grad_ref), custom_call_target="tpu_custom_call" | custom-call | flops 1000000000 | bytes 5242880 | tf_op jit(solution)/shard_map/attention_back/pallas_call | solution.py:1270
  207.6 5.6 %multiply_reduce_fusion.2 = (f32[512]{0:T(512)S(1)}, f32[8,128]{1,0:T(8,128)S(1)}, f32[8,128]{1,0:T(8,128)S(1)}, f32[512]{0:T(512)S(1)}, f32[8,128,512]{2,1,0:T(8,128)S(1)}) fusion(f32[8,128]{1,0:T(8,128)S(1)} %add_rsqrt_fusion.2, f32[8,128,512]{2,1,0:T(8,128)S(1)} %copy-done.22, f32[8,128]{1,0:T(8,128)S(1)} %broadcast_multiply_fusion.10, ...), kind=kOutput, calls=%fused_computation.75 | convolution fusion | flops 1620571136 | bytes 13168640 | tf_op jit(solution)/shard_map/nsp,dp->nsd/dot_general | solution.py:1480
  213.3 0.7 fusion.51
  214.5 12.2 %feed_back.3 = (bf16[1024,2048]{1,0:T(8,128)(2,1)S(1)}, bf16[1024,2048]{1,0:T(8,128)(2,1)S(1)}, f32[1024,512]{1,0:T(8,128)S(1)}, f32[1,2048]{1,0:T(1,128)S(1)}) custom-call(bf16[1024,512]{1,0:T(8,128)(2,1)S(1)} %bitcast.173, bf16[1024,512]{1,0:T(8,128)(2,1)S(1)} %bitcast.168, bf16[512,6144]{1,0:T(8,128)(2,1)S(1)} %bitcast.195, ...), custom_call_target="tpu_custom_call" | custom-call | flops 6442450944 | bytes 12582912 | tf_op jit(solution)/shard_map/feed_back/pallas_call | solution.py:1324
  226.8 2.0 multiply_reduce_fusion.3
  228.9 1.2 copy-done.16
  230.1 1.6 fusion.52
  231.7 0.5 broadcast.495
  232.3 0.7 reduce.23
  232.9 1.4 convert_reduce_fusion.2
  234.4 1.4 convert_reduce_fusion.3
  236.4 0.7 reduce.24
  237.1 2.1 convolution_convert_fusion.2.grad_ref
  239.2 1.9 copy-done.3
  241.1 9.4 %attention_back.3 = bf16[8,128,1536]{2,1,0:T(8,128)(2,1)S(1)} custom-call(f32[8,1,128]{2,1,0:T(1,128)S(1)} %compare_convert_fusion.mask_ref, bf16[8,128,1536]{2,1,0:T(8,128)(2,1)S(1)} %copy-done.3, bf16[8,128,512]{2,1,0:T(8,128)(2,1)S(1)} %convolution_convert_fusion.2.grad_ref), custom_call_target="tpu_custom_call" | custom-call | flops 1000000000 | bytes 5242880 | tf_op jit(solution)/shard_map/attention_back/pallas_call | solution.py:1270
  251.7 1.0 copy.60.inverse_ref
  252.7 4.4 %convolution_add_fusion.grad_ref = f32[8,128,512]{2,1,0:T(8,128)S(1)} fusion(bf16[8,128,1536]{2,1,0:T(8,128)(2,1)S(1)} %attention_back.3, bf16[512,6144]{1,0:T(8,128)(2,1)} %bitcast.187, f32[8,128]{1,0:T(8,128)S(1)} %broadcast_multiply_fusion, f32[8,128]{1,0:T(8,128)S(1)} %add_rsqrt_fusion.3, f32[8,128,512]{2,1,0:T(8,128)} %copy-done.26, ...), kind=kOutput, calls=%fused_computation.118 | convolution fusion | flops 1614807040 | bytes 11028480 | tf_op jit(solution)/shard_map/nsp,dp->nsd/dot_general | solution.py:1480
  257.2 1.8 embed_back.1
  259.4 0.8 copy.64
  260.2 0.7 reshape_squeeze.3.refs_15_
  260.9 2.7 fusion.29
  263.7 89.8 %exchange_gradients.1 = (f32[2,32,2048]{2,1,0:T(8,128)}, f32[2,32,4096]{2,1,0:T(8,128)}, f32[1908,512]{1,0:T(8,128)}, f32[40,128]{1,0:T(8,128)}, f32[8,128]{1,0:T(8,128)}) custom-call(bf16[1024,512]{1,0:T(8,128)(2,1)} %bitcast.212, bf16[1024,1536]{1,0:T(8,128)(2,1)} %bitcast.167, bf16[1024,512]{1,0:T(8,128)(2,1)} %bitcast.170, bf16[1024,512]{1,0:T(8,128)(2,1)} %bitcast.210, ...), custom_call_target="tpu_custom_call" | custom-call | bytes 200000000 | tf_op jit(solution)/shard_map/exchange_gradients/pallas_call | solution.py:600
  353.5 1.2 slice.257
  354.7 0.7 while.23
  356.1 0.6 slice_multiply_fusion.1
  356.8 10.9 %fusion.69 = (bf16[1908,512]{1,0:T(8,128)(2,1)}, f32[1908,512]{1,0:T(8,128)}, f32[1908,512]{1,0:T(8,128)}, f32[1908,512]{1,0:T(8,128)}) fusion(f32[1908,512]{1,0:T(8,128)} %get-tuple-element.421, f32[1908,512]{1,0:T(8,128)} %get-tuple-element.144, f32[]{:T(128)S(6)} %min.3, f32[1908,512]{1,0:T(8,128)} %param.28, f32[1908,512]{1,0:T(8,128)} %param.32), kind=kLoop, calls=%fused_computation.195 | loop fusion | flops 15630336 | bytes 29306884 | tf_op jit(solution)/shard_map/convert_element_type | solution.py:1890
  367.7 0.6 fusion.67
  368.3 1.5 fusion.65
  369.9 2.5 fusion.63
  (195 shorter events, 8.3 us)
Async XLA Ops:
  7.2 256.5 %reduce-scatter.2.cloned.1.call-start = ((), (), s32[]{:S(2)}) async-start(), calls=%async_computation.5 | async-start | bytes 4456448 | tf_op jit(solution)/shard_map/reduce_scatter | solution.py:1773
  10.2 83.4 %copy-start.49 = (s32[4,2]{0,1:T(2,128)S(1)}, s32[4,2]{0,1:T(2,128)}, u32[]{:S(2)}) copy-start(s32[4,2]{0,1:T(2,128)} %param.21) | copy-start | bytes 100
  93.3 2.1 copy-start.18
  94.9 3.4 copy-start.47
  95.5 2.9 copy-start.39
  100.4 11.9 %slice-start = ((s8[6291456]{0:T(1024)(128)(4,1)}), s8[4194304]{0:T(1024)(128)(4,1)S(1)}, s32[]{:S(2)}) async-start(s8[6291456]{0:T(1024)(128)(4,1)} %bitcast.188), calls=%async_computation.7 | async-start | bytes 8388608
  100.9 4.7 %copy-start.32 = (bf16[8,128,512]{2,1,0:T(8,128)(2,1)}, bf16[8,128,512]{2,1,0:T(8,128)(2,1)S(1)}, u32[]{:S(2)}) copy-start(bf16[8,128,512]{2,1,0:T(8,128)(2,1)S(1)} %get-tuple-element.209) | copy-start | bytes 3145732
  101.0 11.3 %copy-start.8 = (f32[8,128,512]{2,1,0:T(8,128)}, f32[8,128,512]{2,1,0:T(8,128)S(1)}, u32[]{:S(2)}) copy-start(f32[8,128,512]{2,1,0:T(8,128)S(1)} %get-tuple-element.210.normal_ref) | copy-start | bytes 6291460
  101.0 11.3 %slice-start.1 = ((s8[6291456]{0:T(1024)(128)(4,1)}), s8[2097152]{0:T(1024)(128)(4,1)S(1)}, s32[]{:S(2)}) async-start(s8[6291456]{0:T(1024)(128)(4,1)} %bitcast.188), calls=%async_computation.8 | async-start | bytes 4194304
  105.6 6.6 %copy-start.2 = (bf16[8,128,1536]{2,1,0:T(8,128)(2,1)}, bf16[8,128,1536]{2,1,0:T(8,128)(2,1)S(1)}, u32[]{:S(2)}) copy-start(bf16[8,128,1536]{2,1,0:T(8,128)(2,1)S(1)} %add_convert_fusion.1.packed_ref) | copy-start | bytes 9437188
  112.3 1.1 copy-start.10
  113.4 5.0 %copy-start.26 = (f32[8,128,512]{2,1,0:T(8,128)}, f32[8,128,512]{2,1,0:T(8,128)S(1)}, u32[]{:S(2)}) copy-start(f32[8,128,512]{2,1,0:T(8,128)S(1)} %get-tuple-element.253) | copy-start | bytes 6291460
  114.2 4.2 %copy-start.12 = (bf16[8,128,512]{2,1,0:T(8,128)(2,1)}, bf16[8,128,512]{2,1,0:T(8,128)(2,1)S(1)}, u32[]{:S(2)}) copy-start(bf16[8,128,512]{2,1,0:T(8,128)(2,1)S(1)} %fusion.40) | copy-start | bytes 3145732
  114.2 7.8 %slice-start.4 = ((s8[6291456]{0:T(1024)(128)(4,1)}), s8[2097152]{0:T(1024)(128)(4,1)S(1)}, s32[]{:S(2)}) async-start(s8[6291456]{0:T(1024)(128)(4,1)} %bitcast.199), calls=%async_computation.11 | async-start | bytes 4194304
  118.4 3.6 slice-start.5
  121.1 17.4 %copy-start.21 = (f32[8,128,512]{2,1,0:T(8,128)}, f32[8,128,512]{2,1,0:T(8,128)S(1)}, u32[]{:S(2)}) copy-start(f32[8,128,512]{2,1,0:T(8,128)S(1)} %get-tuple-element.255) | copy-start | bytes 6291460
  122.0 1.9 copy-start.33
  123.8 5.2 %copy-start.4 = (bf16[8,128,1536]{2,1,0:T(8,128)(2,1)}, bf16[8,128,1536]{2,1,0:T(8,128)(2,1)S(1)}, u32[]{:S(2)}) copy-start(bf16[8,128,1536]{2,1,0:T(8,128)(2,1)S(1)} %add_convert_fusion.packed_ref) | copy-start | bytes 9437188
  129.1 1.0 copy-start.11
  130.1 5.2 %copy-start.23 = (f32[8,128,512]{2,1,0:T(8,128)}, f32[8,128,512]{2,1,0:T(8,128)S(1)}, u32[]{:S(2)}) copy-start(f32[8,128,512]{2,1,0:T(8,128)S(1)} %get-tuple-element.257) | copy-start | bytes 6291460
  165.3 15.4 %copy-start.14 = (bf16[8,128,512]{2,1,0:T(8,128)(2,1)}, bf16[8,128,512]{2,1,0:T(8,128)(2,1)S(1)}, u32[]{:S(2)}) copy-start(bf16[8,128,512]{2,1,0:T(8,128)(2,1)S(1)} %fusion.45) | copy-start | bytes 3145732
  165.3 3.2 copy-start.20
  189.8 1.6 copy-start.24
  191.4 2.7 copy-start.28
  194.2 3.8 copy-start.5
  195.0 1.0 copy-start.29
  196.0 11.6 %copy-start.25 = (f32[8,128,512]{2,1,0:T(8,128)S(1)}, f32[8,128,512]{2,1,0:T(8,128)}, u32[]{:S(2)}) copy-start(f32[8,128,512]{2,1,0:T(8,128)} %copy-done.23) | copy-start | bytes 6291460
  198.0 9.7 %copy-start.22 = (f32[8,128,512]{2,1,0:T(8,128)S(1)}, f32[8,128,512]{2,1,0:T(8,128)}, u32[]{:S(2)}) copy-start(f32[8,128,512]{2,1,0:T(8,128)} %copy-done.21) | copy-start | bytes 6291460
  198.0 16.1 %slice-start.2 = ((s8[6291456]{0:T(1024)(128)(4,1)}), s8[4194304]{0:T(1024)(128)(4,1)S(1)}, s32[]{:S(2)}) async-start(s8[6291456]{0:T(1024)(128)(4,1)} %bitcast.193), calls=%async_computation.9 | async-start | bytes 8388608
  207.6 28.2 %copy-start = (bf16[8,128,1536]{2,1,0:T(8,128)(2,1)}, bf16[8,128,1536]{2,1,0:T(8,128)(2,1)S(1)}, u32[]{:S(2)}) copy-start(bf16[8,128,1536]{2,1,0:T(8,128)(2,1)S(1)} %attention_back.2) | copy-start | bytes 9437188
  207.6 6.4 %slice-start.3 = ((s8[6291456]{0:T(1024)(128)(4,1)}), s8[2097152]{0:T(1024)(128)(4,1)S(1)}, s32[]{:S(2)}) async-start(s8[6291456]{0:T(1024)(128)(4,1)} %bitcast.193), calls=%async_computation.10 | async-start | bytes 4194304
  213.3 1.2 copy-start.13
  214.1 12.7 %copy-start.6 = (bf16[8,128,512]{2,1,0:T(8,128)(2,1)}, bf16[8,128,512]{2,1,0:T(8,128)(2,1)S(1)}, u32[]{:S(2)}) copy-start(bf16[8,128,512]{2,1,0:T(8,128)(2,1)S(1)} %fusion.51) | copy-start | bytes 3145732
  214.5 12.3 %copy-start.27 = (f32[8,128,512]{2,1,0:T(8,128)S(1)}, f32[8,128,512]{2,1,0:T(8,128)}, u32[]{:S(2)}) copy-start(f32[8,128,512]{2,1,0:T(8,128)} %copy-done.26) | copy-start | bytes 6291460
  226.8 2.1 copy-start.15
  226.8 3.3 copy-start.16
  230.1 1.7 copy-start.31
  239.2 1.9 copy-start.3
  241.1 9.4 %copy-start.7 = (bf16[8,128,512]{2,1,0:T(8,128)(2,1)S(1)}, bf16[8,128,512]{2,1,0:T(8,128)(2,1)}, u32[]{:S(2)}) copy-start(bf16[8,128,512]{2,1,0:T(8,128)(2,1)} %copy-done.6) | copy-start | bytes 3145732
  241.1 9.6 %copy-start.30 = (bf16[8,128,512]{2,1,0:T(8,128)(2,1)S(1)}, bf16[8,128,512]{2,1,0:T(8,128)(2,1)}, u32[]{:S(2)}) copy-start(bf16[8,128,512]{2,1,0:T(8,128)(2,1)} %fusion.52) | copy-start | bytes 3145732
  250.5 2.2 copy-start.1
  252.7 4.5 %copy-start.9 = (f32[8,128,512]{2,1,0:T(8,128)S(1)}, f32[8,128,512]{2,1,0:T(8,128)}, u32[]{:S(2)}) copy-start(f32[8,128,512]{2,1,0:T(8,128)} %copy-done.8) | copy-start | bytes 6291460
  252.7 4.5 %copy-start.17 = (f32[8,128,1]{2,1,0:T(8,128)S(1)}, f32[8,128,1]{2,1,0:T(8,128)}, u32[]{:S(2)}) copy-start(f32[8,128,1]{2,1,0:T(8,128)} %copy.60.inverse_ref) | copy-start | bytes 12292
  259.0 1.1 copy-start.19
  259.1 1.9 copy-start.48
  354.7 1.4 copy-start.44
  356.7 10.9 %copy-start.43 = (f32[4928]{0:T(1024)S(1)}, f32[4928]{0:T(1024)}, u32[]{:S(2)}) copy-start(f32[4928]{0:T(1024)} %param.25) | copy-start | bytes 59140
  356.7 11.0 %copy-start.45 = (f32[4928]{0:T(1024)S(1)}, f32[4928]{0:T(1024)}, u32[]{:S(2)}) copy-start(f32[4928]{0:T(1024)} %param.29) | copy-start | bytes 59140
  356.7 11.0 %copy-start.46 = (f32[4928]{0:T(1024)S(1)}, f32[4928]{0:T(1024)}, u32[]{:S(2)}) copy-start(f32[4928]{0:T(1024)} %param.33) | copy-start | bytes 59140
  356.7 11.6 %copy-start.35 = (f32[2,32,2048]{2,1,0:T(8,128)S(1)}, f32[2,32,2048]{2,1,0:T(8,128)}, u32[]{:S(2)}) copy-start(f32[2,32,2048]{2,1,0:T(8,128)} %refs_4_.1) | copy-start | bytes 1572868
  356.7 11.6 %copy-start.40 = (f32[2,32,2048]{2,1,0:T(8,128)S(1)}, f32[2,32,2048]{2,1,0:T(8,128)}, u32[]{:S(2)}) copy-start(f32[2,32,2048]{2,1,0:T(8,128)} %param.30) | copy-start | bytes 1572868
  356.7 11.6 %copy-start.41 = (f32[2,32,2048]{2,1,0:T(8,128)S(1)}, f32[2,32,2048]{2,1,0:T(8,128)}, u32[]{:S(2)}) copy-start(f32[2,32,2048]{2,1,0:T(8,128)} %param.34) | copy-start | bytes 1572868
  356.8 11.6 %copy-start.42 = (f32[2,32,2048]{2,1,0:T(8,128)S(1)}, f32[2,32,2048]{2,1,0:T(8,128)}, u32[]{:S(2)}) copy-start(f32[2,32,2048]{2,1,0:T(8,128)} %get-tuple-element.146) | copy-start | bytes 1572868
  356.8 13.1 %copy-start.38 = (f32[2,32,4096]{2,1,0:T(8,128)S(1)}, f32[2,32,4096]{2,1,0:T(8,128)}, u32[]{:S(2)}) copy-start(f32[2,32,4096]{2,1,0:T(8,128)} %get-tuple-element.147) | copy-start | bytes 3145732
  367.6 2.2 copy-start.34
  367.6 2.2 copy-start.36
  367.6 2.2 copy-start.37
Sparse Core Ops, SparseCore 0:
  190.0 70.3 reduce-scatter.1

commit v13 on v12

--- a/solution.py
+++ b/solution.py
@@ -1340,6 +1340,51 @@
     )(middle, d_down, weights, weights, up_bias.reshape(1, FF))
 
 
+def products_kernel(left_one, right_one, left_two, right_two, out_ref):
+    step = pl.program_id(0)
+    half_way = pl.num_programs(0) // 2
+
+    def fill(left, right):
+        def rows_of(j, carry):
+            at = pl.ds(pl.multiple_of(j * 128, 128), 128)
+            out_ref[at, :] = contract(left[:, at], right[...], 0, 0).astype(jnp.bfloat16)
+            return carry
+
+        lax.fori_loop(0, D // 128, rows_of, 0)
+
+    @pl.when(step < half_way)
+    def _():
+        fill(left_one, right_one)
+
+    @pl.when(step >= half_way)
+    def _():
+        fill(left_two, right_two)
+
+
+def products(pairs):
+    (left_one, right_one), (left_two, right_two) = pairs
+    tokens = left_one.shape[0]
+    columns = FF // 2
+    left = pl.BlockSpec((tokens, D), lambda i: (0, 0))
+    return pl.pallas_call(
+        products_kernel,
+        grid=(4,),
+        out_shape=jax.ShapeDtypeStruct((D, 2 * FF), jnp.bfloat16),
+        in_specs=[
+            left,
+            pl.BlockSpec((tokens, columns), lambda i: (0, jnp.minimum(i, 1))),
+            left,
+            pl.BlockSpec((tokens, columns), lambda i: (0, jnp.maximum(i - 2, 0))),
+        ],
+        out_specs=pl.BlockSpec((D, columns), lambda i: (0, i)),
+        compiler_params=pltpu.CompilerParams(vmem_limit_bytes=24 * 1024 * 1024),
+        cost_estimate=pl.CostEstimate(
+            flops=4 * tokens * D * FF, bytes_accessed=4 * D * FF + 8 * tokens * FF, transcendentals=0
+        ),
+        name="products",
+    )(left_one, right_one, left_two, right_two)
+
+
 def embed_back_kernel(grad_ref, normal_ref, inverse_ref, gain_ref, rows_ref, vec_ref):
     grad, normal = grad_ref[0], normal_ref[0]
     scaled = grad * gain_ref[...]
@@ -1768,7 +1813,10 @@
         by_scatter = []
 
         def scatter(pairs, after):
-            both = jnp.concatenate([weight_gradient(*pair) for pair in pairs], axis=1)
+            if by_hand:
+                both = products(pairs)
+            else:
+                both = jnp.concatenate([weight_gradient(*pair) for pair in pairs], axis=1)
             both, after = lax.optimization_barrier((both, after))
             by_scatter.append(lax.psum_scatter(both, "zero", scatter_dimension=0, tiled=True))
             return after

time: 388 us -> 397 us (1.023)
  local copies, waits for them, and re-layouts: 16.2 us -> 25.1 us
  Pallas kernels: 253 us -> 261 us
  other arithmetic: 45.6 us -> 41.5 us
    unnamed x116 -> x126, local copies, waits for them, and re-layouts: 10.1 us -> 19.1 us
    pallas_call x0 -> x1, Pallas kernels: none -> 8.66 us  [products(): pl.pallas_call(products_kernel, grid=(4,), out_shape=jax.ShapeDtypeStruct...]
    dot_general x2 -> x0, matrix products: 4.75 us -> none  [weight_gradient(): lax.dot_general(left, right, (((0,), (0,)), ((), ())), preferred_element_...]
  transfers between devices with their start and end apart: 1 -> 1, of which waited for: 0 -> 0; matrix products, arithmetic and copies ran while one was open for 9% -> 8% of each run, Pallas kernels for 9% -> 8%
where the time goes in v13:
time: 397 us; the launch traced here: 390 us
  Pallas kernels  261 us (66%)
  matrix products  42.9 us (11%)
  other arithmetic  41.5 us (10%)
  local copies, waits for them, and re-layouts  25.1 us (6%)
  between operations  17.4 us (4%)
    pallas_call x1, Pallas kernels, exchange_gradients(): pl.pallas_call(functools.partial(gradient_kernel, tuple(chunks), len(pair...  89.3 us
    pallas_call x1, Pallas kernels, exchange_start(): pl.pallas_call(functools.partial(start_kernel, shard_rows, room), out_sha...  83.1 us
    pallas_call x4, Pallas kernels, attention_call(): pl.pallas_call(kernel, grid=(count,), out_shape=jax.ShapeDtypeStruct((cou...  30.7 us
    pallas_call x2, Pallas kernels, feed_back(): pl.pallas_call(feed_back_kernel, grid=(tokens // rows,), out_shape=(jax.S...  25.1 us
    pallas_call x1, Pallas kernels, contrastive(): pl.pallas_call(contrastive_kernel, out_shape=(jax.ShapeDtypeStruct((8, 12...  22.7 us
    dot_general x7, matrix products, matmul(): return jnp.dot(left, right, preferred_element_type=jnp.float32)  20 us
    unnamed x126, local copies, waits for them, and re-layouts  19.1 us
    dot_general x2, matrix products, layer_backward(): jnp.einsum('nsp,dp->nsd', d_packed, in_weights, preferred_element_type=jn...  10.9 us
  transfers between devices with their start and end apart: 1, of which 0 were waited for; matrix products, arithmetic and copies ran while one was open for 8% of the time, Pallas kernels for 8%

profile of v13, /device:TPU:0, one launch (start us, length us, event | category | flops | bytes accessed | tf_op | source)
XLA Modules:
  0.0 389.9 jit_solution(891175829011181898)
XLA Ops:
  7.2 0.9 copy.54.refs_0_
  8.1 0.7 convert_element_type.213
  8.9 0.7 convert_bitcast_fusion
  9.6 0.7 convert.15
  10.3 83.1 %exchange_start.1 = (s32[1024,1]{1,0:T(8,128)S(1)}, s32[1024,1]{1,0:T(8,128)S(1)}, bf16[32,8,128]{2,1,0:T(8,128)(2,1)S(1)}, s32[32,1,128]{2,1,0:T(1,128)S(1)}, b...) custom-call(s32[1024,1]{1,0:T(8,128)S(1)} %copy.54.refs_0_, ...), custom_call_target="tpu_custom_call" | custom-call | bytes 150000000 | tf_op jit(solution)/shard_map/exchange_start/pallas_call | solution.py:965
  94.0 0.7 slice_reduce_fusion.1
  95.5 2.8 fusion.43
  98.3 0.8 while.22
  99.5 0.6 multiply_reduce_fusion.13
  100.7 4.6 %add_convert_fusion.1.packed_ref = bf16[8,128,1536]{2,1,0:T(8,128)(2,1)S(1)} fusion(bf16[8,128,512]{2,1,0:T(8,128)(2,1)S(1)} %get-tuple-element.209, f32[1536]{0:T(1024)S(1)} %get-tuple-element.251, bf16[512,6144]{1,0:T(8,128)(2,1)} %bitcast.181), kind=kOutput, calls=%fused_computation.41 | convolution fusion | flops 1613758464 | bytes 5773312 | tf_op jit(solution)/shard_map/dot_general | solution.py:78
  105.3 6.7 %attention.2 = bf16[8,128,512]{2,1,0:T(8,128)(2,1)S(1)} custom-call(f32[8,1,128]{2,1,0:T(1,128)S(1)} %compare_convert_fusion.mask_ref, bf16[8,128,1536]{2,1,0:T(8,128)(2,1)S(1)} %add_convert_fusion.1.packed_ref), custom_call_target="tpu_custom_call" | custom-call | flops 1000000000 | bytes 5242880 | tf_op jit(solution)/shard_map/attention/pallas_call | solution.py:1270
  112.0 0.9 fusion.78
  113.9 4.2 %fusion.17 = bf16[8,128,2048]{2,1,0:T(8,128)(2,1)S(1)} fusion(f32[2048]{0:T(1024)S(1)} %get-tuple-element.237, bf16[8,128,512]{2,1,0:T(8,128)(2,1)S(1)} %fusion.40, bf16[512,6144]{1,0:T(8,128)(2,1)S(1)} %bitcast.187), kind=kOutput, calls=%fused_computation.32 | convolution fusion | flops 2168455168 | bytes 7348224 | tf_op jit(solution)/shard_map/dot_general | solution.py:78
  118.1 2.7 fusion.79
  121.7 1.8 add_convert_fusion.packed_ref
  123.5 5.2 %attention.3 = bf16[8,128,512]{2,1,0:T(8,128)(2,1)S(1)} custom-call(f32[8,1,128]{2,1,0:T(1,128)S(1)} %compare_convert_fusion.mask_ref, bf16[8,128,1536]{2,1,0:T(8,128)(2,1)S(1)} %add_convert_fusion.packed_ref), custom_call_target="tpu_custom_call" | custom-call | flops 1000000000 | bytes 5242880 | tf_op jit(solution)/shard_map/attention/pallas_call | solution.py:1270
  128.8 1.0 fusion.80
  130.6 4.6 %fusion.22 = bf16[8,128,2048]{2,1,0:T(8,128)(2,1)S(1)} fusion(f32[2048]{0:T(1024)S(1)} %get-tuple-element.236, bf16[8,128,512]{2,1,0:T(8,128)(2,1)S(1)} %fusion.41, bf16[512,6144]{1,0:T(8,128)(2,1)S(1)} %bitcast.197), kind=kOutput, calls=%fused_computation.37 | convolution fusion | flops 2168455168 | bytes 7348224 | tf_op jit(solution)/shard_map/dot_general | solution.py:78
  135.2 2.7 fusion.81
  138.5 1.2 multiply_reduce_fusion.10
  139.9 22.7 %contrastive.1 = (f32[8,128]{1,0:T(8,128)S(1)}, f32[2,2,8,512]{3,2,1,0:T(8,128)S(1)}) custom-call(bf16[2,8,512]{2,1,0:T(8,128)(2,1)S(1)} %reshape.574.block_ref, s32[128,128]{1,0:T(8,128)S(1)} %reshape.575.false_ref, s32[128,1]{1,0:T(8,128)S(1)} %reshape_reshape.16.pair_ref), custom_call_target="tpu_custom_call" | custom-call | flops 1000000000 | bytes 3000000 | tf_op jit(solution)/shard_map/contrastive/pallas_call | solution.py:1173
  162.7 1.4 fusion.35
  164.1 2.1 fusion.45
  166.3 3.2 copy-done.23
  169.5 12.5 %feed_back.2 = (bf16[1024,2048]{1,0:T(8,128)(2,1)S(1)}, bf16[1024,2048]{1,0:T(8,128)(2,1)S(1)}, f32[1024,512]{1,0:T(8,128)S(1)}, f32[1,2048]{1,0:T(1,128)S(1)}) custom-call(bf16[1024,512]{1,0:T(8,128)(2,1)S(1)} %bitcast.174, bf16[1024,512]{1,0:T(8,128)(2,1)S(1)} %bitcast.170, bf16[512,6144]{1,0:T(8,128)(2,1)S(1)} %bitcast.199, ...), custom_call_target="tpu_custom_call" | custom-call | flops 6442450944 | bytes 12582912 | tf_op jit(solution)/shard_map/feed_back/pallas_call | solution.py:1324
  181.9 1.9 fusion.44
  183.8 8.7 %products.1 = bf16[512,4096]{1,0:T(8,128)(2,1)S(1)} custom-call(bf16[1024,512]{1,0:T(8,128)(2,1)S(1)} %bitcast.175, bf16[1024,2048]{1,0:T(8,128)(2,1)S(1)} %get-tuple-element.129.right_one, bf16[1024,512]{1,0:T(8,128)(2,1)S(1)} %bitcast.171, bf16[1024,2048]{1,0:T(8,128)(2,1)S(1)} %get-tuple-element.130.right_two), custom_call_target="tpu_custom_call" | custom-call | flops 4294967296 | bytes 20971520 | tf_op jit(solution)/shard_map/products/pallas_call | solution.py:1369
  192.5 2.0 copy-done.14
  194.5 1.6 copy-done.29
  196.1 2.8 multiply_reduce_fusion.1
  198.9 0.8 fusion.49
  199.7 1.0 copy-done.35
  200.7 1.8 convolution_convert_fusion.1.grad_ref
  202.5 9.5 %attention_back.2 = bf16[8,128,1536]{2,1,0:T(8,128)(2,1)S(1)} custom-call(f32[8,1,128]{2,1,0:T(1,128)S(1)} %compare_convert_fusion.mask_ref, bf16[8,128,1536]{2,1,0:T(8,128)(2,1)S(1)} %copy-done.5, bf16[8,128,512]{2,1,0:T(8,128)(2,1)S(1)} %convolution_convert_fusion.1.grad_ref), custom_call_target="tpu_custom_call" | custom-call | flops 1000000000 | bytes 5242880 | tf_op jit(solution)/shard_map/attention_back/pallas_call | solution.py:1270
  212.0 7.4 %multiply_reduce_fusion.2 = (f32[512]{0:T(512)S(1)}, f32[8,128]{1,0:T(8,128)S(1)}, f32[8,128]{1,0:T(8,128)S(1)}, f32[512]{0:T(512)S(1)}, f32[8,128,512]{2,1,0:T(8,128)S(1)}) fusion(f32[8,128]{1,0:T(8,128)S(1)} %add_rsqrt_fusion.2, f32[8,128,512]{2,1,0:T(8,128)} %copy-done.24, f32[8,128]{1,0:T(8,128)S(1)} %broadcast_multiply_fusion.10, ...), kind=kOutput, calls=%fused_computation.72 | convolution fusion | flops 1620571136 | bytes 13168640 | tf_op jit(solution)/shard_map/nsp,dp->nsd/dot_general | solution.py:1525
  219.4 0.8 fusion.51
  220.7 3.3 copy-done.22
  224.0 12.6 %feed_back.3 = (bf16[1024,2048]{1,0:T(8,128)(2,1)S(1)}, bf16[1024,2048]{1,0:T(8,128)(2,1)S(1)}, f32[1024,512]{1,0:T(8,128)S(1)}, f32[1,2048]{1,0:T(1,128)S(1)}) custom-call(bf16[1024,512]{1,0:T(8,128)(2,1)S(1)} %bitcast.169, bf16[1024,512]{1,0:T(8,128)(2,1)S(1)} %bitcast.164, bf16[512,6144]{1,0:T(8,128)(2,1)S(1)} %bitcast.189, ...), custom_call_target="tpu_custom_call" | custom-call | flops 6442450944 | bytes 12582912 | tf_op jit(solution)/shard_map/feed_back/pallas_call | solution.py:1324
  236.7 1.9 multiply_reduce_fusion.3
  238.7 1.3 copy-done.18
  240.1 1.6 fusion.52
  241.7 1.0 copy.60.inverse_ref
  243.2 0.7 reduce.24
  243.9 0.7 reduce.23
  244.6 2.1 convolution_convert_fusion.grad_ref
  246.8 1.9 copy-done.3
  248.6 9.4 %attention_back.3 = bf16[8,128,1536]{2,1,0:T(8,128)(2,1)S(1)} custom-call(f32[8,1,128]{2,1,0:T(1,128)S(1)} %compare_convert_fusion.mask_ref, bf16[8,128,1536]{2,1,0:T(8,128)(2,1)S(1)} %copy-done.3, bf16[8,128,512]{2,1,0:T(8,128)(2,1)S(1)} %convolution_convert_fusion.grad_ref), custom_call_target="tpu_custom_call" | custom-call | flops 1000000000 | bytes 5242880 | tf_op jit(solution)/shard_map/attention_back/pallas_call | solution.py:1270
  259.0 1.3 copy-done.36
  261.5 0.8 copy-done.32
  262.4 0.6 copy-done.39
  263.0 3.5 convolution_add_fusion.grad_ref
  266.5 1.6 embed_back.1
  268.7 0.8 copy.64
  269.6 0.7 reshape_squeeze.3.refs_15_
  270.3 0.5 slice.245
  270.8 2.7 fusion.29
  273.5 89.3 %exchange_gradients.1 = (f32[2,32,2048]{2,1,0:T(8,128)}, f32[2,32,4096]{2,1,0:T(8,128)}, f32[1908,512]{1,0:T(8,128)}, f32[40,128]{1,0:T(8,128)}, f32[8,128]{1,0:T(8,128)}) custom-call(bf16[1024,512]{1,0:T(8,128)(2,1)} %bitcast.206, bf16[1024,1536]{1,0:T(8,128)(2,1)} %bitcast.163, bf16[1024,512]{1,0:T(8,128)(2,1)} %bitcast.166, bf16[1024,512]{1,0:T(8,128)(2,1)} %bitcast.204, ...), custom_call_target="tpu_custom_call" | custom-call | bytes 200000000 | tf_op jit(solution)/shard_map/exchange_gradients/pallas_call | solution.py:600
  362.8 1.2 slice.257
  364.0 1.0 while.23
  365.8 0.6 slice_multiply_fusion.1
  366.4 4.1 %fusion.63 = (bf16[2,32,4096]{2,1,0:T(8,128)(2,1)}, f32[2,32,4096]{2,1,0:T(8,128)}, f32[2,32,4096]{2,1,0:T(8,128)}, f32[2,32,4096]{2,1,0:T(8,128)}) fusion(f32[2,32,4096]{2,1,0:T(8,128)S(1)} %copy-done.42, f32[2,32,4096]{2,1,0:T(8,128)} %get-tuple-element.147, f32[]{:T(128)S(6)} %min.3, f32[2,32,4096]{2,1,0:T(8,128)S(1)} %copy-done.46, f32[2,32,4096]{2,1,0:T(8,128)} %param.35), kind=kLoop, calls=%fused_computation.189 | loop fusion | flops 4194304 | bytes 7864324 | tf_op jit(solution)/shard_map/convert_element_type | solution.py:1941
  370.6 2.9 fusion.65
  373.5 0.6 fusion.67
  374.1 7.6 %fusion.69 = (bf16[1908,512]{1,0:T(8,128)(2,1)}, f32[1908,512]{1,0:T(8,128)}, f32[1908,512]{1,0:T(8,128)}, f32[1908,512]{1,0:T(8,128)}) fusion(f32[1908,512]{1,0:T(8,128)S(1)} %copy-done.34, f32[1908,512]{1,0:T(8,128)} %get-tuple-element.144, f32[]{:T(128)S(6)} %min.3, f32[1908,512]{1,0:T(8,128)S(1)} %copy-done.43, f32[1908,512]{1,0:T(8,128)S(1)} %copy-done.44), kind=kLoop, calls=%fused_computation.192 | loop fusion | flops 15630336 | bytes 29306884 | tf_op jit(solution)/shard_map/convert_element_type | solution.py:1938
  (202 shorter events, 9.6 us)
Async XLA Ops:
  7.2 266.3 %reduce-scatter.2.cloned.1.call-start = ((), (), s32[]{:S(2)}) async-start(), calls=%async_computation.5 | async-start | bytes 4456448 | tf_op jit(solution)/shard_map/reduce_scatter | solution.py:1821
  10.2 83.4 %copy-start.55 = (s32[4,2]{0,1:T(2,128)S(1)}, s32[4,2]{0,1:T(2,128)}, u32[]{:S(2)}) copy-start(s32[4,2]{0,1:T(2,128)} %param.21) | copy-start | bytes 100
  93.3 2.1 copy-start.20
  94.9 3.4 copy-start.53
  95.5 2.9 copy-start.47
  100.1 11.9 %slice-start = ((s8[6291456]{0:T(1024)(128)(4,1)}), s8[4194304]{0:T(1024)(128)(4,1)S(1)}, s32[]{:S(2)}) async-start(s8[6291456]{0:T(1024)(128)(4,1)} %bitcast.184), calls=%async_computation.7 | async-start | bytes 8388608
  100.6 4.7 %copy-start.40 = (bf16[8,128,512]{2,1,0:T(8,128)(2,1)}, bf16[8,128,512]{2,1,0:T(8,128)(2,1)S(1)}, u32[]{:S(2)}) copy-start(bf16[8,128,512]{2,1,0:T(8,128)(2,1)S(1)} %get-tuple-element.209) | copy-start | bytes 3145732
  100.6 11.4 %copy-start.8 = (f32[8,128,512]{2,1,0:T(8,128)}, f32[8,128,512]{2,1,0:T(8,128)S(1)}, u32[]{:S(2)}) copy-start(f32[8,128,512]{2,1,0:T(8,128)S(1)} %get-tuple-element.210.normal_ref) | copy-start | bytes 6291460
  100.6 11.4 %slice-start.1 = ((s8[6291456]{0:T(1024)(128)(4,1)}), s8[2097152]{0:T(1024)(128)(4,1)S(1)}, s32[]{:S(2)}) async-start(s8[6291456]{0:T(1024)(128)(4,1)} %bitcast.184), calls=%async_computation.8 | async-start | bytes 4194304
  105.3 6.7 %copy-start.2 = (bf16[8,128,1536]{2,1,0:T(8,128)(2,1)}, bf16[8,128,1536]{2,1,0:T(8,128)(2,1)S(1)}, u32[]{:S(2)}) copy-start(bf16[8,128,1536]{2,1,0:T(8,128)(2,1)S(1)} %add_convert_fusion.1.packed_ref) | copy-start | bytes 9437188
  112.0 1.1 copy-start.10
  113.0 5.0 %copy-start.30 = (f32[8,128,512]{2,1,0:T(8,128)}, f32[8,128,512]{2,1,0:T(8,128)S(1)}, u32[]{:S(2)}) copy-start(f32[8,128,512]{2,1,0:T(8,128)S(1)} %get-tuple-element.253) | copy-start | bytes 6291460
  113.9 4.2 %copy-start.12 = (bf16[8,128,512]{2,1,0:T(8,128)(2,1)}, bf16[8,128,512]{2,1,0:T(8,128)(2,1)S(1)}, u32[]{:S(2)}) copy-start(bf16[8,128,512]{2,1,0:T(8,128)(2,1)S(1)} %fusion.40) | copy-start | bytes 3145732
  113.9 7.8 %slice-start.2 = ((s8[6291456]{0:T(1024)(128)(4,1)}), s8[2097152]{0:T(1024)(128)(4,1)S(1)}, s32[]{:S(2)}) async-start(s8[6291456]{0:T(1024)(128)(4,1)} %bitcast.193), calls=%async_computation.9 | async-start | bytes 4194304
  118.1 3.6 slice-start.3
  120.8 17.7 %copy-start.24 = (f32[8,128,512]{2,1,0:T(8,128)}, f32[8,128,512]{2,1,0:T(8,128)S(1)}, u32[]{:S(2)}) copy-start(f32[8,128,512]{2,1,0:T(8,128)S(1)} %get-tuple-element.255) | copy-start | bytes 6291460
  121.6 1.9 copy-start.41
  123.5 5.2 %copy-start.4 = (bf16[8,128,1536]{2,1,0:T(8,128)(2,1)}, bf16[8,128,1536]{2,1,0:T(8,128)(2,1)S(1)}, u32[]{:S(2)}) copy-start(bf16[8,128,1536]{2,1,0:T(8,128)(2,1)S(1)} %add_convert_fusion.packed_ref) | copy-start | bytes 9437188
  128.7 1.0 copy-start.11
  129.8 5.4 %copy-start.28 = (f32[8,128,512]{2,1,0:T(8,128)}, f32[8,128,512]{2,1,0:T(8,128)S(1)}, u32[]{:S(2)}) copy-start(f32[8,128,512]{2,1,0:T(8,128)S(1)} %get-tuple-element.257) | copy-start | bytes 6291460
  137.9 24.7 %copy-start.26 = (f32[8,128,512]{2,1,0:T(8,128)}, f32[8,128,512]{2,1,0:T(8,128)S(1)}, u32[]{:S(2)}) copy-start(f32[8,128,512]{2,1,0:T(8,128)S(1)} %get-tuple-element.259) | copy-start | bytes 6291460
  166.3 17.6 %copy-start.15 = (bf16[8,128,512]{2,1,0:T(8,128)(2,1)}, bf16[8,128,512]{2,1,0:T(8,128)(2,1)S(1)}, u32[]{:S(2)}) copy-start(bf16[8,128,512]{2,1,0:T(8,128)(2,1)S(1)} %fusion.45) | copy-start | bytes 3145732
  166.3 3.2 copy-start.23
  169.4 12.5 %copy-start.27 = (f32[8,128,512]{2,1,0:T(8,128)S(1)}, f32[8,128,512]{2,1,0:T(8,128)}, u32[]{:S(2)}) copy-start(f32[8,128,512]{2,1,0:T(8,128)} %copy-done.26) | copy-start | bytes 6291460
  192.5 2.0 copy-start.14
  194.5 1.6 copy-start.29
  196.1 2.8 copy-start.33
  198.9 3.6 copy-start.5
  199.7 1.0 copy-start.35
  211.9 49.0 %copy-start = (bf16[8,128,1536]{2,1,0:T(8,128)(2,1)}, bf16[8,128,1536]{2,1,0:T(8,128)(2,1)S(1)}, u32[]{:S(2)}) copy-start(bf16[8,128,1536]{2,1,0:T(8,128)(2,1)S(1)} %attention_back.2) | copy-start | bytes 9437188
  212.0 7.4 %copy-start.25 = (f32[8,128,512]{2,1,0:T(8,128)S(1)}, f32[8,128,512]{2,1,0:T(8,128)}, u32[]{:S(2)}) copy-start(f32[8,128,512]{2,1,0:T(8,128)} %copy-done.24) | copy-start | bytes 6291460
  219.4 1.2 copy-start.13
  220.2 16.4 %copy-start.6 = (bf16[8,128,512]{2,1,0:T(8,128)(2,1)}, bf16[8,128,512]{2,1,0:T(8,128)(2,1)S(1)}, u32[]{:S(2)}) copy-start(bf16[8,128,512]{2,1,0:T(8,128)(2,1)S(1)} %fusion.51) | copy-start | bytes 3145732
  220.7 3.3 copy-start.22
  224.0 12.7 %copy-start.31 = (f32[8,128,512]{2,1,0:T(8,128)S(1)}, f32[8,128,512]{2,1,0:T(8,128)}, u32[]{:S(2)}) copy-start(f32[8,128,512]{2,1,0:T(8,128)} %copy-done.30) | copy-start | bytes 6291460
  236.6 2.1 copy-start.17
  236.6 3.4 copy-start.18
  240.1 1.7 copy-start.38
  246.8 1.9 copy-start.3
  248.6 9.4 %copy-start.37 = (bf16[8,128,512]{2,1,0:T(8,128)(2,1)S(1)}, bf16[8,128,512]{2,1,0:T(8,128)(2,1)}, u32[]{:S(2)}) copy-start(bf16[8,128,512]{2,1,0:T(8,128)(2,1)} %fusion.52) | copy-start | bytes 3145732
  248.6 9.6 %copy-start.7 = (bf16[8,128,512]{2,1,0:T(8,128)(2,1)S(1)}, bf16[8,128,512]{2,1,0:T(8,128)(2,1)}, u32[]{:S(2)}) copy-start(bf16[8,128,512]{2,1,0:T(8,128)(2,1)} %copy-done.6) | copy-start | bytes 3145732
  258.0 3.5 copy-start.1
  258.3 2.0 copy-start.36
  258.5 2.3 copy-start.16
  260.7 1.6 copy-start.32
  260.7 2.2 copy-start.39
  263.0 3.5 copy-start.9
  263.0 3.5 copy-start.19
  268.2 5.3 %copy-start.56 = (bf16[8,128,512]{2,1,0:T(8,128)(2,1)}, bf16[8,128,512]{2,1,0:T(8,128)(2,1)S(1)}, u32[]{:S(2)}) copy-start(bf16[8,128,512]{2,1,0:T(8,128)(2,1)S(1)} %get-tuple-element.139) | copy-start | bytes 3145732
  268.2 1.3 copy-start.21
  268.2 2.6 copy-start.54
  364.0 1.8 copy-start.50
  364.0 2.5 copy-start.42
  364.0 2.5 copy-start.46
  364.0 6.6 %copy-start.45 = (f32[2,32,2048]{2,1,0:T(8,128)S(1)}, f32[2,32,2048]{2,1,0:T(8,128)}, u32[]{:S(2)}) copy-start(f32[2,32,2048]{2,1,0:T(8,128)} %refs_4_.1) | copy-start | bytes 1572868
  364.0 6.6 %copy-start.48 = (f32[2,32,2048]{2,1,0:T(8,128)S(1)}, f32[2,32,2048]{2,1,0:T(8,128)}, u32[]{:S(2)}) copy-start(f32[2,32,2048]{2,1,0:T(8,128)} %param.30) | copy-start | bytes 1572868
  364.0 9.5 %copy-start.52 = (f32[4928]{0:T(1024)S(1)}, f32[4928]{0:T(1024)}, u32[]{:S(2)}) copy-start(f32[4928]{0:T(1024)} %param.33) | copy-start | bytes 59140
  366.4 7.0 %copy-start.51 = (f32[4928]{0:T(1024)S(1)}, f32[4928]{0:T(1024)}, u32[]{:S(2)}) copy-start(f32[4928]{0:T(1024)} %param.29) | copy-start | bytes 59140
  366.4 7.7 %copy-start.43 = (f32[1908,512]{1,0:T(8,128)S(1)}, f32[1908,512]{1,0:T(8,128)}, u32[]{:S(2)}) copy-start(f32[1908,512]{1,0:T(8,128)} %param.28) | copy-start | bytes 11722756
  366.4 7.7 %copy-start.44 = (f32[1908,512]{1,0:T(8,128)S(1)}, f32[1908,512]{1,0:T(8,128)}, u32[]{:S(2)}) copy-start(f32[1908,512]{1,0:T(8,128)} %param.32) | copy-start | bytes 11722756
  370.6 2.9 copy-start.49
  370.6 3.5 copy-start.34
Sparse Core Ops, SparseCore 0:
  194.6 70.6 reduce-scatter.1
